TPU v7x, 32 devices: a whole 2x2x4 slice. The times are simulated.
32 devices in a mesh: batch: 8 (over z, x), chan: 4 (over y, core).
Axes of the slice: x: 2, y: 2, z: 4, core: 2. Of those that a mesh axis runs over, the one named last changes fastest.
Arguments:
- features: bfloat16 [16, 8, 32, 2048], P('batch', None, None, 'chan'), may hold values from -6 to 6
- image_ids: int32 [16, 8, 32], P('batch'), may hold values from 0 to 3, as said below
- reduce_weight: bfloat16 [2048, 512], P('chan', 'batch'), may hold values from -0.125 to 0.125
- spatial_weight: bfloat16 [9, 512, 512], P(None, 'batch', 'chan'), may hold values from -0.09375 to 0.09375
- expand_weight: bfloat16 [512, 2048], P('batch', 'chan'), may hold values from -0.25 to 0.25
- head_weights: bfloat16 [9, 2048, 4, 512], P(None, 'chan', None, 'batch'), may hold values from -0.046875 to 0.046875
- distil_weights: bfloat16 [2, 9, 4, 512, 512], P(None, None, None, 'batch', 'chan'), may hold values from -0.09375 to 0.09375
- block_scale: float32 [2, 512], P(None, 'chan'), may hold values from 0.5 to 1.5
- block_shift: float32 [2, 512], P(None, 'chan'), may hold values from -0.5 to 0.5
- head_scale: float32 [4, 512], P(None, 'chan'), may hold values from 0.5 to 1.5
- head_shift: float32 [4, 512], P(None, 'chan'), may hold values from -0.5 to 0.5
- gate_bias: float32 [2, 512], P(None, 'chan'), may hold values from -3 to 3
- output_scale: float32 [2048], P('chan'), may hold values from 0.5 to 1.5
- output_shift: float32 [2048], P('chan'), may hold values from -0.5 to 0.5
- depth_cotangent: bfloat16 [16, 8, 32, 512], P('batch', None, None, 'chan'), may hold values from -6 to 6
- segment_cotangent: bfloat16 [16, 8, 32, 512], P('batch', None, None, 'chan'), may hold values from -6 to 6
Outputs:
- depth_stream: bfloat16 [16, 8, 32, 512], P('batch', None, None, 'chan')
- segment_stream: bfloat16 [16, 8, 32, 512], P('batch', None, None, 'chan')
- features_grad: float32 [16, 8, 32, 2048], P('batch', None, None, 'chan')
- reduce_grad: float32 [2048, 512], P('chan', 'batch')
- spatial_grad: float32 [9, 512, 512], P(None, 'batch', 'chan')
- expand_grad: float32 [512, 2048], P('batch', 'chan')
- heads_grad: float32 [9, 2048, 4, 512], P(None, 'chan', None, 'batch')
- distil_grad: float32 [2, 9, 4, 512, 512], P(None, None, None, 'batch', 'chan')
- block_scale_grad: float32 [2, 512], P(None, 'chan')
- block_shift_grad: float32 [2, 512], P(None, 'chan')
- head_scale_grad: float32 [4, 512], P(None, 'chan')
- head_shift_grad: float32 [4, 512], P(None, 'chan')
- gate_bias_grad: float32 [2, 512], P(None, 'chan')
- output_scale_grad: float32 [2048], P('chan')
- output_shift_grad: float32 [2048], P('chan')
Inputs may be any that keep to these rules, and one draw needn't show every extreme that they name: `image_ids`: in each canvas the ids 0, 1, 2 and 3 each mark one rectangle of pixels, and the four rectangles cover the canvas.
All inputs are finite; a program needn't handle non-finite values.
Results may differ from a plain program's by a relative error of at most 0.033.
Values may be sent and summed in bfloat16 or wider, within the bound.
A program may use at most 256 MiB of HBM per device.

v0:
```python
import jax
import jax.numpy as jnp
from jax import lax
from jax.sharding import PartitionSpec as P

EPSILON = 1e-05
OFFSETS = ((-1, -1), (-1, 0), (-1, 1), (0, -1), (0, 0), (0, 1), (1, -1), (1, 0), (1, 1))
OWN_HEAD = (0, 3)
SOURCE_START = (1, 0)


def silu_slope(values):
    sig = jax.nn.sigmoid(values)
    return sig * (1.0 + values * (1.0 - sig))


def shifted(values, vertical, lateral):
    row_count, column_count = (values.shape[1], values.shape[2])
    widths = [(0, 0)] * values.ndim
    widths[1] = (1, 1)
    widths[2] = (1, 1)
    padded = jnp.pad(values, widths)
    return padded[
        :, 1 + vertical : 1 + vertical + row_count, 1 + lateral : 1 + lateral + column_count
    ]


def tap_masks(image_ids):
    row_count, column_count = (image_ids.shape[1], image_ids.shape[2])
    padded = jnp.pad(image_ids, ((0, 0), (1, 1), (1, 1)), constant_values=-1)
    masks = []
    for vertical, lateral in OFFSETS:
        beside = padded[
            :, 1 + vertical : 1 + vertical + row_count, 1 + lateral : 1 + lateral + column_count
        ]
        masks.append((beside == image_ids).astype(jnp.float32))
    return jnp.stack(masks)


def conv_forward(inputs, weight, masks):
    total = 0.0
    for number, (vertical, lateral) in enumerate(OFFSETS):
        moved = shifted(inputs, vertical, lateral) * masks[number][..., None].astype(inputs.dtype)
        total = total + jnp.einsum(
            "nhwc,co->nhwo", moved, weight[number], preferred_element_type=jnp.float32
        )
    return total


def conv_input_grad(grads, weight, masks):
    total = 0.0
    for number, (vertical, lateral) in enumerate(OFFSETS):
        term = jnp.einsum(
            "nhwo,co->nhwc", grads, weight[number], preferred_element_type=jnp.float32
        )
        total = total + shifted(term * masks[number][..., None], -vertical, -lateral)
    return total


def conv_weight_grad(inputs, grads, masks):
    pieces = []
    for number, (vertical, lateral) in enumerate(OFFSETS):
        moved = shifted(inputs, vertical, lateral) * masks[number][..., None].astype(inputs.dtype)
        pieces.append(jnp.einsum("nhwc,nhwo->co", moved, grads, preferred_element_type=jnp.float32))
    return jnp.stack(pieces)


def pixel_sum(values):
    return jnp.sum(values, axis=(0, 1, 2))


def normalize(values, scale, shift, count):
    total, squares = lax.psum((pixel_sum(values), pixel_sum(values * values)), "batch")
    center = total / count
    inverse = lax.rsqrt(squares / count - center * center + EPSILON)
    normed = (values - center) * inverse
    return (normed, inverse, normed * scale + shift)


def grad_sums(first_sum, second_sum):
    return lax.psum((first_sum, second_sum), "batch")


def normalize_back(grads, normed, inverse, scale, shift_sum, scale_sum, count):
    return scale * inverse * (grads - (shift_sum + normed * scale_sum) / count)


def channel_gather(values):
    return lax.all_gather(values, "chan", axis=4, tiled=True)


def channel_sum(values):
    return lax.psum_scatter(
        values.astype(jnp.bfloat16), "chan", scatter_dimension=4, tiled=True
    ).astype(jnp.float32)


def fetch_weights(reduce_weight, spatial_weight, expand_weight, head_weights, distil_weights):
    return (
        lax.all_gather(reduce_weight, "batch", axis=1, tiled=True),
        lax.all_gather(spatial_weight, "batch", axis=1, tiled=True),
        lax.all_gather(expand_weight, "batch", axis=0, tiled=True),
        lax.all_gather(head_weights, "batch", axis=3, tiled=True),
        lax.all_gather(distil_weights, "batch", axis=3, tiled=True),
    )


def scatter_weights(grads):
    reduce_grad, spatial_grad, expand_grad, heads_grad, distil_grad = grads
    return (
        lax.psum_scatter(reduce_grad, "batch", scatter_dimension=1, tiled=True),
        lax.psum_scatter(spatial_grad, "batch", scatter_dimension=1, tiled=True),
        lax.psum_scatter(expand_grad, "batch", scatter_dimension=0, tiled=True),
        lax.psum_scatter(heads_grad, "batch", scatter_dimension=3, tiled=True),
        lax.psum_scatter(distil_grad, "batch", scatter_dimension=3, tiled=True),
    )


def micro_step(inputs, image_ids, depth_cot, segment_cot, gathered, small, batch_count):
    reduce_full, spatial_full, expand_full, heads_full, distil_full = gathered
    block_scale, block_shift, head_scale, head_shift, gate_bias, output_scale, output_shift = small
    masks = tap_masks(image_ids)
    canvases, row_count, column_count = image_ids.shape
    count = float(batch_count * canvases * row_count * column_count)
    first_partial = jnp.einsum(
        "nhwc,co->nhwo", inputs, reduce_full, preferred_element_type=jnp.float32
    )
    first = channel_sum(first_partial[:, :, :, None, :])
    first_norm, first_inv, first_out = normalize(first, block_scale[0:1], block_shift[0:1], count)
    first_act = jax.nn.silu(first_out).astype(jnp.bfloat16)
    first_full = channel_gather(first_act)[:, :, :, 0, :]
    second = conv_forward(first_full, spatial_full, masks)[:, :, :, None, :]
    second_norm, second_inv, second_out = normalize(
        second, block_scale[1:2], block_shift[1:2], count
    )
    second_act = jax.nn.silu(second_out).astype(jnp.bfloat16)
    second_full = channel_gather(second_act)[:, :, :, 0, :]
    third = jnp.einsum(
        "nhwc,co->nhwo", second_full, expand_full, preferred_element_type=jnp.float32
    )[:, :, :, None, :]
    third_norm, third_inv, third_out = normalize(
        third, output_scale[None], output_shift[None], count
    )
    summed = third_out[:, :, :, 0, :] + inputs.astype(jnp.float32)
    block_out = jax.nn.silu(summed).astype(jnp.bfloat16)
    heads_flat = heads_full.reshape(heads_full.shape[0], heads_full.shape[1], -1)
    head_partial = conv_forward(block_out, heads_flat, masks)
    head_pre = channel_sum(
        head_partial.reshape(head_partial.shape[:3] + (heads_full.shape[2], heads_full.shape[3]))
    )
    head_norm, head_inv, head_out = normalize(head_pre, head_scale, head_shift, count)
    head_act = jax.nn.silu(head_out).astype(jnp.bfloat16)
    head_full = channel_gather(head_act)
    head_width = head_full.shape[4]
    gate_pre = [0.0, 0.0]
    message = [0.0, 0.0]
    for number, (vertical, lateral) in enumerate(OFFSETS):
        moved = shifted(head_full, vertical, lateral) * masks[number][:, :, :, None, None].astype(
            jnp.bfloat16
        )
        for stream in range(2):
            weights_here = distil_full[stream, number]
            first_source = SOURCE_START[stream]
            sources = moved[:, :, :, first_source : first_source + 3].reshape(
                moved.shape[:3] + (3 * head_width,)
            )
            gate_pre[stream] = gate_pre[stream] + jnp.einsum(
                "nhwc,co->nhwo",
                moved[:, :, :, OWN_HEAD[stream]],
                weights_here[0],
                preferred_element_type=jnp.float32,
            )
            message[stream] = message[stream] + jnp.einsum(
                "nhwc,co->nhwo",
                sources,
                weights_here[1:].reshape(3 * head_width, -1),
                preferred_element_type=jnp.float32,
            )
    cotangents = (depth_cot.astype(jnp.float32), segment_cot.astype(jnp.float32))
    outputs, message_grads, gate_grads = ([], [], [])
    for stream in range(2):
        gate_value = jax.nn.sigmoid(gate_pre[stream] + gate_bias[stream])
        own_feature = head_act[:, :, :, OWN_HEAD[stream]].astype(jnp.float32)
        outputs.append((own_feature + gate_value * message[stream]).astype(jnp.bfloat16))
        message_grads.append((cotangents[stream] * gate_value).astype(jnp.bfloat16))
        gate_grads.append(
            (cotangents[stream] * message[stream] * gate_value * (1.0 - gate_value)).astype(
                jnp.bfloat16
            )
        )
    spread_grad = 0.0
    distil_parts = [[], []]
    for number, (vertical, lateral) in enumerate(OFFSETS):
        tap_mask = masks[number][:, :, :, None, None]
        moved = shifted(head_full, vertical, lateral) * tap_mask.astype(jnp.bfloat16)
        tap_grad = jnp.zeros(head_full.shape, jnp.float32)
        for stream in range(2):
            weights_here = distil_full[stream, number]
            first_source = SOURCE_START[stream]
            sources = moved[:, :, :, first_source : first_source + 3].reshape(
                moved.shape[:3] + (3 * head_width,)
            )
            own_grad = jnp.einsum(
                "nhwo,co->nhwc",
                gate_grads[stream],
                weights_here[0],
                preferred_element_type=jnp.float32,
            )
            source_grad = jnp.einsum(
                "nhwo,co->nhwc",
                message_grads[stream],
                weights_here[1:].reshape(3 * head_width, -1),
                preferred_element_type=jnp.float32,
            )
            tap_grad = tap_grad.at[:, :, :, OWN_HEAD[stream]].add(own_grad)
            tap_grad = tap_grad.at[:, :, :, first_source : first_source + 3].add(
                source_grad.reshape(source_grad.shape[:3] + (3, head_width))
            )
            gate_weight_grad = jnp.einsum(
                "nhwc,nhwo->co",
                moved[:, :, :, OWN_HEAD[stream]],
                gate_grads[stream],
                preferred_element_type=jnp.float32,
            )
            source_weight_grad = jnp.einsum(
                "nhwc,nhwo->co", sources, message_grads[stream], preferred_element_type=jnp.float32
            )
            distil_parts[stream].append(
                jnp.concatenate(
                    [gate_weight_grad[None], source_weight_grad.reshape(3, head_width, -1)], axis=0
                )
            )
        spread_grad = spread_grad + shifted(tap_grad * tap_mask, -vertical, -lateral)
    distil_grad = jnp.stack([jnp.stack(distil_parts[0]), jnp.stack(distil_parts[1])])
    head_grad = channel_sum(spread_grad)
    head_grad = (
        head_grad.at[:, :, :, OWN_HEAD[0]]
        .add(cotangents[0])
        .at[:, :, :, OWN_HEAD[1]]
        .add(cotangents[1])
    )
    head_grad = head_grad * silu_slope(head_out)
    gate_sums = jnp.stack(
        [pixel_sum(gate_grads[0].astype(jnp.float32)), pixel_sum(gate_grads[1].astype(jnp.float32))]
    )
    shift_sums, scale_sums = grad_sums(
        jnp.concatenate([pixel_sum(head_grad), gate_sums], axis=0), pixel_sum(head_grad * head_norm)
    )
    head_pre_grad = normalize_back(
        head_grad, head_norm, head_inv, head_scale, shift_sums[:4], scale_sums, count
    ).astype(jnp.bfloat16)
    head_pre_full = channel_gather(head_pre_grad)
    head_flat_grad = head_pre_full.reshape(head_pre_full.shape[:3] + (-1,))
    block_grad = conv_input_grad(head_flat_grad, heads_flat, masks)
    heads_grad = conv_weight_grad(block_out, head_flat_grad, masks).reshape(heads_full.shape)
    summed_grad = block_grad * silu_slope(summed)
    third_grad = summed_grad[:, :, :, None, :]
    third_shift, third_scale = grad_sums(pixel_sum(third_grad), pixel_sum(third_grad * third_norm))
    third_pre = normalize_back(
        third_grad, third_norm, third_inv, output_scale[None], third_shift, third_scale, count
    ).astype(jnp.bfloat16)[:, :, :, 0, :]
    expand_grad = jnp.einsum(
        "nhwc,nhwo->co", second_full, third_pre, preferred_element_type=jnp.float32
    )
    second_grad = channel_sum(
        jnp.einsum("nhwo,co->nhwc", third_pre, expand_full, preferred_element_type=jnp.float32)[
            :, :, :, None, :
        ]
    )
    second_grad = second_grad * silu_slope(second_out)
    second_shift, second_scale = grad_sums(
        pixel_sum(second_grad), pixel_sum(second_grad * second_norm)
    )
    second_pre = normalize_back(
        second_grad, second_norm, second_inv, block_scale[1:2], second_shift, second_scale, count
    ).astype(jnp.bfloat16)[:, :, :, 0, :]
    spatial_grad = conv_weight_grad(first_full, second_pre, masks)
    first_grad = channel_sum(conv_input_grad(second_pre, spatial_full, masks)[:, :, :, None, :])
    first_grad = first_grad * silu_slope(first_out)
    first_shift, first_scale = grad_sums(pixel_sum(first_grad), pixel_sum(first_grad * first_norm))
    first_pre = normalize_back(
        first_grad, first_norm, first_inv, block_scale[0:1], first_shift, first_scale, count
    ).astype(jnp.bfloat16)
    first_pre_full = channel_gather(first_pre)[:, :, :, 0, :]
    reduce_grad = jnp.einsum(
        "nhwc,nhwo->co", inputs, first_pre_full, preferred_element_type=jnp.float32
    )
    input_grad = summed_grad + jnp.einsum(
        "nhwo,co->nhwc", first_pre_full, reduce_full, preferred_element_type=jnp.float32
    )
    weight_grads = (reduce_grad, spatial_grad, expand_grad, heads_grad, distil_grad)
    small_grads = (
        jnp.concatenate([first_scale, second_scale], axis=0),
        jnp.concatenate([first_shift, second_shift], axis=0),
        scale_sums,
        shift_sums[:4],
        shift_sums[4:],
        third_scale[0],
        third_shift[0],
    )
    return (outputs[0], outputs[1], input_grad, weight_grads, small_grads)


def local(
    features,
    image_ids,
    reduce_weight,
    spatial_weight,
    expand_weight,
    head_weights,
    distil_weights,
    block_scale,
    block_shift,
    head_scale,
    head_shift,
    gate_bias,
    output_scale,
    output_shift,
    depth_cotangent,
    segment_cotangent,
):
    batch_count = lax.axis_size("batch")
    small = (
        block_scale,
        block_shift,
        head_scale,
        head_shift,
        gate_bias,
        output_scale,
        output_shift,
    )
    depth_list, segment_list, input_list = ([], [], [])
    weight_total = None
    small_total = None
    for micro_index in range(features.shape[0]):
        gathered = fetch_weights(
            reduce_weight, spatial_weight, expand_weight, head_weights, distil_weights
        )
        canvas_pick = slice(micro_index, micro_index + 1)
        depth_out, segment_out, input_grad, weight_grads, small_grads = micro_step(
            features[canvas_pick],
            image_ids[canvas_pick],
            depth_cotangent[canvas_pick],
            segment_cotangent[canvas_pick],
            gathered,
            small,
            batch_count,
        )
        weight_grads = scatter_weights(weight_grads)
        weight_total = (
            weight_grads
            if weight_total is None
            else jax.tree.map(jnp.add, weight_total, weight_grads)
        )
        small_total = (
            small_grads if small_total is None else jax.tree.map(jnp.add, small_total, small_grads)
        )
        depth_list.append(depth_out)
        segment_list.append(segment_out)
        input_list.append(input_grad)
    reduce_grad, spatial_grad, expand_grad, heads_grad, distil_grad = weight_total
    scale_mid, shift_mid, scale_heads, shift_heads, bias_gates, scale_out, shift_out = small_total
    return (
        jnp.concatenate(depth_list, axis=0),
        jnp.concatenate(segment_list, axis=0),
        jnp.concatenate(input_list, axis=0),
        reduce_grad,
        spatial_grad,
        expand_grad,
        heads_grad,
        distil_grad,
        scale_mid,
        shift_mid,
        scale_heads,
        shift_heads,
        bias_gates,
        scale_out,
        shift_out,
    )


def solution(mesh):
    placed = (
        P("batch", None, None, "chan"),
        P("batch", None, None),
        P("chan", "batch"),
        P(None, "batch", "chan"),
        P("batch", "chan"),
        P(None, "chan", None, "batch"),
        P(None, None, None, "batch", "chan"),
        P(None, "chan"),
        P(None, "chan"),
        P(None, "chan"),
        P(None, "chan"),
        P(None, "chan"),
        P("chan"),
        P("chan"),
        P("batch", None, None, "chan"),
        P("batch", None, None, "chan"),
    )
    return jax.shard_map(
        local,
        mesh=mesh,
        in_specs=placed,
        out_specs=(
            P("batch", None, None, "chan"),
            P("batch", None, None, "chan"),
            P("batch", None, None, "chan"),
            P("chan", "batch"),
            P(None, "batch", "chan"),
            P("batch", "chan"),
            P(None, "chan", None, "batch"),
            P(None, None, None, "batch", "chan"),
            P(None, "chan"),
            P(None, "chan"),
            P(None, "chan"),
            P(None, "chan"),
            P(None, "chan"),
            P("chan"),
            P("chan"),
        ),
        check_vma=False,
    )
```

profile of v0, /device:TPU:0, one launch (start us, length us, event | category | flops | bytes accessed | tf_op | source)
XLA Modules:
  0.0 2860.8 jit_solution(6492665959203156966)
XLA Ops:
  8.1 33.2 %all_gather.50 = bf16[512,512]{0,1:T(8,128)(2,1)S(1)} all-gather(bf16[512,64]{0,1:T(8,128)(2,1)} %param.170), channel_id=1, replica_groups=mesh['batch'=8,'chan'=4] {'batch'}, dimensions={1}, use_global_device_ids=true | all-gather | bytes 589824 | tf_op jit(solution)/shard_map/all_gather | solution.py:100
  48.3 4.9 copy.291
  55.5 32.1 %all_gather.54 = bf16[512,512]{1,0:T(8,128)(2,1)S(1)} all-gather(bf16[64,512]{1,0:T(8,128)(2,1)S(1)} %copy-done.255), channel_id=1, replica_groups=mesh['batch'=8,'chan'=4] {'batch'}, dimensions={0}, use_global_device_ids=true | all-gather | bytes 589824 | tf_op jit(solution)/shard_map/all_gather | solution.py:102
  91.0 43.1 %all-reduce.64 = (f32[1,128]{1,0:T(1,128)S(1)}, f32[1,128]{1,0:T(1,128)S(1)}, f32[1,128]{1,0:T(1,128)S(1)}, f32[1,128]{1,0:T(1,128)S(1)}) all-reduce(f32[1,128]{1,0:T(1,128)S(1)} %bitcast.3264, f32[1,128]{1,0:T(1,128)S(1)} %bitcast.3263, f32[1,128]{1,0:T(1,128)S(1)} %bitcast.3262, ...), channel_id=1, replica_groups=mesh['batch'=8,'chan'=4] {'batch'}, use_global_device_ids=true, to_apply=%region_22.23 | all-reduce | flops 512 | bytes 4096 | tf_op jit(solution)/shard_map/psum | solution.py:73
  134.8 5.9 all_gather.51
  140.7 5.9 all_gather.58
  154.6 20.8 all-reduce.63
  176.0 5.8 all-gather
  181.9 5.9 all-gather.1
  189.1 25.2 all-reduce.62
  215.6 244.8 %all-gather.12.cloned.1.call-done = bf16[9,512,4,512]{1,2,0,3:T(4,128)(2,1)} async-done(((bf16[9,512,4,64]{1,2,0,3:T(4,128)(2,1)}), bf16[9,512,4,512]{1,2,0,3:T(4,128)(2,1)}) %all-gather.12.cloned.1.call-update) | async-done | bytes 18874384 | tf_op jit(solution)/shard_map/all_gather | solution.py:103
  460.4 16.4 fusion.1277
  478.1 4.2 copy.309
  485.6 6.5 copy.307
  492.1 4.5 reshape.6178
  496.6 6.5 copy.305
  503.1 4.5 reshape.6177
  507.5 6.5 copy.303
  514.0 4.5 reshape.6176
  518.5 6.5 copy.301
  524.9 4.5 reshape.6175
  529.4 6.5 copy.299
  535.9 4.5 reshape.6174
  540.4 6.5 copy.297
  546.9 4.5 reshape.6173
  551.3 6.5 copy.295
  557.8 4.5 reshape.6172
  562.3 6.5 copy.293
  568.7 4.9 reshape.6171
  594.7 8.4 copy.483
  603.1 7.0 reshape.6410
  622.9 6.8 copy.479
  629.8 7.0 reshape.6406
  640.4 22.7 reduce-scatter.45.cloned.1.call-done
  666.3 22.3 all-reduce.61
  692.4 85.1 %all-gather.16.cloned.1.call-done = bf16[2,9,4,512,128]{4,3,2,1,0:T(8,128)(2,1)} async-done(((bf16[2,9,4,64,128]{4,3,2,1,0:T(8,128)(2,1)}), bf16[2,9,4,512,128]{4,3,2,1,0:T(8,128)(2,1)}) %all-gather.16.cloned.1.call-update) | async-done | bytes 9437200 | tf_op jit(solution)/shard_map/all_gather | solution.py:104
  777.5 5.8 fusion.1278
  783.3 10.7 all-gather.18.cloned.1.call-done
  800.5 11.7 all-gather.14.cloned.1.call-done
  818.8 7.6 fusion.388
  904.3 7.5 fusion.380
  929.3 3.8 reshape.6033
  1093.0 6.4 copy.485
  1099.5 7.1 reshape.6412
  1137.9 6.4 copy.491
  1144.3 7.0 reshape.6418
  1154.5 22.0 reduce-scatter.57.cloned.1.call-done
  1181.5 37.1 %all-reduce.60 = (f32[4,128]{1,0:T(4,128)S(1)}, f32[6,128]{1,0:T(8,128)S(1)}, f32[4,128]{1,0:T(4,128)S(1)}, f32[6,128]{1,0:T(8,128)S(1)}) all-reduce(f32[4,128]{1,0:T(4,128)S(1)} %get-tuple-element.1198, f32[6,128]{1,0:T(8,128)S(1)} %pad_maximum_fusion.22, ...), channel_id=1, replica_groups=mesh['batch'=8,'chan'=4] {'batch'}, use_global_device_ids=true, to_apply=%region_63.64 | all-reduce | flops 2560 | bytes 20480 | tf_op jit(solution)/shard_map/psum | solution.py:81
  1226.1 4.5 copy.508
  1233.6 4.4 copy.506
  1241.1 4.6 copy.504
  1248.7 4.4 copy.502
  1294.2 17.5 all-reduce.59
  1328.2 10.0 copy-done
  1360.7 10.4 reduce-scatter.53.cloned.1.call-done
  1372.6 21.3 all-reduce.58
  1409.3 38.0 %add.1862 = f32[9,512,4,512]{3,1,2,0:T(8,128)} add(f32[9,512,4,512]{3,1,2,0:T(8,128)} %bitcast_dynamic-update-slice_fusion.9, f32[9,512,4,512]{3,1,2,0:T(8,128)} %copy-done) | non-fusion elementwise | flops 9437184 | bytes 113246208 | tf_op jit(solution)/shard_map/add | solution.py:353
  1447.4 43.9 %copy.372 = f32[9,512,4,512]{1,2,0,3:T(4,128)} copy(f32[9,512,4,512]{3,1,2,0:T(8,128)} %add.1862) | data formatting | bytes 75497472 | tf_op jit(solution)/shard_map/add | solution.py:353
  1568.8 19.0 all-reduce.57
  1588.8 5.8 all_gather.62
  1595.7 5.9 all_gather.64
  1617.4 4.2 add.1860
  1642.0 15.4 maximum_add_fusion
  1669.4 1177.0 %all-reduce.67.cloned.1.call-done = f32[9,512,4,512]{1,2,0,3:T(4,128)} async-done(((f32[9,512,4,512]{1,2,0,3:T(4,128)}), f32[9,512,4,512]{1,2,0,3:T(4,128)}) %all-reduce.67.cloned.1.call-update) | async-done | bytes 37748752
  (1495 shorter events, 622.0 us)
Async XLA Ops:
  8.0 79.6 %reduce-scatter.43.cloned.1.call-start = ((), (), s32[]{:S(2)}) async-start(), calls=%async_computation.25 | async-start | bytes 327680
  45.0 44.6 %reduce-scatter.47.cloned.1.call-start = ((), (), s32[]{:S(2)}) async-start(), calls=%async_computation.27 | async-start | bytes 327680
  47.7 98.9 %all-gather.10.cloned.1.call-start = ((), (), s32[]{:S(2)}) async-start(), calls=%async_computation.14 | async-start | bytes 1327104 | tf_op jit(solution)/shard_map/all_gather | solution.py:101
  48.3 412.1 %all-gather.12.cloned.1.call-start = ((), (), s32[]{:S(2)}) async-start(), calls=%async_computation.15 | async-start | bytes 21233664 | tf_op jit(solution)/shard_map/all_gather | solution.py:103
  53.2 80.9 %copy-start.405 = (f32[2,128]{1,0:T(2,128)S(1)}, f32[2,128]{1,0:T(2,128)}, u32[]{:S(2)}) copy-start(f32[2,128]{1,0:T(2,128)} %param.175) | copy-start | bytes 3076
  53.2 584.2 %reduce-scatter.49.cloned.1.call-start = ((), (), s32[]{:S(2)}) async-start(), calls=%async_computation.28 | async-start | bytes 1310720
  53.9 95.2 %copy-start.393 = (f32[128]{0:T(128)}, f32[128]{0:T(128)S(1)}, u32[]{:S(2)}) copy-start(f32[128]{0:T(128)S(1)} %get-tuple-element.1252) | copy-start | bytes 1540
  53.9 122.0 %copy-start.388 = (f32[128]{0:T(128)}, f32[128]{0:T(128)S(1)}, u32[]{:S(2)}) copy-start(f32[128]{0:T(128)S(1)} %get-tuple-element.1251) | copy-start | bytes 1540
  54.6 521.6 %copy-start.341 = (bf16[8,32]{1,0:T(8,128)(2,1)}, bf16[8,32]{1,0:T(8,128)(2,1)S(1)}, u32[]{:S(2)}) copy-start(bf16[8,32]{1,0:T(8,128)(2,1)S(1)} %get-tuple-element.1215) | copy-start | bytes 1540
  54.6 522.4 %copy-start.338 = (bf16[8,32]{1,0:T(8,128)(2,1)}, bf16[8,32]{1,0:T(8,128)(2,1)S(1)}, u32[]{:S(2)}) copy-start(bf16[8,32]{1,0:T(8,128)(2,1)S(1)} %get-tuple-element.1213) | copy-start | bytes 1540
  54.6 526.3 %copy-start.335 = (bf16[8,32]{1,0:T(8,128)(2,1)}, bf16[8,32]{1,0:T(8,128)(2,1)S(1)}, u32[]{:S(2)}) copy-start(bf16[8,32]{1,0:T(8,128)(2,1)S(1)} %get-tuple-element.1211) | copy-start | bytes 1540
  54.6 555.8 %copy-start.332 = (bf16[8,32]{1,0:T(8,128)(2,1)}, bf16[8,32]{1,0:T(8,128)(2,1)S(1)}, u32[]{:S(2)}) copy-start(bf16[8,32]{1,0:T(8,128)(2,1)S(1)} %get-tuple-element.1209) | copy-start | bytes 1540
  54.6 559.7 %copy-start.328 = (bf16[8,32]{1,0:T(8,128)(2,1)}, bf16[8,32]{1,0:T(8,128)(2,1)S(1)}, u32[]{:S(2)}) copy-start(bf16[8,32]{1,0:T(8,128)(2,1)S(1)} %get-tuple-element.1207) | copy-start | bytes 1540
  54.7 561.3 %copy-start.324 = (bf16[8,32]{1,0:T(8,128)(2,1)}, bf16[8,32]{1,0:T(8,128)(2,1)S(1)}, u32[]{:S(2)}) copy-start(bf16[8,32]{1,0:T(8,128)(2,1)S(1)} %get-tuple-element.1205) | copy-start | bytes 1540
  54.7 562.9 %copy-start.321 = (bf16[8,32]{1,0:T(8,128)(2,1)}, bf16[8,32]{1,0:T(8,128)(2,1)S(1)}, u32[]{:S(2)}) copy-start(bf16[8,32]{1,0:T(8,128)(2,1)S(1)} %get-tuple-element.1203) | copy-start | bytes 1540
  54.7 849.6 %copy-start.299 = (bf16[8,32]{1,0:T(8,128)(2,1)}, bf16[8,32]{1,0:T(8,128)(2,1)S(1)}, u32[]{:S(2)}) copy-start(bf16[8,32]{1,0:T(8,128)(2,1)S(1)} %get-tuple-element.1058) | copy-start | bytes 1540
  55.4 518.3 %copy-start.344 = (bf16[8,32]{1,0:T(8,128)(2,1)}, bf16[8,32]{1,0:T(8,128)(2,1)S(1)}, u32[]{:S(2)}) copy-start(bf16[8,32]{1,0:T(8,128)(2,1)S(1)} %get-tuple-element.1229) | copy-start | bytes 1540
  55.4 523.2 %copy-start.318 = (bf16[8,32]{1,0:T(8,128)(2,1)}, bf16[8,32]{1,0:T(8,128)(2,1)S(1)}, u32[]{:S(2)}) copy-start(bf16[8,32]{1,0:T(8,128)(2,1)S(1)} %get-tuple-element.1227) | copy-start | bytes 1540
  55.4 524.0 %copy-start.315 = (bf16[8,32]{1,0:T(8,128)(2,1)}, bf16[8,32]{1,0:T(8,128)(2,1)S(1)}, u32[]{:S(2)}) copy-start(bf16[8,32]{1,0:T(8,128)(2,1)S(1)} %get-tuple-element.1225) | copy-start | bytes 1540
  55.4 527.7 %copy-start.312 = (bf16[8,32]{1,0:T(8,128)(2,1)}, bf16[8,32]{1,0:T(8,128)(2,1)S(1)}, u32[]{:S(2)}) copy-start(bf16[8,32]{1,0:T(8,128)(2,1)S(1)} %get-tuple-element.1223) | copy-start | bytes 1540
  55.4 530.1 %copy-start.309 = (bf16[8,32]{1,0:T(8,128)(2,1)}, bf16[8,32]{1,0:T(8,128)(2,1)S(1)}, u32[]{:S(2)}) copy-start(bf16[8,32]{1,0:T(8,128)(2,1)S(1)} %get-tuple-element.1221) | copy-start | bytes 1540
  55.4 763.4 %copy-start.296 = (bf16[8,32]{1,0:T(8,128)(2,1)}, bf16[8,32]{1,0:T(8,128)(2,1)S(1)}, u32[]{:S(2)}) copy-start(bf16[8,32]{1,0:T(8,128)(2,1)S(1)} %get-tuple-element.1074) | copy-start | bytes 1540
  55.4 763.4 %copy-start.303 = (bf16[8,32]{1,0:T(8,128)(2,1)}, bf16[8,32]{1,0:T(8,128)(2,1)S(1)}, u32[]{:S(2)}) copy-start(bf16[8,32]{1,0:T(8,128)(2,1)S(1)} %get-tuple-element.1217) | copy-start | bytes 1540
  55.4 763.4 %copy-start.306 = (bf16[8,32]{1,0:T(8,128)(2,1)}, bf16[8,32]{1,0:T(8,128)(2,1)S(1)}, u32[]{:S(2)}) copy-start(bf16[8,32]{1,0:T(8,128)(2,1)S(1)} %get-tuple-element.1219) | copy-start | bytes 1540
  87.6 101.2 %copy-start.25 = (bf16[512,512]{1,0:T(8,128)(2,1)}, bf16[512,512]{1,0:T(8,128)(2,1)S(1)}, u32[]{:S(2)}) copy-start(bf16[512,512]{1,0:T(8,128)(2,1)S(1)} %all_gather.54) | copy-start | bytes 1572868
  88.9 61.7 %copy-start.210 = (bf16[1,8,32,1,128]{4,2,1,3,0:T(8,128)(2,1)}, bf16[1,8,32,1,128]{4,2,1,3,0:T(8,128)(2,1)S(1)}, u32[]{:S(2)}) copy-start(bf16[1,8,32,1,128]{4,2,1,3,0:T(8,128)(2,1)S(1)} %copy.478) | copy-start | bytes 196612
  90.9 60.0 %copy-start.208 = (bf16[1,8,32,1,128]{4,2,1,3,0:T(8,128)(2,1)}, bf16[1,8,32,1,128]{4,2,1,3,0:T(8,128)(2,1)S(1)}, u32[]{:S(2)}) copy-start(bf16[1,8,32,1,128]{4,2,1,3,0:T(8,128)(2,1)S(1)} %copy.482) | copy-start | bytes 196612
  154.5 59.8 %copy-start.390 = (f32[512]{0:T(512)S(1)}, f32[512]{0:T(512)}, u32[]{:S(2)}) copy-start(f32[512]{0:T(512)} %param.180) | copy-start | bytes 6148
  154.6 60.4 %copy-start.403 = (f32[512]{0:T(512)S(1)}, f32[512]{0:T(512)}, u32[]{:S(2)}) copy-start(f32[512]{0:T(512)} %param.181) | copy-start | bytes 6148
  215.6 374.7 %copy-start.3 = (bf16[1,8,32,512]{3,2,1,0:T(8,128)(2,1)}, bf16[1,8,32,512]{3,2,1,0:T(8,128)(2,1)S(1)}, u32[]{:S(2)}) copy-start(bf16[1,8,32,512]{3,2,1,0:T(8,128)(2,1)S(1)} %get-tuple-element.1170) | copy-start | bytes 786436
  215.6 403.7 %copy-start.1 = (bf16[1,8,32,512]{3,2,1,0:T(8,128)(2,1)}, bf16[1,8,32,512]{3,2,1,0:T(8,128)(2,1)S(1)}, u32[]{:S(2)}) copy-start(bf16[1,8,32,512]{3,2,1,0:T(8,128)(2,1)S(1)} %get-tuple-element.1169) | copy-start | bytes 786436
  610.2 53.0 %reduce-scatter.45.cloned.1.call-start = ((), (), s32[]{:S(2)}) async-start(), calls=%async_computation.26 | async-start | bytes 1310720
  636.8 140.7 %all-gather.16.cloned.1.call-start = ((), (), s32[]{:S(2)}) async-start(), calls=%async_computation.17 | async-start | bytes 10616832 | tf_op jit(solution)/shard_map/all_gather | solution.py:104
  637.4 156.6 %all-gather.18.cloned.1.call-start = ((), (), s32[]{:S(2)}) async-start(), calls=%async_computation.18 | async-start | bytes 1310720 | tf_op jit(solution)/shard_map/all_gather | solution.py:89
  639.3 49.3 %copy-start.301 = (f32[4,128]{1,0:T(4,128)S(1)}, f32[4,128]{1,0:T(4,128)}, u32[]{:S(2)}) copy-start(f32[4,128]{1,0:T(4,128)} %param.177) | copy-start | bytes 6148
  639.3 50.5 %copy-start.355 = (f32[4,128]{1,0:T(4,128)S(1)}, f32[4,128]{1,0:T(4,128)}, u32[]{:S(2)}) copy-start(f32[4,128]{1,0:T(4,128)} %param.178) | copy-start | bytes 6148
  640.4 50.6 %copy-start.72 = (bf16[1,8,32,4,128]{4,2,1,3,0:T(8,128)(2,1)}, bf16[1,8,32,4,128]{4,2,1,3,0:T(8,128)(2,1)S(1)}, u32[]{:S(2)}) copy-start(bf16[1,8,32,4,128]{4,2,1,3,0:T(8,128)(2,1)S(1)} %copy.484) | copy-start | bytes 786436
  640.4 51.4 %copy-start.407 = (f32[2,128]{1,0:T(2,128)S(1)}, f32[2,128]{1,0:T(2,128)}, u32[]{:S(2)}) copy-start(f32[2,128]{1,0:T(2,128)} %param.179) | copy-start | bytes 3076
  666.1 117.2 %copy-start.74 = (bf16[1,8,32,4,128]{4,2,1,3,0:T(8,128)(2,1)}, bf16[1,8,32,4,128]{4,2,1,3,0:T(8,128)(2,1)S(1)}, u32[]{:S(2)}) copy-start(bf16[1,8,32,4,128]{4,2,1,3,0:T(8,128)(2,1)S(1)} %copy.480) | copy-start | bytes 786436
  691.1 121.2 %all-gather.14.cloned.1.call-start = ((), (), s32[]{:S(2)}) async-start(), calls=%async_computation.16 | async-start | bytes 1310720 | tf_op jit(solution)/shard_map/all_gather | solution.py:89
  691.8 459.6 %reduce-scatter.51.cloned.1.call-start = ((), (), s32[]{:S(2)}) async-start(), calls=%async_computation.29 | async-start | bytes 1310720
  826.5 54.8 %copy-start.43 = (bf16[1,8,32,4,512]{4,2,1,3,0:T(8,128)(2,1)}, bf16[1,8,32,4,512]{4,2,1,3,0:T(8,128)(2,1)S(1)}, u32[]{:S(2)}) copy-start(bf16[1,8,32,4,512]{4,2,1,3,0:T(8,128)(2,1)S(1)} %get-tuple-element.1165) | copy-start | bytes 3145732
  826.5 62.0 %copy-start.40 = (bf16[1,8,32,4,512]{4,2,1,3,0:T(8,128)(2,1)}, bf16[1,8,32,4,512]{4,2,1,3,0:T(8,128)(2,1)S(1)}, u32[]{:S(2)}) copy-start(bf16[1,8,32,4,512]{4,2,1,3,0:T(8,128)(2,1)S(1)} %get-tuple-element.1166) | copy-start | bytes 3145732
  826.5 67.3 %copy-start.37 = (bf16[1,8,32,4,512]{4,2,1,3,0:T(8,128)(2,1)}, bf16[1,8,32,4,512]{4,2,1,3,0:T(8,128)(2,1)S(1)}, u32[]{:S(2)}) copy-start(bf16[1,8,32,4,512]{4,2,1,3,0:T(8,128)(2,1)S(1)} %get-tuple-element.1167) | copy-start | bytes 3145732
  911.8 158.7 %copy-start.33 = (bf16[1,8,32,4,512]{4,2,1,3,0:T(8,128)(2,1)}, bf16[1,8,32,4,512]{4,2,1,3,0:T(8,128)(2,1)S(1)}, u32[]{:S(2)}) copy-start(bf16[1,8,32,4,512]{4,2,1,3,0:T(8,128)(2,1)S(1)} %get-tuple-element.1157) | copy-start | bytes 3145732
  911.8 158.9 %copy-start.31 = (bf16[1,8,32,4,512]{4,2,1,3,0:T(8,128)(2,1)}, bf16[1,8,32,4,512]{4,2,1,3,0:T(8,128)(2,1)S(1)}, u32[]{:S(2)}) copy-start(bf16[1,8,32,4,512]{4,2,1,3,0:T(8,128)(2,1)S(1)} %get-tuple-element.1158) | copy-start | bytes 3145732
  911.8 159.1 %copy-start.29 = (bf16[1,8,32,4,512]{4,2,1,3,0:T(8,128)(2,1)}, bf16[1,8,32,4,512]{4,2,1,3,0:T(8,128)(2,1)S(1)}, u32[]{:S(2)}) copy-start(bf16[1,8,32,4,512]{4,2,1,3,0:T(8,128)(2,1)S(1)} %get-tuple-element.1159) | copy-start | bytes 3145732
  1050.0 70.8 %copy-start.92 = (bf16[1,8,32,128]{3,2,1,0:T(8,128)(2,1)}, bf16[1,8,32,128]{3,2,1,0:T(8,128)(2,1)S(1)}, u32[]{:S(2)}) copy-start(bf16[1,8,32,128]{3,2,1,0:T(8,128)(2,1)S(1)} %get-tuple-element.1188) | copy-start | bytes 196612
  1050.0 71.1 %copy-start.88 = (bf16[1,8,32,128]{3,2,1,0:T(8,128)(2,1)}, bf16[1,8,32,128]{3,2,1,0:T(8,128)(2,1)S(1)}, u32[]{:S(2)}) copy-start(bf16[1,8,32,128]{3,2,1,0:T(8,128)(2,1)S(1)} %get-tuple-element.1186) | copy-start | bytes 196612
  1074.9 55.7 %copy-start.86 = (bf16[1,8,32,128]{3,2,1,0:T(8,128)(2,1)}, bf16[1,8,32,128]{3,2,1,0:T(8,128)(2,1)S(1)}, u32[]{:S(2)}) copy-start(bf16[1,8,32,128]{3,2,1,0:T(8,128)(2,1)S(1)} %get-tuple-element.1185) | copy-start | bytes 196612
  1074.9 55.9 %copy-start.80 = (bf16[1,8,32,128]{3,2,1,0:T(8,128)(2,1)}, bf16[1,8,32,128]{3,2,1,0:T(8,128)(2,1)S(1)}, u32[]{:S(2)}) copy-start(bf16[1,8,32,128]{3,2,1,0:T(8,128)(2,1)S(1)} %get-tuple-element.1183) | copy-start | bytes 196612
  1106.6 69.9 %reduce-scatter.57.cloned.1.call-start = ((), (), s32[]{:S(2)}) async-start(), calls=%async_computation.32 | async-start | bytes 1310720
  1151.4 104.7 %all-gather.20.cloned.1.call-start = ((), (), s32[]{:S(2)}) async-start(), calls=%async_computation.19 | async-start | bytes 1310720 | tf_op jit(solution)/shard_map/all_gather | solution.py:89
  1221.0 38.7 %all-gather.22.cloned.1.call-start = ((), (), s32[]{:S(2)}) async-start(), calls=%async_computation.20 | async-start | bytes 1310720 | tf_op jit(solution)/shard_map/all_gather | solution.py:89
  1223.0 136.3 %reduce-scatter.59.cloned.1.call-start = ((), (), s32[]{:S(2)}) async-start(), calls=%async_computation.33 | async-start | bytes 327680
  1294.1 52.8 %copy-start.96 = (f32[1,8,32,512]{3,2,1,0:T(8,128)}, f32[1,8,32,512]{3,2,1,0:T(8,128)S(1)}, u32[]{:S(2)}) copy-start(f32[1,8,32,512]{3,2,1,0:T(8,128)S(1)} %get-tuple-element.1269) | copy-start | bytes 1572868
  1315.2 55.9 %reduce-scatter.53.cloned.1.call-start = ((), (), s32[]{:S(2)}) async-start(), calls=%async_computation.30 | async-start | bytes 327680
  1353.1 206.4 %reduce-scatter.61.cloned.1.call-start = ((), (), s32[]{:S(2)}) async-start(), calls=%async_computation.34 | async-start | bytes 327680
  1398.9 164.1 %reduce-scatter.55.cloned.1.call-start = ((), (), s32[]{:S(2)}) async-start(), calls=%async_computation.31 | async-start | bytes 327680
  1403.6 1442.9 %all-reduce.67.cloned.1.call-start = ((), (), s32[]{:S(2)}) async-start(), calls=%async_computation.35 | async-start | bytes 75497472
  1491.3 1361.9 %reduce-scatter.39.cloned.1.call-start = ((), (), s32[]{:S(2)}) async-start(), calls=%async_computation.23 | async-start | bytes 1179648 | tf_op jit(solution)/shard_map/reduce_scatter | solution.py:113
  1548.0 1305.2 %reduce-scatter.35.cloned.1.call-start = ((), (), s32[]{:S(2)}) async-start(), calls=%async_computation.21 | async-start | bytes 1179648 | tf_op jit(solution)/shard_map/reduce_scatter | solution.py:111
  1604.9 1248.2 %reduce-scatter.37.cloned.1.call-start = ((), (), s32[]{:S(2)}) async-start(), calls=%async_computation.22 | async-start | bytes 2654208 | tf_op jit(solution)/shard_map/reduce_scatter | solution.py:112
  1621.6 1231.6 %reduce-scatter.41.cloned.1.call-start = ((), (), s32[]{:S(2)}) async-start(), calls=%async_computation.24 | async-start | bytes 21233664 | tf_op jit(solution)/shard_map/reduce_scatter | solution.py:115
  (384 other events, 2106.4 us)
Sparse Core Ops, SparseCore 0:
  45.2 21.2 reduce-scatter.42
  69.6 20.0 reduce-scatter.46
  610.3 24.7 reduce-scatter.48
  638.2 24.8 reduce-scatter.44
  1106.7 24.8 reduce-scatter.50
  1151.5 24.9 reduce-scatter.56
  1221.2 13.1 all-gather.19
  1236.5 16.8 all-gather.21
  1315.3 17.8 reduce-scatter.58
  1353.2 17.7 reduce-scatter.52
  1399.0 16.3 reduce-scatter.60
  1418.5 20.0 reduce-scatter.54
  1548.1 215.3 reduce-scatter.38
  1767.7 168.9 reduce-scatter.34
  1940.7 206.5 reduce-scatter.36
  2152.1 596.7 reduce-scatter.40
Sparse Core Ops, SparseCore 1:
  50.3 44.8 all-gather.9
  97.2 363.2 all-gather.11
  639.5 138.0 all-gather.15
  779.1 14.8 all-gather.17
  795.6 16.7 all-gather.13
  1491.3 1355.0 all-reduce.66
where the time goes:
time: 2880 us; the launch traced here: 2860 us
  waiting for transfers between devices  1590 us (55%)
  local copies, waits for them, and re-layouts  574 us (20%)
  blocking collectives  307 us (11%)
  matrix products  229 us (8%)
  other arithmetic  138 us (5%)
    unnamed x33, waiting for transfers between devices  1230 us
    all_gather x1, waiting for transfers between devices, fetch_weights(): lax.all_gather(head_weights, 'batch', axis=3, tiled=True)  245 us
    unnamed x905, local copies, waits for them, and re-layouts  206 us
    psum x4, blocking collectives, normalize(): lax.psum((pixel_sum(values), pixel_sum(values * values)), 'batch')  111 us
    another operation x38, local copies, waits for them, and re-layouts  109 us
    psum x4, blocking collectives, grad_sums(): return lax.psum((first_sum, second_sum), 'batch')  94.9 us
    slice x54, local copies, waits for them, and re-layouts, micro_step(): moved[:, :, :, first_source:first_source + 3]  88.2 us
    all_gather x1, waiting for transfers between devices, fetch_weights(): lax.all_gather(distil_weights, 'batch', axis=3, tiled=True)  85.1 us
  transfers between devices with their start and end apart: 22, of which 9 were waited for; matrix products, arithmetic and copies ran while one was open for 14% of the time, Pallas kernels for 0%

commit v1 on v0

--- a/solution.py
+++ b/solution.py
@@ -301,7 +301,7 @@
     return (outputs[0], outputs[1], input_grad, weight_grads, small_grads)
 
 
-def local(
+def gathered_local(
     features,
     image_ids,
     reduce_weight,
@@ -379,7 +379,270 @@
     )
 
 
+def canvas_sum(values):
+    return jnp.sum(values, axis=(1, 2))
+
+
+def spread(values):
+    return values[:, None, None, :]
+
+
+def normalize_each(values, scale, shift, count):
+    total, squares = lax.psum((canvas_sum(values), canvas_sum(values * values)), "batch")
+    center = total / count
+    inverse = lax.rsqrt(squares / count - center * center + EPSILON)
+    normed = (values - spread(center)) * spread(inverse)
+    return (normed, inverse, normed * scale + shift)
+
+
+def normalize_each_back(grads, normed, inverse, scale, count):
+    shift_sum, scale_sum = lax.psum((canvas_sum(grads), canvas_sum(grads * normed)), "batch")
+    back = scale * spread(inverse) * (grads - (spread(shift_sum) + normed * spread(scale_sum)) / count)
+    return (back.astype(jnp.bfloat16), shift_sum, scale_sum)
+
+
+def sum_chan(values):
+    return lax.psum_scatter(
+        values.astype(jnp.bfloat16), "chan", scatter_dimension=3, tiled=True
+    ).astype(jnp.float32)
+
+
+def gather_chan(values):
+    return lax.all_gather(values, "chan", axis=3, tiled=True)
+
+
+def sum_batch(values, axis):
+    return lax.psum_scatter(
+        values.astype(jnp.bfloat16), "batch", scatter_dimension=axis, tiled=True
+    ).astype(jnp.float32)
+
+
+def distil_matrix(weights):
+    taps = weights.shape[1]
+    width = weights.shape[3]
+    columns = []
+    for stream in range(2):
+        for part in range(2):
+            rows = []
+            for head in range(4):
+                source = head - SOURCE_START[stream]
+                if part == 0 and head == OWN_HEAD[stream]:
+                    rows.append(weights[stream, :, 0])
+                elif part == 1 and 0 <= source < 3:
+                    rows.append(weights[stream, :, 1 + source])
+                else:
+                    rows.append(jnp.zeros((taps, width, weights.shape[4]), weights.dtype))
+            columns.append(jnp.concatenate(rows, axis=1))
+    return jnp.concatenate(columns, axis=2)
+
+
+def distil_blocks(grads, width):
+    outs = []
+    for stream in range(2):
+        gate = grads[:, :, (2 * stream) * 128 : (2 * stream + 1) * 128]
+        message = grads[:, :, (2 * stream + 1) * 128 : (2 * stream + 2) * 128]
+        own = OWN_HEAD[stream]
+        first = SOURCE_START[stream]
+        pieces = [gate[:, own * width : (own + 1) * width]]
+        for source in range(3):
+            pieces.append(message[:, (first + source) * width : (first + source + 1) * width])
+        outs.append(jnp.stack(pieces, axis=1))
+    return jnp.stack(outs)
+
+
+def stationary_local(
+    features,
+    image_ids,
+    reduce_weight,
+    spatial_weight,
+    expand_weight,
+    head_weights,
+    distil_weights,
+    block_scale,
+    block_shift,
+    head_scale,
+    head_shift,
+    gate_bias,
+    output_scale,
+    output_shift,
+    depth_cotangent,
+    segment_cotangent,
+):
+    groups = lax.axis_size("batch")
+    place = lax.axis_index("batch")
+    lane = lax.axis_index("chan")
+    canvases, row_count, column_count = image_ids.shape
+    count = float(groups * row_count * column_count)
+    pixels = row_count * column_count
+    width = head_weights.shape[3]
+    reduce_full = lax.all_gather(reduce_weight, "batch", axis=1, tiled=True)
+    spatial_full = lax.all_gather(spatial_weight, "batch", axis=1, tiled=True)
+    expand_full = lax.all_gather(expand_weight, "batch", axis=0, tiled=True)
+    ids_full = lax.all_gather(image_ids, "batch", axis=0, tiled=True)
+    masks = tap_masks(image_ids)
+    masks_full = tap_masks(ids_full)
+    first = sum_chan(
+        jnp.einsum("nhwc,co->nhwo", features, reduce_full, preferred_element_type=jnp.float32)
+    )
+    first_norm, first_inv, first_out = normalize_each(first, block_scale[0], block_shift[0], count)
+    first_full = gather_chan(jax.nn.silu(first_out).astype(jnp.bfloat16))
+    second = conv_forward(first_full, spatial_full, masks)
+    second_norm, second_inv, second_out = normalize_each(
+        second, block_scale[1], block_shift[1], count
+    )
+    second_full = gather_chan(jax.nn.silu(second_out).astype(jnp.bfloat16))
+    third = jnp.einsum(
+        "nhwc,co->nhwo", second_full, expand_full, preferred_element_type=jnp.float32
+    )
+    third_norm, third_inv, third_out = normalize_each(third, output_scale, output_shift, count)
+    summed = third_out + features.astype(jnp.float32)
+    block_out = jax.nn.silu(summed).astype(jnp.bfloat16)
+
+    block_all = lax.all_gather(block_out, "batch", axis=0, tiled=True)
+    heads_flat = head_weights.reshape(9, head_weights.shape[1], -1)
+    head_partial = conv_forward(block_all, heads_flat, masks_full).astype(jnp.bfloat16)
+    head_parts = head_partial.reshape(groups, canvases, pixels, 2, 2 * width).transpose(3, 1, 0, 2, 4)
+    head_parts = head_parts.reshape((2 * canvases,) + head_parts.shape[2:])
+    head_pre = lax.psum_scatter(head_parts, "chan", scatter_dimension=0, tiled=True)[0].astype(
+        jnp.float32
+    )
+    half = lane // 2
+
+    def mine(values):
+        whole = lax.all_gather(values, "chan", axis=1, tiled=True)
+        part = lax.dynamic_slice_in_dim(whole, place * width, width, axis=1)
+        return lax.dynamic_slice_in_dim(part.reshape(2, 2 * width), half, 1, axis=0)[0]
+
+    my_scale, my_shift = mine(head_scale), mine(head_shift)
+    center = jnp.sum(head_pre, axis=(0, 1)) / count
+    spreads = jnp.sum(head_pre * head_pre, axis=(0, 1)) / count
+    head_inv = lax.rsqrt(spreads - center * center + EPSILON)
+    head_norm = (head_pre - center) * head_inv
+    head_out = head_norm * my_scale + my_shift
+    head_act = jax.nn.silu(head_out).astype(jnp.bfloat16)
+    head_all = lax.all_gather(head_act, "chan", axis=0).reshape(
+        2, canvases, groups, pixels, 2 * width
+    )
+    head_full = head_all.transpose(2, 1, 3, 0, 4).reshape(
+        groups * canvases, row_count, column_count, 4 * width
+    )
+    mixed = distil_matrix(distil_weights)
+    pre = sum_batch(conv_forward(head_full, mixed, masks_full), 0)
+    own_part = jnp.concatenate(
+        [head_full[..., :width], head_full[..., 3 * width :]], axis=-1
+    )
+    own_all = lax.all_to_all(own_part, "batch", split_axis=0, concat_axis=0, tiled=True).reshape(
+        groups, canvases, row_count, column_count, 2, width
+    )
+    per = groups // 4
+    own_all = lax.dynamic_slice_in_dim(own_all, lane * per, per, axis=0)
+    own_all = own_all.transpose(4, 1, 2, 3, 0, 5).reshape(
+        2, canvases, row_count, column_count, per * width
+    )
+    cots = (depth_cotangent.astype(jnp.float32), segment_cotangent.astype(jnp.float32))
+    outputs, pre_grads, gate_sums = ([], [], [])
+    for stream in range(2):
+        gate_pre = pre[..., (2 * stream) * 128 : (2 * stream + 1) * 128]
+        message = pre[..., (2 * stream + 1) * 128 : (2 * stream + 2) * 128]
+        gate = jax.nn.sigmoid(gate_pre + gate_bias[stream])
+        outputs.append(
+            (own_all[stream].astype(jnp.float32) + gate * message).astype(jnp.bfloat16)
+        )
+        gate_grad = (cots[stream] * message * gate * (1.0 - gate)).astype(jnp.bfloat16)
+        gate_sums.append(pixel_sum(gate_grad.astype(jnp.float32)))
+        pre_grads.append(gate_grad)
+        pre_grads.append((cots[stream] * gate).astype(jnp.bfloat16))
+    pre_grad_all = lax.all_gather(
+        jnp.concatenate(pre_grads, axis=-1), "batch", axis=0, tiled=True
+    )
+    distil_grad = distil_blocks(conv_weight_grad(head_full, pre_grad_all, masks_full), width)
+    spread_grad = conv_input_grad(pre_grad_all, mixed, masks_full).astype(jnp.bfloat16)
+    spread_parts = spread_grad.reshape(groups, canvases, pixels, 2, 2 * width).transpose(3, 1, 0, 2, 4)
+    spread_parts = spread_parts.reshape((2 * canvases,) + spread_parts.shape[2:])
+    head_grad = lax.psum_scatter(spread_parts, "chan", scatter_dimension=0, tiled=True)[0].astype(
+        jnp.float32
+    )
+    cot_pair = jnp.stack([depth_cotangent, segment_cotangent]).reshape(
+        2, canvases, pixels, 4 // 2 * width
+    )
+    cot_all = lax.all_gather(cot_pair, ("batch", "chan"), axis=0)
+    cot_all = cot_all.reshape(groups, 4, 2, canvases, pixels, 2, width)
+    cot_mine = lax.dynamic_index_in_dim(cot_all, place // 2, axis=1, keepdims=False)
+    cot_mine = lax.dynamic_index_in_dim(cot_mine, half, axis=1, keepdims=False)
+    cot_mine = lax.dynamic_index_in_dim(cot_mine, lane % 2, axis=1, keepdims=False)
+    cot_mine = lax.dynamic_index_in_dim(cot_mine, place % 2, axis=2, keepdims=False)
+    zeros = jnp.zeros_like(cot_mine)
+    cot_wide = jnp.where(
+        half == 0,
+        jnp.concatenate([cot_mine, zeros], axis=-1),
+        jnp.concatenate([zeros, cot_mine], axis=-1),
+    )
+    head_grad = (head_grad + cot_wide.astype(jnp.float32)) * silu_slope(head_out)
+    head_shift_sum = jnp.sum(head_grad, axis=(0, 1))
+    head_scale_sum = jnp.sum(head_grad * head_norm, axis=(0, 1))
+    head_pre_grad = (
+        my_scale * head_inv * (head_grad - (head_shift_sum + head_norm * head_scale_sum) / count)
+    ).astype(jnp.bfloat16)
+    head_grad_all = lax.all_gather(head_pre_grad, "chan", axis=0).reshape(
+        2, canvases, groups, pixels, 2 * width
+    )
+    head_grad_all = head_grad_all.transpose(2, 1, 3, 0, 4).reshape(
+        groups * canvases, row_count, column_count, 4 * width
+    )
+    heads_grad = conv_weight_grad(block_all, head_grad_all, masks_full).reshape(head_weights.shape)
+    block_grad = sum_batch(conv_input_grad(head_grad_all, heads_flat, masks_full), 0)
+    summed_grad = block_grad * silu_slope(summed)
+    third_pre, third_shift, third_scale = normalize_each_back(
+        summed_grad, third_norm, third_inv, output_scale, count
+    )
+    expand_grad = sum_batch(
+        jnp.einsum("nhwc,nhwo->co", second_full, third_pre, preferred_element_type=jnp.float32), 0
+    )
+    second_grad = sum_chan(
+        jnp.einsum("nhwo,co->nhwc", third_pre, expand_full, preferred_element_type=jnp.float32)
+    ) * silu_slope(second_out)
+    second_pre, second_shift, second_scale = normalize_each_back(
+        second_grad, second_norm, second_inv, block_scale[1], count
+    )
+    spatial_grad = sum_batch(conv_weight_grad(first_full, second_pre, masks), 1)
+    first_grad = sum_chan(conv_input_grad(second_pre, spatial_full, masks)) * silu_slope(first_out)
+    first_pre, first_shift, first_scale = normalize_each_back(
+        first_grad, first_norm, first_inv, block_scale[0], count
+    )
+    first_pre_full = gather_chan(first_pre)
+    reduce_grad = sum_batch(
+        jnp.einsum("nhwc,nhwo->co", features, first_pre_full, preferred_element_type=jnp.float32), 1
+    )
+    features_grad = summed_grad + jnp.einsum(
+        "nhwo,co->nhwc", first_pre_full, reduce_full, preferred_element_type=jnp.float32
+    )
+    sums = jnp.stack([head_scale_sum, head_shift_sum]).reshape(2, 1, 2, width)
+    wide = jnp.zeros((2, 2, 2, groups * width), jnp.float32)
+    sums = lax.dynamic_update_slice(wide, sums, (0, half, 0, place * width)).reshape(2, 4, -1)
+    sums = lax.psum(sums, ("batch", "chan"))
+    sums = lax.dynamic_slice_in_dim(sums, lane * 128, 128, axis=2)
+    gate_total = lax.psum(jnp.stack(gate_sums), "batch")
+    return (
+        outputs[0],
+        outputs[1],
+        features_grad,
+        reduce_grad,
+        spatial_grad,
+        expand_grad,
+        heads_grad,
+        distil_grad,
+        jnp.stack([jnp.sum(first_scale, 0), jnp.sum(second_scale, 0)]),
+        jnp.stack([jnp.sum(first_shift, 0), jnp.sum(second_shift, 0)]),
+        sums[0],
+        sums[1],
+        gate_total,
+        jnp.sum(third_scale, 0),
+        jnp.sum(third_shift, 0),
+    )
+
+
 def solution(mesh):
+    local = stationary_local if mesh.shape["batch"] <= 8 else gathered_local
     placed = (
         P("batch", None, None, "chan"),
         P("batch", None, None),

time: 2880 us -> 1200 us (0.42)
  waiting for transfers between devices: 1590 us -> 452 us
  local copies, waits for them, and re-layouts: 574 us -> 91.9 us
  other arithmetic: 138 us -> 44.2 us
  matrix products: 229 us -> 282 us
    unnamed x33 -> x19, waiting for transfers between devices: 1230 us -> 17.7 us
    reduce_scatter x4 -> x7, waiting for transfers between devices: 0.01 us -> 254 us  [the longest x5 216 us: sum_batch(): lax.psum_scatter(values.astype(jnp.bfloat16), 'batch', scatter_dimension=...]
    all_gather x7 -> x6, waiting for transfers between devices: 352 us -> 128 us  [the longest x1 58.4 us: stationary_local(): lax.all_gather(jnp.concatenate(pre_grads, axis=-1), 'batch', axis=0, tile...]
    unnamed x905 -> x324, local copies, waits for them, and re-layouts: 206 us -> 29.5 us
    dot_general x228 -> x6, matrix products: 120 us -> 8.24 us  [the longest x1 1.51 us: stationary_local(): jnp.einsum('nhwc,co->nhwo', features, reduce_full, preferred_element_type...]
    another operation x38 -> x5, local copies, waits for them, and re-layouts: 109 us -> 2.04 us  [the longest x1 1.82 us: distil_blocks(): outs.append(jnp.stack(pieces, axis=1))]
    slice x56 -> x1, local copies, waits for them, and re-layouts: 94 us -> 0.55 us  [stationary_local(): head_full[..., :width]]
    dot_general x36 -> x27, matrix products: 22 us -> 98.4 us  [conv_input_grad(): jnp.einsum('nhwo,co->nhwc', grads, weight[number], preferred_element_type...]
  transfers between devices with their start and end apart: 22 -> 17, of which waited for: 9 -> 14; matrix products, arithmetic and copies ran while one was open for 14% -> 12% of each run, Pallas kernels for 0% -> 0%
where the time goes in v1:
time: 1200 us; the launch traced here: 1190 us
  waiting for transfers between devices  452 us (38%)
  blocking collectives  293 us (24%)
  matrix products  282 us (24%)
  local copies, waits for them, and re-layouts  91.9 us (8%)
  other arithmetic  44.2 us (4%)
  between operations  18 us (2%)
    reduce_scatter x5, waiting for transfers between devices, sum_batch(): lax.psum_scatter(values.astype(jnp.bfloat16), 'batch', scatter_dimension=...  216 us
    dot_general x27, matrix products, conv_input_grad(): jnp.einsum('nhwo,co->nhwc', grads, weight[number], preferred_element_type...  98.4 us
    dot_general x27, matrix products, conv_forward(): jnp.einsum('nhwc,co->nhwo', moved, weight[number], preferred_element_type...  96.1 us
    dot_general x27, matrix products, conv_weight_grad(): jnp.einsum('nhwc,nhwo->co', moved, grads, preferred_element_type=jnp.floa...  78.8 us
    psum x3, blocking collectives, normalize_each_back(): lax.psum((canvas_sum(grads), canvas_sum(grads * normed)), 'batch')  63.9 us
    all_gather x1, waiting for transfers between devices, stationary_local(): lax.all_gather(jnp.concatenate(pre_grads, axis=-1), 'batch', axis=0, tile...  58.4 us
    psum x3, blocking collectives, normalize_each(): lax.psum((canvas_sum(values), canvas_sum(values * values)), 'batch')  58.2 us
    all_to_all x1, waiting for transfers between devices, stationary_local(): lax.all_to_all(own_part, 'batch', split_axis=0, concat_axis=0, tiled=True)  51.8 us
  transfers between devices with their start and end apart: 17, of which 14 were waited for; matrix products, arithmetic and copies ran while one was open for 12% of the time, Pallas kernels for 0%

profile of v1, /device:TPU:0, one launch (start us, length us, event | category | flops | bytes accessed | tf_op | source)
XLA Modules:
  0.0 1187.3 jit_solution(14161090750943174640)
XLA Ops:
  8.1 33.2 %all_gather.46 = bf16[512,512]{0,1:T(8,128)(2,1)S(1)} all-gather(bf16[512,64]{0,1:T(8,128)(2,1)} %param.18), channel_id=1, replica_groups=mesh['batch'=8,'chan'=4] {'batch'}, dimensions={1}, use_global_device_ids=true | all-gather | bytes 589824 | tf_op jit(solution)/shard_map/all_gather | solution.py:478
  49.8 33.9 %all_gather.50 = bf16[512,512]{1,0:T(8,128)(2,1)} all-gather(bf16[64,512]{1,0:T(8,128)(2,1)S(1)} %copy-done.111), channel_id=1, replica_groups=mesh['batch'=8,'chan'=4] {'batch'}, dimensions={0}, use_global_device_ids=true | all-gather | bytes 589824 | tf_op jit(solution)/shard_map/all_gather | solution.py:480
  85.5 21.6 %all-reduce.36 = (f32[2,128]{1,0:T(2,128)S(1)}, f32[2,128]{1,0:T(2,128)S(1)}) all-reduce(f32[2,128]{1,0:T(2,128)S(1)} %get-tuple-element.88, f32[2,128]{1,0:T(2,128)S(1)} %get-tuple-element.87), channel_id=1, replica_groups=mesh['batch'=8,'chan'=4] {'batch'}, use_global_device_ids=true, to_apply=%region_4.5 | all-reduce | flops 512 | bytes 4096 | tf_op jit(solution)/shard_map/psum | solution.py:391
  108.3 7.4 all_gather.47
  125.6 17.1 %all-reduce.35 = (f32[2,128]{1,0:T(2,128)S(1)}, f32[2,128]{1,0:T(2,128)S(1)}) all-reduce(f32[2,128]{1,0:T(2,128)S(1)} %get-tuple-element.86, f32[2,128]{1,0:T(2,128)S(1)} %get-tuple-element.85), channel_id=1, replica_groups=mesh['batch'=8,'chan'=4] {'batch'}, use_global_device_ids=true, to_apply=%region_8.9 | all-reduce | flops 512 | bytes 4096 | tf_op jit(solution)/shard_map/psum | solution.py:391
  143.8 6.6 all_gather.49
  152.7 19.4 %all-reduce.34 = (f32[2,512]{1,0:T(2,128)S(1)}, f32[2,512]{1,0:T(2,128)S(1)}) all-reduce(f32[2,512]{1,0:T(2,128)S(1)} %get-tuple-element.80, f32[2,512]{1,0:T(2,128)S(1)} %get-tuple-element.79), channel_id=1, replica_groups=mesh['batch'=8,'chan'=4] {'batch'}, use_global_device_ids=true, to_apply=%region_12.13 | all-reduce | flops 2048 | bytes 16384 | tf_op jit(solution)/shard_map/psum | solution.py:391
  174.6 30.9 %all_gather.52 = s32[16,8,32]{2,1,0:T(8,128)S(1)} all-gather(s32[2,8,32]{2,1,0:T(8,128)S(1)} %copy-done.120), channel_id=1, replica_groups=mesh['batch'=8,'chan'=4] {'batch'}, dimensions={0}, use_global_device_ids=true | all-gather | bytes 18432 | tf_op jit(solution)/shard_map/all_gather | solution.py:481
  209.1 35.8 %all-gather.10.cloned.1.call-done = bf16[16,8,32,512]{3,2,1,0:T(8,128)(2,1)} async-done(((bf16[2,8,32,512]{3,2,1,0:T(8,128)(2,1)}), bf16[16,8,32,512]{3,2,1,0:T(8,128)(2,1)}) %all-gather.10.cloned.1.call-update) | async-done | bytes 4194320 | tf_op jit(solution)/shard_map/all_gather | solution.py:501
  244.8 5.7 fusion.45
  271.8 12.0 %add_convert_fusion.1 = bf16[16,8,32,256]{3,2,1,0:T(8,128)(2,1)S(1)} fusion(f32[16,8,32,256]{3,2,1,0:T(8,128)} %fusion.45, f32[16,8,32,256]{3,2,1,0:T(8,128)} %fusion.48, f32[16,8,32,256]{3,2,1,0:T(8,128)} %fusion.51, f32[16,8,32,256]{3,2,1,0:T(8,128)} %fusion.54, f32[16,8,32,256]{3,2,1,0:T(8,128)} %fusion.57, f32[16,8,32,256]{3,2,1,0:T(8,128)} %fusion.60, ...), kind=kOutput, calls=%fused_computation.85 | convolution fusion | flops 1083179008 | bytes 40108032 | tf_op jit(solution)/shard_map/nhwc,co->nhwo/dot_general | solution.py:44
  289.4 5.2 all_gather.54
  294.7 5.1 all_gather.53
  300.1 19.3 %reduce-scatter.17.cloned.1.call-done = bf16[1,8,256,128]{3,2,1,0:T(8,128)(2,1)} async-done(((bf16[4,8,256,128]{3,2,1,0:T(8,128)(2,1)}), bf16[1,8,256,128]{3,2,1,0:T(8,128)(2,1)}) %reduce-scatter.17.cloned.1.call-update) | async-done | bytes 524304 | tf_op jit(solution)/shard_map/reduce_scatter | solution.py:506
  327.4 20.1 %all-gather.12.cloned.1.call-done = bf16[4,8,256,128]{3,2,1,0:T(8,128)(2,1)} async-done(((bf16[1,8,256,128]{3,2,1,0:T(8,128)(2,1)}), bf16[4,8,256,128]{3,2,1,0:T(8,128)(2,1)}) %all-gather.12.cloned.1.call-update) | async-done | bytes 2097168 | tf_op jit(solution)/shard_map/all_gather | solution.py:523
  347.6 5.1 copy.296
  355.9 7.7 fusion.75
  366.2 5.2 fusion.375
  371.4 4.6 fusion.374
  376.0 4.6 fusion.372
  380.6 4.5 fusion.371
  385.1 4.5 fusion.369
  389.6 4.5 fusion.370
  394.2 19.8 %add_convert_fusion = bf16[16,8,32,512]{3,2,1,0:T(8,128)(2,1)} fusion(f32[16,8,32,512]{3,2,1,0:T(8,128)S(1)} %fusion.376, f32[16,8,32,512]{3,2,1,0:T(8,128)} %fusion.375, f32[16,8,32,512]{3,2,1,0:T(8,128)} %fusion.374, f32[16,8,32,512]{3,2,1,0:T(8,128)S(1)} %fusion.373, f32[16,8,32,512]{3,2,1,0:T(8,128)} %fusion.372, f32[16,8,32,512]{3,2,1,0:T(8,128)} %fusion.371, ...), kind=kOutput, calls=%fused_computation.25 | convolution fusion | flops 1092616192 | bytes 73662464 | tf_op jit(solution)/shard_map/nhwc,co->nhwo/dot_general | solution.py:44
  417.8 5.5 all-to-all-start
  423.4 51.8 %all-to-all-done = bf16[16,8,32,128]{3,2,1,0:T(8,128)(2,1)} async-done(((bf16[16,8,32,128]{3,2,1,0:T(8,128)(2,1)}), bf16[16,8,32,128]{3,2,1,0:T(8,128)(2,1)}, u32[]{:S(2)}, u32[]{:S(2)}) %all-to-all-start) | async-done | bytes 1048608 | tf_op jit(solution)/shard_map/all_to_all | solution.py:534
  475.2 5.0 reshape.294
  485.8 60.6 %reduce-scatter.19.cloned.1.call-done = bf16[2,8,32,512]{3,2,1,0:T(8,128)(2,1)} async-done(((bf16[16,8,32,512]{3,2,1,0:T(8,128)(2,1)}), bf16[2,8,32,512]{3,2,1,0:T(8,128)(2,1)}) %reduce-scatter.19.cloned.1.call-update) | async-done | bytes 524304 | tf_op jit(solution)/shard_map/reduce_scatter | solution.py:415
  550.6 12.2 %copy.307 = bf16[32,2,2,256,128]{3,4,2,1,0:T(8,128)(2,1)} copy(bf16[32,2,2,256,128]{4,3,2,1,0:T(8,128)(2,1)} %all-gather.16.cloned.1.call-done) | data formatting | bytes 16777216 | tf_op jit(solution)/shard_map/all_gather | solution.py:568
  565.4 58.4 %all-gather.14.cloned.1.call-done = bf16[16,8,32,512]{3,2,1,0:T(8,128)(2,1)} async-done(((bf16[2,8,32,512]{3,2,1,0:T(8,128)(2,1)}), bf16[16,8,32,512]{3,2,1,0:T(8,128)(2,1)}) %all-gather.14.cloned.1.call-update) | async-done | bytes 4194320 | tf_op jit(solution)/shard_map/all_gather | solution.py:555
  623.8 5.7 convolution_multiply_fusion.7
  649.9 12.7 %fusion.17 = bf16[16,8,32,256]{3,2,1,0:T(8,128)(2,1)} fusion(f32[16,8,32,256]{3,2,1,0:T(8,128)} %convolution_multiply_fusion.7, f32[16,8,32,256]{3,2,1,0:T(8,128)} %convolution_multiply_fusion.6, f32[16,8,32,256]{3,2,1,0:T(8,128)} %convolution_multiply_fusion.5, f32[16,8,32,256]{3,2,1,0:T(8,128)} %convolution_multiply_fusion.4, ...), kind=kOutput, calls=%fused_computation.50 | convolution fusion | flops 1083179008 | bytes 40108032 | tf_op jit(solution)/shard_map/nhwo,co->nhwc/dot_general | solution.py:53
  662.6 4.0 reshape.295
  670.2 5.0 fusion.122
  681.5 18.3 %reduce-scatter.21.cloned.1.call-done = bf16[1,8,256,128]{3,2,1,0:T(8,128)(2,1)} async-done(((bf16[4,8,256,128]{3,2,1,0:T(8,128)(2,1)}), bf16[1,8,256,128]{3,2,1,0:T(8,128)(2,1)}) %reduce-scatter.21.cloned.1.call-update) | async-done | bytes 524304 | tf_op jit(solution)/shard_map/reduce_scatter | solution.py:562
  703.3 4.4 fusion.146
  711.8 14.1 %all-gather.18.cloned.1.call-done = bf16[32,256,128]{2,1,0:T(8,128)(2,1)} async-done(((bf16[8,256,128]{2,1,0:T(8,128)(2,1)}), bf16[32,256,128]{2,1,0:T(8,128)(2,1)}) %all-gather.18.cloned.1.call-update) | async-done | bytes 2097168 | tf_op jit(solution)/shard_map/all_gather | solution.py:586
  725.9 5.1 copy.310
  731.1 3.6 reshape.299
  734.7 4.2 broadcast_multiply_fusion.7
  738.9 4.1 broadcast_multiply_fusion.6
  743.0 4.2 broadcast_multiply_fusion.5
  747.2 4.1 broadcast_multiply_fusion.4
  751.3 4.1 broadcast_multiply_fusion.3
  755.5 4.0 broadcast_multiply_fusion.2
  759.5 4.1 broadcast_multiply_fusion.1
  763.6 4.1 broadcast_multiply_fusion
  767.7 22.7 %fusion.8 = bf16[16,8,32,512]{3,2,1,0:T(8,128)(2,1)} fusion(f32[16,8,32,512]{3,2,1,0:T(8,128)} %broadcast_multiply_fusion.7, f32[16,8,32,512]{3,2,1,0:T(8,128)} %broadcast_multiply_fusion.6, f32[16,8,32,512]{3,2,1,0:T(8,128)} %broadcast_multiply_fusion.5, f32[16,8,32,512]{3,2,1,0:T(8,128)} %broadcast_multiply_fusion.4, ...), kind=kOutput, calls=%fused_computation.24 | convolution fusion | flops 1092616192 | bytes 73662464 | tf_op jit(solution)/shard_map/nhwo,co->nhwc/dot_general | solution.py:53
  790.5 5.0 fusion.164
  801.9 41.8 %psum.110 = f32[2,4,512]{2,1,0:T(4,128)S(1)} all-reduce(f32[2,4,512]{2,1,0:T(4,128)S(1)} %reshape.300), channel_id=1, replica_groups=mesh['batch'=8,'chan'=4] {'batch','chan'}, use_global_device_ids=true, to_apply=%region_42.43 | all-reduce | flops 4096 | bytes 32768 | tf_op jit(solution)/shard_map/psum | solution.py:622
  847.6 6.5 fusion.177
  865.8 13.8 %reduce-scatter.23.cloned.1.call-done = bf16[2,8,32,512]{3,2,1,0:T(8,128)(2,1)} async-done(((bf16[16,8,32,512]{3,2,1,0:T(8,128)(2,1)}), bf16[2,8,32,512]{3,2,1,0:T(8,128)(2,1)}) %reduce-scatter.23.cloned.1.call-update) | async-done | bytes 524304 | tf_op jit(solution)/shard_map/reduce_scatter | solution.py:415
  881.4 20.6 %all-reduce.33 = (f32[2,512]{1,0:T(2,128)S(1)}, f32[2,512]{1,0:T(2,128)S(1)}) all-reduce(f32[2,512]{1,0:T(2,128)S(1)} %get-tuple-element.76, f32[2,512]{1,0:T(2,128)S(1)} %get-tuple-element.75), channel_id=1, replica_groups=mesh['batch'=8,'chan'=4] {'batch'}, use_global_device_ids=true, to_apply=%region_24.25 | all-reduce | flops 2048 | bytes 16384 | tf_op jit(solution)/shard_map/psum | solution.py:399
  910.2 6.6 fusion.207
  916.8 12.2 %reduce-scatter.33.cloned.1.call-done = bf16[128,512]{1,0:T(8,128)(2,1)} async-done(((bf16[512,512]{1,0:T(8,128)(2,1)}), bf16[128,512]{1,0:T(8,128)(2,1)}) %reduce-scatter.33.cloned.1.call-update) | async-done | bytes 131088
  930.9 21.4 %all-reduce.32 = (f32[2,128]{1,0:T(2,128)S(1)}, f32[2,128]{1,0:T(2,128)S(1)}) all-reduce(f32[2,128]{1,0:T(2,128)S(1)} %get-tuple-element.82, f32[2,128]{1,0:T(2,128)S(1)} %get-tuple-element.81), channel_id=1, replica_groups=mesh['batch'=8,'chan'=4] {'batch'}, use_global_device_ids=true, to_apply=%region_29.30 | all-reduce | flops 512 | bytes 4096 | tf_op jit(solution)/shard_map/psum | solution.py:399
  962.7 6.5 fusion.213
  975.7 4.7 reduce-scatter.35.cloned.1.call-done
  982.4 21.9 %all-reduce.31 = (f32[2,128]{1,0:T(2,128)S(1)}, f32[2,128]{1,0:T(2,128)S(1)}, f32[2,128]{1,0:T(2,128)}) all-reduce(f32[2,128]{1,0:T(2,128)S(1)} %get-tuple-element.84, f32[2,128]{1,0:T(2,128)S(1)} %get-tuple-element.83, f32[2,128]{1,0:T(2,128)S(1)} %copy-done.146), channel_id=1, replica_groups=mesh['batch'=8,'chan'=4] {'batch'}, use_global_device_ids=true, to_apply=%region_34.35 | all-reduce | flops 768 | bytes 6144 | tf_op jit(solution)/shard_map/psum | solution.py:399
  1004.4 6.7 all_gather.60
  1019.4 6.3 fusion.219
  1030.2 15.8 %reduce-scatter.29.cloned.1.call-done = bf16[64,512]{1,0:T(8,128)(2,1)} async-done(((bf16[512,512]{1,0:T(8,128)(2,1)}), bf16[64,512]{1,0:T(8,128)(2,1)}) %reduce-scatter.29.cloned.1.call-update) | async-done | bytes 65552 | tf_op jit(solution)/shard_map/reduce_scatter | solution.py:415
  1050.1 60.2 %reduce-scatter.25.cloned.1.call-done = bf16[512,64]{0,1:T(8,128)(2,1)} async-done(((bf16[512,512]{0,1:T(8,128)(2,1)}), bf16[512,64]{0,1:T(8,128)(2,1)}) %reduce-scatter.25.cloned.1.call-update) | async-done | bytes 65552 | tf_op jit(solution)/shard_map/reduce_scatter | solution.py:415
  1111.8 65.8 %reduce-scatter.27.cloned.1.call-done = bf16[9,64,128]{2,1,0:T(8,128)(2,1)} async-done(((bf16[9,512,128]{2,1,0:T(8,128)(2,1)}), bf16[9,64,128]{2,1,0:T(8,128)(2,1)}) %reduce-scatter.27.cloned.1.call-update) | async-done | bytes 147472 | tf_op jit(solution)/shard_map/reduce_scatter | solution.py:415
  (493 shorter events, 197.5 us)
Async XLA Ops:
  8.0 41.0 %copy-start.153 = (f32[2,128]{1,0:T(2,128)S(1)}, f32[2,128]{1,0:T(2,128)}, u32[]{:S(2)}) copy-start(f32[2,128]{1,0:T(2,128)} %param.24) | copy-start | bytes 3076
  8.0 41.0 %copy-start.154 = (f32[2,128]{1,0:T(2,128)S(1)}, f32[2,128]{1,0:T(2,128)}, u32[]{:S(2)}) copy-start(f32[2,128]{1,0:T(2,128)} %param.23) | copy-start | bytes 3076
  8.0 41.0 %copy-start.120 = (s32[2,8,32]{2,1,0:T(8,128)S(1)}, s32[2,8,32]{2,1,0:T(8,128)}, u32[]{:S(2)}) copy-start(s32[2,8,32]{2,1,0:T(8,128)} %param.17) | copy-start | bytes 6148
  8.0 41.8 %copy-start.111 = (bf16[64,512]{1,0:T(8,128)(2,1)S(1)}, bf16[64,512]{1,0:T(8,128)(2,1)}, u32[]{:S(2)}) copy-start(bf16[64,512]{1,0:T(8,128)(2,1)} %param.20) | copy-start | bytes 196612
  8.1 75.7 %reduce-scatter.31.cloned.1.call-start = ((), (), s32[]{:S(2)}) async-start(), calls=%async_computation.24 | async-start | bytes 655360
  48.4 70.1 %all-gather.8.cloned.1.call-start = ((), (), s32[]{:S(2)}) async-start(), calls=%async_computation.11 | async-start | bytes 1327104 | tf_op jit(solution)/shard_map/all_gather | solution.py:479
  49.0 195.9 %all-gather.10.cloned.1.call-start = ((), (), s32[]{:S(2)}) async-start(), calls=%async_computation.12 | async-start | bytes 4718592 | tf_op jit(solution)/shard_map/all_gather | solution.py:501
  49.1 66.7 %copy-start.136 = (f32[128]{0:T(128)}, f32[128]{0:T(128)S(1)}, u32[]{:S(2)}) copy-start(f32[128]{0:T(128)S(1)} %get-tuple-element.245) | copy-start | bytes 1540
  49.1 66.7 %copy-start.142 = (f32[128]{0:T(128)}, f32[128]{0:T(128)S(1)}, u32[]{:S(2)}) copy-start(f32[128]{0:T(128)S(1)} %get-tuple-element.241) | copy-start | bytes 1540
  49.1 94.2 %copy-start.132 = (f32[128]{0:T(128)}, f32[128]{0:T(128)S(1)}, u32[]{:S(2)}) copy-start(f32[128]{0:T(128)S(1)} %get-tuple-element.246) | copy-start | bytes 1540
  49.1 94.2 %copy-start.134 = (f32[128]{0:T(128)}, f32[128]{0:T(128)S(1)}, u32[]{:S(2)}) copy-start(f32[128]{0:T(128)S(1)} %get-tuple-element.240) | copy-start | bytes 1540
  124.3 47.9 %copy-start.121 = (f32[512]{0:T(512)S(1)}, f32[512]{0:T(512)}, u32[]{:S(2)}) copy-start(f32[512]{0:T(512)} %param.28) | copy-start | bytes 6148
  124.3 49.1 %copy-start.30 = (bf16[2,8,32,512]{3,2,1,0:T(8,128)(2,1)S(1)}, bf16[2,8,32,512]{3,2,1,0:T(8,128)(2,1)}, u32[]{:S(2)}) copy-start(bf16[2,8,32,512]{3,2,1,0:T(8,128)(2,1)} %param.16) | copy-start | bytes 1572868
  124.3 49.1 %copy-start.138 = (f32[512]{0:T(512)S(1)}, f32[512]{0:T(512)}, u32[]{:S(2)}) copy-start(f32[512]{0:T(512)} %param.29) | copy-start | bytes 6148
  152.7 97.8 %copy-start.9 = (f32[2,8,32,512]{3,2,1,0:T(8,128)}, f32[2,8,32,512]{3,2,1,0:T(8,128)S(1)}, u32[]{:S(2)}) copy-start(f32[2,8,32,512]{3,2,1,0:T(8,128)S(1)} %get-tuple-element.244) | copy-start | bytes 3145732
  174.6 144.8 %reduce-scatter.17.cloned.1.call-start = ((), (), s32[]{:S(2)}) async-start(), calls=%async_computation.13 | async-start | bytes 2621440 | tf_op jit(solution)/shard_map/reduce_scatter | solution.py:506
  206.4 149.4 %copy-start.91 = (bf16[16,8,32]{2,1,0:T(8,128)(2,1)}, bf16[16,8,32]{2,1,0:T(8,128)(2,1)S(1)}, u32[]{:S(2)}) copy-start(bf16[16,8,32]{2,1,0:T(8,128)(2,1)S(1)} %get-tuple-element.208) | copy-start | bytes 24580
  206.4 149.4 %copy-start.93 = (bf16[16,8,32]{2,1,0:T(8,128)(2,1)}, bf16[16,8,32]{2,1,0:T(8,128)(2,1)S(1)}, u32[]{:S(2)}) copy-start(bf16[16,8,32]{2,1,0:T(8,128)(2,1)S(1)} %get-tuple-element.196) | copy-start | bytes 24580
  206.4 149.4 %copy-start.95 = (bf16[16,8,32]{2,1,0:T(8,128)(2,1)}, bf16[16,8,32]{2,1,0:T(8,128)(2,1)S(1)}, u32[]{:S(2)}) copy-start(bf16[16,8,32]{2,1,0:T(8,128)(2,1)S(1)} %get-tuple-element.198) | copy-start | bytes 24580
  206.4 149.4 %copy-start.97 = (bf16[16,8,32]{2,1,0:T(8,128)(2,1)}, bf16[16,8,32]{2,1,0:T(8,128)(2,1)S(1)}, u32[]{:S(2)}) copy-start(bf16[16,8,32]{2,1,0:T(8,128)(2,1)S(1)} %get-tuple-element.200) | copy-start | bytes 24580
  206.4 149.4 %copy-start.99 = (bf16[16,8,32]{2,1,0:T(8,128)(2,1)}, bf16[16,8,32]{2,1,0:T(8,128)(2,1)S(1)}, u32[]{:S(2)}) copy-start(bf16[16,8,32]{2,1,0:T(8,128)(2,1)S(1)} %get-tuple-element.202) | copy-start | bytes 24580
  206.4 149.4 %copy-start.101 = (bf16[16,8,32]{2,1,0:T(8,128)(2,1)}, bf16[16,8,32]{2,1,0:T(8,128)(2,1)S(1)}, u32[]{:S(2)}) copy-start(bf16[16,8,32]{2,1,0:T(8,128)(2,1)S(1)} %get-tuple-element.204) | copy-start | bytes 24580
  206.5 149.4 %copy-start.103 = (bf16[16,8,32]{2,1,0:T(8,128)(2,1)}, bf16[16,8,32]{2,1,0:T(8,128)(2,1)S(1)}, u32[]{:S(2)}) copy-start(bf16[16,8,32]{2,1,0:T(8,128)(2,1)S(1)} %get-tuple-element.111) | copy-start | bytes 24580
  206.5 149.4 %copy-start.105 = (bf16[16,8,32]{2,1,0:T(8,128)(2,1)}, bf16[16,8,32]{2,1,0:T(8,128)(2,1)S(1)}, u32[]{:S(2)}) copy-start(bf16[16,8,32]{2,1,0:T(8,128)(2,1)S(1)} %get-tuple-element.206) | copy-start | bytes 24580
  209.0 41.5 %copy-start.60 = (bf16[1,512,4,64]{1,3,2,0:T(8,128)(2,1)}, bf16[1,512,4,64]{1,3,2,0:T(8,128)(2,1)S(1)}, u32[]{:S(2)}) copy-start(bf16[1,512,4,64]{1,3,2,0:T(8,128)(2,1)S(1)} %get-tuple-element.158) | copy-start | bytes 786436
  209.0 41.5 %copy-start.62 = (bf16[1,512,4,64]{1,3,2,0:T(8,128)(2,1)}, bf16[1,512,4,64]{1,3,2,0:T(8,128)(2,1)S(1)}, u32[]{:S(2)}) copy-start(bf16[1,512,4,64]{1,3,2,0:T(8,128)(2,1)S(1)} %get-tuple-element.159) | copy-start | bytes 786436
  209.0 44.4 %copy-start.64 = (bf16[1,512,4,64]{1,3,2,0:T(8,128)(2,1)}, bf16[1,512,4,64]{1,3,2,0:T(8,128)(2,1)S(1)}, u32[]{:S(2)}) copy-start(bf16[1,512,4,64]{1,3,2,0:T(8,128)(2,1)S(1)} %get-tuple-element.152) | copy-start | bytes 786436
  209.0 47.4 %copy-start.66 = (bf16[1,512,4,64]{1,3,2,0:T(8,128)(2,1)}, bf16[1,512,4,64]{1,3,2,0:T(8,128)(2,1)S(1)}, u32[]{:S(2)}) copy-start(bf16[1,512,4,64]{1,3,2,0:T(8,128)(2,1)S(1)} %get-tuple-element.153) | copy-start | bytes 786436
  209.0 50.6 %copy-start.68 = (bf16[1,512,4,64]{1,3,2,0:T(8,128)(2,1)}, bf16[1,512,4,64]{1,3,2,0:T(8,128)(2,1)S(1)}, u32[]{:S(2)}) copy-start(bf16[1,512,4,64]{1,3,2,0:T(8,128)(2,1)S(1)} %get-tuple-element.154) | copy-start | bytes 786436
  209.1 53.8 %copy-start.70 = (bf16[1,512,4,64]{1,3,2,0:T(8,128)(2,1)}, bf16[1,512,4,64]{1,3,2,0:T(8,128)(2,1)S(1)}, u32[]{:S(2)}) copy-start(bf16[1,512,4,64]{1,3,2,0:T(8,128)(2,1)S(1)} %get-tuple-element.155) | copy-start | bytes 786436
  209.1 59.8 %copy-start.72 = (bf16[1,512,4,64]{1,3,2,0:T(8,128)(2,1)}, bf16[1,512,4,64]{1,3,2,0:T(8,128)(2,1)S(1)}, u32[]{:S(2)}) copy-start(bf16[1,512,4,64]{1,3,2,0:T(8,128)(2,1)S(1)} %get-tuple-element.156) | copy-start | bytes 786436
  285.8 39.4 %copy-start.59 = (bf16[2,9,4,64,128]{4,3,2,1,0:T(8,128)(2,1)S(1)}, bf16[2,9,4,64,128]{4,3,2,1,0:T(8,128)(2,1)}, u32[]{:S(2)}) copy-start(bf16[2,9,4,64,128]{4,3,2,1,0:T(8,128)(2,1)} %param.22) | copy-start | bytes 3538948
  289.4 58.2 %all-gather.12.cloned.1.call-start = ((), (), s32[]{:S(2)}) async-start(), calls=%async_computation.14 | async-start | bytes 2621440 | tf_op jit(solution)/shard_map/all_gather | solution.py:523
  300.1 24.7 %copy-start.147 = (f32[128]{0:T(128)}, f32[128]{0:T(128)S(1)}, u32[]{:S(2)}) copy-start(f32[128]{0:T(128)S(1)} %fusion.423) | copy-start | bytes 1540
  322.6 30.1 %copy-start.140 = (f32[128]{0:T(128)}, f32[128]{0:T(128)S(1)}, u32[]{:S(2)}) copy-start(f32[128]{0:T(128)S(1)} %get-tuple-element.109) | copy-start | bytes 1540
  324.8 221.6 %reduce-scatter.19.cloned.1.call-start = ((), (), s32[]{:S(2)}) async-start(), calls=%async_computation.15 | async-start | bytes 4718592 | tf_op jit(solution)/shard_map/reduce_scatter | solution.py:415
  363.6 26.0 %copy-start.21 = (bf16[16,8,32,256]{3,2,1,0:T(8,128)(2,1)}, bf16[16,8,32,256]{3,2,1,0:T(8,128)(2,1)S(1)}, u32[]{:S(2)}) copy-start(bf16[16,8,32,256]{3,2,1,0:T(8,128)(2,1)S(1)} %get-tuple-element.161) | copy-start | bytes 6291460
  414.0 136.6 %all-gather.16.cloned.1.call-start = ((), (), s32[]{:S(2)}) async-start(), calls=%async_computation.18 | async-start | bytes 8650752 | tf_op jit(solution)/shard_map/all_gather | solution.py:568
  417.8 57.3 %all-to-all-start = ((bf16[16,8,32,128]{3,2,1,0:T(8,128)(2,1)}), bf16[16,8,32,128]{3,2,1,0:T(8,128)(2,1)}, u32[]{:S(2)}, u32[]{:S(2)}) async-start(bf16[16,8,32,128]{3,2,1,0:T(8,128)(2,1)} %pad_maximum_fusion.1), calls=%async_computation.1 | async-start | bytes 2097152 | tf_op jit(solution)/shard_map/all_to_all | solution.py:534
  423.3 200.4 %all-gather.14.cloned.1.call-start = ((), (), s32[]{:S(2)}) async-start(), calls=%async_computation.16 | async-start | bytes 4718592 | tf_op jit(solution)/shard_map/all_gather | solution.py:555
  550.5 149.3 %reduce-scatter.21.cloned.1.call-start = ((), (), s32[]{:S(2)}) async-start(), calls=%async_computation.17 | async-start | bytes 2621440 | tf_op jit(solution)/shard_map/reduce_scatter | solution.py:562
  669.9 56.0 %all-gather.18.cloned.1.call-start = ((), (), s32[]{:S(2)}) async-start(), calls=%async_computation.23 | async-start | bytes 2621440 | tf_op jit(solution)/shard_map/all_gather | solution.py:586
  679.4 22.6 %copy-start.151 = (f32[128]{0:T(128)S(1)}, f32[128]{0:T(128)}, u32[]{:S(2)}) copy-start(f32[128]{0:T(128)} %get-tuple-element.108) | copy-start | bytes 1540
  703.2 176.4 %reduce-scatter.23.cloned.1.call-start = ((), (), s32[]{:S(2)}) async-start(), calls=%async_computation.19 | async-start | bytes 4718592 | tf_op jit(solution)/shard_map/reduce_scatter | solution.py:415
  790.4 138.6 %reduce-scatter.33.cloned.1.call-start = ((), (), s32[]{:S(2)}) async-start(), calls=%async_computation.25 | async-start | bytes 655360
  801.5 46.0 %copy-start.106 = (bf16[16,8,32]{2,1,0:T(8,128)(2,1)S(1)}, bf16[16,8,32]{2,1,0:T(8,128)(2,1)}, u32[]{:S(2)}) copy-start(bf16[16,8,32]{2,1,0:T(8,128)(2,1)} %copy-done.105) | copy-start | bytes 24580
  863.6 38.3 %copy-start.131 = (f32[2,512]{1,0:T(2,128)S(1)}, f32[2,512]{1,0:T(2,128)}, u32[]{:S(2)}) copy-start(f32[2,512]{1,0:T(2,128)} %get-tuple-element.212) | copy-start | bytes 12292
  865.8 37.3 %copy-start.56 = (bf16[512,512]{1,0:T(8,128)(2,1)S(1)}, bf16[512,512]{1,0:T(8,128)(2,1)}, u32[]{:S(2)}) copy-start(bf16[512,512]{1,0:T(8,128)(2,1)} %all_gather.50) | copy-start | bytes 1572868
  910.1 42.3 %copy-start.145 = (f32[2,128]{1,0:T(2,128)S(1)}, f32[2,128]{1,0:T(2,128)}, u32[]{:S(2)}) copy-start(f32[2,128]{1,0:T(2,128)} %get-tuple-element.231) | copy-start | bytes 3076
  910.1 42.4 %copy-start.25 = (bf16[9,512,128]{2,1,0:T(8,128)(2,1)S(1)}, bf16[9,512,128]{2,1,0:T(8,128)(2,1)}, u32[]{:S(2)}) copy-start(bf16[9,512,128]{2,1,0:T(8,128)(2,1)} %all-gather.8.cloned.1.call-done) | copy-start | bytes 3538948
  910.1 42.4 %copy-start.119 = (f32[2,8,32]{2,1,0:T(8,128)S(1)}, f32[2,8,32]{2,1,0:T(8,128)}, u32[]{:S(2)}) copy-start(f32[2,8,32]{2,1,0:T(8,128)} %get-tuple-element.225) | copy-start | bytes 6148
  910.1 42.8 %copy-start.118 = (f32[2,8,32]{2,1,0:T(8,128)S(1)}, f32[2,8,32]{2,1,0:T(8,128)}, u32[]{:S(2)}) copy-start(f32[2,8,32]{2,1,0:T(8,128)} %get-tuple-element.223) | copy-start | bytes 6148
  910.1 70.4 %reduce-scatter.35.cloned.1.call-start = ((), (), s32[]{:S(2)}) async-start(), calls=%async_computation.26 | async-start | bytes 655360
  916.8 36.4 %copy-start.117 = (f32[2,8,32]{2,1,0:T(8,128)S(1)}, f32[2,8,32]{2,1,0:T(8,128)}, u32[]{:S(2)}) copy-start(f32[2,8,32]{2,1,0:T(8,128)} %get-tuple-element.221) | copy-start | bytes 6148
  916.8 36.7 %copy-start.116 = (f32[2,8,32]{2,1,0:T(8,128)S(1)}, f32[2,8,32]{2,1,0:T(8,128)}, u32[]{:S(2)}) copy-start(f32[2,8,32]{2,1,0:T(8,128)} %get-tuple-element.219) | copy-start | bytes 6148
  916.8 37.0 %copy-start.115 = (f32[2,8,32]{2,1,0:T(8,128)S(1)}, f32[2,8,32]{2,1,0:T(8,128)}, u32[]{:S(2)}) copy-start(f32[2,8,32]{2,1,0:T(8,128)} %get-tuple-element.217) | copy-start | bytes 6148
  930.3 23.9 %copy-start.114 = (f32[2,8,32]{2,1,0:T(8,128)S(1)}, f32[2,8,32]{2,1,0:T(8,128)}, u32[]{:S(2)}) copy-start(f32[2,8,32]{2,1,0:T(8,128)} %get-tuple-element.215) | copy-start | bytes 6148
  962.3 83.7 %reduce-scatter.29.cloned.1.call-start = ((), (), s32[]{:S(2)}) async-start(), calls=%async_computation.22 | async-start | bytes 589824 | tf_op jit(solution)/shard_map/reduce_scatter | solution.py:415
  970.5 33.7 %copy-start.144 = (f32[2,128]{1,0:T(2,128)S(1)}, f32[2,128]{1,0:T(2,128)}, u32[]{:S(2)}) copy-start(f32[2,128]{1,0:T(2,128)} %get-tuple-element.229) | copy-start | bytes 3076
  970.6 139.8 %reduce-scatter.25.cloned.1.call-start = ((), (), s32[]{:S(2)}) async-start(), calls=%async_computation.20 | async-start | bytes 589824 | tf_op jit(solution)/shard_map/reduce_scatter | solution.py:415
  971.6 40.2 %copy-start.32 = (bf16[2,8,32,512]{3,2,1,0:T(8,128)(2,1)S(1)}, bf16[2,8,32,512]{3,2,1,0:T(8,128)(2,1)}, u32[]{:S(2)}) copy-start(bf16[2,8,32,512]{3,2,1,0:T(8,128)(2,1)} %param.16) | copy-start | bytes 1572868
  1013.2 164.5 %reduce-scatter.27.cloned.1.call-start = ((), (), s32[]{:S(2)}) async-start(), calls=%async_computation.21 | async-start | bytes 1327104 | tf_op jit(solution)/shard_map/reduce_scatter | solution.py:415
  1025.7 23.0 %copy-start.29 = (bf16[512,512]{0,1:T(8,128)(2,1)S(1)}, bf16[512,512]{0,1:T(8,128)(2,1)}, u32[]{:S(2)}) copy-start(bf16[512,512]{0,1:T(8,128)(2,1)} %copy-done.28) | copy-start | bytes 1572868
  1025.7 23.0 %copy-start.58 = (bf16[2,8,32,512]{3,2,1,0:T(8,128)(2,1)S(1)}, bf16[2,8,32,512]{3,2,1,0:T(8,128)(2,1)}, u32[]{:S(2)}) copy-start(bf16[2,8,32,512]{3,2,1,0:T(8,128)(2,1)} %copy-done.57) | copy-start | bytes 1572868
  (108 other events, 784.5 us)
Sparse Core Ops, SparseCore 0:
  48.5 22.7 reduce-scatter.30
  289.5 29.8 reduce-scatter.16
  324.9 22.5 all-gather.11
  417.8 124.4 all-gather.15
  550.6 73.1 all-gather.13
  670.0 29.6 reduce-scatter.20
  703.3 22.5 all-gather.17
  910.1 18.8 reduce-scatter.32
  962.5 17.9 reduce-scatter.34
  984.0 61.9 reduce-scatter.28
  1049.4 60.9 reduce-scatter.24
  1114.0 63.5 reduce-scatter.26
Sparse Core Ops, SparseCore 1:
  51.1 43.4 all-gather.7
  174.6 70.1 all-gather.9
  414.1 132.2 reduce-scatter.18
  790.5 89.0 reduce-scatter.22

commit v2 on v1

--- a/solution.py
+++ b/solution.py
@@ -1,6 +1,10 @@
+import functools
+
 import jax
 import jax.numpy as jnp
 from jax import lax
+from jax.experimental import pallas as pl
+from jax.experimental.pallas import tpu as pltpu
 from jax.sharding import PartitionSpec as P
 
 EPSILON = 1e-05
@@ -436,18 +440,865 @@
     return jnp.concatenate(columns, axis=2)
 
 
-def distil_blocks(grads, width):
-    outs = []
+MESH = pl.DeviceIdType.MESH
+PIXELS = 256
+PAD = 32
+LANES = 128
+
+
+def whereabouts():
+    place, lane = lax.axis_index("batch"), lax.axis_index("chan")
+    return place, lane, place // 2, place % 2, lane // 2, lane % 2
+
+
+def along(depth, step):
+    return 2 * ((depth // 2 + step // 2) % 2) + (depth % 2 + step % 2) % 2
+
+
+def push(source, target, send_sem, recv_sem, place, lane):
+    return pltpu.make_async_remote_copy(
+        src_ref=source,
+        dst_ref=target,
+        send_sem=send_sem,
+        recv_sem=recv_sem,
+        device_id=(place, lane),
+        device_id_type=MESH,
+    )
+
+
+def greet(peers):
+    barrier = pltpu.get_barrier_semaphore()
+    for place, lane in peers:
+        pl.semaphore_signal(barrier, inc=1, device_id=(place, lane), device_id_type=MESH)
+    pl.semaphore_wait(barrier, len(peers))
+
+
+def batch_peers():
+    place, lane, depth, side, _, _ = whereabouts()
+    peers = [(along(depth, step) * 2 + side, lane) for step in range(1, 4)]
+    return peers + [(along(depth, step) * 2 + 1 - side, lane) for step in range(4)]
+
+
+def link_peers():
+    place, lane, depth, side, _, _ = whereabouts()
+    return [(along(depth, step) * 2 + side, lane) for step in range(1, 4)] + [
+        (depth * 2 + 1 - side, lane)
+    ]
+
+
+def chan_peers():
+    place, lane, _, _, _, _ = whereabouts()
+    return [(place, (lane + step) % 4) for step in range(1, 4)]
+
+
+def clear_edges(turned):
+    edge = jnp.zeros((3, PAD, turned.shape[2]), turned.dtype)
+    turned[:, 0:PAD] = edge
+    turned[:, PAD + PIXELS :] = edge
+
+
+def fill_columns(value, mask, turned, columns, row):
+    width = value.shape[1]
+    wide = value.astype(jnp.float32)
+    inner = slice(PAD, PAD + PIXELS)
+    turned[0, inner] = pltpu.roll(wide, 1, 0).astype(jnp.bfloat16)
+    turned[1, inner] = value
+    turned[2, inner] = pltpu.roll(wide, PIXELS - 1, 0).astype(jnp.bfloat16)
+    for number, (vertical, lateral) in enumerate(OFFSETS):
+        start = PAD + 32 * vertical
+        columns[row : row + PIXELS, number * width : (number + 1) * width] = (
+            turned[lateral + 1, start : start + PIXELS] * mask[:, number : number + 1]
+        )
+
+
+def own_block(source, everything, recv_sem, z_sem, x_sem):
+    place, lane, depth, side, _, _ = whereabouts()
+    mine = everything.at[place]
+    for step in range(1, 4):
+        push(
+            mine, mine, z_sem.at[step - 1], recv_sem.at[place], along(depth, step) * 2 + side, lane
+        ).start()
+    push(mine, mine, x_sem.at[0], recv_sem.at[place], depth * 2 + 1 - side, lane).start()
+
+
+def next_block(step, everything, recv_sem, z_sem, x_sem):
+    place, lane, depth, side, _, _ = whereabouts()
+    far = step // 2
+    block = along(depth, far) * 2 + (side + step % 2) % 2
+    here = everything.at[block]
+
+    @pl.when(step > 0)
+    def _():
+        push(here, here, z_sem.at[0], recv_sem.at[block], place, lane).wait_recv()
+
+    @pl.when((step > 0) & (step % 2 == 0))
+    def _():
+        push(here, here, x_sem.at[far], recv_sem.at[block], depth * 2 + 1 - side, lane).start()
+
+    return block
+
+
+def sent_blocks(everything, recv_sem, z_sem, x_sem):
+    place, lane, depth, side, _, _ = whereabouts()
+    mine = everything.at[place]
+    for step in range(3):
+        push(mine, mine, z_sem.at[step], recv_sem.at[place], place, lane).wait_send()
+    for step in range(4):
+        push(mine, mine, x_sem.at[step], recv_sem.at[place], place, lane).wait_send()
+
+
+def send_pieces(part, block, stage, got, stage_sem, got_sem):
+    place, lane, _, _, _, _ = whereabouts()
+    for micro in range(2):
+        for half in range(2):
+            piece = part[micro * PIXELS : (micro + 1) * PIXELS, half * LANES : (half + 1) * LANES]
+            target = half * 2 + micro
+
+            @pl.when(target == lane)
+            def _():
+                got[lane, block] = piece
+
+            @pl.when(target != lane)
+            def _():
+                stage[target, block] = piece
+                push(
+                    stage.at[target, block],
+                    got.at[lane, block],
+                    stage_sem.at[target, block],
+                    got_sem.at[lane, block],
+                    place,
+                    target,
+                ).start()
+
+
+def await_pieces(stage, got, stage_sem, got_sem):
+    place, lane, _, _, _, _ = whereabouts()
+
+    def body(block, _):
+        for step in range(1, 4):
+            other = (lane + step) % 4
+            push(
+                stage.at[other, block],
+                got.at[other, block],
+                stage_sem.at[other, block],
+                got_sem.at[other, block],
+                place,
+                lane,
+            ).wait()
+        return 0
+
+    lax.fori_loop(0, 8, body, 0)
+
+
+CHUNKS = 4
+
+
+def spread_chunk(chunk, values, out_sem, in_sem):
+    place, lane, _, _, upper, core = whereabouts()
+    here = values.at[upper, core, pl.ds(2 * chunk, 2)]
+    push(
+        here, here, out_sem.at[0, chunk], in_sem.at[upper, core, chunk], place, upper * 2 + 1 - core
+    ).start()
+    push(
+        here, here, out_sem.at[1, chunk], in_sem.at[upper, core, chunk], place, 2 - 2 * upper + core
+    ).start()
+
+
+def finish_chunks(values, out_sem, in_sem):
+    place, lane, _, _, upper, core = whereabouts()
+
+    def relay(chunk, _):
+        here = values.at[1 - upper, core, pl.ds(2 * chunk, 2)]
+        copy = push(
+            here,
+            here,
+            out_sem.at[2, chunk],
+            in_sem.at[1 - upper, core, chunk],
+            place,
+            upper * 2 + 1 - core,
+        )
+        copy.wait_recv()
+        copy.start()
+        return 0
+
+    lax.fori_loop(0, CHUNKS, relay, 0)
+
+    def close(chunk, _):
+        for half in range(2):
+            here = values.at[half, 1 - core, pl.ds(2 * chunk, 2)]
+            push(
+                here, here, out_sem.at[0, chunk], in_sem.at[half, 1 - core, chunk], place, lane
+            ).wait_recv()
+        here = values.at[upper, core, pl.ds(2 * chunk, 2)]
+        for path in range(3):
+            push(
+                here, here, out_sem.at[path, chunk], in_sem.at[upper, core, chunk], place, lane
+            ).wait_send()
+        return 0
+
+    lax.fori_loop(0, CHUNKS, close, 0)
+
+
+def heads_kernel(
+    count,
+    block_ref,
+    weight_ref,
+    mask_ref,
+    scale_ref,
+    shift_ref,
+    all_ref,
+    act_ref,
+    norm_ref,
+    inverse_ref,
+    turned,
+    columns,
+    stage,
+    got,
+    recv_sem,
+    z_sem,
+    x_sem,
+    stage_sem,
+    got_sem,
+    out_sem,
+    in_sem,
+):
+    place, lane, depth, side, upper, core = whereabouts()
+    greet(link_peers() + chan_peers())
+    all_ref[place] = block_ref[...]
+    own_block(block_ref, all_ref, recv_sem, z_sem, x_sem)
+    clear_edges(turned)
+
+    def body(step, _):
+        block = next_block(step, all_ref, recv_sem, z_sem, x_sem)
+        for micro in range(2):
+            fill_columns(
+                all_ref[block, micro], mask_ref[block, micro], turned, columns, micro * PIXELS
+            )
+        part = jnp.dot(columns[...], weight_ref[...], preferred_element_type=jnp.float32)
+        send_pieces(part.astype(jnp.bfloat16), block, stage, got, stage_sem, got_sem)
+        return 0
+
+    lax.fori_loop(0, 8, body, 0)
+    await_pieces(stage, got, stage_sem, got_sem)
+
+    def collect(block, sums):
+        value = got[0, block].astype(jnp.float32)
+        for other in range(1, 4):
+            value = value + got[other, block].astype(jnp.float32)
+        norm_ref[block] = value
+        return (
+            sums[0] + jnp.sum(value, axis=0, keepdims=True),
+            sums[1] + jnp.sum(value * value, axis=0, keepdims=True),
+        )
+
+    zero = jnp.zeros((1, LANES), jnp.float32)
+    total, squares = lax.fori_loop(0, 8, collect, (zero, zero))
+    center = total / count
+    inverse = lax.rsqrt(squares / count - center * center + EPSILON)
+    inverse_ref[...] = inverse
+
+    def activate(chunk, _):
+        for item in range(2):
+            block = 2 * chunk + item
+            normed = (norm_ref[block] - center) * inverse
+            norm_ref[block] = normed
+            out = normed * scale_ref[...] + shift_ref[...]
+            act_ref[upper, core, block] = (out * jax.nn.sigmoid(out)).astype(jnp.bfloat16)
+        spread_chunk(chunk, act_ref, out_sem, in_sem)
+        return 0
+
+    lax.fori_loop(0, CHUNKS, activate, 0)
+    finish_chunks(act_ref, out_sem, in_sem)
+    sent_blocks(all_ref, recv_sem, z_sem, x_sem)
+
+
+def vmem(count):
+    return [pl.BlockSpec(memory_space=pltpu.VMEM)] * count
+
+
+def chan_scratch():
+    return [
+        pltpu.VMEM((4, 8, PIXELS, LANES), jnp.bfloat16),
+        pltpu.VMEM((4, 8, PIXELS, LANES), jnp.bfloat16),
+    ]
+
+
+def gather_sems():
+    return [
+        pltpu.SemaphoreType.DMA((8,)),
+        pltpu.SemaphoreType.DMA((3,)),
+        pltpu.SemaphoreType.DMA((4,)),
+    ]
+
+
+def chan_sems():
+    return [
+        pltpu.SemaphoreType.DMA((4, 8)),
+        pltpu.SemaphoreType.DMA((4, 8)),
+        pltpu.SemaphoreType.DMA((3, CHUNKS)),
+        pltpu.SemaphoreType.DMA((2, 2, CHUNKS)),
+    ]
+
+
+def kernel_params(number):
+    return pltpu.CompilerParams(
+        collective_id=number, has_side_effects=True, vmem_limit_bytes=60 * 2**20
+    )
+
+
+def run_heads(count, block_out, weight, masks, scale, shift):
+    return pl.pallas_call(
+        functools.partial(heads_kernel, count),
+        name="heads",
+        out_shape=(
+            jax.ShapeDtypeStruct((8, 2, PIXELS, 512), jnp.bfloat16),
+            jax.ShapeDtypeStruct((2, 2, 8, PIXELS, LANES), jnp.bfloat16),
+            jax.ShapeDtypeStruct((8, PIXELS, LANES), jnp.float32),
+            jax.ShapeDtypeStruct((1, LANES), jnp.float32),
+        ),
+        in_specs=vmem(5),
+        out_specs=tuple(vmem(4)),
+        scratch_shapes=[
+            pltpu.VMEM((3, 2 * PAD + PIXELS, 512), jnp.bfloat16),
+            pltpu.VMEM((2 * PIXELS, 9 * 512), jnp.bfloat16),
+        ]
+        + chan_scratch()
+        + gather_sems()
+        + chan_sems(),
+        compiler_params=kernel_params(1),
+    )(block_out, weight, masks, scale, shift)
+
+
+def reduce_far(step, part, send_buf, recv_buf, send_sem, recv_sem):
+    place, lane, depth, side, _, _ = whereabouts()
+    far = 3 - step
+    send_buf[far] = part.astype(jnp.bfloat16)
+    push(
+        send_buf.at[far],
+        recv_buf.at[far],
+        send_sem.at[far],
+        recv_sem.at[far],
+        depth * 2 + 1 - side,
+        lane,
+    ).start()
+
+
+def reduce_near(step, part, keep, side_buf, side_sem, send_buf, recv_buf, send_sem, recv_sem):
+    place, lane, depth, side, _, _ = whereabouts()
+    far = 3 - step
+    push(
+        side_buf.at[far], side_buf.at[far], side_sem.at[far], side_sem.at[far], place, lane
+    ).wait_recv()
+    total = part + side_buf[far].astype(jnp.float32)
+
+    @pl.when(far == 0)
+    def _():
+        keep[...] = total
+
+    @pl.when(far > 0)
+    def _():
+        send_buf[far] = total.astype(jnp.bfloat16)
+        push(
+            send_buf.at[far],
+            recv_buf.at[far],
+            send_sem.at[far],
+            recv_sem.at[far],
+            along(depth, far) * 2 + side,
+            lane,
+        ).start()
+
+
+def reduce_close(keep, far_buf, far_sem, far_recv, send_buf, recv_buf, send_sem, recv_sem):
+    place, lane, _, _, _, _ = whereabouts()
+    for far in range(4):
+        push(
+            far_buf.at[far], far_buf.at[far], far_sem.at[far], far_recv.at[far], place, lane
+        ).wait_send()
+    for far in range(1, 4):
+        push(
+            send_buf.at[far], recv_buf.at[far], send_sem.at[far], recv_sem.at[far], place, lane
+        ).wait()
+        keep[...] = keep[...] + recv_buf[far].astype(jnp.float32)
+
+
+def reduce_scratch():
+    return [
+        pltpu.VMEM((2 * PIXELS, 512), jnp.float32),
+        pltpu.VMEM((4, 2 * PIXELS, 512), jnp.bfloat16),
+        pltpu.VMEM((4, 2 * PIXELS, 512), jnp.bfloat16),
+        pltpu.VMEM((4, 2 * PIXELS, 512), jnp.bfloat16),
+        pltpu.VMEM((4, 2 * PIXELS, 512), jnp.bfloat16),
+        pltpu.SemaphoreType.DMA((4,)),
+        pltpu.SemaphoreType.DMA((4,)),
+        pltpu.SemaphoreType.DMA((4,)),
+        pltpu.SemaphoreType.DMA((4,)),
+    ]
+
+
+def far_block(step):
+    _, _, depth, side, _, _ = whereabouts()
+    return along(depth, 3 - step) * 2 + 1 - side
+
+
+def near_block(step):
+    _, _, depth, side, _, _ = whereabouts()
+    return along(depth, 3 - step) * 2 + side
+
+
+def lane_index():
+    return lax.broadcasted_iota(jnp.int32, (PIXELS, LANES), 1)
+
+
+def distil_kernel(
+    count,
+    act_ref,
+    mixed_ref,
+    back_ref,
+    mask_ref,
+    cot_ref,
+    packed_ref,
+    bias_ref,
+    norm_ref,
+    inverse_ref,
+    scale_ref,
+    shift_ref,
+    stream_ref,
+    grad_ref,
+    gate_ref,
+    back_act_ref,
+    sums_ref,
+    turned,
+    columns,
+    turned_wide,
+    columns_wide,
+    grads_all,
+    own_stage,
+    own_got,
+    cot_all,
+    keep,
+    far_send,
+    far_got,
+    near_send,
+    near_got,
+    far_sem,
+    far_recv,
+    near_sem,
+    near_recv,
+    stage,
+    got,
+    own_sem,
+    own_recv,
+    cot_sem,
+    cot_recv,
+    recv_sem,
+    z_sem,
+    x_sem,
+    stage_sem,
+    got_sem,
+    out_sem,
+    in_sem,
+):
+    place, lane, depth, side, upper, core = whereabouts()
+    half_width = LANES // 2
+    greet(batch_peers() + chan_peers())
+    low = lane_index() < half_width
+    source = place // 2 == lane
+
+    for parity in range(2):
+        target = 2 * lane + parity
+
+        @pl.when(target == place)
+        def _():
+            cot_all[place] = packed_ref[parity]
+
+        @pl.when(target != place)
+        def _():
+            push(
+                packed_ref.at[parity],
+                cot_all.at[place],
+                cot_sem.at[parity],
+                cot_recv.at[place],
+                target,
+                lane,
+            ).start()
+
+    @pl.when(source)
+    def _():
+        def pack(step, _):
+            block = along(depth, step // 2) * 2 + (side + step % 2) % 2
+            for micro in range(2):
+                own_stage[block, micro] = jnp.where(
+                    low, act_ref[0, micro, block], act_ref[1, micro, block]
+                )
+
+            @pl.when(block == place)
+            def _():
+                own_got[place % 2] = own_stage[block]
+
+            @pl.when(block != place)
+            def _():
+                push(
+                    own_stage.at[block],
+                    own_got.at[place % 2],
+                    own_sem.at[block],
+                    own_recv.at[place % 2],
+                    block,
+                    lane,
+                ).start()
+
+            return 0
+
+        lax.fori_loop(0, 8, pack, 0)
+
+    clear_edges(turned)
+    clear_edges(turned_wide)
+    grad_ref[...] = jnp.zeros_like(grad_ref)
+
+    def partial(block):
+        for micro in range(2):
+            value = jnp.concatenate([act_ref[0, micro, block], act_ref[1, micro, block]], axis=1)
+            fill_columns(value, mask_ref[block, micro], turned, columns, micro * PIXELS)
+        return jnp.dot(columns[...], mixed_ref[...], preferred_element_type=jnp.float32)
+
+    def far_step(step, _):
+        reduce_far(step, partial(far_block(step)), far_send, far_got, far_sem, far_recv)
+        return 0
+
+    lax.fori_loop(0, 4, far_step, 0)
+
+    def near_step(step, _):
+        reduce_near(
+            step,
+            partial(near_block(step)),
+            keep,
+            far_got,
+            far_recv,
+            near_send,
+            near_got,
+            near_sem,
+            near_recv,
+        )
+        return 0
+
+    lax.fori_loop(0, 4, near_step, 0)
+    for parity in range(2):
+        owner = 2 * lane + parity
+
+        @pl.when(owner != place)
+        def _():
+            push(
+                own_got.at[parity],
+                own_got.at[parity],
+                own_sem.at[0],
+                own_recv.at[parity],
+                place,
+                lane,
+            ).wait_recv()
+
+    reduce_close(
+        keep, far_send, far_sem, far_recv, near_send, near_got, near_sem, near_recv
+    )
     for stream in range(2):
-        gate = grads[:, :, (2 * stream) * 128 : (2 * stream + 1) * 128]
-        message = grads[:, :, (2 * stream + 1) * 128 : (2 * stream + 2) * 128]
-        own = OWN_HEAD[stream]
-        first = SOURCE_START[stream]
-        pieces = [gate[:, own * width : (own + 1) * width]]
-        for source in range(3):
-            pieces.append(message[:, (first + source) * width : (first + source + 1) * width])
-        outs.append(jnp.stack(pieces, axis=1))
-    return jnp.stack(outs)
+        bias_sum = jnp.zeros((1, LANES), jnp.float32)
+        for micro in range(2):
+            rows = slice(micro * PIXELS, (micro + 1) * PIXELS)
+            first = own_got[0, micro].astype(jnp.float32)
+            second = own_got[1, micro].astype(jnp.float32)
+            if stream == 0:
+                second = pltpu.roll(second, half_width, 1)
+            else:
+                first = pltpu.roll(first, half_width, 1)
+            own = jnp.where(low, first, second)
+            column = 2 * stream * LANES
+            gate = jax.nn.sigmoid(
+                keep[rows, column : column + LANES] + bias_ref[stream : stream + 1]
+            )
+            message = keep[rows, column + LANES : column + 2 * LANES]
+            cot = cot_ref[stream, micro].astype(jnp.float32)
+            stream_ref[stream, micro] = (own + gate * message).astype(jnp.bfloat16)
+            gate_grad = (cot * message * gate * (1.0 - gate)).astype(jnp.bfloat16)
+            bias_sum = bias_sum + jnp.sum(gate_grad.astype(jnp.float32), axis=0, keepdims=True)
+            grads_all[place, micro, :, column : column + LANES] = gate_grad
+            grads_all[place, micro, :, column + LANES : column + 2 * LANES] = (cot * gate).astype(
+                jnp.bfloat16
+            )
+        gate_ref[stream : stream + 1] = bias_sum
+    own_block(None, grads_all, recv_sem, z_sem, x_sem)
+
+    @pl.when(source)
+    def _():
+        for step in range(1, 8):
+            other = (place + step) % 8
+            push(
+                cot_all.at[other],
+                cot_all.at[other],
+                cot_sem.at[0],
+                cot_recv.at[other],
+                place,
+                lane,
+            ).wait_recv()
+
+    width = 2 * half_width // 2
+
+    def body(step, _):
+        block = next_block(step, grads_all, recv_sem, z_sem, x_sem)
+        for micro in range(2):
+            fill_columns(
+                grads_all[block, micro],
+                mask_ref[block, micro],
+                turned_wide,
+                columns_wide,
+                micro * PIXELS,
+            )
+        part = jnp.dot(columns_wide[...], back_ref[...], preferred_element_type=jnp.float32)
+        pieces = []
+        for micro in range(2):
+            extra = cot_all[block, micro].astype(jnp.float32)
+            rows = part[micro * PIXELS : (micro + 1) * PIXELS]
+            pieces.append(
+                jnp.concatenate(
+                    [
+                        rows[:, :LANES] + jnp.where(low & source, extra, 0.0),
+                        rows[:, LANES:] + jnp.where(low | ~source, 0.0, extra),
+                    ],
+                    axis=1,
+                )
+            )
+        part = jnp.concatenate(pieces, axis=0).astype(jnp.bfloat16)
+        send_pieces(part, block, stage, got, stage_sem, got_sem)
+        value = jnp.concatenate(
+            [
+                jnp.concatenate([act_ref[half, micro, block] for half in range(2)], axis=1)
+                for micro in range(2)
+            ],
+            axis=0,
+        ).T
+        for number in range(9):
+            product = jnp.dot(
+                value,
+                columns_wide[:, number * 512 : (number + 1) * 512],
+                preferred_element_type=jnp.float32,
+            )
+            for stream in range(2):
+                for part_index in range(4):
+                    head = (
+                        OWN_HEAD[stream]
+                        if part_index == 0
+                        else SOURCE_START[stream] + part_index - 1
+                    )
+                    column = (2 * stream + (part_index > 0)) * LANES
+                    grad_ref[stream, 8 - number, part_index] += product[
+                        head * width : (head + 1) * width, column : column + LANES
+                    ]
+        return 0
+
+    lax.fori_loop(0, 8, body, 0)
+    await_pieces(stage, got, stage_sem, got_sem)
+    normalize_gradient(
+        count,
+        got,
+        norm_ref,
+        inverse_ref,
+        scale_ref,
+        shift_ref,
+        back_act_ref,
+        sums_ref,
+        keep,
+        out_sem,
+        in_sem,
+    )
+    sent_blocks(grads_all, recv_sem, z_sem, x_sem)
+    for parity in range(2):
+        target = 2 * lane + parity
+
+        @pl.when(target != place)
+        def _():
+            push(
+                packed_ref.at[parity],
+                cot_all.at[place],
+                cot_sem.at[parity],
+                cot_recv.at[place],
+                target,
+                lane,
+            ).wait_send()
+
+    @pl.when(source)
+    def _():
+        for step in range(1, 8):
+            block = (place + step) % 8
+            push(
+                own_stage.at[block],
+                own_got.at[0],
+                own_sem.at[block],
+                own_recv.at[0],
+                block,
+                lane,
+            ).wait_send()
+
+
+def normalize_gradient(
+    count,
+    got,
+    norm_ref,
+    inverse_ref,
+    scale_ref,
+    shift_ref,
+    back_act_ref,
+    sums_ref,
+    keep,
+    out_sem,
+    in_sem,
+):
+    place, lane, depth, side, upper, core = whereabouts()
+
+    def collect(block, sums):
+        value = got[0, block].astype(jnp.float32)
+        for other in range(1, 4):
+            value = value + got[other, block].astype(jnp.float32)
+        normed = norm_ref[block]
+        value = value * silu_slope(normed * scale_ref[...] + shift_ref[...])
+        keep[pl.ds(block // 4 * PIXELS, PIXELS), pl.ds(block % 4 * LANES, LANES)] = value
+        return (
+            sums[0] + jnp.sum(value, axis=0, keepdims=True),
+            sums[1] + jnp.sum(value * normed, axis=0, keepdims=True),
+        )
+
+    zero = jnp.zeros((1, LANES), jnp.float32)
+    shift_sum, scale_sum = lax.fori_loop(0, 8, collect, (zero, zero))
+    sums_ref[0:1] = scale_sum
+    sums_ref[1:2] = shift_sum
+    factor = scale_ref[...] * inverse_ref[...]
+
+    def activate(chunk, _):
+        for item in range(2):
+            block = 2 * chunk + item
+            value = keep[pl.ds(block // 4 * PIXELS, PIXELS), pl.ds(block % 4 * LANES, LANES)]
+            back_act_ref[upper, core, block] = (
+                factor * (value - (shift_sum + norm_ref[block] * scale_sum) / count)
+            ).astype(jnp.bfloat16)
+        spread_chunk(chunk, back_act_ref, out_sem, in_sem)
+        return 0
+
+    lax.fori_loop(0, CHUNKS, activate, 0)
+    finish_chunks(back_act_ref, out_sem, in_sem)
+
+
+def run_distil(
+    count, acts, mixed, mixed_back, masks, cots, packed, bias, norm, inverse, scale, shift
+):
+    return pl.pallas_call(
+        functools.partial(distil_kernel, count),
+        name="distil",
+        out_shape=(
+            jax.ShapeDtypeStruct((2, 2, PIXELS, LANES), jnp.bfloat16),
+            jax.ShapeDtypeStruct((2, 9, 4, 64, LANES), jnp.float32),
+            jax.ShapeDtypeStruct((2, LANES), jnp.float32),
+            jax.ShapeDtypeStruct((2, 2, 8, PIXELS, LANES), jnp.bfloat16),
+            jax.ShapeDtypeStruct((2, LANES), jnp.float32),
+        ),
+        in_specs=vmem(11),
+        out_specs=tuple(vmem(5)),
+        scratch_shapes=[
+            pltpu.VMEM((3, 2 * PAD + PIXELS, 256), jnp.bfloat16),
+            pltpu.VMEM((2 * PIXELS, 9 * 256), jnp.bfloat16),
+            pltpu.VMEM((3, 2 * PAD + PIXELS, 512), jnp.bfloat16),
+            pltpu.VMEM((2 * PIXELS, 9 * 512), jnp.bfloat16),
+            pltpu.VMEM((8, 2, PIXELS, 512), jnp.bfloat16),
+            pltpu.VMEM((8, 2, PIXELS, LANES), jnp.bfloat16),
+            pltpu.VMEM((2, 2, PIXELS, LANES), jnp.bfloat16),
+            pltpu.VMEM((8, 2, PIXELS, LANES), jnp.bfloat16),
+        ]
+        + reduce_scratch()
+        + chan_scratch()
+        + [
+            pltpu.SemaphoreType.DMA((8,)),
+            pltpu.SemaphoreType.DMA((2,)),
+            pltpu.SemaphoreType.DMA((2,)),
+            pltpu.SemaphoreType.DMA((8,)),
+        ]
+        + gather_sems()
+        + chan_sems(),
+        compiler_params=kernel_params(2),
+    )(acts, mixed, mixed_back, masks, cots, packed, bias, norm, inverse, scale, shift)
+
+
+def back_kernel(
+    grads_ref,
+    all_ref,
+    weight_ref,
+    mask_ref,
+    out_ref,
+    wgrad_ref,
+    turned,
+    columns,
+    keep,
+    far_send,
+    far_got,
+    near_send,
+    near_got,
+    far_sem,
+    far_recv,
+    near_sem,
+    near_recv,
+):
+    greet(link_peers())
+    clear_edges(turned)
+    wgrad_ref[...] = jnp.zeros_like(wgrad_ref)
+
+    def partial(block):
+        for micro in range(2):
+            value = jnp.concatenate([grads_ref[0, micro, block], grads_ref[1, micro, block]], axis=1)
+            fill_columns(value, mask_ref[block, micro], turned, columns, micro * PIXELS)
+        return jnp.dot(columns[...], weight_ref[...], preferred_element_type=jnp.float32)
+
+    def weigh(block):
+        value = jnp.concatenate([all_ref[block, micro] for micro in range(2)], axis=0).T
+        for number in range(9):
+            wgrad_ref[8 - number] += jnp.dot(
+                value,
+                columns[:, number * 256 : (number + 1) * 256],
+                preferred_element_type=jnp.float32,
+            )
+
+    def far_step(step, _):
+        block = far_block(step)
+        reduce_far(step, partial(block), far_send, far_got, far_sem, far_recv)
+        weigh(block)
+        return 0
+
+    lax.fori_loop(0, 4, far_step, 0)
+
+    def near_step(step, _):
+        block = near_block(step)
+        part = partial(block)
+        weigh(block)
+        reduce_near(
+            step, part, keep, far_got, far_recv, near_send, near_got, near_sem, near_recv
+        )
+        return 0
+
+    lax.fori_loop(0, 4, near_step, 0)
+    reduce_close(keep, far_send, far_sem, far_recv, near_send, near_got, near_sem, near_recv)
+    out_ref[...] = keep[...]
+
+
+def run_back(grads, block_all, weight, masks):
+    return pl.pallas_call(
+        back_kernel,
+        name="back",
+        out_shape=(
+            jax.ShapeDtypeStruct((2 * PIXELS, 512), jnp.float32),
+            jax.ShapeDtypeStruct((9, 512, 256), jnp.float32),
+        ),
+        in_specs=vmem(4),
+        out_specs=tuple(vmem(2)),
+        scratch_shapes=[
+            pltpu.VMEM((3, 2 * PAD + PIXELS, 256), jnp.bfloat16),
+            pltpu.VMEM((2 * PIXELS, 9 * 256), jnp.bfloat16),
+        ]
+        + reduce_scratch(),
+        compiler_params=kernel_params(3),
+    )(grads, block_all, weight, masks)
 
 
 def stationary_local(
@@ -498,99 +1349,55 @@
     summed = third_out + features.astype(jnp.float32)
     block_out = jax.nn.silu(summed).astype(jnp.bfloat16)
 
-    block_all = lax.all_gather(block_out, "batch", axis=0, tiled=True)
-    heads_flat = head_weights.reshape(9, head_weights.shape[1], -1)
-    head_partial = conv_forward(block_all, heads_flat, masks_full).astype(jnp.bfloat16)
-    head_parts = head_partial.reshape(groups, canvases, pixels, 2, 2 * width).transpose(3, 1, 0, 2, 4)
-    head_parts = head_parts.reshape((2 * canvases,) + head_parts.shape[2:])
-    head_pre = lax.psum_scatter(head_parts, "chan", scatter_dimension=0, tiled=True)[0].astype(
-        jnp.float32
-    )
+    mask_columns = jnp.pad(
+        masks_full.reshape(9, groups, canvases, pixels).transpose(1, 2, 3, 0),
+        ((0, 0), (0, 0), (0, 0), (0, 7)),
+    ).astype(jnp.bfloat16)
     half = lane // 2
 
     def mine(values):
         whole = lax.all_gather(values, "chan", axis=1, tiled=True)
         part = lax.dynamic_slice_in_dim(whole, place * width, width, axis=1)
-        return lax.dynamic_slice_in_dim(part.reshape(2, 2 * width), half, 1, axis=0)[0]
+        return lax.dynamic_slice_in_dim(part.reshape(2, 2 * width), half, 1, axis=0)
 
     my_scale, my_shift = mine(head_scale), mine(head_shift)
-    center = jnp.sum(head_pre, axis=(0, 1)) / count
-    spreads = jnp.sum(head_pre * head_pre, axis=(0, 1)) / count
-    head_inv = lax.rsqrt(spreads - center * center + EPSILON)
-    head_norm = (head_pre - center) * head_inv
-    head_out = head_norm * my_scale + my_shift
-    head_act = jax.nn.silu(head_out).astype(jnp.bfloat16)
-    head_all = lax.all_gather(head_act, "chan", axis=0).reshape(
-        2, canvases, groups, pixels, 2 * width
-    )
-    head_full = head_all.transpose(2, 1, 3, 0, 4).reshape(
-        groups * canvases, row_count, column_count, 4 * width
+    heads_flat = head_weights.reshape(9, head_weights.shape[1], -1)
+    block_all, head_acts, head_norm, head_inv = run_heads(
+        count,
+        block_out.reshape(canvases, pixels, -1),
+        heads_flat.reshape(-1, heads_flat.shape[2]),
+        mask_columns,
+        my_scale,
+        my_shift,
     )
     mixed = distil_matrix(distil_weights)
-    pre = sum_batch(conv_forward(head_full, mixed, masks_full), 0)
-    own_part = jnp.concatenate(
-        [head_full[..., :width], head_full[..., 3 * width :]], axis=-1
-    )
-    own_all = lax.all_to_all(own_part, "batch", split_axis=0, concat_axis=0, tiled=True).reshape(
-        groups, canvases, row_count, column_count, 2, width
-    )
-    per = groups // 4
-    own_all = lax.dynamic_slice_in_dim(own_all, lane * per, per, axis=0)
-    own_all = own_all.transpose(4, 1, 2, 3, 0, 5).reshape(
-        2, canvases, row_count, column_count, per * width
-    )
-    cots = (depth_cotangent.astype(jnp.float32), segment_cotangent.astype(jnp.float32))
-    outputs, pre_grads, gate_sums = ([], [], [])
-    for stream in range(2):
-        gate_pre = pre[..., (2 * stream) * 128 : (2 * stream + 1) * 128]
-        message = pre[..., (2 * stream + 1) * 128 : (2 * stream + 2) * 128]
-        gate = jax.nn.sigmoid(gate_pre + gate_bias[stream])
-        outputs.append(
-            (own_all[stream].astype(jnp.float32) + gate * message).astype(jnp.bfloat16)
-        )
-        gate_grad = (cots[stream] * message * gate * (1.0 - gate)).astype(jnp.bfloat16)
-        gate_sums.append(pixel_sum(gate_grad.astype(jnp.float32)))
-        pre_grads.append(gate_grad)
-        pre_grads.append((cots[stream] * gate).astype(jnp.bfloat16))
-    pre_grad_all = lax.all_gather(
-        jnp.concatenate(pre_grads, axis=-1), "batch", axis=0, tiled=True
-    )
-    distil_grad = distil_blocks(conv_weight_grad(head_full, pre_grad_all, masks_full), width)
-    spread_grad = conv_input_grad(pre_grad_all, mixed, masks_full).astype(jnp.bfloat16)
-    spread_parts = spread_grad.reshape(groups, canvases, pixels, 2, 2 * width).transpose(3, 1, 0, 2, 4)
-    spread_parts = spread_parts.reshape((2 * canvases,) + spread_parts.shape[2:])
-    head_grad = lax.psum_scatter(spread_parts, "chan", scatter_dimension=0, tiled=True)[0].astype(
-        jnp.float32
-    )
-    cot_pair = jnp.stack([depth_cotangent, segment_cotangent]).reshape(
-        2, canvases, pixels, 4 // 2 * width
-    )
-    cot_all = lax.all_gather(cot_pair, ("batch", "chan"), axis=0)
-    cot_all = cot_all.reshape(groups, 4, 2, canvases, pixels, 2, width)
-    cot_mine = lax.dynamic_index_in_dim(cot_all, place // 2, axis=1, keepdims=False)
-    cot_mine = lax.dynamic_index_in_dim(cot_mine, half, axis=1, keepdims=False)
-    cot_mine = lax.dynamic_index_in_dim(cot_mine, lane % 2, axis=1, keepdims=False)
-    cot_mine = lax.dynamic_index_in_dim(cot_mine, place % 2, axis=2, keepdims=False)
-    zeros = jnp.zeros_like(cot_mine)
-    cot_wide = jnp.where(
-        half == 0,
-        jnp.concatenate([cot_mine, zeros], axis=-1),
-        jnp.concatenate([zeros, cot_mine], axis=-1),
-    )
-    head_grad = (head_grad + cot_wide.astype(jnp.float32)) * silu_slope(head_out)
-    head_shift_sum = jnp.sum(head_grad, axis=(0, 1))
-    head_scale_sum = jnp.sum(head_grad * head_norm, axis=(0, 1))
-    head_pre_grad = (
-        my_scale * head_inv * (head_grad - (head_shift_sum + head_norm * head_scale_sum) / count)
-    ).astype(jnp.bfloat16)
-    head_grad_all = lax.all_gather(head_pre_grad, "chan", axis=0).reshape(
-        2, canvases, groups, pixels, 2 * width
-    )
-    head_grad_all = head_grad_all.transpose(2, 1, 3, 0, 4).reshape(
-        groups * canvases, row_count, column_count, 4 * width
-    )
-    heads_grad = conv_weight_grad(block_all, head_grad_all, masks_full).reshape(head_weights.shape)
-    block_grad = sum_batch(conv_input_grad(head_grad_all, heads_flat, masks_full), 0)
+    mixed_back = mixed[::-1].transpose(0, 2, 1).reshape(-1, mixed.shape[1])
+    heads_back = heads_flat[::-1].transpose(0, 2, 1).reshape(-1, heads_flat.shape[1])
+    cots = jnp.stack([depth_cotangent, segment_cotangent]).reshape(2, canvases, pixels, 128)
+    packed = jnp.stack(
+        [
+            jnp.concatenate([cots[0, :, :, :width], cots[1, :, :, :width]], axis=-1),
+            jnp.concatenate([cots[0, :, :, width:], cots[1, :, :, width:]], axis=-1),
+        ]
+    )
+    streams, distil_grad, gate_sums, head_grads, head_sums = run_distil(
+        count,
+        head_acts,
+        mixed.reshape(-1, mixed.shape[2]),
+        mixed_back,
+        mask_columns,
+        cots,
+        packed,
+        gate_bias,
+        head_norm,
+        head_inv,
+        my_scale,
+        my_shift,
+    )
+    outputs = streams.reshape((2,) + image_ids.shape + (128,))
+    block_grad, heads_grad = run_back(head_grads, block_all, heads_back, mask_columns)
+    block_grad = block_grad.reshape(features.shape)
+    heads_grad = heads_grad.reshape(head_weights.shape)
     summed_grad = block_grad * silu_slope(summed)
     third_pre, third_shift, third_scale = normalize_each_back(
         summed_grad, third_norm, third_inv, output_scale, count
@@ -616,12 +1423,12 @@
     features_grad = summed_grad + jnp.einsum(
         "nhwo,co->nhwc", first_pre_full, reduce_full, preferred_element_type=jnp.float32
     )
-    sums = jnp.stack([head_scale_sum, head_shift_sum]).reshape(2, 1, 2, width)
+    sums = head_sums.reshape(2, 1, 2, width)
     wide = jnp.zeros((2, 2, 2, groups * width), jnp.float32)
     sums = lax.dynamic_update_slice(wide, sums, (0, half, 0, place * width)).reshape(2, 4, -1)
     sums = lax.psum(sums, ("batch", "chan"))
     sums = lax.dynamic_slice_in_dim(sums, lane * 128, 128, axis=2)
-    gate_total = lax.psum(jnp.stack(gate_sums), "batch")
+    gate_total = lax.psum(gate_sums, "batch")
     return (
         outputs[0],
         outputs[1],
@@ -642,7 +1449,7 @@
 
 
 def solution(mesh):
-    local = stationary_local if mesh.shape["batch"] <= 8 else gathered_local
+    local = stationary_local if dict(mesh.shape) == {"batch": 8, "chan": 4} else gathered_local
     placed = (
         P("batch", None, None, "chan"),
         P("batch", None, None),

time: 1200 us -> 930 us (0.78)
  Pallas kernels: 0 us -> 338 us
  waiting for transfers between devices: 452 us -> 142 us
  matrix products: 282 us -> 26.7 us
  other arithmetic: 44.2 us -> 19.9 us
    pallas_call x0 -> x3, Pallas kernels: none -> 338 us  [the longest x1 176 us: run_distil(): pl.pallas_call(functools.partial(distil_kernel, count), name='distil', ou...]
    all_gather x5 -> x0, waiting for transfers between devices: 128 us -> none  [the longest x1 58.4 us: stationary_local(): lax.all_gather(jnp.concatenate(pre_grads, axis=-1), 'batch', axis=0, tile...]
    reduce_scatter x5 -> x3, waiting for transfers between devices: 216 us -> 109 us  [sum_batch(): lax.psum_scatter(values.astype(jnp.bfloat16), 'batch', scatter_dimension=...]
    dot_general x27 -> x9, matrix products: 98.4 us -> 3.99 us  [conv_input_grad(): jnp.einsum('nhwo,co->nhwc', grads, weight[number], preferred_element_type...]
    dot_general x27 -> x9, matrix products: 96.1 us -> 5.02 us  [conv_forward(): jnp.einsum('nhwc,co->nhwo', moved, weight[number], preferred_element_type...]
    dot_general x27 -> x9, matrix products: 78.8 us -> 9.05 us  [conv_weight_grad(): jnp.einsum('nhwc,nhwo->co', moved, grads, preferred_element_type=jnp.floa...]
    all_to_all x1 -> x0, waiting for transfers between devices: 51.8 us -> none  [stationary_local(): lax.all_to_all(own_part, 'batch', split_axis=0, concat_axis=0, tiled=True)]
    another operation x5 -> x13, local copies, waits for them, and re-layouts: 2.04 us -> 48.9 us  [the longest x1 1.82 us: distil_blocks(): outs.append(jnp.stack(pieces, axis=1))]
  transfers between devices with their start and end apart: 17 -> 7, of which waited for: 14 -> 4; matrix products, arithmetic and copies ran while one was open for 12% -> 11% of each run, Pallas kernels for 0% -> 0%
where the time goes in v2:
time: 930 us; the launch traced here: 928 us
  Pallas kernels  338 us (36%)
  blocking collectives  288 us (31%)
  waiting for transfers between devices  142 us (15%)
  local copies, waits for them, and re-layouts  96.3 us (10%)
  matrix products  26.7 us (3%)
  other arithmetic  19.9 us (2%)
  between operations  16.8 us (2%)
    pallas_call x1, Pallas kernels, run_distil(): pl.pallas_call(functools.partial(distil_kernel, count), name='distil', ou...  176 us
    reduce_scatter x3, waiting for transfers between devices, sum_batch(): lax.psum_scatter(values.astype(jnp.bfloat16), 'batch', scatter_dimension=...  109 us
    pallas_call x1, Pallas kernels, run_heads(): pl.pallas_call(functools.partial(heads_kernel, count), name='heads', out_...  87 us
    pallas_call x1, Pallas kernels, run_back(): pl.pallas_call(back_kernel, name='back', out_shape=(jax.ShapeDtypeStruct(...  74.9 us
    psum x3, blocking collectives, normalize_each_back(): lax.psum((canvas_sum(grads), canvas_sum(grads * normed)), 'batch')  63.9 us
    psum x3, blocking collectives, normalize_each(): lax.psum((canvas_sum(values), canvas_sum(values * values)), 'batch')  58.2 us
    psum x1, blocking collectives, stationary_local(): sums = lax.psum(sums, ('batch', 'chan'))  37 us
    all_gather x1, blocking collectives, stationary_local(): expand_full = lax.all_gather(expand_weight, 'batch', axis=0, tiled=True)  33.6 us
  transfers between devices with their start and end apart: 7, of which 4 were waited for; matrix products, arithmetic and copies ran while one was open for 11% of the time, Pallas kernels for 0%

profile of v2, /device:TPU:0, one launch (start us, length us, event | category | flops | bytes accessed | tf_op | source)
XLA Modules:
  0.0 927.7 jit_solution(6368332890864804563)
XLA Ops:
  8.1 33.2 %all_gather.27 = bf16[512,512]{0,1:T(8,128)(2,1)S(1)} all-gather(bf16[512,64]{0,1:T(8,128)(2,1)} %param.18), channel_id=1, replica_groups=mesh['batch'=8,'chan'=4] {'batch'}, dimensions={1}, use_global_device_ids=true | all-gather | bytes 589824 | tf_op jit(solution)/shard_map/all_gather | solution.py:1329
  41.3 1.7 convolution_convert_fusion.1
  43.0 2.0 copy.214
  45.0 2.8 reshape.211
  50.7 5.1 all_gather.33
  55.9 5.1 all_gather.34
  61.3 31.2 %all_gather.32 = s32[16,8,32]{2,1,0:T(8,128)S(1)} all-gather(s32[2,8,32]{2,1,0:T(8,128)S(1)} %copy-done.52), channel_id=1, replica_groups=mesh['batch'=8,'chan'=4] {'batch'}, dimensions={0}, use_global_device_ids=true | all-gather | bytes 18432 | tf_op jit(solution)/shard_map/all_gather | solution.py:1332
  93.8 1.9 reverse_bitcast_fusion
  97.0 3.2 reshape.203
  100.2 3.2 reshape.204
  103.4 3.2 reshape.205
  106.6 3.2 reshape.206
  109.8 3.2 reshape.207
  113.1 3.3 reshape.208
  116.3 3.2 reshape.209
  119.5 3.2 reshape.210
  122.8 1.3 eq.64
  124.0 9.7 %stack.136 = bf16[9,8,2,256]{0,3,2,1:T(8,128)(2,1)S(1)} concatenate(bf16[1,8,2,256]{0,3,2,1:T(8,128)(2,1)} %reshape.203, bf16[1,8,2,256]{0,3,2,1:T(8,128)(2,1)} %reshape.204, bf16[1,8,2,256]{0,3,2,1:T(8,128)(2,1)} %reshape.205, bf16[1,8,2,256]{0,3,2,1:T(8,128)(2,1)} %reshape.206, bf16[1,8,2,256]{0,3,2,1:T(8,128)(2,1)} %eq.64, bf16[1,8,2,256]{0,3,2,1:T(8,128)(2,1)} %reshape.207, ...), dimensions={0} | concatenate | bytes 147456 | tf_op jit(solution)/shard_map/stack | solution.py:41
  133.7 1.3 pad.63.mask_ref
  135.0 5.4 copy.213
  140.4 8.0 reshape.202.weight_ref
  148.4 4.3 copy.166
  152.7 1.7 rev.7
  156.6 33.6 %all_gather.31 = bf16[512,512]{1,0:T(8,128)(2,1)} all-gather(bf16[64,512]{1,0:T(8,128)(2,1)S(1)} %copy-done.44), channel_id=1, replica_groups=mesh['batch'=8,'chan'=4] {'batch'}, dimensions={0}, use_global_device_ids=true | all-gather | bytes 589824 | tf_op jit(solution)/shard_map/all_gather | solution.py:1331
  190.2 1.2 reshape.212
  191.9 21.5 %all-reduce.17 = (f32[2,128]{1,0:T(2,128)S(1)}, f32[2,128]{1,0:T(2,128)S(1)}) all-reduce(f32[2,128]{1,0:T(2,128)S(1)} %get-tuple-element.63, f32[2,128]{1,0:T(2,128)S(1)} %get-tuple-element.62), channel_id=1, replica_groups=mesh['batch'=8,'chan'=4] {'batch'}, use_global_device_ids=true, to_apply=%region_4.5 | all-reduce | flops 512 | bytes 4096 | tf_op jit(solution)/shard_map/psum | solution.py:395
  214.1 7.2 all_gather.28
  221.4 2.6 fusion.45
  224.2 1.5 fusion.86
  225.7 1.4 convolution_add_fusion.9
  229.4 17.3 %all-reduce.16 = (f32[2,128]{1,0:T(2,128)S(1)}, f32[2,128]{1,0:T(2,128)S(1)}) all-reduce(f32[2,128]{1,0:T(2,128)S(1)} %get-tuple-element.61, f32[2,128]{1,0:T(2,128)S(1)} %get-tuple-element.60), channel_id=1, replica_groups=mesh['batch'=8,'chan'=4] {'batch'}, use_global_device_ids=true, to_apply=%region_8.9 | all-reduce | flops 512 | bytes 4096 | tf_op jit(solution)/shard_map/psum | solution.py:395
  247.3 6.6 all_gather.30
  254.4 19.4 %all-reduce.15 = (f32[2,512]{1,0:T(2,128)S(1)}, f32[2,512]{1,0:T(2,128)S(1)}) all-reduce(f32[2,512]{1,0:T(2,128)S(1)} %get-tuple-element.55, f32[2,512]{1,0:T(2,128)S(1)} %get-tuple-element.54), channel_id=1, replica_groups=mesh['batch'=8,'chan'=4] {'batch'}, use_global_device_ids=true, to_apply=%region_12.13 | all-reduce | flops 2048 | bytes 16384 | tf_op jit(solution)/shard_map/psum | solution.py:395
  274.4 1.2 multiply_convert_fusion.1
  275.6 87.0 %heads.1 = (bf16[8,2,256,512]{3,2,1,0:T(8,128)(2,1)}, bf16[2,2,8,256,128]{4,3,2,1,0:T(8,128)(2,1)}, f32[8,256,128]{2,1,0:T(8,128)}, f32[1,128]{1,0:T(1,128)}) custom-call(bf16[2,256,512]{2,1,0:T(8,128)(2,1)} %bitcast.354, bf16[4608,256]{1,0:T(8,128)(2,1)} %reshape.202.weight_ref, bf16[8,2,256,16]{3,2,1,0:T(8,128)(2,1)} %pad.63.mask_ref, ...), custom_call_target="tpu_custom_call" | custom-call | tf_op jit(solution)/shard_map/heads/pallas_call | solution.py:750
  362.6 176.4 %distil.1 = (bf16[2,2,256,128]{3,2,1,0:T(8,128)(2,1)}, f32[2,9,4,64,128]{4,3,2,1,0:T(8,128)}, f32[2,128]{1,0:T(2,128)}, bf16[2,2,8,256,128]{4,3,2,1,0:T(8,128)(2,1)}, f32[2,128]{1,0:T(2,128)}) custom-call(bf16[2,2,8,256,128]{4,3,2,1,0:T(8,128)(2,1)} %get-tuple-element.26.act_ref, bf16[2304,512]{1,0:T(8,128)(2,1)} %bitcast.342, bf16[4608,256]{1,0:T(8,128)(2,1)} %bitcast.345, ...), custom_call_target="tpu_custom_call" | custom-call | tf_op jit(solution)/shard_map/distil/pallas_call | solution.py:1189
  539.0 74.9 %back.1 = (f32[512,512]{1,0:T(8,128)}, f32[9,512,256]{2,1,0:T(8,128)}) custom-call(bf16[2,2,8,256,128]{4,3,2,1,0:T(8,128)(2,1)} %get-tuple-element.30.grads_ref, bf16[8,2,256,512]{3,2,1,0:T(8,128)(2,1)} %get-tuple-element.31.all_ref, bf16[2304,512]{1,0:T(8,128)(2,1)} %bitcast.344, bf16[8,2,256,16]{3,2,1,0:T(8,128)(2,1)} %pad.63.mask_ref), custom_call_target="tpu_custom_call" | custom-call | tf_op jit(solution)/shard_map/back/pallas_call | solution.py:1286
  614.0 1.9 fusion.124
  615.9 20.5 %all-reduce.14 = (f32[2,512]{1,0:T(2,128)}, f32[2,512]{1,0:T(2,128)}) all-reduce(f32[2,512]{1,0:T(2,128)S(1)} %get-tuple-element.53, f32[2,512]{1,0:T(2,128)S(1)} %get-tuple-element.52), channel_id=1, replica_groups=mesh['batch'=8,'chan'=4] {'batch'}, use_global_device_ids=true, to_apply=%region_16.17 | all-reduce | flops 2048 | bytes 16384 | tf_op jit(solution)/shard_map/psum | solution.py:403
  638.1 1.3 convolution_convert_fusion
  639.4 2.9 copy.216
  642.3 2.8 reshape.213
  645.1 20.7 %reduce-scatter.21.cloned.1.call-done = bf16[128,512]{1,0:T(8,128)(2,1)} async-done(((bf16[512,512]{1,0:T(8,128)(2,1)}), bf16[128,512]{1,0:T(8,128)(2,1)}) %reduce-scatter.21.cloned.1.call-update) | async-done | bytes 131088
  665.9 1.2 reshape.214
  667.8 21.5 %all-reduce.13 = (f32[2,128]{1,0:T(2,128)S(1)}, f32[2,128]{1,0:T(2,128)S(1)}) all-reduce(f32[2,128]{1,0:T(2,128)S(1)} %get-tuple-element.57, f32[2,128]{1,0:T(2,128)S(1)} %get-tuple-element.56), channel_id=1, replica_groups=mesh['batch'=8,'chan'=4] {'batch'}, use_global_device_ids=true, to_apply=%region_21.22 | all-reduce | flops 512 | bytes 4096 | tf_op jit(solution)/shard_map/psum | solution.py:403
  692.2 1.6 fusion.4
  693.7 2.9 copy.218
  696.6 2.8 reshape.215
  699.5 2.5 fusion.6
  706.2 11.3 %reduce-scatter.23.cloned.1.call-done = bf16[128,512]{1,0:T(8,128)(2,1)} async-done(((bf16[512,512]{1,0:T(8,128)(2,1)}), bf16[128,512]{1,0:T(8,128)(2,1)}) %reduce-scatter.23.cloned.1.call-update) | async-done | bytes 131088
  717.5 1.2 reshape.216
  719.4 21.9 %all-reduce.12 = (f32[2,128]{1,0:T(2,128)S(1)}, f32[2,128]{1,0:T(2,128)S(1)}, f32[2,128]{1,0:T(2,128)}) all-reduce(f32[2,128]{1,0:T(2,128)S(1)} %get-tuple-element.59, f32[2,128]{1,0:T(2,128)S(1)} %get-tuple-element.58, f32[2,128]{1,0:T(2,128)S(1)} %copy-done.84), channel_id=1, replica_groups=mesh['batch'=8,'chan'=4] {'batch'}, use_global_device_ids=true, to_apply=%region_26.27 | all-reduce | flops 768 | bytes 6144 | tf_op jit(solution)/shard_map/psum | solution.py:403
  741.4 6.5 all_gather.35
  748.0 1.3 fusion.7
  752.3 1.0 fusion.20
  755.6 6.1 copy.189
  762.0 37.0 %psum.110 = f32[2,4,512]{2,1,0:T(4,128)S(1)} all-reduce(f32[2,4,512]{2,1,0:T(4,128)S(1)} %reshape.163), channel_id=1, replica_groups=mesh['batch'=8,'chan'=4] {'batch','chan'}, use_global_device_ids=true, to_apply=%region_34.35 | all-reduce | flops 4096 | bytes 32768 | tf_op jit(solution)/shard_map/psum | solution.py:1429
  800.4 1.5 convert_element_type.210
  803.1 1.4 convolution_add_fusion
  804.5 42.7 %reduce-scatter.13.cloned.1.call-done = bf16[512,64]{0,1:T(8,128)(2,1)} async-done(((bf16[512,512]{0,1:T(8,128)(2,1)}), bf16[512,64]{0,1:T(8,128)(2,1)}) %reduce-scatter.13.cloned.1.call-update) | async-done | bytes 65552 | tf_op jit(solution)/shard_map/reduce_scatter | solution.py:419
  847.2 1.5 convert_element_type.207
  848.7 66.3 %reduce-scatter.15.cloned.1.call-done = bf16[9,64,128]{2,1,0:T(8,128)(2,1)} async-done(((bf16[9,512,128]{2,1,0:T(8,128)(2,1)}), bf16[9,64,128]{2,1,0:T(8,128)(2,1)}) %reduce-scatter.15.cloned.1.call-update) | async-done | bytes 147472 | tf_op jit(solution)/shard_map/reduce_scatter | solution.py:419
  915.1 1.6 convert_element_type.208
  916.7 3.4 copy.282
  (260 shorter events, 31.3 us)
Async XLA Ops:
  8.0 182.2 %reduce-scatter.19.cloned.1.call-start = ((), (), s32[]{:S(2)}) async-start(), calls=%async_computation.10 | async-start | bytes 655360
  41.3 3.7 copy-start.6
  45.0 3.5 copy-start.30
  45.0 4.2 copy-start.29
  47.8 8.1 copy-start.82
  47.8 13.5 %copy-start.52 = (s32[2,8,32]{2,1,0:T(8,128)S(1)}, s32[2,8,32]{2,1,0:T(8,128)}, u32[]{:S(2)}) copy-start(s32[2,8,32]{2,1,0:T(8,128)} %param.17) | copy-start | bytes 6148
  47.8 45.5 %copy-start.28 = (bf16[2,9,4,64,128]{4,3,2,1,0:T(8,128)(2,1)S(1)}, bf16[2,9,4,64,128]{4,3,2,1,0:T(8,128)(2,1)}, u32[]{:S(2)}) copy-start(bf16[2,9,4,64,128]{4,3,2,1,0:T(8,128)(2,1)} %param.22) | copy-start | bytes 3538948
  47.8 176.3 %all-gather.2.cloned.1.call-start = ((), (), s32[]{:S(2)}) async-start(), calls=%async_computation.6 | async-start | bytes 1327104 | tf_op jit(solution)/shard_map/all_gather | solution.py:1330
  48.4 617.5 %reduce-scatter.21.cloned.1.call-start = ((), (), s32[]{:S(2)}) async-start(), calls=%async_computation.11 | async-start | bytes 655360
  93.8 6.3 copy-start.42
  96.0 7.4 copy-start.41
  96.0 10.6 %copy-start.40 = (bf16[16,8,32]{2,1,0:T(8,128)(2,1)S(1)}, bf16[16,8,32]{2,1,0:T(8,128)(2,1)}, u32[]{:S(2)}) copy-start(bf16[16,8,32]{2,1,0:T(8,128)(2,1)} %get-tuple-element.121) | copy-start | bytes 24580
  100.2 9.7 %copy-start.39 = (bf16[16,8,32]{2,1,0:T(8,128)(2,1)S(1)}, bf16[16,8,32]{2,1,0:T(8,128)(2,1)}, u32[]{:S(2)}) copy-start(bf16[16,8,32]{2,1,0:T(8,128)(2,1)} %get-tuple-element.120) | copy-start | bytes 24580
  103.4 9.7 %copy-start.38 = (bf16[16,8,32]{2,1,0:T(8,128)(2,1)S(1)}, bf16[16,8,32]{2,1,0:T(8,128)(2,1)}, u32[]{:S(2)}) copy-start(bf16[16,8,32]{2,1,0:T(8,128)(2,1)} %get-tuple-element.119) | copy-start | bytes 24580
  106.6 9.7 %copy-start.37 = (bf16[16,8,32]{2,1,0:T(8,128)(2,1)S(1)}, bf16[16,8,32]{2,1,0:T(8,128)(2,1)}, u32[]{:S(2)}) copy-start(bf16[16,8,32]{2,1,0:T(8,128)(2,1)} %get-tuple-element.118) | copy-start | bytes 24580
  109.8 9.7 %copy-start.36 = (bf16[16,8,32]{2,1,0:T(8,128)(2,1)S(1)}, bf16[16,8,32]{2,1,0:T(8,128)(2,1)}, u32[]{:S(2)}) copy-start(bf16[16,8,32]{2,1,0:T(8,128)(2,1)} %get-tuple-element.117) | copy-start | bytes 24580
  124.0 11.0 %copy-start.1 = (bf16[9,512,4,64]{1,3,2,0:T(8,128)(2,1)S(1)}, bf16[9,512,4,64]{1,3,2,0:T(8,128)(2,1)}, u32[]{:S(2)}) copy-start(bf16[9,512,4,64]{1,3,2,0:T(8,128)(2,1)} %param.21) | copy-start | bytes 7077892
  152.7 3.9 copy-start.44
  155.9 68.1 %copy-start.69 = (f32[128]{0:T(128)}, f32[128]{0:T(128)S(1)}, u32[]{:S(2)}) copy-start(f32[128]{0:T(128)S(1)} %get-tuple-element.156) | copy-start | bytes 1540
  155.9 68.1 %copy-start.73 = (f32[128]{0:T(128)}, f32[128]{0:T(128)S(1)}, u32[]{:S(2)}) copy-start(f32[128]{0:T(128)S(1)} %get-tuple-element.153) | copy-start | bytes 1540
  214.0 10.0 %copy-start.55 = (f32[2,128]{1,0:T(2,128)}, f32[2,128]{1,0:T(2,128)S(1)}, u32[]{:S(2)}) copy-start(f32[2,128]{1,0:T(2,128)S(1)} %get-tuple-element.145) | copy-start | bytes 3076
  214.0 10.0 %copy-start.57 = (f32[2,128]{1,0:T(2,128)}, f32[2,128]{1,0:T(2,128)S(1)}, u32[]{:S(2)}) copy-start(f32[2,128]{1,0:T(2,128)S(1)} %get-tuple-element.148) | copy-start | bytes 3076
  221.4 6.4 copy-start.4
  224.0 4.0 copy-start.19
  224.1 4.3 copy-start.17
  224.1 4.6 copy-start.15
  224.1 4.9 copy-start.13
  228.4 18.3 %copy-start.65 = (f32[128]{0:T(128)S(1)}, f32[128]{0:T(128)}, u32[]{:S(2)}) copy-start(f32[128]{0:T(128)} %get-tuple-element.157) | copy-start | bytes 1540
  228.4 18.8 %copy-start.67 = (f32[128]{0:T(128)S(1)}, f32[128]{0:T(128)}, u32[]{:S(2)}) copy-start(f32[128]{0:T(128)} %get-tuple-element.152) | copy-start | bytes 1540
  228.7 25.2 %copy-start.26 = (bf16[512,512]{1,0:T(8,128)(2,1)S(1)}, bf16[512,512]{1,0:T(8,128)(2,1)}, u32[]{:S(2)}) copy-start(bf16[512,512]{1,0:T(8,128)(2,1)} %all_gather.31) | copy-start | bytes 1572868
  229.3 44.4 %copy-start.53 = (f32[512]{0:T(512)S(1)}, f32[512]{0:T(512)}, u32[]{:S(2)}) copy-start(f32[512]{0:T(512)} %param.28) | copy-start | bytes 6148
  229.3 45.0 %copy-start.8 = (bf16[2,8,32,512]{3,2,1,0:T(8,128)(2,1)S(1)}, bf16[2,8,32,512]{3,2,1,0:T(8,128)(2,1)}, u32[]{:S(2)}) copy-start(bf16[2,8,32,512]{3,2,1,0:T(8,128)(2,1)} %param.16) | copy-start | bytes 1572868
  229.4 45.0 %copy-start.71 = (f32[512]{0:T(512)S(1)}, f32[512]{0:T(512)}, u32[]{:S(2)}) copy-start(f32[512]{0:T(512)} %param.29) | copy-start | bytes 6148
  247.2 26.5 %copy-start.59 = (f32[2,128]{1,0:T(2,128)}, f32[2,128]{1,0:T(2,128)S(1)}, u32[]{:S(2)}) copy-start(f32[2,128]{1,0:T(2,128)S(1)} %get-tuple-element.147) | copy-start | bytes 3076
  247.2 26.5 %copy-start.61 = (f32[2,128]{1,0:T(2,128)}, f32[2,128]{1,0:T(2,128)S(1)}, u32[]{:S(2)}) copy-start(f32[2,128]{1,0:T(2,128)S(1)} %get-tuple-element.149) | copy-start | bytes 3076
  253.9 21.7 %copy-start.31 = (bf16[2,8,32,512]{3,2,1,0:T(8,128)(2,1)}, bf16[2,8,32,512]{3,2,1,0:T(8,128)(2,1)S(1)}, u32[]{:S(2)}) copy-start(bf16[2,8,32,512]{3,2,1,0:T(8,128)(2,1)S(1)} %all_gather.30) | copy-start | bytes 1572868
  539.0 75.0 %copy-start.54 = (f32[512]{0:T(512)S(1)}, f32[512]{0:T(512)}, u32[]{:S(2)}) copy-start(f32[512]{0:T(512)} %param.28) | copy-start | bytes 6148
  539.0 74.9 %copy-start.72 = (f32[512]{0:T(512)S(1)}, f32[512]{0:T(512)}, u32[]{:S(2)}) copy-start(f32[512]{0:T(512)} %param.29) | copy-start | bytes 6148
  615.8 22.3 %copy-start.27 = (bf16[512,512]{1,0:T(8,128)(2,1)S(1)}, bf16[512,512]{1,0:T(8,128)(2,1)}, u32[]{:S(2)}) copy-start(bf16[512,512]{1,0:T(8,128)(2,1)} %all_gather.31) | copy-start | bytes 1572868
  645.0 22.5 %copy-start.60 = (f32[2,128]{1,0:T(2,128)S(1)}, f32[2,128]{1,0:T(2,128)}, u32[]{:S(2)}) copy-start(f32[2,128]{1,0:T(2,128)} %copy-done.59) | copy-start | bytes 3076
  645.0 22.5 %copy-start.62 = (f32[2,128]{1,0:T(2,128)S(1)}, f32[2,128]{1,0:T(2,128)}, u32[]{:S(2)}) copy-start(f32[2,128]{1,0:T(2,128)} %copy-done.61) | copy-start | bytes 3076
  645.0 22.6 %copy-start.66 = (f32[128]{0:T(128)S(1)}, f32[128]{0:T(128)}, u32[]{:S(2)}) copy-start(f32[128]{0:T(128)} %get-tuple-element.157) | copy-start | bytes 1540
  645.0 22.6 %copy-start.68 = (f32[128]{0:T(128)S(1)}, f32[128]{0:T(128)}, u32[]{:S(2)}) copy-start(f32[128]{0:T(128)} %get-tuple-element.152) | copy-start | bytes 1540
  645.0 44.3 %copy-start.80 = (f32[2,128]{1,0:T(2,128)S(1)}, f32[2,128]{1,0:T(2,128)}, u32[]{:S(2)}) copy-start(f32[2,128]{1,0:T(2,128)} %get-tuple-element.146) | copy-start | bytes 3076
  645.0 44.5 %copy-start.3 = (bf16[9,512,128]{2,1,0:T(8,128)(2,1)S(1)}, bf16[9,512,128]{2,1,0:T(8,128)(2,1)}, u32[]{:S(2)}) copy-start(bf16[9,512,128]{2,1,0:T(8,128)(2,1)} %all-gather.2.cloned.1.call-done) | copy-start | bytes 3538948
  645.1 44.5 %copy-start.51 = (f32[2,8,32]{2,1,0:T(8,128)S(1)}, f32[2,8,32]{2,1,0:T(8,128)}, u32[]{:S(2)}) copy-start(f32[2,8,32]{2,1,0:T(8,128)} %get-tuple-element.80) | copy-start | bytes 6148
  645.1 44.8 %copy-start.50 = (f32[2,8,32]{2,1,0:T(8,128)S(1)}, f32[2,8,32]{2,1,0:T(8,128)}, u32[]{:S(2)}) copy-start(f32[2,8,32]{2,1,0:T(8,128)} %get-tuple-element.142) | copy-start | bytes 6148
  645.1 72.4 %reduce-scatter.23.cloned.1.call-start = ((), (), s32[]{:S(2)}) async-start(), calls=%async_computation.12 | async-start | bytes 655360
  667.8 22.4 %copy-start.49 = (f32[2,8,32]{2,1,0:T(8,128)S(1)}, f32[2,8,32]{2,1,0:T(8,128)}, u32[]{:S(2)}) copy-start(f32[2,8,32]{2,1,0:T(8,128)} %get-tuple-element.130) | copy-start | bytes 6148
  699.4 101.0 %reduce-scatter.17.cloned.1.call-start = ((), (), s32[]{:S(2)}) async-start(), calls=%async_computation.9 | async-start | bytes 589824 | tf_op jit(solution)/shard_map/reduce_scatter | solution.py:419
  702.0 145.2 %reduce-scatter.13.cloned.1.call-start = ((), (), s32[]{:S(2)}) async-start(), calls=%async_computation.7 | async-start | bytes 589824 | tf_op jit(solution)/shard_map/reduce_scatter | solution.py:419
  705.1 14.1 %copy-start.56 = (f32[2,128]{1,0:T(2,128)S(1)}, f32[2,128]{1,0:T(2,128)}, u32[]{:S(2)}) copy-start(f32[2,128]{1,0:T(2,128)} %copy-done.55) | copy-start | bytes 3076
  705.1 14.1 %copy-start.58 = (f32[2,128]{1,0:T(2,128)S(1)}, f32[2,128]{1,0:T(2,128)}, u32[]{:S(2)}) copy-start(f32[2,128]{1,0:T(2,128)} %copy-done.57) | copy-start | bytes 3076
  705.1 14.1 %copy-start.70 = (f32[128]{0:T(128)S(1)}, f32[128]{0:T(128)}, u32[]{:S(2)}) copy-start(f32[128]{0:T(128)} %copy-done.69) | copy-start | bytes 1540
  705.1 14.1 %copy-start.74 = (f32[128]{0:T(128)S(1)}, f32[128]{0:T(128)}, u32[]{:S(2)}) copy-start(f32[128]{0:T(128)} %copy-done.73) | copy-start | bytes 1540
  705.1 14.3 %copy-start.84 = (f32[2,128]{1,0:T(2,128)S(1)}, f32[2,128]{1,0:T(2,128)}, u32[]{:S(2)}) copy-start(f32[2,128]{1,0:T(2,128)} %get-tuple-element.36) | copy-start | bytes 3076
  705.1 36.2 %copy-start.79 = (f32[2,128]{1,0:T(2,128)S(1)}, f32[2,128]{1,0:T(2,128)}, u32[]{:S(2)}) copy-start(f32[2,128]{1,0:T(2,128)} %get-tuple-element.144) | copy-start | bytes 3076
  706.2 41.8 %copy-start.9 = (bf16[2,8,32,512]{3,2,1,0:T(8,128)(2,1)S(1)}, bf16[2,8,32,512]{3,2,1,0:T(8,128)(2,1)}, u32[]{:S(2)}) copy-start(bf16[2,8,32,512]{3,2,1,0:T(8,128)(2,1)} %param.16) | copy-start | bytes 1572868
  749.2 165.8 %reduce-scatter.15.cloned.1.call-start = ((), (), s32[]{:S(2)}) async-start(), calls=%async_computation.8 | async-start | bytes 1327104 | tf_op jit(solution)/shard_map/reduce_scatter | solution.py:419
  755.6 6.1 copy-start.83
  755.6 44.0 %copy-start.35 = (bf16[2,2,256,128]{3,2,1,0:T(8,128)(2,1)S(1)}, bf16[2,2,256,128]{3,2,1,0:T(8,128)(2,1)}, u32[]{:S(2)}) copy-start(bf16[2,2,256,128]{3,2,1,0:T(8,128)(2,1)} %get-tuple-element.29) | copy-start | bytes 786436
  755.6 44.8 %copy-start.78 = (f32[2,128]{1,0:T(2,128)S(1)}, f32[2,128]{1,0:T(2,128)}, u32[]{:S(2)}) copy-start(f32[2,128]{1,0:T(2,128)} %copy-done.77) | copy-start | bytes 3076
  755.6 44.8 %copy-start.76 = (f32[2,128]{1,0:T(2,128)S(1)}, f32[2,128]{1,0:T(2,128)}, u32[]{:S(2)}) copy-start(f32[2,128]{1,0:T(2,128)} %copy-done.75) | copy-start | bytes 3076
  755.6 47.5 %copy-start.7 = (bf16[512,512]{0,1:T(8,128)(2,1)S(1)}, bf16[512,512]{0,1:T(8,128)(2,1)}, u32[]{:S(2)}) copy-start(bf16[512,512]{0,1:T(8,128)(2,1)} %copy-done.6) | copy-start | bytes 1572868
  (30 other events, 56.6 us)
Sparse Core Ops, SparseCore 0:
  47.9 22.7 reduce-scatter.18
  645.2 20.6 reduce-scatter.20
  699.5 17.9 reduce-scatter.22
  721.1 62.0 reduce-scatter.16
  786.4 60.7 reduce-scatter.12
  851.5 63.5 reduce-scatter.14
Sparse Core Ops, SparseCore 1:
  50.7 42.7 all-gather.1

commit v3 on v2

--- a/solution.py
+++ b/solution.py
@@ -383,63 +383,6 @@
     )
 
 
-def canvas_sum(values):
-    return jnp.sum(values, axis=(1, 2))
-
-
-def spread(values):
-    return values[:, None, None, :]
-
-
-def normalize_each(values, scale, shift, count):
-    total, squares = lax.psum((canvas_sum(values), canvas_sum(values * values)), "batch")
-    center = total / count
-    inverse = lax.rsqrt(squares / count - center * center + EPSILON)
-    normed = (values - spread(center)) * spread(inverse)
-    return (normed, inverse, normed * scale + shift)
-
-
-def normalize_each_back(grads, normed, inverse, scale, count):
-    shift_sum, scale_sum = lax.psum((canvas_sum(grads), canvas_sum(grads * normed)), "batch")
-    back = scale * spread(inverse) * (grads - (spread(shift_sum) + normed * spread(scale_sum)) / count)
-    return (back.astype(jnp.bfloat16), shift_sum, scale_sum)
-
-
-def sum_chan(values):
-    return lax.psum_scatter(
-        values.astype(jnp.bfloat16), "chan", scatter_dimension=3, tiled=True
-    ).astype(jnp.float32)
-
-
-def gather_chan(values):
-    return lax.all_gather(values, "chan", axis=3, tiled=True)
-
-
-def sum_batch(values, axis):
-    return lax.psum_scatter(
-        values.astype(jnp.bfloat16), "batch", scatter_dimension=axis, tiled=True
-    ).astype(jnp.float32)
-
-
-def distil_matrix(weights):
-    taps = weights.shape[1]
-    width = weights.shape[3]
-    columns = []
-    for stream in range(2):
-        for part in range(2):
-            rows = []
-            for head in range(4):
-                source = head - SOURCE_START[stream]
-                if part == 0 and head == OWN_HEAD[stream]:
-                    rows.append(weights[stream, :, 0])
-                elif part == 1 and 0 <= source < 3:
-                    rows.append(weights[stream, :, 1 + source])
-                else:
-                    rows.append(jnp.zeros((taps, width, weights.shape[4]), weights.dtype))
-            columns.append(jnp.concatenate(rows, axis=1))
-    return jnp.concatenate(columns, axis=2)
-
-
 MESH = pl.DeviceIdType.MESH
 PIXELS = 256
 PAD = 32
@@ -451,8 +394,42 @@
     return place, lane, place // 2, place % 2, lane // 2, lane % 2
 
 
-def along(depth, step):
-    return 2 * ((depth // 2 + step // 2) % 2) + (depth % 2 + step % 2) % 2
+def ranked(depth, rank):
+    high, low = depth // 2, depth % 2
+    up, odd = rank // 2, rank % 2
+    return (
+        (1 - odd) * (1 - up) * depth
+        + odd * (1 - up) * (1 + low)
+        + (1 - odd) * up * (2 - 2 * low + high)
+        + odd * up * (3 - 3 * high)
+    )
+
+
+def middle(depth):
+    return (depth // 2 + depth % 2) % 2
+
+
+def inner(depth):
+    return 1 + depth % 2
+
+
+def outer(depth):
+    return 3 * (depth // 2)
+
+
+def onward(depth, rank):
+    second = (1 - rank % 2) * (rank // 2)
+    return outer(depth) + second * (3 - depth - outer(depth))
+
+
+def homeward(depth, rank):
+    second = (1 - rank % 2) * (rank // 2) * middle(depth)
+    return inner(depth) + second * (outer(depth) - inner(depth))
+
+
+def staggered(step):
+    late = ((step + 1) % 2) * ((step + 6) // 7) + step // 7
+    return (1 - late) * ((step + 1) // 2) + late * (step // 2 - 1 + step // 7), late
 
 
 def push(source, target, send_sem, recv_sem, place, lane):
@@ -474,21 +451,100 @@
 
 
 def batch_peers():
+    place, lane, _, _, _, _ = whereabouts()
+    return [((place + step) % 8, lane) for step in range(1, 8)]
+
+
+def line_peers():
     place, lane, depth, side, _, _ = whereabouts()
-    peers = [(along(depth, step) * 2 + side, lane) for step in range(1, 4)]
-    return peers + [(along(depth, step) * 2 + 1 - side, lane) for step in range(4)]
-
-
-def link_peers():
-    place, lane, depth, side, _, _ = whereabouts()
-    return [(along(depth, step) * 2 + side, lane) for step in range(1, 4)] + [
-        (depth * 2 + 1 - side, lane)
-    ]
+    peers = [(ranked(depth, rank) * 2 + side, lane) for rank in range(1, 4)]
+    return peers + [(depth * 2 + 1 - side, lane)]
 
 
 def chan_peers():
     place, lane, _, _, _, _ = whereabouts()
     return [(place, (lane + step) % 4) for step in range(1, 4)]
+
+
+class Gather:
+    def __init__(self, values, recv, cross, line, parts):
+        self.values, self.recv, self.cross, self.line, self.parts = values, recv, cross, line, parts
+
+    def view(self, block, part):
+        return self.values.at[block] if self.parts == 1 else self.values.at[block, part]
+
+    def copy(self, block, part, sem, depth, side):
+        lane = lax.axis_index("chan")
+        here = self.view(block, part)
+        return push(here, here, sem, self.recv.at[block, part], depth * 2 + side, lane)
+
+    def start(self):
+        place, lane, depth, side, _, _ = whereabouts()
+        for part in range(self.parts):
+            self.copy(place, part, self.line.at[0, 0, part], inner(depth), side).start()
+
+            @pl.when(middle(depth) == 1)
+            def _():
+                self.copy(place, part, self.line.at[1, 0, part], outer(depth), side).start()
+
+            self.copy(place, part, self.cross.at[0, part], depth, 1 - side).start()
+
+    def near(self, rank):
+        place, lane, depth, side, _, _ = whereabouts()
+        block = ranked(depth, rank) * 2 + side
+        for part in range(self.parts):
+            self.copy(block, part, self.cross.at[rank, part], depth, side).wait_recv()
+
+            @pl.when(middle(depth) == 1)
+            def _():
+                self.copy(
+                    block, part, self.line.at[0, rank, part], onward(depth, rank), side
+                ).start()
+
+            self.copy(block, part, self.cross.at[rank, part], depth, 1 - side).start()
+        return block
+
+    def far(self, rank):
+        place, lane, depth, side, _, _ = whereabouts()
+        block = ranked(depth, rank) * 2 + 1 - side
+        for part in range(self.parts):
+            self.copy(block, part, self.cross.at[rank, part], depth, side).wait_recv()
+        return block
+
+    def next(self, step):
+        place, lane, depth, side, _, _ = whereabouts()
+        rank, late = staggered(step)
+
+        @pl.when((late == 0) & (step > 0))
+        def _():
+            self.near(rank)
+
+        @pl.when(late == 1)
+        def _():
+            self.far(rank)
+
+        return ranked(depth, rank) * 2 + (side + late) % 2
+
+    def close(self):
+        place, lane, depth, side, _, _ = whereabouts()
+        for part in range(self.parts):
+            for rank in range(4):
+                self.copy(place, part, self.cross.at[rank, part], depth, side).wait_send()
+            self.copy(place, part, self.line.at[0, 0, part], depth, side).wait_send()
+
+            @pl.when(middle(depth) == 1)
+            def _():
+                self.copy(place, part, self.line.at[1, 0, part], depth, side).wait_send()
+                for rank in range(1, 4):
+                    self.copy(place, part, self.line.at[0, rank, part], depth, side).wait_send()
+
+
+def gather_sems(parts):
+    return [
+        pltpu.SemaphoreType.DMA((8, parts)),
+        pltpu.SemaphoreType.DMA((4, parts)),
+        pltpu.SemaphoreType.DMA((2, 4, parts)),
+    ]
 
 
 def clear_edges(turned):
@@ -500,51 +556,15 @@
 def fill_columns(value, mask, turned, columns, row):
     width = value.shape[1]
     wide = value.astype(jnp.float32)
-    inner = slice(PAD, PAD + PIXELS)
-    turned[0, inner] = pltpu.roll(wide, 1, 0).astype(jnp.bfloat16)
-    turned[1, inner] = value
-    turned[2, inner] = pltpu.roll(wide, PIXELS - 1, 0).astype(jnp.bfloat16)
+    inside = slice(PAD, PAD + PIXELS)
+    turned[0, inside] = pltpu.roll(wide, 1, 0).astype(jnp.bfloat16)
+    turned[1, inside] = value
+    turned[2, inside] = pltpu.roll(wide, PIXELS - 1, 0).astype(jnp.bfloat16)
     for number, (vertical, lateral) in enumerate(OFFSETS):
         start = PAD + 32 * vertical
         columns[row : row + PIXELS, number * width : (number + 1) * width] = (
             turned[lateral + 1, start : start + PIXELS] * mask[:, number : number + 1]
         )
-
-
-def own_block(source, everything, recv_sem, z_sem, x_sem):
-    place, lane, depth, side, _, _ = whereabouts()
-    mine = everything.at[place]
-    for step in range(1, 4):
-        push(
-            mine, mine, z_sem.at[step - 1], recv_sem.at[place], along(depth, step) * 2 + side, lane
-        ).start()
-    push(mine, mine, x_sem.at[0], recv_sem.at[place], depth * 2 + 1 - side, lane).start()
-
-
-def next_block(step, everything, recv_sem, z_sem, x_sem):
-    place, lane, depth, side, _, _ = whereabouts()
-    far = step // 2
-    block = along(depth, far) * 2 + (side + step % 2) % 2
-    here = everything.at[block]
-
-    @pl.when(step > 0)
-    def _():
-        push(here, here, z_sem.at[0], recv_sem.at[block], place, lane).wait_recv()
-
-    @pl.when((step > 0) & (step % 2 == 0))
-    def _():
-        push(here, here, x_sem.at[far], recv_sem.at[block], depth * 2 + 1 - side, lane).start()
-
-    return block
-
-
-def sent_blocks(everything, recv_sem, z_sem, x_sem):
-    place, lane, depth, side, _, _ = whereabouts()
-    mine = everything.at[place]
-    for step in range(3):
-        push(mine, mine, z_sem.at[step], recv_sem.at[place], place, lane).wait_send()
-    for step in range(4):
-        push(mine, mine, x_sem.at[step], recv_sem.at[place], place, lane).wait_send()
 
 
 def send_pieces(part, block, stage, got, stage_sem, got_sem):
@@ -597,10 +617,10 @@
     place, lane, _, _, upper, core = whereabouts()
     here = values.at[upper, core, pl.ds(2 * chunk, 2)]
     push(
-        here, here, out_sem.at[0, chunk], in_sem.at[upper, core, chunk], place, upper * 2 + 1 - core
+        here, here, out_sem.at[1, chunk], in_sem.at[upper, core, chunk], place, 2 - 2 * upper + core
     ).start()
     push(
-        here, here, out_sem.at[1, chunk], in_sem.at[upper, core, chunk], place, 2 - 2 * upper + core
+        here, here, out_sem.at[0, chunk], in_sem.at[upper, core, chunk], place, upper * 2 + 1 - core
     ).start()
 
 
@@ -639,13 +659,745 @@
     lax.fori_loop(0, CHUNKS, close, 0)
 
 
+def vmem(count):
+    return [pl.BlockSpec(memory_space=pltpu.VMEM)] * count
+
+
+def chan_scratch():
+    return [
+        pltpu.VMEM((4, 8, PIXELS, LANES), jnp.bfloat16),
+        pltpu.VMEM((4, 8, PIXELS, LANES), jnp.bfloat16),
+    ]
+
+
+def chan_sems():
+    return [
+        pltpu.SemaphoreType.DMA((4, 8)),
+        pltpu.SemaphoreType.DMA((4, 8)),
+        pltpu.SemaphoreType.DMA((3, CHUNKS)),
+        pltpu.SemaphoreType.DMA((2, 2, CHUNKS)),
+    ]
+
+
+def kernel_params(number):
+    return pltpu.CompilerParams(
+        collective_id=number, has_side_effects=True, vmem_limit_bytes=60 * 2**20
+    )
+
+
+class Exchange:
+    def __init__(self, values, send, recv, axis):
+        self.values, self.send, self.recv, self.axis = values, send, recv, axis
+
+    def steps(self):
+        place, lane, _, _, _, _ = whereabouts()
+        if self.axis == "batch":
+            return [(step - 1, (place + step) % 8, lane, (place + step) % 8) for step in range(1, 8)]
+        return [(step - 1, place, (lane + step) % 4, (lane + step) % 4) for step in range(1, 4)]
+
+    def mine(self):
+        place, lane, _, _, _, _ = whereabouts()
+        return place if self.axis == "batch" else lane
+
+    def start(self):
+        here = self.values.at[self.mine()]
+        for number, place, lane, _ in self.steps():
+            push(here, here, self.send.at[number], self.recv.at[self.mine()], place, lane).start()
+
+    def wait(self):
+        for number, place, lane, slot in self.steps():
+            there = self.values.at[slot]
+            push(there, there, self.send.at[number], self.recv.at[slot], place, lane).wait_recv()
+
+    def close(self):
+        here = self.values.at[self.mine()]
+        for number, place, lane, _ in self.steps():
+            push(here, here, self.send.at[number], self.recv.at[self.mine()], place, lane).wait_send()
+
+    def total(self):
+        result = self.values[0]
+        for slot in range(1, self.values.shape[0]):
+            result = result + self.values[slot]
+        return result
+
+
+class Pieces:
+    def __init__(self, stage, got, send, recv):
+        self.stage, self.got, self.send, self.recv = stage, got, send, recv
+
+    def start(self, part):
+        place, lane, _, _, _, _ = whereabouts()
+        for slot in range(4):
+            self.stage[slot] = part[:, slot * LANES : (slot + 1) * LANES].astype(jnp.bfloat16)
+        for step in (2, 1, 3):
+            slot = (lane + step) % 4
+            push(
+                self.stage.at[slot],
+                self.got.at[lane],
+                self.send.at[slot],
+                self.recv.at[lane],
+                place,
+                slot,
+            ).start()
+
+    def finish(self):
+        place, lane, _, _, _, _ = whereabouts()
+        self.got[lane] = self.stage[lane]
+        for step in range(1, 4):
+            slot = (lane + step) % 4
+            push(
+                self.stage.at[slot],
+                self.got.at[slot],
+                self.send.at[slot],
+                self.recv.at[slot],
+                place,
+                lane,
+            ).wait()
+        result = self.got[0].astype(jnp.float32)
+        for slot in range(1, 4):
+            result = result + self.got[slot].astype(jnp.float32)
+        return result
+
+
+def micro_rows(micro):
+    return slice(micro * PIXELS, (micro + 1) * PIXELS)
+
+
+def moments(value, other):
+    rows = []
+    for micro in range(2):
+        part = value[micro_rows(micro)]
+        rows.append(jnp.sum(part, axis=0, keepdims=True))
+        rows.append(jnp.sum(part * other[micro_rows(micro)], axis=0, keepdims=True))
+    return rows
+
+
+def tile_rows(rows, height):
+    width = rows[0].shape[1]
+    return jnp.concatenate(rows + [jnp.zeros((height - len(rows), width), jnp.float32)], axis=0)
+
+
+def normed_part(value, totals, micro, count):
+    center = totals[2 * micro : 2 * micro + 1] / count
+    inverse = lax.rsqrt(totals[2 * micro + 1 : 2 * micro + 2] / count - center * center + EPSILON)
+    return (value[micro_rows(micro)] - center) * inverse, inverse
+
+
+def dot_last(first, second):
+    return lax.dot_general(
+        first, second, (((1,), (1,)), ((), ())), preferred_element_type=jnp.float32
+    )
+
+
+def front_kernel(
+    count,
+    x_ref,
+    ids_ref,
+    reduce_ref,
+    spatial_ref,
+    expand_ref,
+    block_ref,
+    output_ref,
+    head_ref,
+    y_ref,
+    norm3_ref,
+    inverse3_ref,
+    norm12_ref,
+    inverse12_ref,
+    act1_ref,
+    act2_ref,
+    reduce_all,
+    spatial_all,
+    expand_all,
+    mask_all,
+    mine_ref,
+    turned,
+    columns,
+    stage,
+    got,
+    sums1,
+    sums2,
+    sums3,
+    head_all,
+    *sems,
+):
+    place, lane, depth, side, upper, core = whereabouts()
+    reduces = Gather(reduce_all, *sems[0:3], 1)
+    spatials = Gather(spatial_all, *sems[3:6], 1)
+    expands = Gather(expand_all, *sems[6:9], 1)
+    masks = Gather(mask_all, *sems[9:12], 1)
+    pieces = Pieces(stage, got, sems[12], sems[13])
+    first_sums = Exchange(sums1, sems[14], sems[15], "batch")
+    second_sums = Exchange(sums2, sems[16], sems[17], "batch")
+    third_sums = Exchange(sums3, sems[18], sems[19], "batch")
+    heads = Exchange(head_all, sems[20], sems[21], "chan")
+    first_acts = Exchange(act1_ref, sems[22], sems[23], "chan")
+    second_acts = Exchange(act2_ref, sems[24], sems[25], "chan")
+
+    greet(batch_peers() + chan_peers())
+    reduce_all[place] = reduce_ref[...]
+    reduces.start()
+    spatial_all[place] = spatial_ref[...]
+    spatials.start()
+    expand_all[place] = expand_ref[...]
+    expands.start()
+    head_all[lane] = head_ref[...]
+    heads.start()
+    clear_edges(turned)
+    pixel = lax.broadcasted_iota(jnp.int32, (PIXELS, LANES), 0)
+    column = lax.broadcasted_iota(jnp.int32, (PIXELS, LANES), 1)
+    for micro in range(2):
+        ids = ids_ref[micro]
+        mask = jnp.zeros((PIXELS, LANES), jnp.float32)
+        for number, (vertical, lateral) in enumerate(OFFSETS):
+            offset = 32 * vertical + lateral
+            beside = ids if offset == 0 else pltpu.roll(ids, (-offset) % PIXELS, 0)
+            row, col = (pixel >> 5) + vertical, (pixel & 31) + lateral
+            inside = (row >= 0) & (row < 8) & (col >= 0) & (col < 32)
+            same = (beside == ids) & inside & (column == number)
+            mask = jnp.where(same, 1.0, mask)
+        mask_all[place, micro] = mask.astype(jnp.bfloat16)
+    masks.start()
+
+    for rank in range(1, 4):
+        reduces.near(rank)
+    for rank in range(4):
+        reduces.far(rank)
+    x = x_ref[...].reshape(2 * PIXELS, x_ref.shape[2])
+    pieces.start(dot_last(x, reduce_all[...].reshape(512, 512)))
+    for rank in range(1, 4):
+        spatials.near(rank)
+    first = pieces.finish()
+    sums1[place] = tile_rows(moments(first, first), 8)
+    first_sums.start()
+    for rank in range(1, 4):
+        expands.near(rank)
+    first_sums.wait()
+    totals = first_sums.total()
+    rows = []
+    for micro in range(2):
+        normed, inverse = normed_part(first, totals, micro, count)
+        norm12_ref[0, micro_rows(micro)] = normed
+        rows.append(inverse)
+        out = normed * block_ref[0:1] + block_ref[2:3]
+        act1_ref[lane, micro_rows(micro)] = (out * jax.nn.sigmoid(out)).astype(jnp.bfloat16)
+    first_acts.start()
+    for rank in range(1, 4):
+        masks.near(rank)
+    for rank in range(4):
+        spatials.far(rank)
+    first_acts.wait()
+    for micro in range(2):
+        value = jnp.concatenate([act1_ref[slot, micro_rows(micro)] for slot in range(4)], axis=1)
+        fill_columns(value, mask_all[place, micro], turned, columns, micro * PIXELS)
+    second = jnp.zeros((2 * PIXELS, LANES), jnp.float32)
+    for number in range(9):
+        second = second + jnp.dot(
+            columns[:, number * 512 : (number + 1) * 512],
+            spatial_all[:, number].reshape(512, LANES),
+            preferred_element_type=jnp.float32,
+        )
+    sums2[place] = tile_rows(moments(second, second), 8)
+    second_sums.start()
+    for rank in range(4):
+        expands.far(rank)
+    second_sums.wait()
+    totals = second_sums.total()
+    for micro in range(2):
+        normed, inverse = normed_part(second, totals, micro, count)
+        norm12_ref[1, micro_rows(micro)] = normed
+        rows.append(inverse)
+        out = normed * block_ref[1:2] + block_ref[3:4]
+        act2_ref[lane, micro_rows(micro)] = (out * jax.nn.sigmoid(out)).astype(jnp.bfloat16)
+    second_acts.start()
+    inverse12_ref[...] = tile_rows(rows, 8)
+    heads.wait()
+    half_width = LANES // 2
+    low = lax.broadcasted_iota(jnp.int32, (1, LANES), 1) < half_width
+    source = place // 2
+    even = place % 2 == 0
+    for kind in range(2):
+        upper_row = head_all[source, pl.ds(4 * kind + 2 * upper, 1)]
+        lower_row = head_all[source, pl.ds(4 * kind + 2 * upper + 1, 1)]
+        mine_ref[kind : kind + 1] = jnp.where(
+            even,
+            jnp.where(low, upper_row, pltpu.roll(lower_row, half_width, 1)),
+            jnp.where(low, pltpu.roll(upper_row, half_width, 1), lower_row),
+        )
+    second_acts.wait()
+    value = jnp.concatenate([act2_ref[slot] for slot in range(4)], axis=1)
+    third = jnp.dot(
+        value, expand_all[...].reshape(512, 512), preferred_element_type=jnp.float32
+    )
+    sums3[place] = tile_rows(moments(third, third), 8)
+    third_sums.start()
+    for rank in range(4):
+        masks.far(rank)
+    third_sums.wait()
+    totals = third_sums.total()
+    rows = []
+    for micro in range(2):
+        normed, inverse = normed_part(third, totals, micro, count)
+        norm3_ref[micro_rows(micro)] = normed
+        rows.append(inverse)
+        out = normed * output_ref[0:1] + output_ref[1:2] + x_ref[micro].astype(jnp.float32)
+        y_ref[micro] = (out * jax.nn.sigmoid(out)).astype(jnp.bfloat16)
+    inverse3_ref[...] = tile_rows(rows, 8)
+    for item in (reduces, spatials, expands, masks, heads, first_acts, second_acts):
+        item.close()
+    for item in (first_sums, second_sums, third_sums):
+        item.close()
+
+
+def exchange_sems(size):
+    return [pltpu.SemaphoreType.DMA((size - 1,)), pltpu.SemaphoreType.DMA((size,))]
+
+
+def run_front(count, x, ids, reduce_rows, spatial, expand, block, output, heads):
+    f32, bf16 = jnp.float32, jnp.bfloat16
+    return pl.pallas_call(
+        functools.partial(front_kernel, count),
+        name="front",
+        out_shape=(
+            jax.ShapeDtypeStruct((2, PIXELS, 512), bf16),
+            jax.ShapeDtypeStruct((2 * PIXELS, 512), f32),
+            jax.ShapeDtypeStruct((8, 512), f32),
+            jax.ShapeDtypeStruct((2, 2 * PIXELS, LANES), f32),
+            jax.ShapeDtypeStruct((8, LANES), f32),
+            jax.ShapeDtypeStruct((4, 2 * PIXELS, LANES), bf16),
+            jax.ShapeDtypeStruct((4, 2 * PIXELS, LANES), bf16),
+            jax.ShapeDtypeStruct((8, 64, 512), bf16),
+            jax.ShapeDtypeStruct((8, 9, 64, LANES), bf16),
+            jax.ShapeDtypeStruct((8, 64, 512), bf16),
+            jax.ShapeDtypeStruct((8, 2, PIXELS, LANES), bf16),
+            jax.ShapeDtypeStruct((2, LANES), f32),
+        ),
+        in_specs=vmem(8),
+        out_specs=tuple(vmem(12)),
+        scratch_shapes=[
+            pltpu.VMEM((3, 2 * PAD + PIXELS, 512), bf16),
+            pltpu.VMEM((2 * PIXELS, 9 * 512), bf16),
+            pltpu.VMEM((4, 2 * PIXELS, LANES), bf16),
+            pltpu.VMEM((4, 2 * PIXELS, LANES), bf16),
+            pltpu.VMEM((8, 8, LANES), f32),
+            pltpu.VMEM((8, 8, LANES), f32),
+            pltpu.VMEM((8, 8, 512), f32),
+            pltpu.VMEM((4, 8, LANES), f32),
+        ]
+        + gather_sems(1) * 4
+        + [pltpu.SemaphoreType.DMA((4,))] * 2
+        + exchange_sems(8) * 3
+        + exchange_sems(4) * 3,
+        compiler_params=kernel_params(1),
+    )(x, ids, reduce_rows, spatial, expand, block, output, heads)
+
+
+class Scatter:
+    def __init__(self, part, far_buf, far_got, near_buf, near_got, sems):
+        self.part, self.far_buf, self.far_got = part, far_buf, far_got
+        self.near_buf, self.near_got = near_buf, near_got
+        self.far_send, self.far_recv, self.near_send, self.near_recv = sems
+
+    def start(self):
+        place, lane, depth, side, _, _ = whereabouts()
+        for level in range(4):
+            self.far_buf[level] = self.part[level * 2 + 1 - side].astype(jnp.bfloat16)
+        push(
+            self.far_buf, self.far_got, self.far_send, self.far_recv, depth * 2 + 1 - side, lane
+        ).start()
+
+    def middle(self):
+        place, lane, depth, side, _, _ = whereabouts()
+        push(self.far_buf, self.far_got, self.far_send, self.far_recv, place, lane).wait()
+        for rank in range(1, 4):
+            level = ranked(depth, rank)
+            self.near_buf[rank - 1] = (
+                self.part[level * 2 + side] + self.far_got[level].astype(jnp.float32)
+            ).astype(jnp.bfloat16)
+            push(
+                self.near_buf.at[rank - 1],
+                self.near_got.at[depth],
+                self.near_send.at[rank - 1],
+                self.near_recv.at[depth],
+                level * 2 + side,
+                lane,
+            ).start()
+
+    def finish(self):
+        place, lane, depth, side, _, _ = whereabouts()
+        result = self.part[place] + self.far_got[depth].astype(jnp.float32)
+        for rank in range(1, 4):
+            level = ranked(depth, rank)
+            push(
+                self.near_buf.at[rank - 1],
+                self.near_got.at[level],
+                self.near_send.at[rank - 1],
+                self.near_recv.at[level],
+                place,
+                lane,
+            ).wait()
+            result = result + self.near_got[level].astype(jnp.float32)
+        return result
+
+
+def scatter_scratch(width):
+    return [
+        pltpu.VMEM((8, 64, width), jnp.float32),
+        pltpu.VMEM((4, 64, width), jnp.bfloat16),
+        pltpu.VMEM((4, 64, width), jnp.bfloat16),
+        pltpu.VMEM((3, 64, width), jnp.bfloat16),
+        pltpu.VMEM((4, 64, width), jnp.bfloat16),
+    ]
+
+
+def scatter_sems():
+    return [
+        pltpu.SemaphoreType.DMA,
+        pltpu.SemaphoreType.DMA,
+        pltpu.SemaphoreType.DMA((3,)),
+        pltpu.SemaphoreType.DMA((4,)),
+    ]
+
+
+def back_part(value, normed, inverse, scale, shift_sum, scale_sum, count):
+    return (scale * inverse * (value - (shift_sum + normed * scale_sum) / count)).astype(
+        jnp.bfloat16
+    )
+
+
+def rear_kernel(
+    count,
+    grad_ref,
+    x_ref,
+    norm3_ref,
+    inverse3_ref,
+    norm12_ref,
+    inverse12_ref,
+    act1_ref,
+    act2_ref,
+    reduce_all,
+    spatial_all,
+    expand_all,
+    mask_ref,
+    block_ref,
+    output_ref,
+    head_ref,
+    gate_ref,
+    features_ref,
+    reduce_out,
+    spatial_out,
+    expand_out,
+    wide_out,
+    small_out,
+    turned,
+    columns,
+    stage,
+    got,
+    stage_next,
+    got_next,
+    sums_a,
+    sums_b,
+    sums_c,
+    head_all,
+    act_all,
+    back3,
+    *rest,
+):
+    expand_bufs, spatial_bufs, reduce_bufs, sems = rest[0:5], rest[5:10], rest[10:15], rest[15:]
+    place, lane, depth, side, upper, core = whereabouts()
+    pieces = Pieces(stage, got, sems[0], sems[1])
+    first = Exchange(sums_a, sems[2], sems[3], "batch")
+    second = Exchange(sums_b, sems[4], sems[5], "batch")
+    third = Exchange(sums_c, sems[6], sems[7], "batch")
+    heads = Exchange(head_all, sems[8], sems[9], "chan")
+    acts = Exchange(act_all, sems[10], sems[11], "chan")
+    expands = Scatter(*expand_bufs, sems[12:16])
+    spatials = Scatter(*spatial_bufs, sems[16:20])
+    reduces = Scatter(*reduce_bufs, sems[20:24])
+    pieces_next = Pieces(stage_next, got_next, sems[24], sems[25])
+
+    greet(batch_peers() + chan_peers())
+    half_width = LANES // 2
+    even = place % 2 == 0
+    mine = lax.broadcasted_iota(jnp.int32, (1, LANES), 1) >> 6 == place % 2
+    rows = []
+    for kind in range(2):
+        own = head_ref[kind : kind + 1]
+        turned_own = pltpu.roll(own, half_width, 1)
+        first_row = jnp.where(mine, jnp.where(even, own, turned_own), 0.0)
+        second_row = jnp.where(mine, jnp.where(even, turned_own, own), 0.0)
+        for half in range(2):
+            for row in (first_row, second_row):
+                rows.append(jnp.where(upper == half, row, 0.0))
+    head_all[lane] = jnp.concatenate(rows, axis=0)
+    heads.start()
+    clear_edges(turned)
+    rows = []
+    for micro in range(2):
+        normed = norm3_ref[micro_rows(micro)]
+        out = normed * output_ref[0:1] + output_ref[1:2] + x_ref[micro].astype(jnp.float32)
+        value = grad_ref[micro_rows(micro)] * silu_slope(out)
+        features_ref[micro] = value
+        rows.append(jnp.sum(value, axis=0, keepdims=True))
+        rows.append(jnp.sum(value * normed, axis=0, keepdims=True))
+    heads.wait()
+    sums_a[place, 0:8] = tile_rows(rows, 8)
+    sums_a[place, 8:16] = jnp.zeros((8, 512), jnp.float32)
+    sums_a[place, 4:6, 0:LANES] = gate_ref[...]
+    sums_a[place, 8:16, 0:LANES] = jnp.where(place // 2 == lane, heads.total(), 0.0)
+    first.start()
+    first.wait()
+    totals = first.total()
+    wide_out[...] = totals
+    for micro in range(2):
+        back3[micro_rows(micro)] = back_part(
+            features_ref[micro],
+            norm3_ref[micro_rows(micro)],
+            inverse3_ref[micro : micro + 1],
+            output_ref[0:1],
+            totals[2 * micro : 2 * micro + 1],
+            totals[2 * micro + 1 : 2 * micro + 2],
+            count,
+        )
+    pieces.start(dot_last(back3[...], expand_all[...].reshape(512, 512)))
+    value = jnp.concatenate([act2_ref[slot] for slot in range(4)], axis=1)
+    expands.part[...] = jnp.dot(
+        value.T, back3[...], preferred_element_type=jnp.float32
+    ).reshape(8, 64, 512)
+    expands.start()
+    grad = pieces.finish()
+    normed = norm12_ref[1]
+    grad = grad * silu_slope(normed * block_ref[1:2] + block_ref[3:4])
+    sums_b[place] = tile_rows(moments(grad, normed), 8)
+    second.start()
+    expands.middle()
+    second.wait()
+    totals = second.total()
+    small_rows = [totals[1:2] + totals[3:4], totals[0:1] + totals[2:3]]
+    for micro in range(2):
+        value = back_part(
+            grad[micro_rows(micro)],
+            normed[micro_rows(micro)],
+            inverse12_ref[2 + micro : 3 + micro],
+            block_ref[1:2],
+            totals[2 * micro : 2 * micro + 1],
+            totals[2 * micro + 1 : 2 * micro + 2],
+            count,
+        )
+        fill_columns(value, mask_ref[micro], turned, columns, micro * PIXELS)
+    part = jnp.zeros((2 * PIXELS, 512), jnp.float32)
+    for number in range(9):
+        part = part + dot_last(
+            columns[:, number * LANES : (number + 1) * LANES],
+            spatial_all[:, 8 - number].reshape(512, LANES),
+        )
+    pieces_next.start(part)
+    value = jnp.concatenate([act1_ref[slot] for slot in range(4)], axis=1)
+    spatials.part[...] = jnp.dot(
+        value.T, columns[...], preferred_element_type=jnp.float32
+    ).reshape(8, 64, 9 * LANES)
+    spatials.start()
+    grad = pieces_next.finish()
+    normed = norm12_ref[0]
+    grad = grad * silu_slope(normed * block_ref[0:1] + block_ref[2:3])
+    sums_c[place] = tile_rows(moments(grad, normed), 8)
+    third.start()
+    spatials.middle()
+    expand_out[...] = expands.finish()
+    third.wait()
+    totals = third.total()
+    small_rows = [totals[1:2] + totals[3:4], small_rows[0], totals[0:1] + totals[2:3], small_rows[1]]
+    small_out[...] = tile_rows(small_rows, 8)
+    for micro in range(2):
+        act_all[lane, micro_rows(micro)] = back_part(
+            grad[micro_rows(micro)],
+            normed[micro_rows(micro)],
+            inverse12_ref[micro : micro + 1],
+            block_ref[0:1],
+            totals[2 * micro : 2 * micro + 1],
+            totals[2 * micro + 1 : 2 * micro + 2],
+            count,
+        )
+    acts.start()
+    acts.wait()
+    value = jnp.concatenate([act_all[slot] for slot in range(4)], axis=1)
+    x = x_ref[...].reshape(2 * PIXELS, 512)
+    reduces.part[...] = jnp.dot(value.T, x, preferred_element_type=jnp.float32).reshape(8, 64, 512)
+    reduces.start()
+    more = jnp.dot(value, reduce_all[...].reshape(512, 512), preferred_element_type=jnp.float32)
+    for micro in range(2):
+        features_ref[micro] = features_ref[micro] + more[micro_rows(micro)]
+    reduces.middle()
+    result = spatials.finish()
+    for number in range(9):
+        spatial_out[8 - number] = result[:, number * LANES : (number + 1) * LANES]
+    reduce_out[...] = reduces.finish().T
+    for item in (first, second, third, heads, acts):
+        item.close()
+
+
+def run_rear(count, *arrays):
+    f32, bf16 = jnp.float32, jnp.bfloat16
+    return pl.pallas_call(
+        functools.partial(rear_kernel, count),
+        name="rear",
+        out_shape=(
+            jax.ShapeDtypeStruct((2, PIXELS, 512), f32),
+            jax.ShapeDtypeStruct((512, 64), f32),
+            jax.ShapeDtypeStruct((9, 64, LANES), f32),
+            jax.ShapeDtypeStruct((64, 512), f32),
+            jax.ShapeDtypeStruct((16, 512), f32),
+            jax.ShapeDtypeStruct((8, LANES), f32),
+        ),
+        in_specs=vmem(16),
+        out_specs=tuple(vmem(6)),
+        scratch_shapes=[
+            pltpu.VMEM((3, 2 * PAD + PIXELS, LANES), bf16),
+            pltpu.VMEM((2 * PIXELS, 9 * LANES), bf16),
+            pltpu.VMEM((4, 2 * PIXELS, LANES), bf16),
+            pltpu.VMEM((4, 2 * PIXELS, LANES), bf16),
+            pltpu.VMEM((4, 2 * PIXELS, LANES), bf16),
+            pltpu.VMEM((4, 2 * PIXELS, LANES), bf16),
+            pltpu.VMEM((8, 16, 512), f32),
+            pltpu.VMEM((8, 8, LANES), f32),
+            pltpu.VMEM((8, 8, LANES), f32),
+            pltpu.VMEM((4, 8, LANES), f32),
+            pltpu.VMEM((4, 2 * PIXELS, LANES), bf16),
+            pltpu.VMEM((2 * PIXELS, 512), bf16),
+        ]
+        + scatter_scratch(512)
+        + scatter_scratch(9 * LANES)
+        + scatter_scratch(512)
+        + [pltpu.SemaphoreType.DMA((4,))] * 2
+        + exchange_sems(8) * 3
+        + exchange_sems(4) * 2
+        + scatter_sems() * 3
+        + [pltpu.SemaphoreType.DMA((4,))] * 2,
+        compiler_params=kernel_params(5),
+    )(*arrays)
+
+
+class Reduce:
+    def __init__(self, part, keep, far_buf, far_got, line_buf, line_got, sems):
+        self.part, self.keep, self.far_buf, self.far_got = part, keep, far_buf, far_got
+        self.line_buf, self.line_got = line_buf, line_got
+        self.far_send, self.far_recv, self.line_send, self.line_recv = sems
+
+    def block(self, step):
+        place, lane, depth, side, _, _ = whereabouts()
+        rank, late = staggered(step)
+        return ranked(depth, 3 - rank) * 2 + (side + 1 + late) % 2
+
+    def line_wait(self, slot):
+        place, lane, _, _, _, _ = whereabouts()
+        push(
+            self.line_buf.at[1],
+            self.line_got.at[slot],
+            self.line_send.at[1],
+            self.line_recv.at[slot],
+            place,
+            lane,
+        ).wait_recv()
+        return self.line_got[slot].astype(jnp.float32)
+
+    def step(self, step):
+        place, lane, depth, side, _, _ = whereabouts()
+        rank, late = staggered(step)
+        rank = 3 - rank
+        owner = ranked(depth, rank)
+
+        @pl.when(late == 0)
+        def _():
+            self.far_buf[rank] = self.part[...].astype(jnp.bfloat16)
+            push(
+                self.far_buf.at[rank],
+                self.far_got.at[rank],
+                self.far_send.at[rank],
+                self.far_recv.at[rank],
+                depth * 2 + 1 - side,
+                lane,
+            ).start()
+
+        @pl.when(late == 1)
+        def _():
+            push(
+                self.far_buf.at[rank],
+                self.far_got.at[rank],
+                self.far_send.at[rank],
+                self.far_recv.at[rank],
+                place,
+                lane,
+            ).wait_recv()
+            self.keep[...] = self.part[...] + self.far_got[rank].astype(jnp.float32)
+
+            @pl.when((middle(depth) == 1) & (rank > 0))
+            def _():
+                self.keep[...] = self.keep[...] + self.line_wait(owner)
+
+            @pl.when(rank > 0)
+            def _():
+                first = (rank % 2) * (1 - rank // 2) * (1 - middle(depth))
+                slot = owner + first * (4 - owner)
+                self.line_buf[rank] = self.keep[...].astype(jnp.bfloat16)
+                push(
+                    self.line_buf.at[rank],
+                    self.line_got.at[slot],
+                    self.line_send.at[rank],
+                    self.line_recv.at[slot],
+                    homeward(depth, rank) * 2 + side,
+                    lane,
+                ).start()
+
+    def close(self):
+        place, lane, depth, side, _, _ = whereabouts()
+        self.keep[...] = self.keep[...] + self.line_wait(depth)
+
+        @pl.when(middle(depth) == 1)
+        def _():
+            self.keep[...] = self.keep[...] + self.line_wait(4)
+
+        for rank in range(4):
+            push(
+                self.far_buf.at[rank],
+                self.far_got.at[rank],
+                self.far_send.at[rank],
+                self.far_recv.at[rank],
+                place,
+                lane,
+            ).wait_send()
+        for rank in range(1, 4):
+            push(
+                self.line_buf.at[rank],
+                self.line_got.at[rank],
+                self.line_send.at[rank],
+                self.line_recv.at[rank],
+                place,
+                lane,
+            ).wait_send()
+
+
+def reduce_scratch():
+    block = (2 * PIXELS, 512)
+    return [
+        pltpu.VMEM(block, jnp.float32),
+        pltpu.VMEM(block, jnp.float32),
+        pltpu.VMEM((4,) + block, jnp.bfloat16),
+        pltpu.VMEM((4,) + block, jnp.bfloat16),
+        pltpu.VMEM((4,) + block, jnp.bfloat16),
+        pltpu.VMEM((5,) + block, jnp.bfloat16),
+        pltpu.SemaphoreType.DMA((4,)),
+        pltpu.SemaphoreType.DMA((4,)),
+        pltpu.SemaphoreType.DMA((4,)),
+        pltpu.SemaphoreType.DMA((5,)),
+    ]
+
+
 def heads_kernel(
     count,
     block_ref,
     weight_ref,
     mask_ref,
-    scale_ref,
-    shift_ref,
+    mine_ref,
     all_ref,
     act_ref,
     norm_ref,
@@ -655,21 +1407,22 @@
     stage,
     got,
     recv_sem,
+    x_sem,
     z_sem,
-    x_sem,
     stage_sem,
     got_sem,
     out_sem,
     in_sem,
 ):
     place, lane, depth, side, upper, core = whereabouts()
-    greet(link_peers() + chan_peers())
+    gather = Gather(all_ref, recv_sem, x_sem, z_sem, 2)
+    greet(line_peers() + chan_peers())
     all_ref[place] = block_ref[...]
-    own_block(block_ref, all_ref, recv_sem, z_sem, x_sem)
+    gather.start()
     clear_edges(turned)
 
     def body(step, _):
-        block = next_block(step, all_ref, recv_sem, z_sem, x_sem)
+        block = gather.next(step)
         for micro in range(2):
             fill_columns(
                 all_ref[block, micro], mask_ref[block, micro], turned, columns, micro * PIXELS
@@ -702,51 +1455,17 @@
             block = 2 * chunk + item
             normed = (norm_ref[block] - center) * inverse
             norm_ref[block] = normed
-            out = normed * scale_ref[...] + shift_ref[...]
+            out = normed * mine_ref[0:1] + mine_ref[1:2]
             act_ref[upper, core, block] = (out * jax.nn.sigmoid(out)).astype(jnp.bfloat16)
         spread_chunk(chunk, act_ref, out_sem, in_sem)
         return 0
 
     lax.fori_loop(0, CHUNKS, activate, 0)
     finish_chunks(act_ref, out_sem, in_sem)
-    sent_blocks(all_ref, recv_sem, z_sem, x_sem)
-
-
-def vmem(count):
-    return [pl.BlockSpec(memory_space=pltpu.VMEM)] * count
-
-
-def chan_scratch():
-    return [
-        pltpu.VMEM((4, 8, PIXELS, LANES), jnp.bfloat16),
-        pltpu.VMEM((4, 8, PIXELS, LANES), jnp.bfloat16),
-    ]
-
-
-def gather_sems():
-    return [
-        pltpu.SemaphoreType.DMA((8,)),
-        pltpu.SemaphoreType.DMA((3,)),
-        pltpu.SemaphoreType.DMA((4,)),
-    ]
-
-
-def chan_sems():
-    return [
-        pltpu.SemaphoreType.DMA((4, 8)),
-        pltpu.SemaphoreType.DMA((4, 8)),
-        pltpu.SemaphoreType.DMA((3, CHUNKS)),
-        pltpu.SemaphoreType.DMA((2, 2, CHUNKS)),
-    ]
-
-
-def kernel_params(number):
-    return pltpu.CompilerParams(
-        collective_id=number, has_side_effects=True, vmem_limit_bytes=60 * 2**20
-    )
-
-
-def run_heads(count, block_out, weight, masks, scale, shift):
+    gather.close()
+
+
+def run_heads(count, block_out, weight, masks, mine):
     return pl.pallas_call(
         functools.partial(heads_kernel, count),
         name="heads",
@@ -756,93 +1475,17 @@
             jax.ShapeDtypeStruct((8, PIXELS, LANES), jnp.float32),
             jax.ShapeDtypeStruct((1, LANES), jnp.float32),
         ),
-        in_specs=vmem(5),
+        in_specs=vmem(4),
         out_specs=tuple(vmem(4)),
         scratch_shapes=[
             pltpu.VMEM((3, 2 * PAD + PIXELS, 512), jnp.bfloat16),
             pltpu.VMEM((2 * PIXELS, 9 * 512), jnp.bfloat16),
         ]
         + chan_scratch()
-        + gather_sems()
+        + gather_sems(2)
         + chan_sems(),
-        compiler_params=kernel_params(1),
-    )(block_out, weight, masks, scale, shift)
-
-
-def reduce_far(step, part, send_buf, recv_buf, send_sem, recv_sem):
-    place, lane, depth, side, _, _ = whereabouts()
-    far = 3 - step
-    send_buf[far] = part.astype(jnp.bfloat16)
-    push(
-        send_buf.at[far],
-        recv_buf.at[far],
-        send_sem.at[far],
-        recv_sem.at[far],
-        depth * 2 + 1 - side,
-        lane,
-    ).start()
-
-
-def reduce_near(step, part, keep, side_buf, side_sem, send_buf, recv_buf, send_sem, recv_sem):
-    place, lane, depth, side, _, _ = whereabouts()
-    far = 3 - step
-    push(
-        side_buf.at[far], side_buf.at[far], side_sem.at[far], side_sem.at[far], place, lane
-    ).wait_recv()
-    total = part + side_buf[far].astype(jnp.float32)
-
-    @pl.when(far == 0)
-    def _():
-        keep[...] = total
-
-    @pl.when(far > 0)
-    def _():
-        send_buf[far] = total.astype(jnp.bfloat16)
-        push(
-            send_buf.at[far],
-            recv_buf.at[far],
-            send_sem.at[far],
-            recv_sem.at[far],
-            along(depth, far) * 2 + side,
-            lane,
-        ).start()
-
-
-def reduce_close(keep, far_buf, far_sem, far_recv, send_buf, recv_buf, send_sem, recv_sem):
-    place, lane, _, _, _, _ = whereabouts()
-    for far in range(4):
-        push(
-            far_buf.at[far], far_buf.at[far], far_sem.at[far], far_recv.at[far], place, lane
-        ).wait_send()
-    for far in range(1, 4):
-        push(
-            send_buf.at[far], recv_buf.at[far], send_sem.at[far], recv_sem.at[far], place, lane
-        ).wait()
-        keep[...] = keep[...] + recv_buf[far].astype(jnp.float32)
-
-
-def reduce_scratch():
-    return [
-        pltpu.VMEM((2 * PIXELS, 512), jnp.float32),
-        pltpu.VMEM((4, 2 * PIXELS, 512), jnp.bfloat16),
-        pltpu.VMEM((4, 2 * PIXELS, 512), jnp.bfloat16),
-        pltpu.VMEM((4, 2 * PIXELS, 512), jnp.bfloat16),
-        pltpu.VMEM((4, 2 * PIXELS, 512), jnp.bfloat16),
-        pltpu.SemaphoreType.DMA((4,)),
-        pltpu.SemaphoreType.DMA((4,)),
-        pltpu.SemaphoreType.DMA((4,)),
-        pltpu.SemaphoreType.DMA((4,)),
-    ]
-
-
-def far_block(step):
-    _, _, depth, side, _, _ = whereabouts()
-    return along(depth, 3 - step) * 2 + 1 - side
-
-
-def near_block(step):
-    _, _, depth, side, _, _ = whereabouts()
-    return along(depth, 3 - step) * 2 + side
+        compiler_params=kernel_params(2),
+    )(block_out, weight, masks, mine)
 
 
 def lane_index():
@@ -860,8 +1503,7 @@
     bias_ref,
     norm_ref,
     inverse_ref,
-    scale_ref,
-    shift_ref,
+    mine_ref,
     stream_ref,
     grad_ref,
     gate_ref,
@@ -875,15 +1517,16 @@
     own_stage,
     own_got,
     cot_all,
+    part_ref,
     keep,
-    far_send,
+    far_buf,
     far_got,
-    near_send,
-    near_got,
+    line_buf,
+    line_got,
     far_sem,
     far_recv,
-    near_sem,
-    near_recv,
+    line_sem,
+    line_recv,
     stage,
     got,
     own_sem,
@@ -891,8 +1534,8 @@
     cot_sem,
     cot_recv,
     recv_sem,
+    x_sem,
     z_sem,
-    x_sem,
     stage_sem,
     got_sem,
     out_sem,
@@ -925,7 +1568,7 @@
     @pl.when(source)
     def _():
         def pack(step, _):
-            block = along(depth, step // 2) * 2 + (side + step % 2) % 2
+            block = (place + step) % 8
             for micro in range(2):
                 own_stage[block, micro] = jnp.where(
                     low, act_ref[0, micro, block], act_ref[1, micro, block]
@@ -960,27 +1603,22 @@
             fill_columns(value, mask_ref[block, micro], turned, columns, micro * PIXELS)
         return jnp.dot(columns[...], mixed_ref[...], preferred_element_type=jnp.float32)
 
-    def far_step(step, _):
-        reduce_far(step, partial(far_block(step)), far_send, far_got, far_sem, far_recv)
+    reduce = Reduce(
+        part_ref,
+        keep,
+        far_buf,
+        far_got,
+        line_buf,
+        line_got,
+        (far_sem, far_recv, line_sem, line_recv),
+    )
+
+    def reduce_step(step, _):
+        part_ref[...] = partial(reduce.block(step))
+        reduce.step(step)
         return 0
 
-    lax.fori_loop(0, 4, far_step, 0)
-
-    def near_step(step, _):
-        reduce_near(
-            step,
-            partial(near_block(step)),
-            keep,
-            far_got,
-            far_recv,
-            near_send,
-            near_got,
-            near_sem,
-            near_recv,
-        )
-        return 0
-
-    lax.fori_loop(0, 4, near_step, 0)
+    lax.fori_loop(0, 8, reduce_step, 0)
     for parity in range(2):
         owner = 2 * lane + parity
 
@@ -995,9 +1633,7 @@
                 lane,
             ).wait_recv()
 
-    reduce_close(
-        keep, far_send, far_sem, far_recv, near_send, near_got, near_sem, near_recv
-    )
+    reduce.close()
     for stream in range(2):
         bias_sum = jnp.zeros((1, LANES), jnp.float32)
         for micro in range(2):
@@ -1023,7 +1659,8 @@
                 jnp.bfloat16
             )
         gate_ref[stream : stream + 1] = bias_sum
-    own_block(None, grads_all, recv_sem, z_sem, x_sem)
+    gather = Gather(grads_all, recv_sem, x_sem, z_sem, 2)
+    gather.start()
 
     @pl.when(source)
     def _():
@@ -1041,7 +1678,7 @@
     width = 2 * half_width // 2
 
     def body(step, _):
-        block = next_block(step, grads_all, recv_sem, z_sem, x_sem)
+        block = gather.next(step)
         for micro in range(2):
             fill_columns(
                 grads_all[block, micro],
@@ -1099,15 +1736,14 @@
         got,
         norm_ref,
         inverse_ref,
-        scale_ref,
-        shift_ref,
+        mine_ref,
         back_act_ref,
         sums_ref,
         keep,
         out_sem,
         in_sem,
     )
-    sent_blocks(grads_all, recv_sem, z_sem, x_sem)
+    gather.close()
     for parity in range(2):
         target = 2 * lane + parity
 
@@ -1141,8 +1777,7 @@
     got,
     norm_ref,
     inverse_ref,
-    scale_ref,
-    shift_ref,
+    mine_ref,
     back_act_ref,
     sums_ref,
     keep,
@@ -1156,7 +1791,7 @@
         for other in range(1, 4):
             value = value + got[other, block].astype(jnp.float32)
         normed = norm_ref[block]
-        value = value * silu_slope(normed * scale_ref[...] + shift_ref[...])
+        value = value * silu_slope(normed * mine_ref[0:1] + mine_ref[1:2])
         keep[pl.ds(block // 4 * PIXELS, PIXELS), pl.ds(block % 4 * LANES, LANES)] = value
         return (
             sums[0] + jnp.sum(value, axis=0, keepdims=True),
@@ -1167,7 +1802,7 @@
     shift_sum, scale_sum = lax.fori_loop(0, 8, collect, (zero, zero))
     sums_ref[0:1] = scale_sum
     sums_ref[1:2] = shift_sum
-    factor = scale_ref[...] * inverse_ref[...]
+    factor = mine_ref[0:1] * inverse_ref[...]
 
     def activate(chunk, _):
         for item in range(2):
@@ -1184,7 +1819,7 @@
 
 
 def run_distil(
-    count, acts, mixed, mixed_back, masks, cots, packed, bias, norm, inverse, scale, shift
+    count, acts, mixed, mixed_back, masks, cots, packed, bias, norm, inverse, mine
 ):
     return pl.pallas_call(
         functools.partial(distil_kernel, count),
@@ -1196,7 +1831,7 @@
             jax.ShapeDtypeStruct((2, 2, 8, PIXELS, LANES), jnp.bfloat16),
             jax.ShapeDtypeStruct((2, LANES), jnp.float32),
         ),
-        in_specs=vmem(11),
+        in_specs=vmem(10),
         out_specs=tuple(vmem(5)),
         scratch_shapes=[
             pltpu.VMEM((3, 2 * PAD + PIXELS, 256), jnp.bfloat16),
@@ -1216,10 +1851,10 @@
             pltpu.SemaphoreType.DMA((2,)),
             pltpu.SemaphoreType.DMA((8,)),
         ]
-        + gather_sems()
+        + gather_sems(2)
         + chan_sems(),
-        compiler_params=kernel_params(2),
-    )(acts, mixed, mixed_back, masks, cots, packed, bias, norm, inverse, scale, shift)
+        compiler_params=kernel_params(3),
+    )(acts, mixed, mixed_back, masks, cots, packed, bias, norm, inverse, mine)
 
 
 def back_kernel(
@@ -1231,17 +1866,18 @@
     wgrad_ref,
     turned,
     columns,
+    part_ref,
     keep,
-    far_send,
+    far_buf,
     far_got,
-    near_send,
-    near_got,
+    line_buf,
+    line_got,
     far_sem,
     far_recv,
-    near_sem,
-    near_recv,
+    line_sem,
+    line_recv,
 ):
-    greet(link_peers())
+    greet(line_peers())
     clear_edges(turned)
     wgrad_ref[...] = jnp.zeros_like(wgrad_ref)
 
@@ -1260,25 +1896,25 @@
                 preferred_element_type=jnp.float32,
             )
 
-    def far_step(step, _):
-        block = far_block(step)
-        reduce_far(step, partial(block), far_send, far_got, far_sem, far_recv)
+    reduce = Reduce(
+        part_ref,
+        keep,
+        far_buf,
+        far_got,
+        line_buf,
+        line_got,
+        (far_sem, far_recv, line_sem, line_recv),
+    )
+
+    def step(step, _):
+        block = reduce.block(step)
+        part_ref[...] = partial(block)
+        reduce.step(step)
         weigh(block)
         return 0
 
-    lax.fori_loop(0, 4, far_step, 0)
-
-    def near_step(step, _):
-        block = near_block(step)
-        part = partial(block)
-        weigh(block)
-        reduce_near(
-            step, part, keep, far_got, far_recv, near_send, near_got, near_sem, near_recv
-        )
-        return 0
-
-    lax.fori_loop(0, 4, near_step, 0)
-    reduce_close(keep, far_send, far_sem, far_recv, near_send, near_got, near_sem, near_recv)
+    lax.fori_loop(0, 8, step, 0)
+    reduce.close()
     out_ref[...] = keep[...]
 
 
@@ -1297,8 +1933,27 @@
             pltpu.VMEM((2 * PIXELS, 9 * 256), jnp.bfloat16),
         ]
         + reduce_scratch(),
-        compiler_params=kernel_params(3),
+        compiler_params=kernel_params(4),
     )(grads, block_all, weight, masks)
+
+
+def distil_matrix(weights):
+    taps = weights.shape[1]
+    width = weights.shape[3]
+    columns = []
+    for stream in range(2):
+        for part in range(2):
+            rows = []
+            for head in range(4):
+                source = head - SOURCE_START[stream]
+                if part == 0 and head == OWN_HEAD[stream]:
+                    rows.append(weights[stream, :, 0])
+                elif part == 1 and 0 <= source < 3:
+                    rows.append(weights[stream, :, 1 + source])
+                else:
+                    rows.append(jnp.zeros((taps, width, weights.shape[4]), weights.dtype))
+            columns.append(jnp.concatenate(rows, axis=1))
+    return jnp.concatenate(columns, axis=2)
 
 
 def stationary_local(
@@ -1319,61 +1974,48 @@
     depth_cotangent,
     segment_cotangent,
 ):
-    groups = lax.axis_size("batch")
-    place = lax.axis_index("batch")
-    lane = lax.axis_index("chan")
     canvases, row_count, column_count = image_ids.shape
-    count = float(groups * row_count * column_count)
     pixels = row_count * column_count
+    count = float(lax.axis_size("batch") * pixels)
     width = head_weights.shape[3]
-    reduce_full = lax.all_gather(reduce_weight, "batch", axis=1, tiled=True)
-    spatial_full = lax.all_gather(spatial_weight, "batch", axis=1, tiled=True)
-    expand_full = lax.all_gather(expand_weight, "batch", axis=0, tiled=True)
-    ids_full = lax.all_gather(image_ids, "batch", axis=0, tiled=True)
-    masks = tap_masks(image_ids)
-    masks_full = tap_masks(ids_full)
-    first = sum_chan(
-        jnp.einsum("nhwc,co->nhwo", features, reduce_full, preferred_element_type=jnp.float32)
-    )
-    first_norm, first_inv, first_out = normalize_each(first, block_scale[0], block_shift[0], count)
-    first_full = gather_chan(jax.nn.silu(first_out).astype(jnp.bfloat16))
-    second = conv_forward(first_full, spatial_full, masks)
-    second_norm, second_inv, second_out = normalize_each(
-        second, block_scale[1], block_shift[1], count
-    )
-    second_full = gather_chan(jax.nn.silu(second_out).astype(jnp.bfloat16))
-    third = jnp.einsum(
-        "nhwc,co->nhwo", second_full, expand_full, preferred_element_type=jnp.float32
-    )
-    third_norm, third_inv, third_out = normalize_each(third, output_scale, output_shift, count)
-    summed = third_out + features.astype(jnp.float32)
-    block_out = jax.nn.silu(summed).astype(jnp.bfloat16)
-
-    mask_columns = jnp.pad(
-        masks_full.reshape(9, groups, canvases, pixels).transpose(1, 2, 3, 0),
-        ((0, 0), (0, 0), (0, 0), (0, 7)),
-    ).astype(jnp.bfloat16)
-    half = lane // 2
-
-    def mine(values):
-        whole = lax.all_gather(values, "chan", axis=1, tiled=True)
-        part = lax.dynamic_slice_in_dim(whole, place * width, width, axis=1)
-        return lax.dynamic_slice_in_dim(part.reshape(2, 2 * width), half, 1, axis=0)
-
-    my_scale, my_shift = mine(head_scale), mine(head_shift)
+    x = features.reshape(canvases, pixels, -1)
+    ids = jnp.broadcast_to(
+        image_ids.reshape(canvases, pixels, 1).astype(jnp.float32), (canvases, pixels, LANES)
+    )
+    block_params = jnp.concatenate([block_scale, block_shift], axis=0)
+    output_params = jnp.stack([output_scale, output_shift])
+    (
+        block_out,
+        norm3,
+        inverse3,
+        norm12,
+        inverse12,
+        act1,
+        act2,
+        reduce_all,
+        spatial_all,
+        expand_all,
+        mask_all,
+        mine,
+    ) = run_front(
+        count,
+        x,
+        ids,
+        reduce_weight.T,
+        spatial_weight,
+        expand_weight,
+        block_params,
+        output_params,
+        jnp.concatenate([head_scale, head_shift], axis=0),
+    )
     heads_flat = head_weights.reshape(9, head_weights.shape[1], -1)
     block_all, head_acts, head_norm, head_inv = run_heads(
-        count,
-        block_out.reshape(canvases, pixels, -1),
-        heads_flat.reshape(-1, heads_flat.shape[2]),
-        mask_columns,
-        my_scale,
-        my_shift,
+        count, block_out, heads_flat.reshape(-1, heads_flat.shape[2]), mask_all, mine
     )
     mixed = distil_matrix(distil_weights)
     mixed_back = mixed[::-1].transpose(0, 2, 1).reshape(-1, mixed.shape[1])
     heads_back = heads_flat[::-1].transpose(0, 2, 1).reshape(-1, heads_flat.shape[1])
-    cots = jnp.stack([depth_cotangent, segment_cotangent]).reshape(2, canvases, pixels, 128)
+    cots = jnp.stack([depth_cotangent, segment_cotangent]).reshape(2, canvases, pixels, LANES)
     packed = jnp.stack(
         [
             jnp.concatenate([cots[0, :, :, :width], cots[1, :, :, :width]], axis=-1),
@@ -1385,71 +2027,58 @@
         head_acts,
         mixed.reshape(-1, mixed.shape[2]),
         mixed_back,
-        mask_columns,
+        mask_all,
         cots,
         packed,
         gate_bias,
         head_norm,
         head_inv,
-        my_scale,
-        my_shift,
-    )
-    outputs = streams.reshape((2,) + image_ids.shape + (128,))
-    block_grad, heads_grad = run_back(head_grads, block_all, heads_back, mask_columns)
-    block_grad = block_grad.reshape(features.shape)
-    heads_grad = heads_grad.reshape(head_weights.shape)
-    summed_grad = block_grad * silu_slope(summed)
-    third_pre, third_shift, third_scale = normalize_each_back(
-        summed_grad, third_norm, third_inv, output_scale, count
-    )
-    expand_grad = sum_batch(
-        jnp.einsum("nhwc,nhwo->co", second_full, third_pre, preferred_element_type=jnp.float32), 0
-    )
-    second_grad = sum_chan(
-        jnp.einsum("nhwo,co->nhwc", third_pre, expand_full, preferred_element_type=jnp.float32)
-    ) * silu_slope(second_out)
-    second_pre, second_shift, second_scale = normalize_each_back(
-        second_grad, second_norm, second_inv, block_scale[1], count
-    )
-    spatial_grad = sum_batch(conv_weight_grad(first_full, second_pre, masks), 1)
-    first_grad = sum_chan(conv_input_grad(second_pre, spatial_full, masks)) * silu_slope(first_out)
-    first_pre, first_shift, first_scale = normalize_each_back(
-        first_grad, first_norm, first_inv, block_scale[0], count
-    )
-    first_pre_full = gather_chan(first_pre)
-    reduce_grad = sum_batch(
-        jnp.einsum("nhwc,nhwo->co", features, first_pre_full, preferred_element_type=jnp.float32), 1
-    )
-    features_grad = summed_grad + jnp.einsum(
-        "nhwo,co->nhwc", first_pre_full, reduce_full, preferred_element_type=jnp.float32
-    )
-    sums = head_sums.reshape(2, 1, 2, width)
-    wide = jnp.zeros((2, 2, 2, groups * width), jnp.float32)
-    sums = lax.dynamic_update_slice(wide, sums, (0, half, 0, place * width)).reshape(2, 4, -1)
-    sums = lax.psum(sums, ("batch", "chan"))
-    sums = lax.dynamic_slice_in_dim(sums, lane * 128, 128, axis=2)
-    gate_total = lax.psum(gate_sums, "batch")
+        mine,
+    )
+    block_grad, heads_grad = run_back(head_grads, block_all, heads_back, mask_all)
+    own_mask = lax.dynamic_index_in_dim(mask_all, lax.axis_index("batch"), 0, keepdims=False)
+    features_grad, reduce_grad, spatial_grad, expand_grad, wide_sums, small_sums = run_rear(
+        count,
+        block_grad,
+        x,
+        norm3,
+        inverse3,
+        norm12,
+        inverse12,
+        act1,
+        act2,
+        reduce_all,
+        spatial_all,
+        expand_all,
+        own_mask,
+        block_params,
+        output_params,
+        head_sums,
+        gate_sums,
+    )
+    streams = streams.reshape((2,) + image_ids.shape + (LANES,))
     return (
-        outputs[0],
-        outputs[1],
-        features_grad,
+        streams[0],
+        streams[1],
+        features_grad.reshape(features.shape),
         reduce_grad,
         spatial_grad,
         expand_grad,
-        heads_grad,
+        heads_grad.reshape(head_weights.shape),
         distil_grad,
-        jnp.stack([jnp.sum(first_scale, 0), jnp.sum(second_scale, 0)]),
-        jnp.stack([jnp.sum(first_shift, 0), jnp.sum(second_shift, 0)]),
-        sums[0],
-        sums[1],
-        gate_total,
-        jnp.sum(third_scale, 0),
-        jnp.sum(third_shift, 0),
+        small_sums[0:2],
+        small_sums[2:4],
+        wide_sums[8:12, :LANES],
+        wide_sums[12:16, :LANES],
+        wide_sums[4:6, :LANES],
+        wide_sums[1] + wide_sums[3],
+        wide_sums[0] + wide_sums[2],
     )
 
 
 def solution(mesh):
-    local = stationary_local if dict(mesh.shape) == {"batch": 8, "chan": 4} else gathered_local
+    fits = dict(mesh.shape) == {"batch": 8, "chan": 4}
+    local = stationary_local if fits else gathered_local
     placed = (
         P("batch", None, None, "chan"),
         P("batch", None, None),

time: 930 us -> 479 us (0.52)
  blocking collectives: 288 us -> 0 us
  waiting for transfers between devices: 142 us -> 0 us
  Pallas kernels: 338 us -> 425 us
  local copies, waits for them, and re-layouts: 96.3 us -> 46.8 us
  matrix products: 26.7 us -> 0 us
  between operations: 16.8 us -> 0.84 us
  other arithmetic: 19.9 us -> 5.18 us
    psum x7 -> x0, blocking collectives: 159 us -> none  [the longest x3 63.9 us: normalize_each_back(): lax.psum((canvas_sum(grads), canvas_sum(grads * normed)), 'batch')]
    pallas_call x0 -> x2, Pallas kernels: none -> 139 us  [the longest x1 74.4 us: run_rear(): pl.pallas_call(functools.partial(rear_kernel, count), name='rear', out_sh...]
    all_gather x8 -> x0, blocking collectives: 129 us -> none  [the longest x1 33.6 us: stationary_local(): expand_full = lax.all_gather(expand_weight, 'batch', axis=0, tiled=True)]
    reduce_scatter x3 -> x0, waiting for transfers between devices: 109 us -> none  [sum_batch(): lax.psum_scatter(values.astype(jnp.bfloat16), 'batch', scatter_dimension=...]
    another operation x11 -> x2, local copies, waits for them, and re-layouts: 35.5 us -> 0.07 us
    unnamed x10 -> x0, waiting for transfers between devices: 32.7 us -> none
    dot_general x33 -> x0, matrix products: 26.7 us -> none  [the longest x9 9.05 us: conv_weight_grad(): jnp.einsum('nhwc,nhwo->co', moved, grads, preferred_element_type=jnp.floa...]
    pallas_call x1, Pallas kernels: 176 us -> 150 us  [run_distil(): pl.pallas_call(functools.partial(distil_kernel, count), name='distil', ou...]
  transfers between devices with their start and end apart: 7 -> 0, of which waited for: 4 -> 0; matrix products, arithmetic and copies ran while one was open for 11% -> 0% of each run, Pallas kernels for 0% -> 0%
where the time goes in v3:
time: 479 us; the launch traced here: 478 us
  Pallas kernels  425 us (89%)
  local copies, waits for them, and re-layouts  46.8 us (10%)
  other arithmetic  5.18 us (1%)
    pallas_call x1, Pallas kernels, run_distil(): pl.pallas_call(functools.partial(distil_kernel, count), name='distil', ou...  150 us
    pallas_call x1, Pallas kernels, run_heads(): pl.pallas_call(functools.partial(heads_kernel, count), name='heads', out_...  76.2 us
    pallas_call x1, Pallas kernels, run_rear(): pl.pallas_call(functools.partial(rear_kernel, count), name='rear', out_sh...  74.4 us
    pallas_call x1, Pallas kernels, run_front(): pl.pallas_call(functools.partial(front_kernel, count), name='front', out_...  64.2 us
    pallas_call x1, Pallas kernels, run_back(): pl.pallas_call(back_kernel, name='back', out_shape=(jax.ShapeDtypeStruct(...  60.6 us
    another operation x2, local copies, waits for them, and re-layouts, stationary_local(): heads_flat.reshape(-1, heads_flat.shape[2])  15.6 us

profile of v3, /device:TPU:0, one launch (start us, length us, event | category | flops | bytes accessed | tf_op | source)
XLA Modules:
  0.0 478.0 jit_solution(6973567103324003101)
XLA Ops:
  0.6 1.4 slice_bitcast_fusion.7
  2.2 0.3 maximum_maximum_fusion
  2.5 0.0 copy-start
  2.5 0.0 copy-start.7
  2.5 0.0 copy-start.8
  2.5 0.0 copy-start.11
  2.6 0.0 copy-start.12
  2.6 0.0 copy-start.6
  2.6 0.0 copy-start.9
  2.6 0.0 copy-start.10
  2.6 1.7 reverse_bitcast_fusion
  4.3 4.3 copy.51
  8.5 0.0 copy-done
  8.5 0.0 copy-done.7
  8.5 0.0 copy-done.8
  8.5 0.6 pad_maximum_fusion.2.output_ref
  9.1 0.0 copy-done.11
  9.1 0.0 copy-done.12
  9.1 0.6 pad_maximum_fusion.4.block_ref
  9.7 0.0 copy-done.6
  9.7 0.1 convert_element_type.12
  9.8 0.8 broadcast_in_dim.2.ids_ref
  10.7 0.0 copy-done.9
  10.7 0.0 copy-done.10
  10.7 0.6 pad_maximum_fusion.3.head_ref
  11.3 64.2 %front.1 = (bf16[2,256,512]{2,1,0:T(8,128)(2,1)}, f32[512,512]{1,0:T(8,128)}, f32[8,512]{1,0:T(8,128)}, f32[2,512,128]{2,1,0:T(8,128)}, f32[8,128]{1,0:T(8,128)}...) custom-call(bf16[2,256,512]{2,1,0:T(8,128)(2,1)} %bitcast.69, ...), custom_call_target="tpu_custom_call" | custom-call | tf_op jit(solution)/shard_map/front/pallas_call | solution.py:958
  75.4 7.7 %copy.54 = bf16[9,512,4,64]{3,2,1,0:T(4,128)(2,1)} copy(bf16[9,512,4,64]{1,3,2,0:T(8,128)(2,1)} %param.21) | data formatting | bytes 4718592 | tf_op jit(solution)/shard_map/reshape;reshape | solution.py:2013
  83.1 0.0 copy-start.4
  83.1 0.0 copy-start.3
  83.1 7.9 %reshape.79.weight_ref = bf16[4608,256]{1,0:T(8,128)(2,1)} reshape(bf16[9,512,4,64]{3,2,1,0:T(4,128)(2,1)} %copy.54) | data formatting | bytes 4718592 | tf_op jit(solution)/shard_map/reshape;reshape | solution.py:2013
  91.0 76.2 %heads.1 = (bf16[8,2,256,512]{3,2,1,0:T(8,128)(2,1)}, bf16[2,2,8,256,128]{4,3,2,1,0:T(8,128)(2,1)}, f32[8,256,128]{2,1,0:T(8,128)}, f32[1,128]{1,0:T(1,128)}) custom-call(bf16[2,256,512]{2,1,0:T(8,128)(2,1)} %get-tuple-element.44.block_ref, bf16[4608,256]{1,0:T(8,128)(2,1)} %reshape.79.weight_ref, bf16[8,2,256,128]{3,2,1,0:T(8,128)(2,1)} %get-tuple-element.45.mask_ref, ...), custom_call_target="tpu_custom_call" | custom-call | tf_op jit(solution)/shard_map/heads/pallas_call | solution.py:1469
  167.2 0.0 copy-done.4
  167.2 0.1 slice_bitcast_fusion.11
  167.3 0.0 copy-done.3
  167.3 0.1 slice_bitcast_fusion.10
  167.4 0.1 maximum_bitcast_fusion
  167.6 0.7 pad_maximum_fusion.1.packed_ref
  168.3 0.7 pad_maximum_fusion.cot_ref
  169.1 0.0 copy-start.1
  169.1 149.9 %distil.1 = (bf16[2,2,256,128]{3,2,1,0:T(8,128)(2,1)}, f32[2,9,4,64,128]{4,3,2,1,0:T(8,128)}, f32[2,128]{1,0:T(2,128)}, bf16[2,2,8,256,128]{4,3,2,1,0:T(8,128)(2,1)}, f32[2,128]{1,0:T(2,128)}) custom-call(bf16[2,2,8,256,128]{4,3,2,1,0:T(8,128)(2,1)} %get-tuple-element.47.act_ref, bf16[2304,512]{1,0:T(8,128)(2,1)} %bitcast.64, bf16[4608,256]{1,0:T(8,128)(2,1)} %bitcast.66, ...), custom_call_target="tpu_custom_call" | custom-call | tf_op jit(solution)/shard_map/distil/pallas_call | solution.py:1824
  318.9 0.0 copy-done.1
  319.0 1.7 rev.7
  320.6 60.6 %back.1 = (f32[512,512]{1,0:T(8,128)}, f32[9,512,256]{2,1,0:T(8,128)}) custom-call(bf16[2,2,8,256,128]{4,3,2,1,0:T(8,128)(2,1)} %get-tuple-element.51.grads_ref, bf16[8,2,256,512]{3,2,1,0:T(8,128)(2,1)} %get-tuple-element.52.all_ref, bf16[2304,512]{1,0:T(8,128)(2,1)} %bitcast.67, bf16[8,2,256,128]{3,2,1,0:T(8,128)(2,1)} %get-tuple-element.45.mask_ref), custom_call_target="tpu_custom_call" | custom-call | tf_op jit(solution)/shard_map/back/pallas_call | solution.py:1922
  381.2 6.0 %copy.52 = f32[9,512,256]{1,2,0:T(8,128)} copy(f32[9,512,256]{2,1,0:T(8,128)} %get-tuple-element.69) | data formatting | bytes 9437184 | tf_op jit(solution)/shard_map/back/pallas_call | solution.py:1922
  387.2 0.0 copy-start.5
  387.2 1.6 dynamic-slice_bitcast_fusion.mask_ref
  388.8 0.0 copy-start.2
  388.8 74.4 %rear.1 = (f32[2,256,512]{2,1,0:T(8,128)}, f32[512,64]{1,0:T(8,128)}, f32[9,64,128]{2,1,0:T(8,128)}, f32[64,512]{1,0:T(8,128)}, f32[16,512]{1,0:T(8,128)}, /*index=5*/f32[8,128]{1,0:T(8,128)}) custom-call(f32[512,512]{1,0:T(8,128)} %get-tuple-element.53.grad_ref, bf16[2,256,512]{2,1,0:T(8,128)(2,1)} %bitcast.70, f32[512,512]{1,0:T(8,128)} %get-tuple-element.54.norm3_ref, ...), custom_call_target="tpu_custom_call" | custom-call | tf_op jit(solution)/shard_map/rear/pallas_call | solution.py:1241
  463.3 1.7 copy.53
  465.0 1.5 slice_add_fusion
  466.4 1.3 fusion.1
  467.8 1.3 fusion.2
  469.1 1.2 slice.93
  470.3 0.0 copy-done.5
  470.3 0.7 fusion
  471.1 2.3 copy.67
  473.3 1.7 copy.68
  475.0 1.6 copy.69
  476.6 0.0 copy-done.2
  476.6 1.4 copy.70
  (3 shorter events, 0.1 us)
Async XLA Ops:
  2.5 6.0 %copy-start = (bf16[9,256,512]{2,1,0:T(8,128)(2,1)}, bf16[9,256,512]{2,1,0:T(8,128)(2,1)S(1)}, u32[]{:S(2)}) copy-start(bf16[9,256,512]{2,1,0:T(8,128)(2,1)S(1)} %maximum_maximum_fusion) | copy-start | bytes 7077892
  2.5 6.0 %copy-start.7 = (f32[512]{0:T(512)S(1)}, f32[512]{0:T(512)}, u32[]{:S(2)}) copy-start(f32[512]{0:T(512)} %param.29) | copy-start | bytes 6148
  2.5 6.0 %copy-start.8 = (f32[512]{0:T(512)S(1)}, f32[512]{0:T(512)}, u32[]{:S(2)}) copy-start(f32[512]{0:T(512)} %param.28) | copy-start | bytes 6148
  2.5 6.6 %copy-start.11 = (f32[2,128]{1,0:T(2,128)S(1)}, f32[2,128]{1,0:T(2,128)}, u32[]{:S(2)}) copy-start(f32[2,128]{1,0:T(2,128)} %param.24) | copy-start | bytes 3076
  2.6 6.6 %copy-start.12 = (f32[2,128]{1,0:T(2,128)S(1)}, f32[2,128]{1,0:T(2,128)}, u32[]{:S(2)}) copy-start(f32[2,128]{1,0:T(2,128)} %param.23) | copy-start | bytes 3076
  2.6 7.2 %copy-start.6 = (s32[2,8,32]{2,1,0:T(8,128)S(1)}, s32[2,8,32]{2,1,0:T(8,128)}, u32[]{:S(2)}) copy-start(s32[2,8,32]{2,1,0:T(8,128)} %param.17) | copy-start | bytes 6148
  2.6 8.1 %copy-start.9 = (f32[4,128]{1,0:T(4,128)S(1)}, f32[4,128]{1,0:T(4,128)}, u32[]{:S(2)}) copy-start(f32[4,128]{1,0:T(4,128)} %param.26) | copy-start | bytes 6148
  2.6 8.1 %copy-start.10 = (f32[4,128]{1,0:T(4,128)S(1)}, f32[4,128]{1,0:T(4,128)}, u32[]{:S(2)}) copy-start(f32[4,128]{1,0:T(4,128)} %param.25) | copy-start | bytes 6148
  83.1 84.1 %copy-start.4 = (bf16[2,8,32,128]{3,2,1,0:T(8,128)(2,1)S(1)}, bf16[2,8,32,128]{3,2,1,0:T(8,128)(2,1)}, u32[]{:S(2)}) copy-start(bf16[2,8,32,128]{3,2,1,0:T(8,128)(2,1)} %param.30) | copy-start | bytes 393220
  83.1 84.2 %copy-start.3 = (bf16[2,8,32,128]{3,2,1,0:T(8,128)(2,1)S(1)}, bf16[2,8,32,128]{3,2,1,0:T(8,128)(2,1)}, u32[]{:S(2)}) copy-start(bf16[2,8,32,128]{3,2,1,0:T(8,128)(2,1)} %param.31) | copy-start | bytes 393220
  169.1 149.9 %copy-start.1 = (bf16[9,512,4,64]{1,3,2,0:T(8,128)(2,1)S(1)}, bf16[9,512,4,64]{1,3,2,0:T(8,128)(2,1)}, u32[]{:S(2)}) copy-start(bf16[9,512,4,64]{1,3,2,0:T(8,128)(2,1)} %param.21) | copy-start | bytes 7077892
  387.2 83.1 %copy-start.5 = (bf16[2,2,256,128]{3,2,1,0:T(8,128)(2,1)S(1)}, bf16[2,2,256,128]{3,2,1,0:T(8,128)(2,1)}, u32[]{:S(2)}) copy-start(bf16[2,2,256,128]{3,2,1,0:T(8,128)(2,1)} %get-tuple-element.50) | copy-start | bytes 786436
  388.8 87.8 %copy-start.2 = (f32[2,9,4,64,128]{4,3,2,1,0:T(8,128)S(1)}, f32[2,9,4,64,128]{4,3,2,1,0:T(8,128)}, u32[]{:S(2)}) copy-start(f32[2,9,4,64,128]{4,3,2,1,0:T(8,128)} %get-tuple-element.147) | copy-start | bytes 7077892

commit v4 on v3

--- a/solution.py
+++ b/solution.py
@@ -428,8 +428,8 @@
 
 
 def staggered(step):
-    late = ((step + 1) % 2) * ((step + 6) // 7) + step // 7
-    return (1 - late) * ((step + 1) // 2) + late * (step // 2 - 1 + step // 7), late
+    late = ((step + 1) % 2) * ((step + 14) // 15) + step // 15
+    return (1 - late) * ((step + 1) // 2) + late * (step // 2 - 1 + step // 15), late
 
 
 def push(source, target, send_sem, recv_sem, place, lane):
@@ -478,52 +478,50 @@
         here = self.view(block, part)
         return push(here, here, sem, self.recv.at[block, part], depth * 2 + side, lane)
 
-    def start(self):
+    def start(self, part=0):
         place, lane, depth, side, _, _ = whereabouts()
-        for part in range(self.parts):
-            self.copy(place, part, self.line.at[0, 0, part], inner(depth), side).start()
-
-            @pl.when(middle(depth) == 1)
-            def _():
-                self.copy(place, part, self.line.at[1, 0, part], outer(depth), side).start()
-
-            self.copy(place, part, self.cross.at[0, part], depth, 1 - side).start()
-
-    def near(self, rank):
+        self.copy(place, part, self.line.at[0, 0, part], inner(depth), side).start()
+
+        @pl.when(middle(depth) == 1)
+        def _():
+            self.copy(place, part, self.line.at[1, 0, part], outer(depth), side).start()
+
+        self.copy(place, part, self.cross.at[0, part], depth, 1 - side).start()
+
+    def near(self, rank, part=0):
         place, lane, depth, side, _, _ = whereabouts()
         block = ranked(depth, rank) * 2 + side
-        for part in range(self.parts):
-            self.copy(block, part, self.cross.at[rank, part], depth, side).wait_recv()
-
-            @pl.when(middle(depth) == 1)
-            def _():
-                self.copy(
-                    block, part, self.line.at[0, rank, part], onward(depth, rank), side
-                ).start()
-
-            self.copy(block, part, self.cross.at[rank, part], depth, 1 - side).start()
-        return block
-
-    def far(self, rank):
+        self.copy(block, part, self.cross.at[rank, part], depth, side).wait_recv()
+
+        @pl.when(middle(depth) == 1)
+        def _():
+            self.copy(block, part, self.line.at[0, rank, part], onward(depth, rank), side).start()
+
+        self.copy(block, part, self.cross.at[rank, part], depth, 1 - side).start()
+
+    def far(self, rank, part=0):
         place, lane, depth, side, _, _ = whereabouts()
         block = ranked(depth, rank) * 2 + 1 - side
-        for part in range(self.parts):
-            self.copy(block, part, self.cross.at[rank, part], depth, side).wait_recv()
-        return block
+        self.copy(block, part, self.cross.at[rank, part], depth, side).wait_recv()
 
     def next(self, step):
         place, lane, depth, side, _, _ = whereabouts()
-        rank, late = staggered(step)
-
-        @pl.when((late == 0) & (step > 0))
-        def _():
-            self.near(rank)
+        item, late = staggered(step)
+        part, rank = item // 4, item % 4
+
+        @pl.when((late == 0) & (rank > 0))
+        def _():
+            self.near(rank, part)
+
+        @pl.when((late == 0) & (item == 3))
+        def _():
+            self.start(1)
 
         @pl.when(late == 1)
         def _():
-            self.far(rank)
-
-        return ranked(depth, rank) * 2 + (side + late) % 2
+            self.far(rank, part)
+
+        return ranked(depth, rank) * 2 + (side + late) % 2, part
 
     def close(self):
         place, lane, depth, side, _, _ = whereabouts()
@@ -553,130 +551,24 @@
     turned[:, PAD + PIXELS :] = edge
 
 
-def fill_columns(value, mask, turned, columns, row):
+def fill_columns(value, mask, turned, columns, row=0, flip=False):
     width = value.shape[1]
+    lanes = slice(0, width)
     wide = value.astype(jnp.float32)
     inside = slice(PAD, PAD + PIXELS)
-    turned[0, inside] = pltpu.roll(wide, 1, 0).astype(jnp.bfloat16)
-    turned[1, inside] = value
-    turned[2, inside] = pltpu.roll(wide, PIXELS - 1, 0).astype(jnp.bfloat16)
+    turned[0, inside, lanes] = pltpu.roll(wide, 1, 0).astype(jnp.bfloat16)
+    turned[1, inside, lanes] = value
+    turned[2, inside, lanes] = pltpu.roll(wide, PIXELS - 1, 0).astype(jnp.bfloat16)
     for number, (vertical, lateral) in enumerate(OFFSETS):
         start = PAD + 32 * vertical
-        columns[row : row + PIXELS, number * width : (number + 1) * width] = (
-            turned[lateral + 1, start : start + PIXELS] * mask[:, number : number + 1]
-        )
-
-
-def send_pieces(part, block, stage, got, stage_sem, got_sem):
-    place, lane, _, _, _, _ = whereabouts()
-    for micro in range(2):
-        for half in range(2):
-            piece = part[micro * PIXELS : (micro + 1) * PIXELS, half * LANES : (half + 1) * LANES]
-            target = half * 2 + micro
-
-            @pl.when(target == lane)
-            def _():
-                got[lane, block] = piece
-
-            @pl.when(target != lane)
-            def _():
-                stage[target, block] = piece
-                push(
-                    stage.at[target, block],
-                    got.at[lane, block],
-                    stage_sem.at[target, block],
-                    got_sem.at[lane, block],
-                    place,
-                    target,
-                ).start()
-
-
-def await_pieces(stage, got, stage_sem, got_sem):
-    place, lane, _, _, _, _ = whereabouts()
-
-    def body(block, _):
-        for step in range(1, 4):
-            other = (lane + step) % 4
-            push(
-                stage.at[other, block],
-                got.at[other, block],
-                stage_sem.at[other, block],
-                got_sem.at[other, block],
-                place,
-                lane,
-            ).wait()
-        return 0
-
-    lax.fori_loop(0, 8, body, 0)
-
-
-CHUNKS = 4
-
-
-def spread_chunk(chunk, values, out_sem, in_sem):
-    place, lane, _, _, upper, core = whereabouts()
-    here = values.at[upper, core, pl.ds(2 * chunk, 2)]
-    push(
-        here, here, out_sem.at[1, chunk], in_sem.at[upper, core, chunk], place, 2 - 2 * upper + core
-    ).start()
-    push(
-        here, here, out_sem.at[0, chunk], in_sem.at[upper, core, chunk], place, upper * 2 + 1 - core
-    ).start()
-
-
-def finish_chunks(values, out_sem, in_sem):
-    place, lane, _, _, upper, core = whereabouts()
-
-    def relay(chunk, _):
-        here = values.at[1 - upper, core, pl.ds(2 * chunk, 2)]
-        copy = push(
-            here,
-            here,
-            out_sem.at[2, chunk],
-            in_sem.at[1 - upper, core, chunk],
-            place,
-            upper * 2 + 1 - core,
-        )
-        copy.wait_recv()
-        copy.start()
-        return 0
-
-    lax.fori_loop(0, CHUNKS, relay, 0)
-
-    def close(chunk, _):
-        for half in range(2):
-            here = values.at[half, 1 - core, pl.ds(2 * chunk, 2)]
-            push(
-                here, here, out_sem.at[0, chunk], in_sem.at[half, 1 - core, chunk], place, lane
-            ).wait_recv()
-        here = values.at[upper, core, pl.ds(2 * chunk, 2)]
-        for path in range(3):
-            push(
-                here, here, out_sem.at[path, chunk], in_sem.at[upper, core, chunk], place, lane
-            ).wait_send()
-        return 0
-
-    lax.fori_loop(0, CHUNKS, close, 0)
+        slot = 8 - number if flip else number
+        columns[row : row + PIXELS, slot * width : (slot + 1) * width] = (
+            turned[lateral + 1, start : start + PIXELS, lanes] * mask[:, number : number + 1]
+        )
 
 
 def vmem(count):
     return [pl.BlockSpec(memory_space=pltpu.VMEM)] * count
-
-
-def chan_scratch():
-    return [
-        pltpu.VMEM((4, 8, PIXELS, LANES), jnp.bfloat16),
-        pltpu.VMEM((4, 8, PIXELS, LANES), jnp.bfloat16),
-    ]
-
-
-def chan_sems():
-    return [
-        pltpu.SemaphoreType.DMA((4, 8)),
-        pltpu.SemaphoreType.DMA((4, 8)),
-        pltpu.SemaphoreType.DMA((3, CHUNKS)),
-        pltpu.SemaphoreType.DMA((2, 2, CHUNKS)),
-    ]
 
 
 def kernel_params(number):
@@ -796,9 +688,12 @@
     reduce_ref,
     spatial_ref,
     expand_ref,
-    block_ref,
-    output_ref,
-    head_ref,
+    block_scale,
+    block_shift,
+    output_scale,
+    output_shift,
+    head_scale,
+    head_shift,
     y_ref,
     norm3_ref,
     inverse3_ref,
@@ -811,6 +706,7 @@
     expand_all,
     mask_all,
     mine_ref,
+    mask_ref,
     turned,
     columns,
     stage,
@@ -841,7 +737,8 @@
     spatials.start()
     expand_all[place] = expand_ref[...]
     expands.start()
-    head_all[lane] = head_ref[...]
+    head_all[lane, 0:4] = head_scale[...]
+    head_all[lane, 4:8] = head_shift[...]
     heads.start()
     clear_edges(turned)
     pixel = lax.broadcasted_iota(jnp.int32, (PIXELS, LANES), 0)
@@ -856,7 +753,8 @@
             inside = (row >= 0) & (row < 8) & (col >= 0) & (col < 32)
             same = (beside == ids) & inside & (column == number)
             mask = jnp.where(same, 1.0, mask)
-        mask_all[place, micro] = mask.astype(jnp.bfloat16)
+        mask_ref[micro] = mask.astype(jnp.bfloat16)
+        mask_all[place, micro] = mask_ref[micro]
     masks.start()
 
     for rank in range(1, 4):
@@ -879,7 +777,7 @@
         normed, inverse = normed_part(first, totals, micro, count)
         norm12_ref[0, micro_rows(micro)] = normed
         rows.append(inverse)
-        out = normed * block_ref[0:1] + block_ref[2:3]
+        out = normed * block_scale[0:1] + block_shift[0:1]
         act1_ref[lane, micro_rows(micro)] = (out * jax.nn.sigmoid(out)).astype(jnp.bfloat16)
     first_acts.start()
     for rank in range(1, 4):
@@ -907,7 +805,7 @@
         normed, inverse = normed_part(second, totals, micro, count)
         norm12_ref[1, micro_rows(micro)] = normed
         rows.append(inverse)
-        out = normed * block_ref[1:2] + block_ref[3:4]
+        out = normed * block_scale[1:2] + block_shift[1:2]
         act2_ref[lane, micro_rows(micro)] = (out * jax.nn.sigmoid(out)).astype(jnp.bfloat16)
     second_acts.start()
     inverse12_ref[...] = tile_rows(rows, 8)
@@ -940,7 +838,7 @@
         normed, inverse = normed_part(third, totals, micro, count)
         norm3_ref[micro_rows(micro)] = normed
         rows.append(inverse)
-        out = normed * output_ref[0:1] + output_ref[1:2] + x_ref[micro].astype(jnp.float32)
+        out = normed * output_scale[...] + output_shift[...] + x_ref[micro].astype(jnp.float32)
         y_ref[micro] = (out * jax.nn.sigmoid(out)).astype(jnp.bfloat16)
     inverse3_ref[...] = tile_rows(rows, 8)
     for item in (reduces, spatials, expands, masks, heads, first_acts, second_acts):
@@ -953,7 +851,7 @@
     return [pltpu.SemaphoreType.DMA((size - 1,)), pltpu.SemaphoreType.DMA((size,))]
 
 
-def run_front(count, x, ids, reduce_rows, spatial, expand, block, output, heads):
+def run_front(count, *arrays):
     f32, bf16 = jnp.float32, jnp.bfloat16
     return pl.pallas_call(
         functools.partial(front_kernel, count),
@@ -971,9 +869,10 @@
             jax.ShapeDtypeStruct((8, 64, 512), bf16),
             jax.ShapeDtypeStruct((8, 2, PIXELS, LANES), bf16),
             jax.ShapeDtypeStruct((2, LANES), f32),
+            jax.ShapeDtypeStruct((2, PIXELS, LANES), bf16),
         ),
-        in_specs=vmem(8),
-        out_specs=tuple(vmem(12)),
+        in_specs=vmem(11),
+        out_specs=tuple(vmem(13)),
         scratch_shapes=[
             pltpu.VMEM((3, 2 * PAD + PIXELS, 512), bf16),
             pltpu.VMEM((2 * PIXELS, 9 * 512), bf16),
@@ -989,7 +888,7 @@
         + exchange_sems(8) * 3
         + exchange_sems(4) * 3,
         compiler_params=kernel_params(1),
-    )(x, ids, reduce_rows, spatial, expand, block, output, heads)
+    )(*arrays)
 
 
 class Scatter:
@@ -1079,16 +978,23 @@
     spatial_all,
     expand_all,
     mask_ref,
-    block_ref,
-    output_ref,
+    block_scale,
+    block_shift,
+    output_scale,
+    output_shift,
     head_ref,
     gate_ref,
     features_ref,
     reduce_out,
     spatial_out,
     expand_out,
-    wide_out,
-    small_out,
+    block_scale_out,
+    block_shift_out,
+    head_scale_out,
+    head_shift_out,
+    gate_out,
+    output_scale_out,
+    output_shift_out,
     turned,
     columns,
     stage,
@@ -1135,7 +1041,7 @@
     rows = []
     for micro in range(2):
         normed = norm3_ref[micro_rows(micro)]
-        out = normed * output_ref[0:1] + output_ref[1:2] + x_ref[micro].astype(jnp.float32)
+        out = normed * output_scale[...] + output_shift[...] + x_ref[micro].astype(jnp.float32)
         value = grad_ref[micro_rows(micro)] * silu_slope(out)
         features_ref[micro] = value
         rows.append(jnp.sum(value, axis=0, keepdims=True))
@@ -1148,13 +1054,17 @@
     first.start()
     first.wait()
     totals = first.total()
-    wide_out[...] = totals
+    head_scale_out[...] = totals[8:12, 0:LANES]
+    head_shift_out[...] = totals[12:16, 0:LANES]
+    gate_out[...] = totals[4:6, 0:LANES]
+    output_scale_out[...] = totals[1:2] + totals[3:4]
+    output_shift_out[...] = totals[0:1] + totals[2:3]
     for micro in range(2):
         back3[micro_rows(micro)] = back_part(
             features_ref[micro],
             norm3_ref[micro_rows(micro)],
             inverse3_ref[micro : micro + 1],
-            output_ref[0:1],
+            output_scale[...],
             totals[2 * micro : 2 * micro + 1],
             totals[2 * micro + 1 : 2 * micro + 2],
             count,
@@ -1167,29 +1077,30 @@
     expands.start()
     grad = pieces.finish()
     normed = norm12_ref[1]
-    grad = grad * silu_slope(normed * block_ref[1:2] + block_ref[3:4])
+    grad = grad * silu_slope(normed * block_scale[1:2] + block_shift[1:2])
     sums_b[place] = tile_rows(moments(grad, normed), 8)
     second.start()
     expands.middle()
     second.wait()
     totals = second.total()
-    small_rows = [totals[1:2] + totals[3:4], totals[0:1] + totals[2:3]]
+    block_scale_out[1:2] = totals[1:2] + totals[3:4]
+    block_shift_out[1:2] = totals[0:1] + totals[2:3]
     for micro in range(2):
         value = back_part(
             grad[micro_rows(micro)],
             normed[micro_rows(micro)],
             inverse12_ref[2 + micro : 3 + micro],
-            block_ref[1:2],
+            block_scale[1:2],
             totals[2 * micro : 2 * micro + 1],
             totals[2 * micro + 1 : 2 * micro + 2],
             count,
         )
-        fill_columns(value, mask_ref[micro], turned, columns, micro * PIXELS)
+        fill_columns(value, mask_ref[micro], turned, columns, micro * PIXELS, True)
     part = jnp.zeros((2 * PIXELS, 512), jnp.float32)
     for number in range(9):
         part = part + dot_last(
             columns[:, number * LANES : (number + 1) * LANES],
-            spatial_all[:, 8 - number].reshape(512, LANES),
+            spatial_all[:, number].reshape(512, LANES),
         )
     pieces_next.start(part)
     value = jnp.concatenate([act1_ref[slot] for slot in range(4)], axis=1)
@@ -1199,21 +1110,21 @@
     spatials.start()
     grad = pieces_next.finish()
     normed = norm12_ref[0]
-    grad = grad * silu_slope(normed * block_ref[0:1] + block_ref[2:3])
+    grad = grad * silu_slope(normed * block_scale[0:1] + block_shift[0:1])
     sums_c[place] = tile_rows(moments(grad, normed), 8)
     third.start()
     spatials.middle()
     expand_out[...] = expands.finish()
     third.wait()
     totals = third.total()
-    small_rows = [totals[1:2] + totals[3:4], small_rows[0], totals[0:1] + totals[2:3], small_rows[1]]
-    small_out[...] = tile_rows(small_rows, 8)
+    block_scale_out[0:1] = totals[1:2] + totals[3:4]
+    block_shift_out[0:1] = totals[0:1] + totals[2:3]
     for micro in range(2):
         act_all[lane, micro_rows(micro)] = back_part(
             grad[micro_rows(micro)],
             normed[micro_rows(micro)],
             inverse12_ref[micro : micro + 1],
-            block_ref[0:1],
+            block_scale[0:1],
             totals[2 * micro : 2 * micro + 1],
             totals[2 * micro + 1 : 2 * micro + 2],
             count,
@@ -1230,8 +1141,8 @@
     reduces.middle()
     result = spatials.finish()
     for number in range(9):
-        spatial_out[8 - number] = result[:, number * LANES : (number + 1) * LANES]
-    reduce_out[...] = reduces.finish().T
+        spatial_out[number] = result[:, number * LANES : (number + 1) * LANES]
+    reduce_out[...] = reduces.finish()
     for item in (first, second, third, heads, acts):
         item.close()
 
@@ -1243,14 +1154,19 @@
         name="rear",
         out_shape=(
             jax.ShapeDtypeStruct((2, PIXELS, 512), f32),
-            jax.ShapeDtypeStruct((512, 64), f32),
+            jax.ShapeDtypeStruct((64, 512), f32),
             jax.ShapeDtypeStruct((9, 64, LANES), f32),
             jax.ShapeDtypeStruct((64, 512), f32),
-            jax.ShapeDtypeStruct((16, 512), f32),
-            jax.ShapeDtypeStruct((8, LANES), f32),
+            jax.ShapeDtypeStruct((2, LANES), f32),
+            jax.ShapeDtypeStruct((2, LANES), f32),
+            jax.ShapeDtypeStruct((4, LANES), f32),
+            jax.ShapeDtypeStruct((4, LANES), f32),
+            jax.ShapeDtypeStruct((2, LANES), f32),
+            jax.ShapeDtypeStruct((1, 512), f32),
+            jax.ShapeDtypeStruct((1, 512), f32),
         ),
-        in_specs=vmem(16),
-        out_specs=tuple(vmem(6)),
+        in_specs=vmem(18),
+        out_specs=tuple(vmem(11)),
         scratch_shapes=[
             pltpu.VMEM((3, 2 * PAD + PIXELS, LANES), bf16),
             pltpu.VMEM((2 * PIXELS, 9 * LANES), bf16),
@@ -1285,359 +1201,385 @@
 
     def block(self, step):
         place, lane, depth, side, _, _ = whereabouts()
-        rank, late = staggered(step)
-        return ranked(depth, 3 - rank) * 2 + (side + 1 + late) % 2
-
-    def line_wait(self, slot):
-        place, lane, _, _, _, _ = whereabouts()
-        push(
-            self.line_buf.at[1],
-            self.line_got.at[slot],
-            self.line_send.at[1],
-            self.line_recv.at[slot],
+        item, late = staggered(step)
+        return ranked(depth, 3 - item % 4) * 2 + (side + 1 + late) % 2, item // 4
+
+    def far_copy(self, micro, rank, place):
+        return push(
+            self.far_buf.at[micro, rank],
+            self.far_got.at[micro, rank],
+            self.far_send.at[micro, rank],
+            self.far_recv.at[micro, rank],
             place,
-            lane,
-        ).wait_recv()
-        return self.line_got[slot].astype(jnp.float32)
+            lax.axis_index("chan"),
+        )
+
+    def line_copy(self, micro, rank, slot, place):
+        return push(
+            self.line_buf.at[micro, rank],
+            self.line_got.at[micro, slot],
+            self.line_send.at[micro, rank],
+            self.line_recv.at[micro, slot],
+            place,
+            lax.axis_index("chan"),
+        )
+
+    def line_value(self, micro, slot):
+        self.line_copy(micro, 0, slot, lax.axis_index("batch")).wait_recv()
+        return self.line_got[micro, slot].astype(jnp.float32)
 
     def step(self, step):
         place, lane, depth, side, _, _ = whereabouts()
-        rank, late = staggered(step)
-        rank = 3 - rank
+        item, late = staggered(step)
+        micro, rank = item // 4, 3 - item % 4
         owner = ranked(depth, rank)
 
         @pl.when(late == 0)
         def _():
-            self.far_buf[rank] = self.part[...].astype(jnp.bfloat16)
-            push(
-                self.far_buf.at[rank],
-                self.far_got.at[rank],
-                self.far_send.at[rank],
-                self.far_recv.at[rank],
-                depth * 2 + 1 - side,
-                lane,
-            ).start()
+            self.far_buf[micro, rank] = self.part[...].astype(jnp.bfloat16)
+            self.far_copy(micro, rank, depth * 2 + 1 - side).start()
 
         @pl.when(late == 1)
         def _():
-            push(
-                self.far_buf.at[rank],
-                self.far_got.at[rank],
-                self.far_send.at[rank],
-                self.far_recv.at[rank],
-                place,
-                lane,
-            ).wait_recv()
-            self.keep[...] = self.part[...] + self.far_got[rank].astype(jnp.float32)
+            self.far_copy(micro, rank, place).wait_recv()
+            self.keep[micro] = self.part[...] + self.far_got[micro, rank].astype(jnp.float32)
 
             @pl.when((middle(depth) == 1) & (rank > 0))
             def _():
-                self.keep[...] = self.keep[...] + self.line_wait(owner)
+                self.keep[micro] = self.keep[micro] + self.line_value(micro, owner)
 
             @pl.when(rank > 0)
             def _():
                 first = (rank % 2) * (1 - rank // 2) * (1 - middle(depth))
                 slot = owner + first * (4 - owner)
-                self.line_buf[rank] = self.keep[...].astype(jnp.bfloat16)
-                push(
-                    self.line_buf.at[rank],
-                    self.line_got.at[slot],
-                    self.line_send.at[rank],
-                    self.line_recv.at[slot],
-                    homeward(depth, rank) * 2 + side,
-                    lane,
+                self.line_buf[micro, rank - 1] = self.keep[micro].astype(jnp.bfloat16)
+                self.line_copy(
+                    micro, rank - 1, slot, homeward(depth, rank) * 2 + side
                 ).start()
 
+    def close(self, micro):
+        place, lane, depth, side, _, _ = whereabouts()
+        self.keep[micro] = self.keep[micro] + self.line_value(micro, depth)
+
+        @pl.when(middle(depth) == 1)
+        def _():
+            self.keep[micro] = self.keep[micro] + self.line_value(micro, 4)
+
+        for rank in range(4):
+            self.far_copy(micro, rank, place).wait_send()
+        for rank in range(3):
+            self.line_copy(micro, rank, 0, place).wait_send()
+
+
+class Channels:
+    def __init__(self, stage, got, stage_sem, got_sem, values, out_sem, in_sem):
+        self.stage, self.got, self.stage_sem, self.got_sem = stage, got, stage_sem, got_sem
+        self.values, self.out_sem, self.in_sem = values, out_sem, in_sem
+
+    def piece(self, slot, target, block, lane):
+        return push(
+            self.stage.at[slot, block],
+            self.got.at[lane, block],
+            self.stage_sem.at[slot, block],
+            self.got_sem.at[lane, block],
+            lax.axis_index("batch"),
+            target,
+        )
+
+    def send(self, part, block, micro):
+        _, lane, _, _, upper, core = whereabouts()
+        for half in range(2):
+            piece = part[:, half * LANES : (half + 1) * LANES]
+            target = half * 2 + micro
+
+            @pl.when(target == lane)
+            def _():
+                self.got[lane, block] = piece
+
+            @pl.when(target != lane)
+            def _():
+                self.stage[target, block] = piece
+                self.piece(target, target, block, lane).start()
+
+    def collect(self, micro, take):
+        _, lane, _, _, _, core = whereabouts()
+
+        @pl.when(core == micro)
+        def _():
+            def body(block, _):
+                for step in range(1, 4):
+                    other = (lane + step) % 4
+                    self.piece(other, other, block, other).wait_recv()
+                take(block)
+                return 0
+
+            lax.fori_loop(0, 8, body, 0)
+
+    def value(self, block):
+        result = self.got[0, block].astype(jnp.float32)
+        for other in range(1, 4):
+            result = result + self.got[other, block].astype(jnp.float32)
+        return result
+
+    def sent(self):
+        _, lane, _, _, _, _ = whereabouts()
+
+        def body(block, _):
+            for step in range(1, 4):
+                other = (lane + step) % 4
+                self.piece(other, other, block, lane).wait_send()
+            return 0
+
+        lax.fori_loop(0, 8, body, 0)
+
+    def chunk(self, path, half, micro, chunk, place_lane):
+        here = self.values.at[half, micro, pl.ds(2 * chunk, 2)]
+        return push(
+            here,
+            here,
+            self.out_sem.at[path, chunk],
+            self.in_sem.at[half, micro, chunk],
+            lax.axis_index("batch"),
+            place_lane,
+        )
+
+    def spread(self, chunk):
+        _, lane, _, _, upper, core = whereabouts()
+        self.chunk(0, upper, core, chunk, 2 - 2 * upper + core).start()
+        self.chunk(1, upper, core, chunk, upper * 2 + 1 - core).start()
+
+    def relay(self, micro):
+        _, lane, _, _, upper, core = whereabouts()
+
+        @pl.when(core == micro)
+        def _():
+            for chunk in range(4):
+                copy = self.chunk(2, 1 - upper, core, chunk, upper * 2 + 1 - core)
+                copy.wait_recv()
+                copy.start()
+
+    def finish(self, micro):
+        _, lane, _, _, upper, core = whereabouts()
+
+        @pl.when(core != micro)
+        def _():
+            for chunk in range(4):
+                for half in range(2):
+                    self.chunk(0, half, micro, chunk, lane).wait_recv()
+
     def close(self):
-        place, lane, depth, side, _, _ = whereabouts()
-        self.keep[...] = self.keep[...] + self.line_wait(depth)
-
-        @pl.when(middle(depth) == 1)
-        def _():
-            self.keep[...] = self.keep[...] + self.line_wait(4)
-
-        for rank in range(4):
-            push(
-                self.far_buf.at[rank],
-                self.far_got.at[rank],
-                self.far_send.at[rank],
-                self.far_recv.at[rank],
-                place,
-                lane,
-            ).wait_send()
-        for rank in range(1, 4):
-            push(
-                self.line_buf.at[rank],
-                self.line_got.at[rank],
-                self.line_send.at[rank],
-                self.line_recv.at[rank],
-                place,
-                lane,
-            ).wait_send()
-
-
-def reduce_scratch():
-    block = (2 * PIXELS, 512)
-    return [
-        pltpu.VMEM(block, jnp.float32),
-        pltpu.VMEM(block, jnp.float32),
-        pltpu.VMEM((4,) + block, jnp.bfloat16),
-        pltpu.VMEM((4,) + block, jnp.bfloat16),
-        pltpu.VMEM((4,) + block, jnp.bfloat16),
-        pltpu.VMEM((5,) + block, jnp.bfloat16),
-        pltpu.SemaphoreType.DMA((4,)),
-        pltpu.SemaphoreType.DMA((4,)),
-        pltpu.SemaphoreType.DMA((4,)),
-        pltpu.SemaphoreType.DMA((5,)),
-    ]
-
-
-def heads_kernel(
+        _, lane, _, _, upper, core = whereabouts()
+        for chunk in range(4):
+            for path in range(3):
+                self.chunk(path, upper, core, chunk, lane).wait_send()
+
+
+def middle_kernel(
     count,
     block_ref,
-    weight_ref,
+    head_ref,
+    distil_ref,
     mask_ref,
+    depth_cot,
+    segment_cot,
+    bias_ref,
     mine_ref,
-    all_ref,
-    act_ref,
-    norm_ref,
-    inverse_ref,
+    depth_out,
+    segment_out,
+    distil_grad,
+    gate_sums,
+    head_sums,
+    back_out,
+    head_grad,
+    block_all,
+    head_weight,
+    mixed,
+    mixed_back,
     turned,
     columns,
-    stage,
-    got,
-    recv_sem,
-    x_sem,
-    z_sem,
-    stage_sem,
-    got_sem,
-    out_sem,
-    in_sem,
-):
-    place, lane, depth, side, upper, core = whereabouts()
-    gather = Gather(all_ref, recv_sem, x_sem, z_sem, 2)
-    greet(line_peers() + chan_peers())
-    all_ref[place] = block_ref[...]
-    gather.start()
-    clear_edges(turned)
-
-    def body(step, _):
-        block = gather.next(step)
-        for micro in range(2):
-            fill_columns(
-                all_ref[block, micro], mask_ref[block, micro], turned, columns, micro * PIXELS
-            )
-        part = jnp.dot(columns[...], weight_ref[...], preferred_element_type=jnp.float32)
-        send_pieces(part.astype(jnp.bfloat16), block, stage, got, stage_sem, got_sem)
-        return 0
-
-    lax.fori_loop(0, 8, body, 0)
-    await_pieces(stage, got, stage_sem, got_sem)
-
-    def collect(block, sums):
-        value = got[0, block].astype(jnp.float32)
-        for other in range(1, 4):
-            value = value + got[other, block].astype(jnp.float32)
-        norm_ref[block] = value
-        return (
-            sums[0] + jnp.sum(value, axis=0, keepdims=True),
-            sums[1] + jnp.sum(value * value, axis=0, keepdims=True),
-        )
-
-    zero = jnp.zeros((1, LANES), jnp.float32)
-    total, squares = lax.fori_loop(0, 8, collect, (zero, zero))
-    center = total / count
-    inverse = lax.rsqrt(squares / count - center * center + EPSILON)
-    inverse_ref[...] = inverse
-
-    def activate(chunk, _):
-        for item in range(2):
-            block = 2 * chunk + item
-            normed = (norm_ref[block] - center) * inverse
-            norm_ref[block] = normed
-            out = normed * mine_ref[0:1] + mine_ref[1:2]
-            act_ref[upper, core, block] = (out * jax.nn.sigmoid(out)).astype(jnp.bfloat16)
-        spread_chunk(chunk, act_ref, out_sem, in_sem)
-        return 0
-
-    lax.fori_loop(0, CHUNKS, activate, 0)
-    finish_chunks(act_ref, out_sem, in_sem)
-    gather.close()
-
-
-def run_heads(count, block_out, weight, masks, mine):
-    return pl.pallas_call(
-        functools.partial(heads_kernel, count),
-        name="heads",
-        out_shape=(
-            jax.ShapeDtypeStruct((8, 2, PIXELS, 512), jnp.bfloat16),
-            jax.ShapeDtypeStruct((2, 2, 8, PIXELS, LANES), jnp.bfloat16),
-            jax.ShapeDtypeStruct((8, PIXELS, LANES), jnp.float32),
-            jax.ShapeDtypeStruct((1, LANES), jnp.float32),
-        ),
-        in_specs=vmem(4),
-        out_specs=tuple(vmem(4)),
-        scratch_shapes=[
-            pltpu.VMEM((3, 2 * PAD + PIXELS, 512), jnp.bfloat16),
-            pltpu.VMEM((2 * PIXELS, 9 * 512), jnp.bfloat16),
-        ]
-        + chan_scratch()
-        + gather_sems(2)
-        + chan_sems(),
-        compiler_params=kernel_params(2),
-    )(block_out, weight, masks, mine)
-
-
-def lane_index():
-    return lax.broadcasted_iota(jnp.int32, (PIXELS, LANES), 1)
-
-
-def distil_kernel(
-    count,
-    act_ref,
-    mixed_ref,
-    back_ref,
-    mask_ref,
-    cot_ref,
-    packed_ref,
-    bias_ref,
+    acts,
     norm_ref,
-    inverse_ref,
-    mine_ref,
-    stream_ref,
-    grad_ref,
-    gate_ref,
-    back_act_ref,
-    sums_ref,
-    turned,
-    columns,
-    turned_wide,
-    columns_wide,
+    head_back,
     grads_all,
+    packed,
     own_stage,
     own_got,
     cot_all,
+    stage,
+    got,
     part_ref,
     keep,
     far_buf,
     far_got,
     line_buf,
     line_got,
-    far_sem,
-    far_recv,
-    line_sem,
-    line_recv,
-    stage,
-    got,
-    own_sem,
-    own_recv,
-    cot_sem,
-    cot_recv,
-    recv_sem,
-    x_sem,
-    z_sem,
-    stage_sem,
-    got_sem,
-    out_sem,
-    in_sem,
+    stats,
+    *sems,
 ):
     place, lane, depth, side, upper, core = whereabouts()
     half_width = LANES // 2
+    source = place // 2 == lane
+    low = lax.broadcasted_iota(jnp.int32, (PIXELS, LANES), 1) < half_width
+    gather = Gather(block_all, *sems[0:3], 2)
+    gather_back = Gather(grads_all, *sems[3:6], 2)
+    reduce = Reduce(part_ref, keep, far_buf, far_got, line_buf, line_got, sems[6:10])
+    ahead = Channels(stage, got, sems[10], sems[11], acts, sems[12], sems[13])
+    behind = Channels(stage, got, sems[10], sems[11], head_back, sems[14], sems[15])
+    own_sem, own_recv, cot_sem, cot_recv = sems[16:20]
+
     greet(batch_peers() + chan_peers())
-    low = lane_index() < half_width
-    source = place // 2 == lane
-
-    for parity in range(2):
-        target = 2 * lane + parity
-
-        @pl.when(target == place)
-        def _():
-            cot_all[place] = packed_ref[parity]
-
-        @pl.when(target != place)
-        def _():
-            push(
-                packed_ref.at[parity],
-                cot_all.at[place],
-                cot_sem.at[parity],
-                cot_recv.at[place],
-                target,
-                lane,
-            ).start()
-
-    @pl.when(source)
-    def _():
-        def pack(step, _):
-            block = (place + step) % 8
-            for micro in range(2):
+    block_all[place] = block_ref[...]
+    gather.start(0)
+    clear_edges(turned)
+    for number in range(9):
+        head_weight[number * 512 : (number + 1) * 512] = head_ref[number].T
+    for micro in range(2):
+        first, second = (ref[micro].astype(jnp.float32) for ref in (depth_cot, segment_cot))
+        packed[0, micro] = jnp.where(low, first, pltpu.roll(second, half_width, 1)).astype(
+            jnp.bfloat16
+        )
+        packed[1, micro] = jnp.where(low, pltpu.roll(first, half_width, 1), second).astype(
+            jnp.bfloat16
+        )
+
+    def cot_copy(parity, slot, target):
+        return push(
+            packed.at[parity], cot_all.at[slot], cot_sem.at[parity], cot_recv.at[slot], target, lane
+        )
+
+    def forward_step(step, _):
+        block, micro = gather.next(step)
+        fill_columns(block_all[block, micro], mask_ref[block, micro], turned, columns)
+        part = jnp.dot(columns[...], head_weight[...], preferred_element_type=jnp.float32)
+        ahead.send(part.astype(jnp.bfloat16), block, micro)
+
+        @pl.when(step == 0)
+        def _():
+            prepare_mixed()
+
+        @pl.when(step == 2)
+        def _():
+            for parity in range(2):
+                target = 2 * lane + parity
+
+                @pl.when(target == place)
+                def _():
+                    cot_all[place] = packed[parity]
+
+                @pl.when(target != place)
+                def _():
+                    cot_copy(parity, place, target).start()
+
+        @pl.when(step == 4)
+        def _():
+            for number in range(9):
+                mixed_back[number * 512 : (number + 1) * 512] = mixed[
+                    number * 256 : (number + 1) * 256
+                ].T
+
+        @pl.when(step == 10)
+        def _():
+            normalize(0)
+
+        @pl.when(step == 14)
+        def _():
+            ahead.relay(0)
+
+        return 0
+
+    def prepare_mixed():
+        width = half_width
+        for number in range(9):
+            for stream in range(2):
+                for head in range(4):
+                    index = head - SOURCE_START[stream]
+                    rows = slice(number * 256 + head * width, number * 256 + (head + 1) * width)
+                    left = slice(2 * stream * LANES, (2 * stream + 1) * LANES)
+                    right = slice((2 * stream + 1) * LANES, (2 * stream + 2) * LANES)
+                    nothing = jnp.zeros((width, LANES), jnp.bfloat16)
+                    mixed[rows, left] = (
+                        distil_ref[stream, number, 0] if head == OWN_HEAD[stream] else nothing
+                    )
+                    mixed[rows, right] = (
+                        distil_ref[stream, number, 1 + index] if 0 <= index < 3 else nothing
+                    )
+
+    def normalize(micro):
+        zero = jnp.zeros((1, LANES), jnp.float32)
+
+        @pl.when(core == micro)
+        def _():
+            stats[0:2] = jnp.zeros((2, LANES), jnp.float32)
+
+        def take(block):
+            value = ahead.value(block)
+            norm_ref[block] = value
+            stats[0:1] += jnp.sum(value, axis=0, keepdims=True)
+            stats[1:2] += jnp.sum(value * value, axis=0, keepdims=True)
+
+        ahead.collect(micro, take)
+
+        @pl.when(core == micro)
+        def _():
+            center = stats[0:1] / count
+            inverse = lax.rsqrt(stats[1:2] / count - center * center + EPSILON)
+            stats[2:3] = inverse
+
+            def activate(chunk, _):
+                for item in range(2):
+                    block = 2 * chunk + item
+                    normed = (norm_ref[block] - center) * inverse
+                    norm_ref[block] = normed
+                    out = normed * mine_ref[0:1] + mine_ref[1:2]
+                    acts[upper, core, block] = (out * jax.nn.sigmoid(out)).astype(jnp.bfloat16)
+                ahead.spread(chunk)
+                return 0
+
+            lax.fori_loop(0, 4, activate, 0)
+
+    lax.fori_loop(0, 16, forward_step, 0)
+    ahead.finish(0)
+
+    def own_copy(block, micro, slot, target):
+        return push(
+            own_stage.at[block, micro],
+            own_got.at[slot, micro],
+            own_sem.at[block, micro],
+            own_recv.at[slot, micro],
+            target,
+            lane,
+        )
+
+    def send_own(micro):
+        @pl.when(source)
+        def _():
+            own_got[place % 2, micro] = jnp.where(
+                low, acts[0, micro, place], acts[1, micro, place]
+            )
+
+            def pack(step, _):
+                block = (place + step) % 8
                 own_stage[block, micro] = jnp.where(
-                    low, act_ref[0, micro, block], act_ref[1, micro, block]
+                    low, acts[0, micro, block], acts[1, micro, block]
                 )
-
-            @pl.when(block == place)
+                own_copy(block, micro, place % 2, block).start()
+                return 0
+
+            lax.fori_loop(1, 8, pack, 0)
+
+    send_own(0)
+
+    def act_value(block, micro):
+        return jnp.concatenate([acts[half, micro, block] for half in range(2)], axis=1)
+
+    def gate(micro):
+        reduce.close(micro)
+        for parity in range(2):
+            @pl.when(2 * lane + parity != place)
             def _():
-                own_got[place % 2] = own_stage[block]
-
-            @pl.when(block != place)
-            def _():
-                push(
-                    own_stage.at[block],
-                    own_got.at[place % 2],
-                    own_sem.at[block],
-                    own_recv.at[place % 2],
-                    block,
-                    lane,
-                ).start()
-
-            return 0
-
-        lax.fori_loop(0, 8, pack, 0)
-
-    clear_edges(turned)
-    clear_edges(turned_wide)
-    grad_ref[...] = jnp.zeros_like(grad_ref)
-
-    def partial(block):
-        for micro in range(2):
-            value = jnp.concatenate([act_ref[0, micro, block], act_ref[1, micro, block]], axis=1)
-            fill_columns(value, mask_ref[block, micro], turned, columns, micro * PIXELS)
-        return jnp.dot(columns[...], mixed_ref[...], preferred_element_type=jnp.float32)
-
-    reduce = Reduce(
-        part_ref,
-        keep,
-        far_buf,
-        far_got,
-        line_buf,
-        line_got,
-        (far_sem, far_recv, line_sem, line_recv),
-    )
-
-    def reduce_step(step, _):
-        part_ref[...] = partial(reduce.block(step))
-        reduce.step(step)
-        return 0
-
-    lax.fori_loop(0, 8, reduce_step, 0)
-    for parity in range(2):
-        owner = 2 * lane + parity
-
-        @pl.when(owner != place)
-        def _():
-            push(
-                own_got.at[parity],
-                own_got.at[parity],
-                own_sem.at[0],
-                own_recv.at[parity],
-                place,
-                lane,
-            ).wait_recv()
-
-    reduce.close()
-    for stream in range(2):
-        bias_sum = jnp.zeros((1, LANES), jnp.float32)
-        for micro in range(2):
-            rows = slice(micro * PIXELS, (micro + 1) * PIXELS)
+                own_copy(0, micro, parity, place).wait_recv()
+
+        for stream, cot_ref in enumerate((depth_cot, segment_cot)):
             first = own_got[0, micro].astype(jnp.float32)
             second = own_got[1, micro].astype(jnp.float32)
             if stream == 0:
@@ -1646,314 +1588,262 @@
                 first = pltpu.roll(first, half_width, 1)
             own = jnp.where(low, first, second)
             column = 2 * stream * LANES
-            gate = jax.nn.sigmoid(
-                keep[rows, column : column + LANES] + bias_ref[stream : stream + 1]
+            gates = jax.nn.sigmoid(
+                keep[micro, :, column : column + LANES] + bias_ref[stream : stream + 1]
             )
-            message = keep[rows, column + LANES : column + 2 * LANES]
-            cot = cot_ref[stream, micro].astype(jnp.float32)
-            stream_ref[stream, micro] = (own + gate * message).astype(jnp.bfloat16)
-            gate_grad = (cot * message * gate * (1.0 - gate)).astype(jnp.bfloat16)
-            bias_sum = bias_sum + jnp.sum(gate_grad.astype(jnp.float32), axis=0, keepdims=True)
+            message = keep[micro, :, column + LANES : column + 2 * LANES]
+            cot = cot_ref[micro].astype(jnp.float32)
+            out_ref = (depth_out, segment_out)[stream]
+            out_ref[micro] = (own + gates * message).astype(jnp.bfloat16)
+            gate_grad = (cot * message * gates * (1.0 - gates)).astype(jnp.bfloat16)
+            bias_sum = jnp.sum(gate_grad.astype(jnp.float32), axis=0, keepdims=True)
+            if micro == 0:
+                gate_sums[stream : stream + 1] = bias_sum
+            else:
+                gate_sums[stream : stream + 1] += bias_sum
             grads_all[place, micro, :, column : column + LANES] = gate_grad
-            grads_all[place, micro, :, column + LANES : column + 2 * LANES] = (cot * gate).astype(
+            grads_all[place, micro, :, column + LANES : column + 2 * LANES] = (cot * gates).astype(
                 jnp.bfloat16
             )
-        gate_ref[stream : stream + 1] = bias_sum
-    gather = Gather(grads_all, recv_sem, x_sem, z_sem, 2)
-    gather.start()
+
+    def distil_step(step, _):
+        block, micro = reduce.block(step)
+        fill_columns(act_value(block, micro), mask_ref[block, micro], turned, columns)
+        part_ref[...] = jnp.dot(
+            columns[:, 0 : 9 * 256], mixed[...], preferred_element_type=jnp.float32
+        )
+        reduce.step(step)
+
+        @pl.when(step == 1)
+        def _():
+            normalize(1)
+
+        @pl.when(step == 4)
+        def _():
+            ahead.relay(1)
+
+        @pl.when(step == 6)
+        def _():
+            ahead.finish(1)
+            send_own(1)
+
+        @pl.when(step == 11)
+        def _():
+            gate(0)
+            gather_back.start(0)
+
+        return 0
+
+    lax.fori_loop(0, 16, distil_step, 0)
+    gate(1)
+    ahead.sent()
+    ahead.close()
+    distil_grad[...] = jnp.zeros_like(distil_grad)
 
     @pl.when(source)
     def _():
         for step in range(1, 8):
             other = (place + step) % 8
-            push(
-                cot_all.at[other],
-                cot_all.at[other],
-                cot_sem.at[0],
-                cot_recv.at[other],
-                place,
-                lane,
-            ).wait_recv()
-
-    width = 2 * half_width // 2
-
-    def body(step, _):
-        block = gather.next(step)
-        for micro in range(2):
-            fill_columns(
-                grads_all[block, micro],
-                mask_ref[block, micro],
-                turned_wide,
-                columns_wide,
-                micro * PIXELS,
-            )
-        part = jnp.dot(columns_wide[...], back_ref[...], preferred_element_type=jnp.float32)
-        pieces = []
-        for micro in range(2):
-            extra = cot_all[block, micro].astype(jnp.float32)
-            rows = part[micro * PIXELS : (micro + 1) * PIXELS]
-            pieces.append(
-                jnp.concatenate(
-                    [
-                        rows[:, :LANES] + jnp.where(low & source, extra, 0.0),
-                        rows[:, LANES:] + jnp.where(low | ~source, 0.0, extra),
-                    ],
-                    axis=1,
-                )
-            )
-        part = jnp.concatenate(pieces, axis=0).astype(jnp.bfloat16)
-        send_pieces(part, block, stage, got, stage_sem, got_sem)
-        value = jnp.concatenate(
+            cot_copy(0, other, place).wait_recv()
+
+    def back_step(step, _):
+        block, micro = gather_back.next(step)
+        fill_columns(
+            grads_all[block, micro], mask_ref[block, micro], turned, columns, flip=True
+        )
+        part = jnp.dot(columns[...], mixed_back[...], preferred_element_type=jnp.float32)
+        extra = cot_all[block, micro].astype(jnp.float32)
+        part = jnp.concatenate(
             [
-                jnp.concatenate([act_ref[half, micro, block] for half in range(2)], axis=1)
-                for micro in range(2)
+                part[:, :LANES] + jnp.where(low & source, extra, 0.0),
+                part[:, LANES:] + jnp.where(low | ~source, 0.0, extra),
             ],
-            axis=0,
-        ).T
+            axis=1,
+        )
+        behind.send(part.astype(jnp.bfloat16), block, micro)
+        value = act_value(block, micro).T
+        width = half_width
         for number in range(9):
             product = jnp.dot(
                 value,
-                columns_wide[:, number * 512 : (number + 1) * 512],
+                columns[:, number * 512 : (number + 1) * 512],
                 preferred_element_type=jnp.float32,
             )
             for stream in range(2):
-                for part_index in range(4):
-                    head = (
-                        OWN_HEAD[stream]
-                        if part_index == 0
-                        else SOURCE_START[stream] + part_index - 1
-                    )
-                    column = (2 * stream + (part_index > 0)) * LANES
-                    grad_ref[stream, 8 - number, part_index] += product[
+                for index in range(4):
+                    head = OWN_HEAD[stream] if index == 0 else SOURCE_START[stream] + index - 1
+                    column = (2 * stream + (index > 0)) * LANES
+                    distil_grad[stream, number, index] += product[
                         head * width : (head + 1) * width, column : column + LANES
                     ]
+
+        @pl.when(step == 10)
+        def _():
+            normalize_back(0)
+
+        @pl.when(step == 14)
+        def _():
+            behind.relay(0)
+
         return 0
 
-    lax.fori_loop(0, 8, body, 0)
-    await_pieces(stage, got, stage_sem, got_sem)
-    normalize_gradient(
-        count,
-        got,
-        norm_ref,
-        inverse_ref,
-        mine_ref,
-        back_act_ref,
-        sums_ref,
-        keep,
-        out_sem,
-        in_sem,
-    )
+    def normalize_back(micro):
+        @pl.when(core == micro)
+        def _():
+            stats[4:6] = jnp.zeros((2, LANES), jnp.float32)
+
+        def spot(block):
+            return pl.ds(block % 2 * PIXELS, PIXELS), pl.ds(block // 2 * LANES, LANES)
+
+        def take(block):
+            normed = norm_ref[block]
+            value = behind.value(block) * silu_slope(normed * mine_ref[0:1] + mine_ref[1:2])
+            wide_ref = head_grad
+            wide_ref[block, :, 0:LANES] = value
+            stats[4:5] += jnp.sum(value, axis=0, keepdims=True)
+            stats[5:6] += jnp.sum(value * normed, axis=0, keepdims=True)
+
+        behind.collect(micro, take)
+
+        @pl.when(core == micro)
+        def _():
+            shift_sum, scale_sum = stats[4:5], stats[5:6]
+            head_sums[0:1] = scale_sum
+            head_sums[1:2] = shift_sum
+            factor = mine_ref[0:1] * stats[2:3]
+
+            def activate(chunk, _):
+                for item in range(2):
+                    block = 2 * chunk + item
+                    value = head_grad[block, :, 0:LANES]
+                    head_back[upper, core, block] = (
+                        factor * (value - (shift_sum + norm_ref[block] * scale_sum) / count)
+                    ).astype(jnp.bfloat16)
+                behind.spread(chunk)
+                return 0
+
+            lax.fori_loop(0, 4, activate, 0)
+
+    lax.fori_loop(0, 16, back_step, 0)
+    behind.finish(0)
+
+    def head_value(block, micro):
+        return jnp.concatenate([head_back[half, micro, block] for half in range(2)], axis=1)
+
+    def weigh(block, micro):
+        fill_columns(block_all[block, micro], mask_ref[block, micro], turned, columns)
+        value = head_value(block, micro).T
+        for number in range(9):
+            head_grad[number] += jnp.dot(
+                value,
+                columns[:, number * 512 : (number + 1) * 512],
+                preferred_element_type=jnp.float32,
+            )
+
+    def block_step(step, _):
+        block, micro = reduce.block(step)
+        fill_columns(
+            head_value(block, micro), mask_ref[block, micro], turned, columns, flip=True
+        )
+        part_ref[...] = jnp.dot(
+            columns[:, 0 : 9 * 256],
+            head_ref[...].reshape(9 * 256, 512),
+            preferred_element_type=jnp.float32,
+        )
+        reduce.step(step)
+
+        @pl.when(step == 1)
+        def _():
+            normalize_back(1)
+            head_grad[...] = jnp.zeros_like(head_grad)
+
+        @pl.when(step == 4)
+        def _():
+            behind.relay(1)
+
+        @pl.when(step == 6)
+        def _():
+            behind.finish(1)
+
+        @pl.when(step > 1)
+        def _():
+            weigh(block, micro)
+
+        return 0
+
+    lax.fori_loop(0, 16, block_step, 0)
+    for step in range(2):
+        block, micro = reduce.block(step)
+        weigh(block, micro)
+    for micro in range(2):
+        reduce.close(micro)
+        back_out[micro_rows(micro)] = keep[micro]
+    behind.sent()
+    behind.close()
     gather.close()
+    gather_back.close()
     for parity in range(2):
-        target = 2 * lane + parity
-
-        @pl.when(target != place)
-        def _():
-            push(
-                packed_ref.at[parity],
-                cot_all.at[place],
-                cot_sem.at[parity],
-                cot_recv.at[place],
-                target,
-                lane,
-            ).wait_send()
+        @pl.when(2 * lane + parity != place)
+        def _():
+            cot_copy(parity, place, place).wait_send()
 
     @pl.when(source)
     def _():
-        for step in range(1, 8):
-            block = (place + step) % 8
-            push(
-                own_stage.at[block],
-                own_got.at[0],
-                own_sem.at[block],
-                own_recv.at[0],
-                block,
-                lane,
-            ).wait_send()
-
-
-def normalize_gradient(
-    count,
-    got,
-    norm_ref,
-    inverse_ref,
-    mine_ref,
-    back_act_ref,
-    sums_ref,
-    keep,
-    out_sem,
-    in_sem,
-):
-    place, lane, depth, side, upper, core = whereabouts()
-
-    def collect(block, sums):
-        value = got[0, block].astype(jnp.float32)
-        for other in range(1, 4):
-            value = value + got[other, block].astype(jnp.float32)
-        normed = norm_ref[block]
-        value = value * silu_slope(normed * mine_ref[0:1] + mine_ref[1:2])
-        keep[pl.ds(block // 4 * PIXELS, PIXELS), pl.ds(block % 4 * LANES, LANES)] = value
-        return (
-            sums[0] + jnp.sum(value, axis=0, keepdims=True),
-            sums[1] + jnp.sum(value * normed, axis=0, keepdims=True),
-        )
-
-    zero = jnp.zeros((1, LANES), jnp.float32)
-    shift_sum, scale_sum = lax.fori_loop(0, 8, collect, (zero, zero))
-    sums_ref[0:1] = scale_sum
-    sums_ref[1:2] = shift_sum
-    factor = mine_ref[0:1] * inverse_ref[...]
-
-    def activate(chunk, _):
-        for item in range(2):
-            block = 2 * chunk + item
-            value = keep[pl.ds(block // 4 * PIXELS, PIXELS), pl.ds(block % 4 * LANES, LANES)]
-            back_act_ref[upper, core, block] = (
-                factor * (value - (shift_sum + norm_ref[block] * scale_sum) / count)
-            ).astype(jnp.bfloat16)
-        spread_chunk(chunk, back_act_ref, out_sem, in_sem)
-        return 0
-
-    lax.fori_loop(0, CHUNKS, activate, 0)
-    finish_chunks(back_act_ref, out_sem, in_sem)
-
-
-def run_distil(
-    count, acts, mixed, mixed_back, masks, cots, packed, bias, norm, inverse, mine
-):
+        for micro in range(2):
+            for step in range(1, 8):
+                own_copy((place + step) % 8, micro, 0, place).wait_send()
+
+
+def run_middle(count, *arrays):
+    f32, bf16 = jnp.float32, jnp.bfloat16
+    block = (PIXELS, 512)
+    dma = pltpu.SemaphoreType.DMA
     return pl.pallas_call(
-        functools.partial(distil_kernel, count),
-        name="distil",
+        functools.partial(middle_kernel, count),
+        name="middle",
         out_shape=(
-            jax.ShapeDtypeStruct((2, 2, PIXELS, LANES), jnp.bfloat16),
-            jax.ShapeDtypeStruct((2, 9, 4, 64, LANES), jnp.float32),
-            jax.ShapeDtypeStruct((2, LANES), jnp.float32),
-            jax.ShapeDtypeStruct((2, 2, 8, PIXELS, LANES), jnp.bfloat16),
-            jax.ShapeDtypeStruct((2, LANES), jnp.float32),
+            jax.ShapeDtypeStruct((2, PIXELS, LANES), bf16),
+            jax.ShapeDtypeStruct((2, PIXELS, LANES), bf16),
+            jax.ShapeDtypeStruct((2, 9, 4, 64, LANES), f32),
+            jax.ShapeDtypeStruct((2, LANES), f32),
+            jax.ShapeDtypeStruct((2, LANES), f32),
+            jax.ShapeDtypeStruct((2 * PIXELS, 512), f32),
+            jax.ShapeDtypeStruct((9, 256, 512), f32),
         ),
-        in_specs=vmem(10),
-        out_specs=tuple(vmem(5)),
+        in_specs=vmem(8),
+        out_specs=tuple(vmem(7)),
         scratch_shapes=[
-            pltpu.VMEM((3, 2 * PAD + PIXELS, 256), jnp.bfloat16),
-            pltpu.VMEM((2 * PIXELS, 9 * 256), jnp.bfloat16),
-            pltpu.VMEM((3, 2 * PAD + PIXELS, 512), jnp.bfloat16),
-            pltpu.VMEM((2 * PIXELS, 9 * 512), jnp.bfloat16),
-            pltpu.VMEM((8, 2, PIXELS, 512), jnp.bfloat16),
-            pltpu.VMEM((8, 2, PIXELS, LANES), jnp.bfloat16),
-            pltpu.VMEM((2, 2, PIXELS, LANES), jnp.bfloat16),
-            pltpu.VMEM((8, 2, PIXELS, LANES), jnp.bfloat16),
+            pltpu.VMEM((8, 2) + block, bf16),
+            pltpu.VMEM((9 * 512, 256), bf16),
+            pltpu.VMEM((9 * 256, 512), bf16),
+            pltpu.VMEM((9 * 512, 256), bf16),
+            pltpu.VMEM((3, 2 * PAD + PIXELS, 512), bf16),
+            pltpu.VMEM((PIXELS, 9 * 512), bf16),
+            pltpu.VMEM((2, 2, 8, PIXELS, LANES), bf16),
+            pltpu.VMEM((8, PIXELS, LANES), f32),
+            pltpu.VMEM((2, 2, 8, PIXELS, LANES), bf16),
+            pltpu.VMEM((8, 2) + block, bf16),
+            pltpu.VMEM((2, 2, PIXELS, LANES), bf16),
+            pltpu.VMEM((8, 2, PIXELS, LANES), bf16),
+            pltpu.VMEM((2, 2, PIXELS, LANES), bf16),
+            pltpu.VMEM((8, 2, PIXELS, LANES), bf16),
+            pltpu.VMEM((4, 8, PIXELS, LANES), bf16),
+            pltpu.VMEM((4, 8, PIXELS, LANES), bf16),
+            pltpu.VMEM(block, f32),
+            pltpu.VMEM((2,) + block, f32),
+            pltpu.VMEM((2, 4) + block, bf16),
+            pltpu.VMEM((2, 4) + block, bf16),
+            pltpu.VMEM((2, 3) + block, bf16),
+            pltpu.VMEM((2, 5) + block, bf16),
+            pltpu.VMEM((8, LANES), f32),
         ]
-        + reduce_scratch()
-        + chan_scratch()
-        + [
-            pltpu.SemaphoreType.DMA((8,)),
-            pltpu.SemaphoreType.DMA((2,)),
-            pltpu.SemaphoreType.DMA((2,)),
-            pltpu.SemaphoreType.DMA((8,)),
-        ]
-        + gather_sems(2)
-        + chan_sems(),
-        compiler_params=kernel_params(3),
-    )(acts, mixed, mixed_back, masks, cots, packed, bias, norm, inverse, mine)
-
-
-def back_kernel(
-    grads_ref,
-    all_ref,
-    weight_ref,
-    mask_ref,
-    out_ref,
-    wgrad_ref,
-    turned,
-    columns,
-    part_ref,
-    keep,
-    far_buf,
-    far_got,
-    line_buf,
-    line_got,
-    far_sem,
-    far_recv,
-    line_sem,
-    line_recv,
-):
-    greet(line_peers())
-    clear_edges(turned)
-    wgrad_ref[...] = jnp.zeros_like(wgrad_ref)
-
-    def partial(block):
-        for micro in range(2):
-            value = jnp.concatenate([grads_ref[0, micro, block], grads_ref[1, micro, block]], axis=1)
-            fill_columns(value, mask_ref[block, micro], turned, columns, micro * PIXELS)
-        return jnp.dot(columns[...], weight_ref[...], preferred_element_type=jnp.float32)
-
-    def weigh(block):
-        value = jnp.concatenate([all_ref[block, micro] for micro in range(2)], axis=0).T
-        for number in range(9):
-            wgrad_ref[8 - number] += jnp.dot(
-                value,
-                columns[:, number * 256 : (number + 1) * 256],
-                preferred_element_type=jnp.float32,
-            )
-
-    reduce = Reduce(
-        part_ref,
-        keep,
-        far_buf,
-        far_got,
-        line_buf,
-        line_got,
-        (far_sem, far_recv, line_sem, line_recv),
-    )
-
-    def step(step, _):
-        block = reduce.block(step)
-        part_ref[...] = partial(block)
-        reduce.step(step)
-        weigh(block)
-        return 0
-
-    lax.fori_loop(0, 8, step, 0)
-    reduce.close()
-    out_ref[...] = keep[...]
-
-
-def run_back(grads, block_all, weight, masks):
-    return pl.pallas_call(
-        back_kernel,
-        name="back",
-        out_shape=(
-            jax.ShapeDtypeStruct((2 * PIXELS, 512), jnp.float32),
-            jax.ShapeDtypeStruct((9, 512, 256), jnp.float32),
-        ),
-        in_specs=vmem(4),
-        out_specs=tuple(vmem(2)),
-        scratch_shapes=[
-            pltpu.VMEM((3, 2 * PAD + PIXELS, 256), jnp.bfloat16),
-            pltpu.VMEM((2 * PIXELS, 9 * 256), jnp.bfloat16),
-        ]
-        + reduce_scratch(),
-        compiler_params=kernel_params(4),
-    )(grads, block_all, weight, masks)
-
-
-def distil_matrix(weights):
-    taps = weights.shape[1]
-    width = weights.shape[3]
-    columns = []
-    for stream in range(2):
-        for part in range(2):
-            rows = []
-            for head in range(4):
-                source = head - SOURCE_START[stream]
-                if part == 0 and head == OWN_HEAD[stream]:
-                    rows.append(weights[stream, :, 0])
-                elif part == 1 and 0 <= source < 3:
-                    rows.append(weights[stream, :, 1 + source])
-                else:
-                    rows.append(jnp.zeros((taps, width, weights.shape[4]), weights.dtype))
-            columns.append(jnp.concatenate(rows, axis=1))
-    return jnp.concatenate(columns, axis=2)
+        + gather_sems(2) * 2
+        + [dma((2, 4)), dma((2, 4)), dma((2, 3)), dma((2, 5))]
+        + [dma((4, 8)), dma((4, 8))]
+        + [dma((3, 4)), dma((2, 2, 4))] * 2
+        + [dma((8, 2)), dma((2, 2)), dma((2,)), dma((8,))],
+        compiler_params=kernel_params(2),
+    )(*arrays)
 
 
 def stationary_local(
@@ -1977,13 +1867,12 @@
     canvases, row_count, column_count = image_ids.shape
     pixels = row_count * column_count
     count = float(lax.axis_size("batch") * pixels)
-    width = head_weights.shape[3]
     x = features.reshape(canvases, pixels, -1)
     ids = jnp.broadcast_to(
         image_ids.reshape(canvases, pixels, 1).astype(jnp.float32), (canvases, pixels, LANES)
     )
-    block_params = jnp.concatenate([block_scale, block_shift], axis=0)
-    output_params = jnp.stack([output_scale, output_shift])
+    block_params = (block_scale, block_shift)
+    output_params = (output_scale[None], output_shift[None])
     (
         block_out,
         norm3,
@@ -1997,6 +1886,7 @@
         expand_all,
         mask_all,
         mine,
+        mask,
     ) = run_front(
         count,
         x,
@@ -2004,40 +1894,35 @@
         reduce_weight.T,
         spatial_weight,
         expand_weight,
-        block_params,
-        output_params,
-        jnp.concatenate([head_scale, head_shift], axis=0),
-    )
-    heads_flat = head_weights.reshape(9, head_weights.shape[1], -1)
-    block_all, head_acts, head_norm, head_inv = run_heads(
-        count, block_out, heads_flat.reshape(-1, heads_flat.shape[2]), mask_all, mine
-    )
-    mixed = distil_matrix(distil_weights)
-    mixed_back = mixed[::-1].transpose(0, 2, 1).reshape(-1, mixed.shape[1])
-    heads_back = heads_flat[::-1].transpose(0, 2, 1).reshape(-1, heads_flat.shape[1])
-    cots = jnp.stack([depth_cotangent, segment_cotangent]).reshape(2, canvases, pixels, LANES)
-    packed = jnp.stack(
-        [
-            jnp.concatenate([cots[0, :, :, :width], cots[1, :, :, :width]], axis=-1),
-            jnp.concatenate([cots[0, :, :, width:], cots[1, :, :, width:]], axis=-1),
-        ]
-    )
-    streams, distil_grad, gate_sums, head_grads, head_sums = run_distil(
+        *block_params,
+        *output_params,
+        head_scale,
+        head_shift,
+    )
+    depth_out, segment_out, distil_grad, gate_sums, head_sums, block_grad, heads_grad = run_middle(
         count,
-        head_acts,
-        mixed.reshape(-1, mixed.shape[2]),
-        mixed_back,
+        block_out,
+        head_weights.transpose(0, 2, 3, 1).reshape(9, -1, head_weights.shape[1]),
+        distil_weights,
         mask_all,
-        cots,
-        packed,
+        depth_cotangent.reshape(canvases, pixels, LANES),
+        segment_cotangent.reshape(canvases, pixels, LANES),
         gate_bias,
-        head_norm,
-        head_inv,
         mine,
     )
-    block_grad, heads_grad = run_back(head_grads, block_all, heads_back, mask_all)
-    own_mask = lax.dynamic_index_in_dim(mask_all, lax.axis_index("batch"), 0, keepdims=False)
-    features_grad, reduce_grad, spatial_grad, expand_grad, wide_sums, small_sums = run_rear(
+    (
+        features_grad,
+        reduce_grad,
+        spatial_grad,
+        expand_grad,
+        block_scale_grad,
+        block_shift_grad,
+        head_scale_grad,
+        head_shift_grad,
+        gate_grad,
+        output_scale_grad,
+        output_shift_grad,
+    ) = run_rear(
         count,
         block_grad,
         x,
@@ -2050,29 +1935,29 @@
         reduce_all,
         spatial_all,
         expand_all,
-        own_mask,
-        block_params,
-        output_params,
+        mask,
+        *block_params,
+        *output_params,
         head_sums,
         gate_sums,
     )
-    streams = streams.reshape((2,) + image_ids.shape + (LANES,))
+    heads_grad = heads_grad.reshape(9, 4, -1, head_weights.shape[1]).transpose(0, 3, 1, 2)
     return (
-        streams[0],
-        streams[1],
+        depth_out.reshape(depth_cotangent.shape),
+        segment_out.reshape(depth_cotangent.shape),
         features_grad.reshape(features.shape),
-        reduce_grad,
+        reduce_grad.T,
         spatial_grad,
         expand_grad,
-        heads_grad.reshape(head_weights.shape),
+        heads_grad,
         distil_grad,
-        small_sums[0:2],
-        small_sums[2:4],
-        wide_sums[8:12, :LANES],
-        wide_sums[12:16, :LANES],
-        wide_sums[4:6, :LANES],
-        wide_sums[1] + wide_sums[3],
-        wide_sums[0] + wide_sums[2],
+        block_scale_grad,
+        block_shift_grad,
+        head_scale_grad,
+        head_shift_grad,
+        gate_grad,
+        output_scale_grad[0],
+        output_shift_grad[0],
     )
 
 

time: 479 us -> 397 us (0.83)
  Pallas kernels: 425 us -> 377 us
  local copies, waits for them, and re-layouts: 46.8 us -> 17.5 us
    pallas_call x3 -> x1, Pallas kernels: 287 us -> 244 us  [run_middle(): pl.pallas_call(functools.partial(middle_kernel, count), name='middle', ou...]
    another operation x4 -> x0, local copies, waits for them, and re-layouts: 15.7 us -> none  [the longest x2 15.6 us: stationary_local(): heads_flat.reshape(-1, heads_flat.shape[2])]
    unnamed x31 -> x41, local copies, waits for them, and re-layouts: 8.74 us -> 16.6 us
    pallas_call x1 -> x0, local copies, waits for them, and re-layouts: 6.05 us -> none  [run_back(): pl.pallas_call(back_kernel, name='back', out_shape=(jax.ShapeDtypeStruct(...]
    transpose x2 -> x0, local copies, waits for them, and re-layouts: 5.92 us -> none  [stationary_local(): mixed_back = mixed[::-1].transpose(0, 2, 1).reshape(-1, mixed.shape[1])]
    pallas_call x1, Pallas kernels: 74.4 us -> 69.4 us  [run_rear(): pl.pallas_call(functools.partial(rear_kernel, count), name='rear', out_sh...]
where the time goes in v4:
time: 397 us; the launch traced here: 396 us
  Pallas kernels  377 us (95%)
  local copies, waits for them, and re-layouts  17.5 us (4%)
    pallas_call x1, Pallas kernels, run_middle(): pl.pallas_call(functools.partial(middle_kernel, count), name='middle', ou...  244 us
    pallas_call x1, Pallas kernels, run_rear(): pl.pallas_call(functools.partial(rear_kernel, count), name='rear', out_sh...  69.4 us
    pallas_call x1, Pallas kernels, run_front(): pl.pallas_call(functools.partial(front_kernel, count), name='front', out_...  64.2 us
    unnamed x41, local copies, waits for them, and re-layouts  16.6 us

profile of v4, /device:TPU:0, one launch (start us, length us, event | category | flops | bytes accessed | tf_op | source)
XLA Modules:
  0.0 396.2 jit_solution(12095182765777368786)
XLA Ops:
  0.6 0.7 convert_element_type.11
  1.3 0.1 convert_element_type.12
  1.4 0.8 broadcast_in_dim.11.ids_ref
  2.3 64.2 %front.1 = (bf16[2,256,512]{2,1,0:T(8,128)(2,1)}, f32[512,512]{1,0:T(8,128)}, f32[8,512]{1,0:T(8,128)}, f32[2,512,128]{2,1,0:T(8,128)}, f32[8,128]{1,0:T(8,128)}...) custom-call(bf16[2,256,512]{2,1,0:T(8,128)(2,1)} %bitcast.20, ...), custom_call_target="tpu_custom_call" | custom-call | tf_op jit(solution)/shard_map/front/pallas_call | solution.py:856
  66.5 243.6 %middle.1 = (bf16[2,256,128]{2,1,0:T(8,128)(2,1)}, bf16[2,256,128]{2,1,0:T(8,128)(2,1)}, f32[2,9,4,64,128]{4,3,2,1,0:T(8,128)}, f32[2,128]{1,0:T(2,128)}, f32[2,...) custom-call(bf16[2,256,512]{2,1,0:T(8,128)(2,1)} %get-tuple-element.46.block_ref, ...), custom_call_target="tpu_custom_call" | custom-call | tf_op jit(solution)/shard_map/middle/pallas_call | solution.py:1801
  310.1 0.0 copy-start.3
  310.1 0.0 copy-start.2
  310.1 69.4 %rear.1 = (f32[2,256,512]{2,1,0:T(8,128)}, f32[64,512]{1,0:T(8,128)}, f32[9,64,128]{2,1,0:T(8,128)}, f32[64,512]{1,0:T(8,128)}, f32[2,128]{1,0:T(2,128)}, /*inde...) custom-call(f32[512,512]{1,0:T(8,128)} %get-tuple-element.51.grad_re, ...), custom_call_target="tpu_custom_call" | custom-call | tf_op jit(solution)/shard_map/rear/pallas_call | solution.py:1152
  379.5 0.0 copy-start.5
  379.5 0.0 copy-start.1
  379.5 0.0 copy-start.4
  379.5 0.0 copy-done.3
  379.5 0.7 copy.46
  380.2 0.0 copy-done.2
  380.2 0.7 copy.47
  380.8 2.3 copy.48
  383.1 0.0 copy-done.5
  383.1 0.7 copy.49
  383.8 0.0 copy-done.1
  383.8 0.7 copy.50
  384.5 0.0 copy-done.4
  384.5 0.7 copy.51
  385.2 0.0 copy-start
  385.2 5.5 %copy.52 = f32[9,512,4,64]{1,3,2,0:T(8,128)} copy(f32[9,512,4,64]{1,3,2,0:T(8,128)} %bitcast.18) | data formatting | bytes 9437184
  390.7 0.0 copy-done
  390.7 0.0 copy-start.12
  390.7 0.0 copy-start.11
  390.7 0.0 copy-start.9
  390.7 0.0 copy-start.8
  390.7 0.0 copy-start.10
  390.7 0.0 copy-start.7
  390.7 0.0 copy-start.6
  390.7 1.4 copy.53
  392.1 0.0 copy-done.12
  392.1 0.6 copy.54
  392.7 0.0 copy-done.11
  392.7 0.6 copy.55
  393.3 0.0 copy-done.9
  393.3 0.6 copy.56
  393.9 0.0 copy-done.8
  393.9 0.6 copy.57
  394.4 0.0 copy-done.10
  394.4 0.6 copy.58
  395.0 0.0 copy-done.7
  395.0 0.6 copy.59
  395.6 0.0 copy-done.6
  395.6 0.6 copy.60
Async XLA Ops:
  310.1 69.5 %copy-start.3 = (bf16[2,256,128]{2,1,0:T(8,128)(2,1)S(1)}, bf16[2,256,128]{2,1,0:T(8,128)(2,1)}, u32[]{:S(2)}) copy-start(bf16[2,256,128]{2,1,0:T(8,128)(2,1)} %get-tuple-element.49) | copy-start | bytes 393220
  310.1 70.1 %copy-start.2 = (bf16[2,256,128]{2,1,0:T(8,128)(2,1)S(1)}, bf16[2,256,128]{2,1,0:T(8,128)(2,1)}, u32[]{:S(2)}) copy-start(bf16[2,256,128]{2,1,0:T(8,128)(2,1)} %get-tuple-element.50) | copy-start | bytes 393220
  379.5 3.6 copy-start.5
  379.5 4.3 %copy-start.1 = (f32[9,64,128]{2,1,0:T(8,128)S(1)}, f32[9,64,128]{2,1,0:T(8,128)}, u32[]{:S(2)}) copy-start(f32[9,64,128]{2,1,0:T(8,128)} %get-tuple-element.96) | copy-start | bytes 884740
  379.5 5.0 %copy-start.4 = (f32[64,512]{1,0:T(8,128)S(1)}, f32[64,512]{1,0:T(8,128)}, u32[]{:S(2)}) copy-start(f32[64,512]{1,0:T(8,128)} %get-tuple-element.97) | copy-start | bytes 393220
  385.2 5.5 %copy-start = (f32[2,9,4,64,128]{4,3,2,1,0:T(8,128)S(1)}, f32[2,9,4,64,128]{4,3,2,1,0:T(8,128)}, u32[]{:S(2)}) copy-start(f32[2,9,4,64,128]{4,3,2,1,0:T(8,128)} %get-tuple-element.99) | copy-start | bytes 7077892
  390.7 1.5 copy-start.12
  390.7 2.0 copy-start.11
  390.7 2.6 copy-start.9
  390.7 3.2 copy-start.8
  390.7 3.7 copy-start.10
  390.7 4.3 %copy-start.7 = (f32[1,512]{1,0:T(1,128)S(1)}, f32[1,512]{1,0:T(1,128)}, u32[]{:S(2)}) copy-start(f32[1,512]{1,0:T(1,128)} %get-tuple-element.75) | copy-start | bytes 6148
  390.7 4.9 %copy-start.6 = (f32[1,512]{1,0:T(1,128)S(1)}, f32[1,512]{1,0:T(1,128)}, u32[]{:S(2)}) copy-start(f32[1,512]{1,0:T(1,128)} %get-tuple-element.76) | copy-start | bytes 6148

commit v5 on v4

--- a/solution.py
+++ b/solution.py
@@ -513,7 +513,7 @@
         def _():
             self.near(rank, part)
 
-        @pl.when((late == 0) & (item == 3))
+        @pl.when((late == 0) & (item == 1))
         def _():
             self.start(1)
 
@@ -679,6 +679,28 @@
     return lax.dot_general(
         first, second, (((1,), (1,)), ((), ())), preferred_element_type=jnp.float32
     )
+
+
+def make_masks(ids_ref, mask_all):
+    rows = 8 * ids_ref.shape[0]
+    ids = ids_ref[...].reshape(rows, PIXELS).T
+    pixel = lax.broadcasted_iota(jnp.int32, (PIXELS, rows), 0)
+    taps = []
+    for vertical, lateral in OFFSETS:
+        offset = 32 * vertical + lateral
+        beside = ids if offset == 0 else pltpu.roll(ids, (-offset) % PIXELS, 0)
+        row, col = (pixel >> 5) + vertical, (pixel & 31) + lateral
+        inside = (row >= 0) & (row < 8) & (col >= 0) & (col < 32)
+        taps.append(jnp.where(inside & (beside == ids), 1.0, 0.0).astype(jnp.bfloat16))
+    taps = jnp.concatenate(taps + [jnp.zeros_like(taps[0])], axis=1)
+    item = lax.broadcasted_iota(jnp.int32, (10 * rows, LANES), 0)
+    lane = lax.broadcasted_iota(jnp.int32, (10 * rows, LANES), 1)
+    for block in range(8):
+        for micro in range(2):
+            chosen = jnp.where(item == lane * rows + (8 * block + micro), 1.0, 0.0)
+            mask_all[block, micro] = jnp.dot(
+                taps, chosen.astype(jnp.bfloat16), preferred_element_type=jnp.float32
+            ).astype(jnp.bfloat16)
 
 
 def front_kernel(
@@ -715,61 +737,50 @@
     sums2,
     sums3,
     head_all,
+    ids_all,
     *sems,
 ):
     place, lane, depth, side, upper, core = whereabouts()
     reduces = Gather(reduce_all, *sems[0:3], 1)
     spatials = Gather(spatial_all, *sems[3:6], 1)
     expands = Gather(expand_all, *sems[6:9], 1)
-    masks = Gather(mask_all, *sems[9:12], 1)
-    pieces = Pieces(stage, got, sems[12], sems[13])
-    first_sums = Exchange(sums1, sems[14], sems[15], "batch")
-    second_sums = Exchange(sums2, sems[16], sems[17], "batch")
-    third_sums = Exchange(sums3, sems[18], sems[19], "batch")
-    heads = Exchange(head_all, sems[20], sems[21], "chan")
-    first_acts = Exchange(act1_ref, sems[22], sems[23], "chan")
-    second_acts = Exchange(act2_ref, sems[24], sems[25], "chan")
+    ids = Exchange(ids_all, sems[9], sems[10], "batch")
+    pieces = Pieces(stage, got, sems[11], sems[12])
+    first_sums = Exchange(sums1, sems[13], sems[14], "batch")
+    second_sums = Exchange(sums2, sems[15], sems[16], "batch")
+    third_sums = Exchange(sums3, sems[17], sems[18], "batch")
+    heads = Exchange(head_all, sems[19], sems[20], "chan")
+    first_acts = Exchange(act1_ref, sems[21], sems[22], "chan")
+    second_acts = Exchange(act2_ref, sems[23], sems[24], "chan")
 
     greet(batch_peers() + chan_peers())
     reduce_all[place] = reduce_ref[...]
+    ids_all[place] = ids_ref[...]
     reduces.start()
+    ids.start()
     spatial_all[place] = spatial_ref[...]
-    spatials.start()
     expand_all[place] = expand_ref[...]
-    expands.start()
     head_all[lane, 0:4] = head_scale[...]
     head_all[lane, 4:8] = head_shift[...]
     heads.start()
     clear_edges(turned)
-    pixel = lax.broadcasted_iota(jnp.int32, (PIXELS, LANES), 0)
-    column = lax.broadcasted_iota(jnp.int32, (PIXELS, LANES), 1)
-    for micro in range(2):
-        ids = ids_ref[micro]
-        mask = jnp.zeros((PIXELS, LANES), jnp.float32)
-        for number, (vertical, lateral) in enumerate(OFFSETS):
-            offset = 32 * vertical + lateral
-            beside = ids if offset == 0 else pltpu.roll(ids, (-offset) % PIXELS, 0)
-            row, col = (pixel >> 5) + vertical, (pixel & 31) + lateral
-            inside = (row >= 0) & (row < 8) & (col >= 0) & (col < 32)
-            same = (beside == ids) & inside & (column == number)
-            mask = jnp.where(same, 1.0, mask)
-        mask_ref[micro] = mask.astype(jnp.bfloat16)
-        mask_all[place, micro] = mask_ref[micro]
-    masks.start()
-
     for rank in range(1, 4):
         reduces.near(rank)
+    spatials.start()
     for rank in range(4):
         reduces.far(rank)
     x = x_ref[...].reshape(2 * PIXELS, x_ref.shape[2])
     pieces.start(dot_last(x, reduce_all[...].reshape(512, 512)))
-    for rank in range(1, 4):
-        spatials.near(rank)
+    ids.wait()
+    make_masks(ids_all, mask_all)
+    mask_ref[...] = mask_all[place]
+    spatials.near(1)
     first = pieces.finish()
     sums1[place] = tile_rows(moments(first, first), 8)
     first_sums.start()
-    for rank in range(1, 4):
-        expands.near(rank)
+    spatials.near(2)
+    expands.start()
+    spatials.near(3)
     first_sums.wait()
     totals = first_sums.total()
     rows = []
@@ -780,10 +791,10 @@
         out = normed * block_scale[0:1] + block_shift[0:1]
         act1_ref[lane, micro_rows(micro)] = (out * jax.nn.sigmoid(out)).astype(jnp.bfloat16)
     first_acts.start()
-    for rank in range(1, 4):
-        masks.near(rank)
+    expands.near(1)
     for rank in range(4):
         spatials.far(rank)
+    expands.near(2)
     first_acts.wait()
     for micro in range(2):
         value = jnp.concatenate([act1_ref[slot, micro_rows(micro)] for slot in range(4)], axis=1)
@@ -797,8 +808,7 @@
         )
     sums2[place] = tile_rows(moments(second, second), 8)
     second_sums.start()
-    for rank in range(4):
-        expands.far(rank)
+    expands.near(3)
     second_sums.wait()
     totals = second_sums.total()
     for micro in range(2):
@@ -822,6 +832,8 @@
             jnp.where(low, upper_row, pltpu.roll(lower_row, half_width, 1)),
             jnp.where(low, pltpu.roll(upper_row, half_width, 1), lower_row),
         )
+    for rank in range(4):
+        expands.far(rank)
     second_acts.wait()
     value = jnp.concatenate([act2_ref[slot] for slot in range(4)], axis=1)
     third = jnp.dot(
@@ -829,8 +841,6 @@
     )
     sums3[place] = tile_rows(moments(third, third), 8)
     third_sums.start()
-    for rank in range(4):
-        masks.far(rank)
     third_sums.wait()
     totals = third_sums.total()
     rows = []
@@ -841,7 +851,7 @@
         out = normed * output_scale[...] + output_shift[...] + x_ref[micro].astype(jnp.float32)
         y_ref[micro] = (out * jax.nn.sigmoid(out)).astype(jnp.bfloat16)
     inverse3_ref[...] = tile_rows(rows, 8)
-    for item in (reduces, spatials, expands, masks, heads, first_acts, second_acts):
+    for item in (reduces, spatials, expands, ids, heads, first_acts, second_acts):
         item.close()
     for item in (first_sums, second_sums, third_sums):
         item.close()
@@ -882,8 +892,10 @@
             pltpu.VMEM((8, 8, LANES), f32),
             pltpu.VMEM((8, 8, 512), f32),
             pltpu.VMEM((4, 8, LANES), f32),
+            pltpu.VMEM((8, 8, PIXELS), f32),
         ]
-        + gather_sems(1) * 4
+        + gather_sems(1) * 3
+        + exchange_sems(8)
         + [pltpu.SemaphoreType.DMA((4,))] * 2
         + exchange_sems(8) * 3
         + exchange_sems(4) * 3,
@@ -984,6 +996,9 @@
     output_shift,
     head_ref,
     gate_ref,
+    block_hbm,
+    back_hbm,
+    masks_hbm,
     features_ref,
     reduce_out,
     spatial_out,
@@ -995,6 +1010,12 @@
     gate_out,
     output_scale_out,
     output_shift_out,
+    head_grad,
+    block_all,
+    head_back,
+    mask_all,
+    turned_wide,
+    columns_wide,
     turned,
     columns,
     stage,
@@ -1022,7 +1043,48 @@
     reduces = Scatter(*reduce_bufs, sems[20:24])
     pieces_next = Pieces(stage_next, got_next, sems[24], sems[25])
 
+    loads = [
+        pltpu.make_async_copy(source, target, sems[26].at[number])
+        for number, (source, target) in enumerate(
+            ((block_hbm, block_all), (back_hbm, head_back), (masks_hbm, mask_all))
+        )
+    ]
+    for load in loads:
+        load.start()
+
+    def weigh(block):
+        for micro in range(2):
+            fill_columns(
+                block_all[block, micro],
+                mask_all[block, micro],
+                turned_wide,
+                columns_wide,
+                micro * PIXELS,
+            )
+        value = jnp.concatenate(
+            [
+                jnp.concatenate([head_back[half, micro, block] for half in range(2)], axis=1)
+                for micro in range(2)
+            ],
+            axis=0,
+        ).T
+
+        def tap(number, _):
+            product = jnp.dot(
+                value,
+                columns_wide[:, pl.ds(pl.multiple_of(number * 512, 512), 512)],
+                preferred_element_type=jnp.float32,
+            )
+            if block == 0:
+                head_grad[number] = product
+            else:
+                head_grad[number] += product
+            return 0
+
+        lax.fori_loop(0, 9, tap, 0)
+
     greet(batch_peers() + chan_peers())
+    clear_edges(turned_wide)
     half_width = LANES // 2
     even = place % 2 == 0
     mine = lax.broadcasted_iota(jnp.int32, (1, LANES), 1) >> 6 == place % 2
@@ -1052,6 +1114,9 @@
     sums_a[place, 4:6, 0:LANES] = gate_ref[...]
     sums_a[place, 8:16, 0:LANES] = jnp.where(place // 2 == lane, heads.total(), 0.0)
     first.start()
+    for load in loads:
+        load.wait()
+    weigh(0)
     first.wait()
     totals = first.total()
     head_scale_out[...] = totals[8:12, 0:LANES]
@@ -1075,11 +1140,13 @@
         value.T, back3[...], preferred_element_type=jnp.float32
     ).reshape(8, 64, 512)
     expands.start()
+    weigh(1)
     grad = pieces.finish()
     normed = norm12_ref[1]
     grad = grad * silu_slope(normed * block_scale[1:2] + block_shift[1:2])
     sums_b[place] = tile_rows(moments(grad, normed), 8)
     second.start()
+    weigh(2)
     expands.middle()
     second.wait()
     totals = second.total()
@@ -1108,11 +1175,13 @@
         value.T, columns[...], preferred_element_type=jnp.float32
     ).reshape(8, 64, 9 * LANES)
     spatials.start()
+    weigh(3)
     grad = pieces_next.finish()
     normed = norm12_ref[0]
     grad = grad * silu_slope(normed * block_scale[0:1] + block_shift[0:1])
     sums_c[place] = tile_rows(moments(grad, normed), 8)
     third.start()
+    weigh(4)
     spatials.middle()
     expand_out[...] = expands.finish()
     third.wait()
@@ -1130,6 +1199,7 @@
             count,
         )
     acts.start()
+    weigh(5)
     acts.wait()
     value = jnp.concatenate([act_all[slot] for slot in range(4)], axis=1)
     x = x_ref[...].reshape(2 * PIXELS, 512)
@@ -1138,7 +1208,9 @@
     more = jnp.dot(value, reduce_all[...].reshape(512, 512), preferred_element_type=jnp.float32)
     for micro in range(2):
         features_ref[micro] = features_ref[micro] + more[micro_rows(micro)]
+    weigh(6)
     reduces.middle()
+    weigh(7)
     result = spatials.finish()
     for number in range(9):
         spatial_out[number] = result[:, number * LANES : (number + 1) * LANES]
@@ -1164,10 +1236,16 @@
             jax.ShapeDtypeStruct((2, LANES), f32),
             jax.ShapeDtypeStruct((1, 512), f32),
             jax.ShapeDtypeStruct((1, 512), f32),
+            jax.ShapeDtypeStruct((9, 256, 512), f32),
         ),
-        in_specs=vmem(18),
-        out_specs=tuple(vmem(11)),
+        in_specs=vmem(18) + [pl.BlockSpec(memory_space=pl.ANY)] * 3,
+        out_specs=tuple(vmem(12)),
         scratch_shapes=[
+            pltpu.VMEM((8, 2, PIXELS, 512), bf16),
+            pltpu.VMEM((2, 2, 8, PIXELS, LANES), bf16),
+            pltpu.VMEM((8, 2, PIXELS, LANES), bf16),
+            pltpu.VMEM((3, 2 * PAD + PIXELS, 512), bf16),
+            pltpu.VMEM((2 * PIXELS, 9 * 512), bf16),
             pltpu.VMEM((3, 2 * PAD + PIXELS, LANES), bf16),
             pltpu.VMEM((2 * PIXELS, 9 * LANES), bf16),
             pltpu.VMEM((4, 2 * PIXELS, LANES), bf16),
@@ -1188,7 +1266,8 @@
         + exchange_sems(8) * 3
         + exchange_sems(4) * 2
         + scatter_sems() * 3
-        + [pltpu.SemaphoreType.DMA((4,))] * 2,
+        + [pltpu.SemaphoreType.DMA((4,))] * 2
+        + [pltpu.SemaphoreType.DMA((3,))],
         compiler_params=kernel_params(5),
     )(*arrays)
 
@@ -1390,8 +1469,8 @@
     gate_sums,
     head_sums,
     back_out,
-    head_grad,
     block_all,
+    head_back,
     head_weight,
     mixed,
     mixed_back,
@@ -1399,7 +1478,7 @@
     columns,
     acts,
     norm_ref,
-    head_back,
+    slope_ref,
     grads_all,
     packed,
     own_stage,
@@ -1450,7 +1529,7 @@
     def forward_step(step, _):
         block, micro = gather.next(step)
         fill_columns(block_all[block, micro], mask_ref[block, micro], turned, columns)
-        part = jnp.dot(columns[...], head_weight[...], preferred_element_type=jnp.float32)
+        part = jnp.dot(columns[0:PIXELS], head_weight[...], preferred_element_type=jnp.float32)
         ahead.send(part.astype(jnp.bfloat16), block, micro)
 
         @pl.when(step == 0)
@@ -1610,7 +1689,7 @@
         block, micro = reduce.block(step)
         fill_columns(act_value(block, micro), mask_ref[block, micro], turned, columns)
         part_ref[...] = jnp.dot(
-            columns[:, 0 : 9 * 256], mixed[...], preferred_element_type=jnp.float32
+            columns[0:PIXELS, 0 : 9 * 256], mixed[...], preferred_element_type=jnp.float32
         )
         reduce.step(step)
 
@@ -1651,7 +1730,7 @@
         fill_columns(
             grads_all[block, micro], mask_ref[block, micro], turned, columns, flip=True
         )
-        part = jnp.dot(columns[...], mixed_back[...], preferred_element_type=jnp.float32)
+        part = jnp.dot(columns[0:PIXELS], mixed_back[...], preferred_element_type=jnp.float32)
         extra = cot_all[block, micro].astype(jnp.float32)
         part = jnp.concatenate(
             [
@@ -1661,7 +1740,66 @@
             axis=1,
         )
         behind.send(part.astype(jnp.bfloat16), block, micro)
-        value = act_value(block, micro).T
+        @pl.when(step == 10)
+        def _():
+            normalize_back(0)
+
+        @pl.when(step == 14)
+        def _():
+            behind.relay(0)
+
+        return 0
+
+    def normalize_back(micro):
+        @pl.when(core == micro)
+        def _():
+            stats[4:6] = jnp.zeros((2, LANES), jnp.float32)
+
+        def take(block):
+            normed = norm_ref[block]
+            value = behind.value(block) * silu_slope(normed * mine_ref[0:1] + mine_ref[1:2])
+            slope_ref[block] = value
+            stats[4:5] += jnp.sum(value, axis=0, keepdims=True)
+            stats[5:6] += jnp.sum(value * normed, axis=0, keepdims=True)
+
+        behind.collect(micro, take)
+
+        @pl.when(core == micro)
+        def _():
+            shift_sum, scale_sum = stats[4:5], stats[5:6]
+            head_sums[0:1] = scale_sum
+            head_sums[1:2] = shift_sum
+            factor = mine_ref[0:1] * stats[2:3]
+
+            def activate(chunk, _):
+                for item in range(2):
+                    block = 2 * chunk + item
+                    value = slope_ref[block]
+                    head_back[upper, core, block] = (
+                        factor * (value - (shift_sum + norm_ref[block] * scale_sum) / count)
+                    ).astype(jnp.bfloat16)
+                behind.spread(chunk)
+                return 0
+
+            lax.fori_loop(0, 4, activate, 0)
+
+    lax.fori_loop(0, 16, back_step, 0)
+    behind.finish(0)
+
+    def head_value(block, micro):
+        return jnp.concatenate([head_back[half, micro, block] for half in range(2)], axis=1)
+
+    def weigh(block):
+        for micro in range(2):
+            fill_columns(
+                grads_all[block, micro],
+                mask_ref[block, micro],
+                turned,
+                columns,
+                micro * PIXELS,
+                True,
+            )
+        value = jnp.concatenate([act_value(block, micro) for micro in range(2)], axis=0).T
         width = half_width
         for number in range(9):
             product = jnp.dot(
@@ -1677,85 +1815,27 @@
                         head * width : (head + 1) * width, column : column + LANES
                     ]
 
-        @pl.when(step == 10)
-        def _():
-            normalize_back(0)
-
-        @pl.when(step == 14)
-        def _():
-            behind.relay(0)
-
-        return 0
-
-    def normalize_back(micro):
-        @pl.when(core == micro)
-        def _():
-            stats[4:6] = jnp.zeros((2, LANES), jnp.float32)
-
-        def spot(block):
-            return pl.ds(block % 2 * PIXELS, PIXELS), pl.ds(block // 2 * LANES, LANES)
-
-        def take(block):
-            normed = norm_ref[block]
-            value = behind.value(block) * silu_slope(normed * mine_ref[0:1] + mine_ref[1:2])
-            wide_ref = head_grad
-            wide_ref[block, :, 0:LANES] = value
-            stats[4:5] += jnp.sum(value, axis=0, keepdims=True)
-            stats[5:6] += jnp.sum(value * normed, axis=0, keepdims=True)
-
-        behind.collect(micro, take)
-
-        @pl.when(core == micro)
-        def _():
-            shift_sum, scale_sum = stats[4:5], stats[5:6]
-            head_sums[0:1] = scale_sum
-            head_sums[1:2] = shift_sum
-            factor = mine_ref[0:1] * stats[2:3]
-
-            def activate(chunk, _):
-                for item in range(2):
-                    block = 2 * chunk + item
-                    value = head_grad[block, :, 0:LANES]
-                    head_back[upper, core, block] = (
-                        factor * (value - (shift_sum + norm_ref[block] * scale_sum) / count)
-                    ).astype(jnp.bfloat16)
-                behind.spread(chunk)
-                return 0
-
-            lax.fori_loop(0, 4, activate, 0)
-
-    lax.fori_loop(0, 16, back_step, 0)
-    behind.finish(0)
-
-    def head_value(block, micro):
-        return jnp.concatenate([head_back[half, micro, block] for half in range(2)], axis=1)
-
-    def weigh(block, micro):
-        fill_columns(block_all[block, micro], mask_ref[block, micro], turned, columns)
-        value = head_value(block, micro).T
-        for number in range(9):
-            head_grad[number] += jnp.dot(
-                value,
-                columns[:, number * 512 : (number + 1) * 512],
-                preferred_element_type=jnp.float32,
-            )
-
     def block_step(step, _):
         block, micro = reduce.block(step)
         fill_columns(
             head_value(block, micro), mask_ref[block, micro], turned, columns, flip=True
         )
         part_ref[...] = jnp.dot(
-            columns[:, 0 : 9 * 256],
+            columns[0:PIXELS, 0 : 9 * 256],
             head_ref[...].reshape(9 * 256, 512),
             preferred_element_type=jnp.float32,
         )
+        item, late = staggered(step)
+
+        @pl.when(late == 1)
+        def _():
+            weigh(item)
+
         reduce.step(step)
 
         @pl.when(step == 1)
         def _():
             normalize_back(1)
-            head_grad[...] = jnp.zeros_like(head_grad)
 
         @pl.when(step == 4)
         def _():
@@ -1765,16 +1845,9 @@
         def _():
             behind.finish(1)
 
-        @pl.when(step > 1)
-        def _():
-            weigh(block, micro)
-
         return 0
 
     lax.fori_loop(0, 16, block_step, 0)
-    for step in range(2):
-        block, micro = reduce.block(step)
-        weigh(block, micro)
     for micro in range(2):
         reduce.close(micro)
         back_out[micro_rows(micro)] = keep[micro]
@@ -1808,20 +1881,20 @@
             jax.ShapeDtypeStruct((2, LANES), f32),
             jax.ShapeDtypeStruct((2, LANES), f32),
             jax.ShapeDtypeStruct((2 * PIXELS, 512), f32),
-            jax.ShapeDtypeStruct((9, 256, 512), f32),
+            jax.ShapeDtypeStruct((8, 2) + block, bf16),
+            jax.ShapeDtypeStruct((2, 2, 8, PIXELS, LANES), bf16),
         ),
         in_specs=vmem(8),
-        out_specs=tuple(vmem(7)),
+        out_specs=tuple(vmem(8)),
         scratch_shapes=[
-            pltpu.VMEM((8, 2) + block, bf16),
             pltpu.VMEM((9 * 512, 256), bf16),
             pltpu.VMEM((9 * 256, 512), bf16),
             pltpu.VMEM((9 * 512, 256), bf16),
             pltpu.VMEM((3, 2 * PAD + PIXELS, 512), bf16),
-            pltpu.VMEM((PIXELS, 9 * 512), bf16),
+            pltpu.VMEM((2 * PIXELS, 9 * 512), bf16),
             pltpu.VMEM((2, 2, 8, PIXELS, LANES), bf16),
             pltpu.VMEM((8, PIXELS, LANES), f32),
-            pltpu.VMEM((2, 2, 8, PIXELS, LANES), bf16),
+            pltpu.VMEM((8, PIXELS, LANES), f32),
             pltpu.VMEM((8, 2) + block, bf16),
             pltpu.VMEM((2, 2, PIXELS, LANES), bf16),
             pltpu.VMEM((8, 2, PIXELS, LANES), bf16),
@@ -1846,6 +1919,45 @@
     )(*arrays)
 
 
+def finish_kernel(count, *refs):
+    sources, targets, held = refs[:count], refs[count : 2 * count], refs[2 * count : 3 * count]
+    sem_in, sem_out = refs[3 * count :]
+
+    def parts(ref):
+        large = len(ref.shape) > 2
+        return [ref.at[number] for number in range(ref.shape[0])] if large else [ref]
+
+    number = 0
+    loads, stores = [], []
+    for source, target, hold in zip(sources, targets, held):
+        for pieces in zip(parts(source), parts(hold), parts(target)):
+            loads.append(pltpu.make_async_copy(pieces[0], pieces[1], sem_in.at[number]))
+            stores.append(pltpu.make_async_copy(pieces[1], pieces[2], sem_out.at[number]))
+            number += 1
+    for load in loads:
+        load.start()
+    for load, store in zip(loads, stores):
+        load.wait()
+        store.start()
+    for store in stores:
+        store.wait()
+
+
+def run_finish(*arrays):
+    anywhere = [pl.BlockSpec(memory_space=pltpu.HBM)] * len(arrays)
+    copies = sum(item.shape[0] if item.ndim > 2 else 1 for item in arrays)
+    return pl.pallas_call(
+        functools.partial(finish_kernel, len(arrays)),
+        name="finish",
+        out_shape=tuple(jax.ShapeDtypeStruct(item.shape, item.dtype) for item in arrays),
+        in_specs=anywhere,
+        out_specs=tuple(anywhere),
+        scratch_shapes=[pltpu.VMEM(item.shape, item.dtype) for item in arrays]
+        + [pltpu.SemaphoreType.DMA((copies,))] * 2,
+        compiler_params=pltpu.CompilerParams(vmem_limit_bytes=60 * 2**20),
+    )(*arrays)
+
+
 def stationary_local(
     features,
     image_ids,
@@ -1868,9 +1980,7 @@
     pixels = row_count * column_count
     count = float(lax.axis_size("batch") * pixels)
     x = features.reshape(canvases, pixels, -1)
-    ids = jnp.broadcast_to(
-        image_ids.reshape(canvases, pixels, 1).astype(jnp.float32), (canvases, pixels, LANES)
-    )
+    ids = jnp.pad(image_ids.reshape(canvases, pixels).astype(jnp.float32), ((0, 6), (0, 0)))
     block_params = (block_scale, block_shift)
     output_params = (output_scale[None], output_shift[None])
     (
@@ -1899,7 +2009,7 @@
         head_scale,
         head_shift,
     )
-    depth_out, segment_out, distil_grad, gate_sums, head_sums, block_grad, heads_grad = run_middle(
+    depth_out, segment_out, distil_grad, gate_sums, head_sums, block_grad, block_all, back_all = run_middle(
         count,
         block_out,
         head_weights.transpose(0, 2, 3, 1).reshape(9, -1, head_weights.shape[1]),
@@ -1922,6 +2032,7 @@
         gate_grad,
         output_scale_grad,
         output_shift_grad,
+        heads_grad,
     ) = run_rear(
         count,
         block_grad,
@@ -1940,13 +2051,15 @@
         *output_params,
         head_sums,
         gate_sums,
-    )
-    heads_grad = heads_grad.reshape(9, 4, -1, head_weights.shape[1]).transpose(0, 3, 1, 2)
-    return (
-        depth_out.reshape(depth_cotangent.shape),
-        segment_out.reshape(depth_cotangent.shape),
-        features_grad.reshape(features.shape),
-        reduce_grad.T,
+        block_all,
+        back_all,
+        mask_all,
+    )
+    outs = run_finish(
+        depth_out,
+        segment_out,
+        features_grad,
+        reduce_grad,
         spatial_grad,
         expand_grad,
         heads_grad,
@@ -1956,8 +2069,20 @@
         head_scale_grad,
         head_shift_grad,
         gate_grad,
-        output_scale_grad[0],
-        output_shift_grad[0],
+        output_scale_grad,
+        output_shift_grad,
+    )
+    heads_grad = outs[6].reshape(9, 4, -1, head_weights.shape[1]).transpose(0, 3, 1, 2)
+    return (
+        outs[0].reshape(depth_cotangent.shape),
+        outs[1].reshape(depth_cotangent.shape),
+        outs[2].reshape(features.shape),
+        outs[3].T,
+        *outs[4:6],
+        heads_grad,
+        *outs[7:13],
+        outs[13][0],
+        outs[14][0],
     )
 
 

time: 397 us -> 378 us (0.952)
  local copies, waits for them, and re-layouts: 17.5 us -> 0.69 us
    unnamed x41 -> x0, local copies, waits for them, and re-layouts: 16.6 us -> none
    pallas_call x1, Pallas kernels: 244 us -> 231 us  [run_middle(): pl.pallas_call(functools.partial(middle_kernel, count), name='middle', ou...]
    pallas_call x0 -> x1, Pallas kernels: none -> 7.63 us  [run_finish(): pl.pallas_call(functools.partial(finish_kernel, len(arrays)), name='finis...]
    pallas_call x1, Pallas kernels: 69.4 us -> 75 us  [run_rear(): pl.pallas_call(functools.partial(rear_kernel, count), name='rear', out_sh...]
where the time goes in v5:
time: 378 us; the launch traced here: 377 us
  Pallas kernels  375 us (99%)
    pallas_call x1, Pallas kernels, run_middle(): pl.pallas_call(functools.partial(middle_kernel, count), name='middle', ou...  231 us
    pallas_call x1, Pallas kernels, run_rear(): pl.pallas_call(functools.partial(rear_kernel, count), name='rear', out_sh...  75 us
    pallas_call x1, Pallas kernels, run_front(): pl.pallas_call(functools.partial(front_kernel, count), name='front', out_...  61.2 us
    pallas_call x1, Pallas kernels, run_finish(): pl.pallas_call(functools.partial(finish_kernel, len(arrays)), name='finis...  7.63 us

profile of v5, /device:TPU:0, one launch (start us, length us, event | category | flops | bytes accessed | tf_op | source)
XLA Modules:
  0.0 377.5 jit_solution(2322102471249153758)
XLA Ops:
  0.6 0.7 convert_element_type.8
  1.3 0.1 convert_element_type.9
  1.4 0.6 pad.4.ids_ref
  2.0 61.2 %front.1 = (bf16[2,256,512]{2,1,0:T(8,128)(2,1)}, f32[512,512]{1,0:T(8,128)}, f32[8,512]{1,0:T(8,128)}, f32[2,512,128]{2,1,0:T(8,128)}, f32[8,128]{1,0:T(8,128)}...) custom-call(bf16[2,256,512]{2,1,0:T(8,128)(2,1)} %bitcast.19, ...), custom_call_target="tpu_custom_call" | custom-call | tf_op jit(solution)/shard_map/front/pallas_call | solution.py:866
  63.2 231.4 %middle.1 = (bf16[2,256,128]{2,1,0:T(8,128)(2,1)}, bf16[2,256,128]{2,1,0:T(8,128)(2,1)}, f32[2,9,4,64,128]{4,3,2,1,0:T(8,128)}, f32[2,128]{1,0:T(2,128)}, f32[2,...) custom-call(bf16[2,256,512]{2,1,0:T(8,128)(2,1)} %get-tuple-element.63, ...), custom_call_target="tpu_custom_call" | custom-call | tf_op jit(solution)/shard_map/middle/pallas_call | solution.py:1874
  294.7 75.0 %rear.1 = (f32[2,256,512]{2,1,0:T(8,128)}, f32[64,512]{1,0:T(8,128)}, f32[9,64,128]{2,1,0:T(8,128)}, f32[64,512]{1,0:T(8,128)}, f32[2,128]{1,0:T(2,128)}, /*inde...) custom-call(f32[512,512]{1,0:T(8,128)} %get-tuple-element.68.grad_re, ...), custom_call_target="tpu_custom_call" | custom-call | tf_op jit(solution)/shard_map/rear/pallas_call | solution.py:1224
  369.7 7.6 %finish.1 = (bf16[2,256,128]{2,1,0:T(8,128)(2,1)}, bf16[2,256,128]{2,1,0:T(8,128)(2,1)}, f32[2,256,512]{2,1,0:T(8,128)}, f32[64,512]{1,0:T(8,128)}, f32[9,64,128...) custom-call(bf16[2,256,128]{2,1,0:T(8,128)(2,1)} %get-tuple-element., ...), custom_call_target="tpu_custom_call" | custom-call | tf_op jit(solution)/shard_map/finish/pallas_call | solution.py:1949

commit v6 on v5

--- a/solution.py
+++ b/solution.py
@@ -513,10 +513,6 @@
         def _():
             self.near(rank, part)
 
-        @pl.when((late == 0) & (item == 1))
-        def _():
-            self.start(1)
-
         @pl.when(late == 1)
         def _():
             self.far(rank, part)
@@ -649,6 +645,26 @@
         for slot in range(1, 4):
             result = result + self.got[slot].astype(jnp.float32)
         return result
+
+
+class Local:
+    def __init__(self, pairs, sems):
+        self.copies = [
+            pltpu.make_async_copy(source, target, sems.at[number])
+            for number, (source, target) in enumerate(pairs)
+        ]
+
+    def start(self, *numbers):
+        for number in numbers:
+            self.copies[number].start()
+
+    def wait(self, *numbers):
+        for number in numbers:
+            self.copies[number].wait()
+
+
+def anywhere(count):
+    return [pl.BlockSpec(memory_space=pl.ANY)] * count
 
 
 def micro_rows(micro):
@@ -716,19 +732,30 @@
     output_shift,
     head_scale,
     head_shift,
+    depth_cot,
+    segment_cot,
     y_ref,
     norm3_ref,
     inverse3_ref,
     norm12_ref,
     inverse12_ref,
+    mine_ref,
+    mask_ref,
+    act1_out,
+    act2_out,
+    reduce_out,
+    spatial_out,
+    expand_out,
+    mask_out,
+    cot_out,
     act1_ref,
     act2_ref,
     reduce_all,
     spatial_all,
     expand_all,
     mask_all,
-    mine_ref,
-    mask_ref,
+    cot_all,
+    packed,
     turned,
     columns,
     stage,
@@ -753,9 +780,29 @@
     first_acts = Exchange(act1_ref, sems[21], sems[22], "chan")
     second_acts = Exchange(act2_ref, sems[23], sems[24], "chan")
 
+    local = Local(
+        (
+            (act1_ref, act1_out),
+            (act2_ref, act2_out),
+            (reduce_all, reduce_out),
+            (spatial_all, spatial_out),
+            (expand_all, expand_out),
+            (mask_all, mask_out),
+            (cot_all, cot_out),
+        ),
+        sems[27],
+    )
+    cot_sem, cot_recv = sems[25:27]
+
+    def cot_copy(parity, slot, target):
+        return push(
+            packed.at[parity], cot_all.at[slot], cot_sem.at[parity], cot_recv.at[slot], target, lane
+        )
+
     greet(batch_peers() + chan_peers())
     reduce_all[place] = reduce_ref[...]
-    ids_all[place] = ids_ref[...]
+    ids_all[place, 0:2] = ids_ref[...].astype(jnp.float32)
+    ids_all[place, 2:8] = jnp.zeros((6, PIXELS), jnp.float32)
     reduces.start()
     ids.start()
     spatial_all[place] = spatial_ref[...]
@@ -774,6 +821,7 @@
     ids.wait()
     make_masks(ids_all, mask_all)
     mask_ref[...] = mask_all[place]
+    local.start(2, 5)
     spatials.near(1)
     first = pieces.finish()
     sums1[place] = tile_rows(moments(first, first), 8)
@@ -781,6 +829,16 @@
     spatials.near(2)
     expands.start()
     spatials.near(3)
+    half_width = LANES // 2
+    left = lax.broadcasted_iota(jnp.int32, (PIXELS, LANES), 1) < half_width
+    for micro in range(2):
+        upper_cot, lower_cot = (ref[micro].astype(jnp.float32) for ref in (depth_cot, segment_cot))
+        packed[0, micro] = jnp.where(left, upper_cot, pltpu.roll(lower_cot, half_width, 1)).astype(
+            jnp.bfloat16
+        )
+        packed[1, micro] = jnp.where(left, pltpu.roll(upper_cot, half_width, 1), lower_cot).astype(
+            jnp.bfloat16
+        )
     first_sums.wait()
     totals = first_sums.total()
     rows = []
@@ -796,6 +854,7 @@
         spatials.far(rank)
     expands.near(2)
     first_acts.wait()
+    local.start(0, 3)
     for micro in range(2):
         value = jnp.concatenate([act1_ref[slot, micro_rows(micro)] for slot in range(4)], axis=1)
         fill_columns(value, mask_all[place, micro], turned, columns, micro * PIXELS)
@@ -809,6 +868,17 @@
     sums2[place] = tile_rows(moments(second, second), 8)
     second_sums.start()
     expands.near(3)
+    for parity in range(2):
+        target = 2 * lane + parity
+
+        @pl.when(target == place)
+        def _():
+            cot_all[place] = packed[parity]
+
+        @pl.when(target != place)
+        def _():
+            cot_copy(parity, place, target).start()
+
     second_sums.wait()
     totals = second_sums.total()
     for micro in range(2):
@@ -820,7 +890,6 @@
     second_acts.start()
     inverse12_ref[...] = tile_rows(rows, 8)
     heads.wait()
-    half_width = LANES // 2
     low = lax.broadcasted_iota(jnp.int32, (1, LANES), 1) < half_width
     source = place // 2
     even = place % 2 == 0
@@ -835,6 +904,7 @@
     for rank in range(4):
         expands.far(rank)
     second_acts.wait()
+    local.start(1, 4)
     value = jnp.concatenate([act2_ref[slot] for slot in range(4)], axis=1)
     third = jnp.dot(
         value, expand_all[...].reshape(512, 512), preferred_element_type=jnp.float32
@@ -851,6 +921,18 @@
         out = normed * output_scale[...] + output_shift[...] + x_ref[micro].astype(jnp.float32)
         y_ref[micro] = (out * jax.nn.sigmoid(out)).astype(jnp.bfloat16)
     inverse3_ref[...] = tile_rows(rows, 8)
+    @pl.when(place // 2 == lane)
+    def _():
+        for step in range(1, 8):
+            cot_copy(0, (place + step) % 8, place).wait_recv()
+
+    local.start(6)
+    for parity in range(2):
+        @pl.when(2 * lane + parity != place)
+        def _():
+            cot_copy(parity, place, place).wait_send()
+
+    local.wait(0, 1, 2, 3, 4, 5, 6)
     for item in (reduces, spatials, expands, ids, heads, first_acts, second_acts):
         item.close()
     for item in (first_sums, second_sums, third_sums):
@@ -863,6 +945,15 @@
 
 def run_front(count, *arrays):
     f32, bf16 = jnp.float32, jnp.bfloat16
+    kept = (
+        (4, 2 * PIXELS, LANES),
+        (4, 2 * PIXELS, LANES),
+        (8, 64, 512),
+        (8, 9, 64, LANES),
+        (8, 64, 512),
+        (8, 2, PIXELS, LANES),
+        (8, 2, PIXELS, LANES),
+    )
     return pl.pallas_call(
         functools.partial(front_kernel, count),
         name="front",
@@ -872,18 +963,15 @@
             jax.ShapeDtypeStruct((8, 512), f32),
             jax.ShapeDtypeStruct((2, 2 * PIXELS, LANES), f32),
             jax.ShapeDtypeStruct((8, LANES), f32),
-            jax.ShapeDtypeStruct((4, 2 * PIXELS, LANES), bf16),
-            jax.ShapeDtypeStruct((4, 2 * PIXELS, LANES), bf16),
-            jax.ShapeDtypeStruct((8, 64, 512), bf16),
-            jax.ShapeDtypeStruct((8, 9, 64, LANES), bf16),
-            jax.ShapeDtypeStruct((8, 64, 512), bf16),
-            jax.ShapeDtypeStruct((8, 2, PIXELS, LANES), bf16),
             jax.ShapeDtypeStruct((2, LANES), f32),
             jax.ShapeDtypeStruct((2, PIXELS, LANES), bf16),
-        ),
-        in_specs=vmem(11),
-        out_specs=tuple(vmem(13)),
-        scratch_shapes=[
+        )
+        + tuple(jax.ShapeDtypeStruct(shape, bf16) for shape in kept),
+        in_specs=vmem(13),
+        out_specs=tuple(vmem(7) + anywhere(7)),
+        scratch_shapes=[pltpu.VMEM(shape, bf16) for shape in kept]
+        + [
+            pltpu.VMEM((2, 2, PIXELS, LANES), bf16),
             pltpu.VMEM((3, 2 * PAD + PIXELS, 512), bf16),
             pltpu.VMEM((2 * PIXELS, 9 * 512), bf16),
             pltpu.VMEM((4, 2 * PIXELS, LANES), bf16),
@@ -898,7 +986,12 @@
         + exchange_sems(8)
         + [pltpu.SemaphoreType.DMA((4,))] * 2
         + exchange_sems(8) * 3
-        + exchange_sems(4) * 3,
+        + exchange_sems(4) * 3
+        + [
+            pltpu.SemaphoreType.DMA((2,)),
+            pltpu.SemaphoreType.DMA((8,)),
+            pltpu.SemaphoreType.DMA((7,)),
+        ],
         compiler_params=kernel_params(1),
     )(*arrays)
 
@@ -909,44 +1002,52 @@
         self.near_buf, self.near_got = near_buf, near_got
         self.far_send, self.far_recv, self.near_send, self.near_recv = sems
 
+    def far_copy(self, level, place):
+        return push(
+            self.far_buf.at[level],
+            self.far_got.at[level],
+            self.far_send.at[level],
+            self.far_recv.at[level],
+            place,
+            lax.axis_index("chan"),
+        )
+
+    def near_copy(self, rank, level, place):
+        return push(
+            self.near_buf.at[rank - 1],
+            self.near_got.at[level],
+            self.near_send.at[rank - 1],
+            self.near_recv.at[level],
+            place,
+            lax.axis_index("chan"),
+        )
+
     def start(self):
         place, lane, depth, side, _, _ = whereabouts()
-        for level in range(4):
+        for rank in (3, 2, 1, 0):
+            level = ranked(depth, rank)
             self.far_buf[level] = self.part[level * 2 + 1 - side].astype(jnp.bfloat16)
-        push(
-            self.far_buf, self.far_got, self.far_send, self.far_recv, depth * 2 + 1 - side, lane
-        ).start()
+            self.far_copy(level, depth * 2 + 1 - side).start()
 
     def middle(self):
         place, lane, depth, side, _, _ = whereabouts()
-        push(self.far_buf, self.far_got, self.far_send, self.far_recv, place, lane).wait()
-        for rank in range(1, 4):
+        for rank in (3, 2, 1):
             level = ranked(depth, rank)
+            self.far_copy(level, place).wait_recv()
             self.near_buf[rank - 1] = (
                 self.part[level * 2 + side] + self.far_got[level].astype(jnp.float32)
             ).astype(jnp.bfloat16)
-            push(
-                self.near_buf.at[rank - 1],
-                self.near_got.at[depth],
-                self.near_send.at[rank - 1],
-                self.near_recv.at[depth],
-                level * 2 + side,
-                lane,
-            ).start()
+            self.near_copy(rank, depth, level * 2 + side).start()
 
     def finish(self):
         place, lane, depth, side, _, _ = whereabouts()
+        self.far_copy(depth, place).wait_recv()
         result = self.part[place] + self.far_got[depth].astype(jnp.float32)
-        for rank in range(1, 4):
+        for level in range(4):
+            self.far_copy(level, place).wait_send()
+        for rank in (3, 2, 1):
             level = ranked(depth, rank)
-            push(
-                self.near_buf.at[rank - 1],
-                self.near_got.at[level],
-                self.near_send.at[rank - 1],
-                self.near_recv.at[level],
-                place,
-                lane,
-            ).wait()
+            self.near_copy(rank, level, place).wait()
             result = result + self.near_got[level].astype(jnp.float32)
         return result
 
@@ -963,8 +1064,8 @@
 
 def scatter_sems():
     return [
-        pltpu.SemaphoreType.DMA,
-        pltpu.SemaphoreType.DMA,
+        pltpu.SemaphoreType.DMA((4,)),
+        pltpu.SemaphoreType.DMA((4,)),
         pltpu.SemaphoreType.DMA((3,)),
         pltpu.SemaphoreType.DMA((4,)),
     ]
@@ -1010,6 +1111,7 @@
     gate_out,
     output_scale_out,
     output_shift_out,
+    head_out,
     head_grad,
     block_all,
     head_back,
@@ -1209,14 +1311,17 @@
     for micro in range(2):
         features_ref[micro] = features_ref[micro] + more[micro_rows(micro)]
     weigh(6)
+    weigh(7)
+    store = pltpu.make_async_copy(head_grad, head_out, sems[26].at[3])
+    store.start()
     reduces.middle()
-    weigh(7)
     result = spatials.finish()
     for number in range(9):
         spatial_out[number] = result[:, number * LANES : (number + 1) * LANES]
     reduce_out[...] = reduces.finish()
     for item in (first, second, third, heads, acts):
         item.close()
+    store.wait()
 
 
 def run_rear(count, *arrays):
@@ -1239,8 +1344,9 @@
             jax.ShapeDtypeStruct((9, 256, 512), f32),
         ),
         in_specs=vmem(18) + [pl.BlockSpec(memory_space=pl.ANY)] * 3,
-        out_specs=tuple(vmem(12)),
+        out_specs=tuple(vmem(11) + anywhere(1)),
         scratch_shapes=[
+            pltpu.VMEM((9, 256, 512), f32),
             pltpu.VMEM((8, 2, PIXELS, 512), bf16),
             pltpu.VMEM((2, 2, 8, PIXELS, LANES), bf16),
             pltpu.VMEM((8, 2, PIXELS, LANES), bf16),
@@ -1267,7 +1373,7 @@
         + exchange_sems(4) * 2
         + scatter_sems() * 3
         + [pltpu.SemaphoreType.DMA((4,))] * 2
-        + [pltpu.SemaphoreType.DMA((3,))],
+        + [pltpu.SemaphoreType.DMA((4,))],
         compiler_params=kernel_params(5),
     )(*arrays)
 
@@ -1456,21 +1562,30 @@
 def middle_kernel(
     count,
     block_ref,
-    head_ref,
-    distil_ref,
-    mask_ref,
-    depth_cot,
-    segment_cot,
     bias_ref,
     mine_ref,
+    head_hbm,
+    distil_hbm,
+    mask_hbm,
+    depth_hbm,
+    segment_hbm,
+    cot_hbm,
     depth_out,
     segment_out,
     distil_grad,
     gate_sums,
     head_sums,
     back_out,
+    block_hbm,
+    back_hbm,
     block_all,
     head_back,
+    head_ref,
+    distil_ref,
+    mask_ref,
+    depth_cot,
+    segment_cot,
+    cot_all,
     head_weight,
     mixed,
     mixed_back,
@@ -1480,10 +1595,8 @@
     norm_ref,
     slope_ref,
     grads_all,
-    packed,
     own_stage,
     own_got,
-    cot_all,
     stage,
     got,
     part_ref,
@@ -1504,27 +1617,30 @@
     reduce = Reduce(part_ref, keep, far_buf, far_got, line_buf, line_got, sems[6:10])
     ahead = Channels(stage, got, sems[10], sems[11], acts, sems[12], sems[13])
     behind = Channels(stage, got, sems[10], sems[11], head_back, sems[14], sems[15])
-    own_sem, own_recv, cot_sem, cot_recv = sems[16:20]
+    own_sem, own_recv = sems[16:18]
+    local = Local(
+        (
+            (head_hbm, head_ref),
+            (mask_hbm, mask_ref),
+            (distil_hbm, distil_ref),
+            (depth_hbm, depth_cot),
+            (segment_hbm, segment_cot),
+            (cot_hbm, cot_all),
+            (block_all, block_hbm),
+            (head_back, back_hbm),
+        ),
+        sems[18],
+    )
+    local.start(0, 1, 2, 3, 4, 5)
 
     greet(batch_peers() + chan_peers())
     block_all[place] = block_ref[...]
     gather.start(0)
     clear_edges(turned)
+    local.wait(0)
     for number in range(9):
         head_weight[number * 512 : (number + 1) * 512] = head_ref[number].T
-    for micro in range(2):
-        first, second = (ref[micro].astype(jnp.float32) for ref in (depth_cot, segment_cot))
-        packed[0, micro] = jnp.where(low, first, pltpu.roll(second, half_width, 1)).astype(
-            jnp.bfloat16
-        )
-        packed[1, micro] = jnp.where(low, pltpu.roll(first, half_width, 1), second).astype(
-            jnp.bfloat16
-        )
-
-    def cot_copy(parity, slot, target):
-        return push(
-            packed.at[parity], cot_all.at[slot], cot_sem.at[parity], cot_recv.at[slot], target, lane
-        )
+    local.wait(1)
 
     def forward_step(step, _):
         block, micro = gather.next(step)
@@ -1534,20 +1650,12 @@
 
         @pl.when(step == 0)
         def _():
+            local.wait(2)
             prepare_mixed()
 
-        @pl.when(step == 2)
-        def _():
-            for parity in range(2):
-                target = 2 * lane + parity
-
-                @pl.when(target == place)
-                def _():
-                    cot_all[place] = packed[parity]
-
-                @pl.when(target != place)
-                def _():
-                    cot_copy(parity, place, target).start()
+        @pl.when(step == 1)
+        def _():
+            gather.start(1)
 
         @pl.when(step == 4)
         def _():
@@ -1616,9 +1724,6 @@
 
             lax.fori_loop(0, 4, activate, 0)
 
-    lax.fori_loop(0, 16, forward_step, 0)
-    ahead.finish(0)
-
     def own_copy(block, micro, slot, target):
         return push(
             own_stage.at[block, micro],
@@ -1645,8 +1750,6 @@
                 return 0
 
             lax.fori_loop(1, 8, pack, 0)
-
-    send_own(0)
 
     def act_value(block, micro):
         return jnp.concatenate([acts[half, micro, block] for half in range(2)], axis=1)
@@ -1704,26 +1807,24 @@
         @pl.when(step == 6)
         def _():
             ahead.finish(1)
+            ahead.sent()
             send_own(1)
 
         @pl.when(step == 11)
         def _():
+            local.wait(3, 4)
             gate(0)
             gather_back.start(0)
 
+        @pl.when(step == 15)
+        def _():
+            gate(1)
+            gather_back.start(1)
+            ahead.close()
+
         return 0
 
-    lax.fori_loop(0, 16, distil_step, 0)
-    gate(1)
-    ahead.sent()
-    ahead.close()
     distil_grad[...] = jnp.zeros_like(distil_grad)
-
-    @pl.when(source)
-    def _():
-        for step in range(1, 8):
-            other = (place + step) % 8
-            cot_copy(0, other, place).wait_recv()
 
     def back_step(step, _):
         block, micro = gather_back.next(step)
@@ -1782,9 +1883,6 @@
                 return 0
 
             lax.fori_loop(0, 4, activate, 0)
-
-    lax.fori_loop(0, 16, back_step, 0)
-    behind.finish(0)
 
     def head_value(block, micro):
         return jnp.concatenate([head_back[half, micro, block] for half in range(2)], axis=1)
@@ -1847,7 +1945,50 @@
 
         return 0
 
-    lax.fori_loop(0, 16, block_step, 0)
+    def schedule(turn, _):
+        phase = turn // 16
+        place_in = turn % 16
+        kind, step = phase, place_in
+        late = (place_in + 1) // 16
+        kind = phase + late
+        step = place_in * (1 - late)
+        back = (1 - (place_in + 15) // 16) * ((phase + 15) // 16)
+        kind = kind - back
+        step = step + 15 * back
+
+        @pl.when(kind == 0)
+        def _():
+            forward_step(step, 0)
+
+        @pl.when((kind == 1) & (step == 0))
+        def _():
+            ahead.finish(0)
+            send_own(0)
+
+        @pl.when(kind == 1)
+        def _():
+            distil_step(step, 0)
+
+        @pl.when((kind == 2) & (step == 0))
+        def _():
+            local.wait(5)
+
+        @pl.when(kind == 2)
+        def _():
+            back_step(step, 0)
+
+        @pl.when((kind == 3) & (step == 0))
+        def _():
+            behind.finish(0)
+            local.start(6)
+
+        @pl.when(kind == 3)
+        def _():
+            block_step(step, 0)
+
+        return 0
+
+    lax.fori_loop(0, 65, schedule, 0)
     for micro in range(2):
         reduce.close(micro)
         back_out[micro_rows(micro)] = keep[micro]
@@ -1855,16 +1996,15 @@
     behind.close()
     gather.close()
     gather_back.close()
-    for parity in range(2):
-        @pl.when(2 * lane + parity != place)
-        def _():
-            cot_copy(parity, place, place).wait_send()
+    local.start(7)
 
     @pl.when(source)
     def _():
         for micro in range(2):
             for step in range(1, 8):
                 own_copy((place + step) % 8, micro, 0, place).wait_send()
+
+    local.wait(6, 7)
 
 
 def run_middle(count, *arrays):
@@ -1884,9 +2024,17 @@
             jax.ShapeDtypeStruct((8, 2) + block, bf16),
             jax.ShapeDtypeStruct((2, 2, 8, PIXELS, LANES), bf16),
         ),
-        in_specs=vmem(8),
-        out_specs=tuple(vmem(8)),
+        in_specs=vmem(3) + anywhere(6),
+        out_specs=tuple(vmem(6) + anywhere(2)),
         scratch_shapes=[
+            pltpu.VMEM((8, 2) + block, bf16),
+            pltpu.VMEM((2, 2, 8, PIXELS, LANES), bf16),
+            pltpu.VMEM((9, 256, 512), bf16),
+            pltpu.VMEM((2, 9, 4, 64, LANES), bf16),
+            pltpu.VMEM((8, 2, PIXELS, LANES), bf16),
+            pltpu.VMEM((2, PIXELS, LANES), bf16),
+            pltpu.VMEM((2, PIXELS, LANES), bf16),
+            pltpu.VMEM((8, 2, PIXELS, LANES), bf16),
             pltpu.VMEM((9 * 512, 256), bf16),
             pltpu.VMEM((9 * 256, 512), bf16),
             pltpu.VMEM((9 * 512, 256), bf16),
@@ -1896,10 +2044,8 @@
             pltpu.VMEM((8, PIXELS, LANES), f32),
             pltpu.VMEM((8, PIXELS, LANES), f32),
             pltpu.VMEM((8, 2) + block, bf16),
-            pltpu.VMEM((2, 2, PIXELS, LANES), bf16),
             pltpu.VMEM((8, 2, PIXELS, LANES), bf16),
             pltpu.VMEM((2, 2, PIXELS, LANES), bf16),
-            pltpu.VMEM((8, 2, PIXELS, LANES), bf16),
             pltpu.VMEM((4, 8, PIXELS, LANES), bf16),
             pltpu.VMEM((4, 8, PIXELS, LANES), bf16),
             pltpu.VMEM(block, f32),
@@ -1914,7 +2060,7 @@
         + [dma((2, 4)), dma((2, 4)), dma((2, 3)), dma((2, 5))]
         + [dma((4, 8)), dma((4, 8))]
         + [dma((3, 4)), dma((2, 2, 4))] * 2
-        + [dma((8, 2)), dma((2, 2)), dma((2,)), dma((8,))],
+        + [dma((8, 2)), dma((2, 2)), dma((8,))],
         compiler_params=kernel_params(2),
     )(*arrays)
 
@@ -1980,7 +2126,7 @@
     pixels = row_count * column_count
     count = float(lax.axis_size("batch") * pixels)
     x = features.reshape(canvases, pixels, -1)
-    ids = jnp.pad(image_ids.reshape(canvases, pixels).astype(jnp.float32), ((0, 6), (0, 0)))
+    cots = [item.reshape(canvases, pixels, LANES) for item in (depth_cotangent, segment_cotangent)]
     block_params = (block_scale, block_shift)
     output_params = (output_scale[None], output_shift[None])
     (
@@ -1989,18 +2135,19 @@
         inverse3,
         norm12,
         inverse12,
+        mine,
+        mask,
         act1,
         act2,
         reduce_all,
         spatial_all,
         expand_all,
         mask_all,
-        mine,
-        mask,
+        cot_all,
     ) = run_front(
         count,
         x,
-        ids,
+        image_ids.reshape(canvases, pixels),
         reduce_weight.T,
         spatial_weight,
         expand_weight,
@@ -2008,17 +2155,18 @@
         *output_params,
         head_scale,
         head_shift,
+        *cots,
     )
     depth_out, segment_out, distil_grad, gate_sums, head_sums, block_grad, block_all, back_all = run_middle(
         count,
         block_out,
+        gate_bias,
+        mine,
         head_weights.transpose(0, 2, 3, 1).reshape(9, -1, head_weights.shape[1]),
         distil_weights,
         mask_all,
-        depth_cotangent.reshape(canvases, pixels, LANES),
-        segment_cotangent.reshape(canvases, pixels, LANES),
-        gate_bias,
-        mine,
+        *cots,
+        cot_all,
     )
     (
         features_grad,

time: 378 us -> 363 us (0.960)
  Pallas kernels: 375 us -> 360 us
    pallas_call x1, Pallas kernels: 231 us -> 223 us  [run_middle(): pl.pallas_call(functools.partial(middle_kernel, count), name='middle', ou...]
    pallas_call x1, Pallas kernels: 75 us -> 67.4 us  [run_rear(): pl.pallas_call(functools.partial(rear_kernel, count), name='rear', out_sh...]
where the time goes in v6:
time: 363 us; the launch traced here: 362 us
  Pallas kernels  360 us (99%)
    pallas_call x1, Pallas kernels, run_middle(): pl.pallas_call(functools.partial(middle_kernel, count), name='middle', ou...  223 us
    pallas_call x1, Pallas kernels, run_rear(): pl.pallas_call(functools.partial(rear_kernel, count), name='rear', out_sh...  67.4 us
    pallas_call x1, Pallas kernels, run_front(): pl.pallas_call(functools.partial(front_kernel, count), name='front', out_...  61.4 us
    pallas_call x1, Pallas kernels, run_finish(): pl.pallas_call(functools.partial(finish_kernel, len(arrays)), name='finis...  7.63 us

profile of v6, /device:TPU:0, one launch (start us, length us, event | category | flops | bytes accessed | tf_op | source)
XLA Modules:
  0.0 361.9 jit_solution(14057394110678966088)
XLA Ops:
  0.6 1.4 reshape.58.ids_ref
  2.0 61.4 %front.1 = (bf16[2,256,512]{2,1,0:T(8,128)(2,1)}, f32[512,512]{1,0:T(8,128)}, f32[8,512]{1,0:T(8,128)}, f32[2,512,128]{2,1,0:T(8,128)}, f32[8,128]{1,0:T(8,128)}...) custom-call(bf16[2,256,512]{2,1,0:T(8,128)(2,1)} %bitcast.19, ...), custom_call_target="tpu_custom_call" | custom-call | tf_op jit(solution)/shard_map/front/pallas_call | solution.py:957
  63.4 223.2 %middle.1 = (bf16[2,256,128]{2,1,0:T(8,128)(2,1)}, bf16[2,256,128]{2,1,0:T(8,128)(2,1)}, f32[2,9,4,64,128]{4,3,2,1,0:T(8,128)}, f32[2,128]{1,0:T(2,128)}, f32[2,...) custom-call(bf16[2,256,512]{2,1,0:T(8,128)(2,1)} %get-tuple-element.64, ...), custom_call_target="tpu_custom_call" | custom-call | tf_op jit(solution)/shard_map/middle/pallas_call | solution.py:2014
  286.6 67.4 %rear.1 = (f32[2,256,512]{2,1,0:T(8,128)}, f32[64,512]{1,0:T(8,128)}, f32[9,64,128]{2,1,0:T(8,128)}, f32[64,512]{1,0:T(8,128)}, f32[2,128]{1,0:T(2,128)}, /*inde...) custom-call(f32[512,512]{1,0:T(8,128)} %get-tuple-element.70.grad_re, ...), custom_call_target="tpu_custom_call" | custom-call | tf_op jit(solution)/shard_map/rear/pallas_call | solution.py:1329
  354.0 7.6 %finish.1 = (bf16[2,256,128]{2,1,0:T(8,128)(2,1)}, bf16[2,256,128]{2,1,0:T(8,128)(2,1)}, f32[2,256,512]{2,1,0:T(8,128)}, f32[64,512]{1,0:T(8,128)}, f32[9,64,128...) custom-call(bf16[2,256,128]{2,1,0:T(8,128)(2,1)} %get-tuple-element., ...), custom_call_target="tpu_custom_call" | custom-call | tf_op jit(solution)/shard_map/finish/pallas_call | solution.py:2095

commit v7 on v6

--- a/solution.py
+++ b/solution.py
@@ -467,8 +467,9 @@
 
 
 class Gather:
-    def __init__(self, values, recv, cross, line, parts):
-        self.values, self.recv, self.cross, self.line, self.parts = values, recv, cross, line, parts
+    def __init__(self, values, recv, cross, line, parts, direct=False):
+        self.values, self.recv, self.cross, self.line = values, recv, cross, line
+        self.parts, self.direct = parts, direct
 
     def view(self, block, part):
         return self.values.at[block] if self.parts == 1 else self.values.at[block, part]
@@ -480,6 +481,13 @@
 
     def start(self, part=0):
         place, lane, depth, side, _, _ = whereabouts()
+        if self.direct:
+            self.copy(place, part, self.cross.at[0, part], depth, 1 - side).start()
+            for rank in range(1, 4):
+                self.copy(
+                    place, part, self.line.at[0, rank, part], ranked(depth, rank), side
+                ).start()
+            return
         self.copy(place, part, self.line.at[0, 0, part], inner(depth), side).start()
 
         @pl.when(middle(depth) == 1)
@@ -493,9 +501,13 @@
         block = ranked(depth, rank) * 2 + side
         self.copy(block, part, self.cross.at[rank, part], depth, side).wait_recv()
 
-        @pl.when(middle(depth) == 1)
-        def _():
-            self.copy(block, part, self.line.at[0, rank, part], onward(depth, rank), side).start()
+        if not self.direct:
+
+            @pl.when(middle(depth) == 1)
+            def _():
+                self.copy(
+                    block, part, self.line.at[0, rank, part], onward(depth, rank), side
+                ).start()
 
         self.copy(block, part, self.cross.at[rank, part], depth, 1 - side).start()
 
@@ -524,6 +536,10 @@
         for part in range(self.parts):
             for rank in range(4):
                 self.copy(place, part, self.cross.at[rank, part], depth, side).wait_send()
+            if self.direct:
+                for rank in range(1, 4):
+                    self.copy(place, part, self.line.at[0, rank, part], depth, side).wait_send()
+                continue
             self.copy(place, part, self.line.at[0, 0, part], depth, side).wait_send()
 
             @pl.when(middle(depth) == 1)
@@ -765,10 +781,14 @@
     sums3,
     head_all,
     ids_all,
+    raw1,
+    raw2,
+    fits1,
+    fits2,
     *sems,
 ):
     place, lane, depth, side, upper, core = whereabouts()
-    reduces = Gather(reduce_all, *sems[0:3], 1)
+    reduces = Gather(reduce_all, *sems[0:3], 1, True)
     spatials = Gather(spatial_all, *sems[3:6], 1)
     expands = Gather(expand_all, *sems[6:9], 1)
     ids = Exchange(ids_all, sems[9], sems[10], "batch")
@@ -777,8 +797,44 @@
     second_sums = Exchange(sums2, sems[15], sems[16], "batch")
     third_sums = Exchange(sums3, sems[17], sems[18], "batch")
     heads = Exchange(head_all, sems[19], sems[20], "chan")
-    first_acts = Exchange(act1_ref, sems[21], sems[22], "chan")
-    second_acts = Exchange(act2_ref, sems[23], sems[24], "chan")
+    first_raw = Exchange(raw1, sems[21], sems[22], "chan")
+    second_raw = Exchange(raw2, sems[23], sems[24], "chan")
+    first_fits = Exchange(fits1, sems[28], sems[29], "chan")
+    second_fits = Exchange(fits2, sems[30], sems[31], "chan")
+
+    def centered(value, raw):
+        rows = moments(value, value)
+        for micro in range(2):
+            raw[lane, micro_rows(micro)] = (
+                value[micro_rows(micro)] - rows[2 * micro] / PIXELS
+            ).astype(jnp.bfloat16)
+        return rows
+
+    def fit(value, rows, totals, layer, fits):
+        inverses, lines = [], []
+        for micro in range(2):
+            normed, inverse = normed_part(value, totals, micro, count)
+            norm12_ref[layer, micro_rows(micro)] = normed
+            inverses.append(inverse)
+            slope = inverse * block_scale[layer : layer + 1]
+            center = totals[2 * micro : 2 * micro + 1] / count
+            lines.append(slope)
+            lines.append(
+                (rows[2 * micro] / PIXELS - center) * slope + block_shift[layer : layer + 1]
+            )
+        fits[lane] = tile_rows(lines, 8)
+        return inverses
+
+    def activate(raw, fits, act):
+        for slot in range(4):
+            for micro in range(2):
+                out = (
+                    raw[slot, micro_rows(micro)].astype(jnp.float32)
+                    * fits[slot, 2 * micro : 2 * micro + 1]
+                    + fits[slot, 2 * micro + 1 : 2 * micro + 2]
+                )
+                act[slot, micro_rows(micro)] = (out * jax.nn.sigmoid(out)).astype(jnp.bfloat16)
+
 
     local = Local(
         (
@@ -801,9 +857,13 @@
 
     greet(batch_peers() + chan_peers())
     reduce_all[place] = reduce_ref[...]
-    ids_all[place, 0:2] = ids_ref[...].astype(jnp.float32)
-    ids_all[place, 2:8] = jnp.zeros((6, PIXELS), jnp.float32)
     reduces.start()
+    ids_all[place] = jnp.zeros((8, PIXELS), jnp.float32)
+    for micro in range(2):
+        for row in range(8):
+            ids_all[place, micro : micro + 1, row * 32 : (row + 1) * 32] = ids_ref[
+                micro, row : row + 1
+            ].astype(jnp.float32)
     ids.start()
     spatial_all[place] = spatial_ref[...]
     expand_all[place] = expand_ref[...]
@@ -824,8 +884,10 @@
     local.start(2, 5)
     spatials.near(1)
     first = pieces.finish()
-    sums1[place] = tile_rows(moments(first, first), 8)
+    first_rows = centered(first, raw1)
+    sums1[place] = tile_rows(first_rows, 8)
     first_sums.start()
+    first_raw.start()
     spatials.near(2)
     expands.start()
     spatials.near(3)
@@ -840,20 +902,15 @@
             jnp.bfloat16
         )
     first_sums.wait()
-    totals = first_sums.total()
-    rows = []
-    for micro in range(2):
-        normed, inverse = normed_part(first, totals, micro, count)
-        norm12_ref[0, micro_rows(micro)] = normed
-        rows.append(inverse)
-        out = normed * block_scale[0:1] + block_shift[0:1]
-        act1_ref[lane, micro_rows(micro)] = (out * jax.nn.sigmoid(out)).astype(jnp.bfloat16)
-    first_acts.start()
+    rows = fit(first, first_rows, first_sums.total(), 0, fits1)
+    first_fits.start()
     expands.near(1)
     for rank in range(4):
         spatials.far(rank)
     expands.near(2)
-    first_acts.wait()
+    first_raw.wait()
+    first_fits.wait()
+    activate(raw1, fits1, act1_ref)
     local.start(0, 3)
     for micro in range(2):
         value = jnp.concatenate([act1_ref[slot, micro_rows(micro)] for slot in range(4)], axis=1)
@@ -865,8 +922,10 @@
             spatial_all[:, number].reshape(512, LANES),
             preferred_element_type=jnp.float32,
         )
-    sums2[place] = tile_rows(moments(second, second), 8)
+    second_rows = centered(second, raw2)
+    sums2[place] = tile_rows(second_rows, 8)
     second_sums.start()
+    second_raw.start()
     expands.near(3)
     for parity in range(2):
         target = 2 * lane + parity
@@ -880,14 +939,8 @@
             cot_copy(parity, place, target).start()
 
     second_sums.wait()
-    totals = second_sums.total()
-    for micro in range(2):
-        normed, inverse = normed_part(second, totals, micro, count)
-        norm12_ref[1, micro_rows(micro)] = normed
-        rows.append(inverse)
-        out = normed * block_scale[1:2] + block_shift[1:2]
-        act2_ref[lane, micro_rows(micro)] = (out * jax.nn.sigmoid(out)).astype(jnp.bfloat16)
-    second_acts.start()
+    rows = rows + fit(second, second_rows, second_sums.total(), 1, fits2)
+    second_fits.start()
     inverse12_ref[...] = tile_rows(rows, 8)
     heads.wait()
     low = lax.broadcasted_iota(jnp.int32, (1, LANES), 1) < half_width
@@ -903,7 +956,9 @@
         )
     for rank in range(4):
         expands.far(rank)
-    second_acts.wait()
+    second_raw.wait()
+    second_fits.wait()
+    activate(raw2, fits2, act2_ref)
     local.start(1, 4)
     value = jnp.concatenate([act2_ref[slot] for slot in range(4)], axis=1)
     third = jnp.dot(
@@ -933,9 +988,9 @@
             cot_copy(parity, place, place).wait_send()
 
     local.wait(0, 1, 2, 3, 4, 5, 6)
-    for item in (reduces, spatials, expands, ids, heads, first_acts, second_acts):
+    for item in (reduces, spatials, expands, ids, heads, first_raw, second_raw):
         item.close()
-    for item in (first_sums, second_sums, third_sums):
+    for item in (first_sums, second_sums, third_sums, first_fits, second_fits):
         item.close()
 
 
@@ -981,6 +1036,10 @@
             pltpu.VMEM((8, 8, 512), f32),
             pltpu.VMEM((4, 8, LANES), f32),
             pltpu.VMEM((8, 8, PIXELS), f32),
+            pltpu.VMEM((4, 2 * PIXELS, LANES), bf16),
+            pltpu.VMEM((4, 2 * PIXELS, LANES), bf16),
+            pltpu.VMEM((4, 8, LANES), f32),
+            pltpu.VMEM((4, 8, LANES), f32),
         ]
         + gather_sems(1) * 3
         + exchange_sems(8)
@@ -991,7 +1050,8 @@
             pltpu.SemaphoreType.DMA((2,)),
             pltpu.SemaphoreType.DMA((8,)),
             pltpu.SemaphoreType.DMA((7,)),
-        ],
+        ]
+        + exchange_sems(4) * 2,
         compiler_params=kernel_params(1),
     )(*arrays)
 
@@ -1085,11 +1145,6 @@
     inverse3_ref,
     norm12_ref,
     inverse12_ref,
-    act1_ref,
-    act2_ref,
-    reduce_all,
-    spatial_all,
-    expand_all,
     mask_ref,
     block_scale,
     block_shift,
@@ -1100,6 +1155,11 @@
     block_hbm,
     back_hbm,
     masks_hbm,
+    act1_hbm,
+    act2_hbm,
+    reduce_hbm,
+    spatial_hbm,
+    expand_hbm,
     features_ref,
     reduce_out,
     spatial_out,
@@ -1116,6 +1176,11 @@
     block_all,
     head_back,
     mask_all,
+    act1_ref,
+    act2_ref,
+    reduce_all,
+    spatial_all,
+    expand_all,
     turned_wide,
     columns_wide,
     turned,
@@ -1145,14 +1210,21 @@
     reduces = Scatter(*reduce_bufs, sems[20:24])
     pieces_next = Pieces(stage_next, got_next, sems[24], sems[25])
 
-    loads = [
-        pltpu.make_async_copy(source, target, sems[26].at[number])
-        for number, (source, target) in enumerate(
-            ((block_hbm, block_all), (back_hbm, head_back), (masks_hbm, mask_all))
-        )
-    ]
-    for load in loads:
-        load.start()
+    local = Local(
+        (
+            (expand_hbm, expand_all),
+            (act2_hbm, act2_ref),
+            (block_hbm, block_all),
+            (back_hbm, head_back),
+            (masks_hbm, mask_all),
+            (spatial_hbm, spatial_all),
+            (act1_hbm, act1_ref),
+            (reduce_hbm, reduce_all),
+            (head_grad, head_out),
+        ),
+        sems[26],
+    )
+    local.start(0, 1, 2, 3, 4, 5, 6, 7)
 
     def weigh(block):
         for micro in range(2):
@@ -1216,8 +1288,7 @@
     sums_a[place, 4:6, 0:LANES] = gate_ref[...]
     sums_a[place, 8:16, 0:LANES] = jnp.where(place // 2 == lane, heads.total(), 0.0)
     first.start()
-    for load in loads:
-        load.wait()
+    local.wait(0, 1, 2, 3, 4)
     weigh(0)
     first.wait()
     totals = first.total()
@@ -1248,6 +1319,7 @@
     grad = grad * silu_slope(normed * block_scale[1:2] + block_shift[1:2])
     sums_b[place] = tile_rows(moments(grad, normed), 8)
     second.start()
+    local.wait(5, 6, 7)
     weigh(2)
     expands.middle()
     second.wait()
@@ -1312,8 +1384,7 @@
         features_ref[micro] = features_ref[micro] + more[micro_rows(micro)]
     weigh(6)
     weigh(7)
-    store = pltpu.make_async_copy(head_grad, head_out, sems[26].at[3])
-    store.start()
+    local.start(8)
     reduces.middle()
     result = spatials.finish()
     for number in range(9):
@@ -1321,7 +1392,7 @@
     reduce_out[...] = reduces.finish()
     for item in (first, second, third, heads, acts):
         item.close()
-    store.wait()
+    local.wait(8)
 
 
 def run_rear(count, *arrays):
@@ -1343,13 +1414,18 @@
             jax.ShapeDtypeStruct((1, 512), f32),
             jax.ShapeDtypeStruct((9, 256, 512), f32),
         ),
-        in_specs=vmem(18) + [pl.BlockSpec(memory_space=pl.ANY)] * 3,
+        in_specs=vmem(13) + anywhere(8),
         out_specs=tuple(vmem(11) + anywhere(1)),
         scratch_shapes=[
             pltpu.VMEM((9, 256, 512), f32),
             pltpu.VMEM((8, 2, PIXELS, 512), bf16),
             pltpu.VMEM((2, 2, 8, PIXELS, LANES), bf16),
             pltpu.VMEM((8, 2, PIXELS, LANES), bf16),
+            pltpu.VMEM((4, 2 * PIXELS, LANES), bf16),
+            pltpu.VMEM((4, 2 * PIXELS, LANES), bf16),
+            pltpu.VMEM((8, 64, 512), bf16),
+            pltpu.VMEM((8, 9, 64, LANES), bf16),
+            pltpu.VMEM((8, 64, 512), bf16),
             pltpu.VMEM((3, 2 * PAD + PIXELS, 512), bf16),
             pltpu.VMEM((2 * PIXELS, 9 * 512), bf16),
             pltpu.VMEM((3, 2 * PAD + PIXELS, LANES), bf16),
@@ -1373,7 +1449,7 @@
         + exchange_sems(4) * 2
         + scatter_sems() * 3
         + [pltpu.SemaphoreType.DMA((4,))] * 2
-        + [pltpu.SemaphoreType.DMA((4,))],
+        + [pltpu.SemaphoreType.DMA((9,))],
         compiler_params=kernel_params(5),
     )(*arrays)
 
@@ -1668,7 +1744,7 @@
         def _():
             normalize(0)
 
-        @pl.when(step == 14)
+        @pl.when(step == 13)
         def _():
             ahead.relay(0)
 
@@ -1796,11 +1872,11 @@
         )
         reduce.step(step)
 
-        @pl.when(step == 1)
+        @pl.when(step == 2)
         def _():
             normalize(1)
 
-        @pl.when(step == 4)
+        @pl.when(step == 5)
         def _():
             ahead.relay(1)
 
@@ -1815,12 +1891,6 @@
             local.wait(3, 4)
             gate(0)
             gather_back.start(0)
-
-        @pl.when(step == 15)
-        def _():
-            gate(1)
-            gather_back.start(1)
-            ahead.close()
 
         return 0
 
@@ -1845,7 +1915,7 @@
         def _():
             normalize_back(0)
 
-        @pl.when(step == 14)
+        @pl.when(step == 13)
         def _():
             behind.relay(0)
 
@@ -1931,11 +2001,11 @@
 
         reduce.step(step)
 
-        @pl.when(step == 1)
+        @pl.when(step == 2)
         def _():
             normalize_back(1)
 
-        @pl.when(step == 4)
+        @pl.when(step == 5)
         def _():
             behind.relay(1)
 
@@ -1946,15 +2016,11 @@
         return 0
 
     def schedule(turn, _):
-        phase = turn // 16
-        place_in = turn % 16
-        kind, step = phase, place_in
-        late = (place_in + 1) // 16
-        kind = phase + late
-        step = place_in * (1 - late)
-        back = (1 - (place_in + 15) // 16) * ((phase + 15) // 16)
-        kind = kind - back
-        step = step + 15 * back
+        phase, spot = (turn + 2) // 16, (turn + 2) % 16
+        seam = (1 - (spot + 12) // 16) * ((phase + 3) // 4)
+        odd = spot % 2
+        kind = phase - seam * odd
+        step = seam * (14 * odd + spot // 2) + (1 - seam) * (spot - 2)
 
         @pl.when(kind == 0)
         def _():
@@ -1973,6 +2039,12 @@
         def _():
             local.wait(5)
 
+        @pl.when((kind == 2) & (step == 4))
+        def _():
+            gate(1)
+            gather_back.start(1)
+            ahead.close()
+
         @pl.when(kind == 2)
         def _():
             back_step(step, 0)
@@ -1988,7 +2060,7 @@
 
         return 0
 
-    lax.fori_loop(0, 65, schedule, 0)
+    lax.fori_loop(0, 66, schedule, 0)
     for micro in range(2):
         reduce.close(micro)
         back_out[micro_rows(micro)] = keep[micro]
@@ -2147,7 +2219,7 @@
     ) = run_front(
         count,
         x,
-        image_ids.reshape(canvases, pixels),
+        image_ids,
         reduce_weight.T,
         spatial_weight,
         expand_weight,
@@ -2189,11 +2261,6 @@
         inverse3,
         norm12,
         inverse12,
-        act1,
-        act2,
-        reduce_all,
-        spatial_all,
-        expand_all,
         mask,
         *block_params,
         *output_params,
@@ -2202,6 +2269,11 @@
         block_all,
         back_all,
         mask_all,
+        act1,
+        act2,
+        reduce_all,
+        spatial_all,
+        expand_all,
     )
     outs = run_finish(
         depth_out,

time: 363 us -> 354 us (0.975)
  Pallas kernels: 360 us -> 351 us
    pallas_call x1, Pallas kernels: 223 us -> 214 us  [run_middle(): pl.pallas_call(functools.partial(middle_kernel, count), name='middle', ou...]
where the time goes in v7:
time: 354 us; the launch traced here: 352 us
  Pallas kernels  351 us (99%)
    pallas_call x1, Pallas kernels, run_middle(): pl.pallas_call(functools.partial(middle_kernel, count), name='middle', ou...  214 us
    pallas_call x1, Pallas kernels, run_rear(): pl.pallas_call(functools.partial(rear_kernel, count), name='rear', out_sh...  69.6 us
    pallas_call x1, Pallas kernels, run_front(): pl.pallas_call(functools.partial(front_kernel, count), name='front', out_...  59.5 us
    pallas_call x1, Pallas kernels, run_finish(): pl.pallas_call(functools.partial(finish_kernel, len(arrays)), name='finis...  7.63 us

profile of v7, /device:TPU:0, one launch (start us, length us, event | category | flops | bytes accessed | tf_op | source)
XLA Modules:
  0.0 351.5 jit_solution(1880092208388832315)
XLA Ops:
  0.6 59.5 %front.1 = (bf16[2,256,512]{2,1,0:T(8,128)(2,1)}, f32[512,512]{1,0:T(8,128)}, f32[8,512]{1,0:T(8,128)}, f32[2,512,128]{2,1,0:T(8,128)}, f32[8,128]{1,0:T(8,128)}...) custom-call(bf16[2,256,512]{2,1,0:T(8,128)(2,1)} %bitcast.19, ...), custom_call_target="tpu_custom_call" | custom-call | tf_op jit(solution)/shard_map/front/pallas_call | solution.py:1012
  60.2 213.9 %middle.1 = (bf16[2,256,128]{2,1,0:T(8,128)(2,1)}, bf16[2,256,128]{2,1,0:T(8,128)(2,1)}, f32[2,9,4,64,128]{4,3,2,1,0:T(8,128)}, f32[2,128]{1,0:T(2,128)}, f32[2,...) custom-call(bf16[2,256,512]{2,1,0:T(8,128)(2,1)} %get-tuple-element.64, ...), custom_call_target="tpu_custom_call" | custom-call | tf_op jit(solution)/shard_map/middle/pallas_call | solution.py:2086
  274.1 69.6 %rear.1 = (f32[2,256,512]{2,1,0:T(8,128)}, f32[64,512]{1,0:T(8,128)}, f32[9,64,128]{2,1,0:T(8,128)}, f32[64,512]{1,0:T(8,128)}, f32[2,128]{1,0:T(2,128)}, /*inde...) custom-call(f32[512,512]{1,0:T(8,128)} %get-tuple-element.70.grad_re, ...), custom_call_target="tpu_custom_call" | custom-call | tf_op jit(solution)/shard_map/rear/pallas_call | solution.py:1400
  343.7 7.6 %finish.1 = (bf16[2,256,128]{2,1,0:T(8,128)(2,1)}, bf16[2,256,128]{2,1,0:T(8,128)(2,1)}, f32[2,256,512]{2,1,0:T(8,128)}, f32[64,512]{1,0:T(8,128)}, f32[9,64,128...) custom-call(bf16[2,256,128]{2,1,0:T(8,128)(2,1)} %get-tuple-element., ...), custom_call_target="tpu_custom_call" | custom-call | tf_op jit(solution)/shard_map/finish/pallas_call | solution.py:2167

commit v8 on v7

--- a/solution.py
+++ b/solution.py
@@ -443,11 +443,19 @@
     )
 
 
-def greet(peers):
+def announce(peers):
     barrier = pltpu.get_barrier_semaphore()
     for place, lane in peers:
         pl.semaphore_signal(barrier, inc=1, device_id=(place, lane), device_id_type=MESH)
-    pl.semaphore_wait(barrier, len(peers))
+
+
+def gathered_peers(peers):
+    pl.semaphore_wait(pltpu.get_barrier_semaphore(), len(peers))
+
+
+def greet(peers):
+    announce(peers)
+    gathered_peers(peers)
 
 
 def batch_peers():
@@ -764,6 +772,7 @@
     expand_out,
     mask_out,
     cot_out,
+    raw_out,
     act1_ref,
     act2_ref,
     reduce_all,
@@ -811,19 +820,19 @@
         return rows
 
     def fit(value, rows, totals, layer, fits):
-        inverses, lines = [], []
+        inverses, offsets, lines = [], [], []
         for micro in range(2):
             normed, inverse = normed_part(value, totals, micro, count)
             norm12_ref[layer, micro_rows(micro)] = normed
             inverses.append(inverse)
             slope = inverse * block_scale[layer : layer + 1]
             center = totals[2 * micro : 2 * micro + 1] / count
+            offset = rows[2 * micro] / PIXELS - center
+            offsets.append(offset * inverse)
             lines.append(slope)
-            lines.append(
-                (rows[2 * micro] / PIXELS - center) * slope + block_shift[layer : layer + 1]
-            )
+            lines.append(offset * slope + block_shift[layer : layer + 1])
         fits[lane] = tile_rows(lines, 8)
-        return inverses
+        return inverses, offsets
 
     def activate(raw, fits, act):
         for slot in range(4):
@@ -845,6 +854,7 @@
             (expand_all, expand_out),
             (mask_all, mask_out),
             (cot_all, cot_out),
+            (raw1, raw_out),
         ),
         sems[27],
     )
@@ -855,22 +865,23 @@
             packed.at[parity], cot_all.at[slot], cot_sem.at[parity], cot_recv.at[slot], target, lane
         )
 
-    greet(batch_peers() + chan_peers())
+    announce(batch_peers() + chan_peers())
     reduce_all[place] = reduce_ref[...]
-    reduces.start()
     ids_all[place] = jnp.zeros((8, PIXELS), jnp.float32)
     for micro in range(2):
         for row in range(8):
             ids_all[place, micro : micro + 1, row * 32 : (row + 1) * 32] = ids_ref[
                 micro, row : row + 1
             ].astype(jnp.float32)
-    ids.start()
     spatial_all[place] = spatial_ref[...]
     expand_all[place] = expand_ref[...]
     head_all[lane, 0:4] = head_scale[...]
     head_all[lane, 4:8] = head_shift[...]
+    clear_edges(turned)
+    gathered_peers(batch_peers() + chan_peers())
+    reduces.start()
+    ids.start()
     heads.start()
-    clear_edges(turned)
     for rank in range(1, 4):
         reduces.near(rank)
     spatials.start()
@@ -902,7 +913,7 @@
             jnp.bfloat16
         )
     first_sums.wait()
-    rows = fit(first, first_rows, first_sums.total(), 0, fits1)
+    rows, offsets = fit(first, first_rows, first_sums.total(), 0, fits1)
     first_fits.start()
     expands.near(1)
     for rank in range(4):
@@ -911,7 +922,7 @@
     first_raw.wait()
     first_fits.wait()
     activate(raw1, fits1, act1_ref)
-    local.start(0, 3)
+    local.start(0, 3, 7)
     for micro in range(2):
         value = jnp.concatenate([act1_ref[slot, micro_rows(micro)] for slot in range(4)], axis=1)
         fill_columns(value, mask_all[place, micro], turned, columns, micro * PIXELS)
@@ -939,7 +950,7 @@
             cot_copy(parity, place, target).start()
 
     second_sums.wait()
-    rows = rows + fit(second, second_rows, second_sums.total(), 1, fits2)
+    rows = rows + fit(second, second_rows, second_sums.total(), 1, fits2)[0] + offsets
     second_fits.start()
     inverse12_ref[...] = tile_rows(rows, 8)
     heads.wait()
@@ -987,7 +998,7 @@
         def _():
             cot_copy(parity, place, place).wait_send()
 
-    local.wait(0, 1, 2, 3, 4, 5, 6)
+    local.wait(0, 1, 2, 3, 4, 5, 6, 7)
     for item in (reduces, spatials, expands, ids, heads, first_raw, second_raw):
         item.close()
     for item in (first_sums, second_sums, third_sums, first_fits, second_fits):
@@ -1021,9 +1032,9 @@
             jax.ShapeDtypeStruct((2, LANES), f32),
             jax.ShapeDtypeStruct((2, PIXELS, LANES), bf16),
         )
-        + tuple(jax.ShapeDtypeStruct(shape, bf16) for shape in kept),
+        + tuple(jax.ShapeDtypeStruct(shape, bf16) for shape in kept + (kept[0],)),
         in_specs=vmem(13),
-        out_specs=tuple(vmem(7) + anywhere(7)),
+        out_specs=tuple(vmem(7) + anywhere(8)),
         scratch_shapes=[pltpu.VMEM(shape, bf16) for shape in kept]
         + [
             pltpu.VMEM((2, 2, PIXELS, LANES), bf16),
@@ -1049,7 +1060,7 @@
         + [
             pltpu.SemaphoreType.DMA((2,)),
             pltpu.SemaphoreType.DMA((8,)),
-            pltpu.SemaphoreType.DMA((7,)),
+            pltpu.SemaphoreType.DMA((8,)),
         ]
         + exchange_sems(4) * 2,
         compiler_params=kernel_params(1),
@@ -1160,6 +1171,7 @@
     reduce_hbm,
     spatial_hbm,
     expand_hbm,
+    raw_hbm,
     features_ref,
     reduce_out,
     spatial_out,
@@ -1181,6 +1193,8 @@
     reduce_all,
     spatial_all,
     expand_all,
+    raw_ref,
+    fits_all,
     turned_wide,
     columns_wide,
     turned,
@@ -1205,6 +1219,7 @@
     third = Exchange(sums_c, sems[6], sems[7], "batch")
     heads = Exchange(head_all, sems[8], sems[9], "chan")
     acts = Exchange(act_all, sems[10], sems[11], "chan")
+    fits = Exchange(fits_all, sems[27], sems[28], "chan")
     expands = Scatter(*expand_bufs, sems[12:16])
     spatials = Scatter(*spatial_bufs, sems[16:20])
     reduces = Scatter(*reduce_bufs, sems[20:24])
@@ -1221,10 +1236,11 @@
             (act1_hbm, act1_ref),
             (reduce_hbm, reduce_all),
             (head_grad, head_out),
+            (raw_hbm, raw_ref),
         ),
         sems[26],
     )
-    local.start(0, 1, 2, 3, 4, 5, 6, 7)
+    local.start(0, 1, 2, 3, 4, 5, 6, 7, 9)
 
     def weigh(block):
         for micro in range(2):
@@ -1257,7 +1273,7 @@
 
         lax.fori_loop(0, 9, tap, 0)
 
-    greet(batch_peers() + chan_peers())
+    announce(batch_peers() + chan_peers())
     clear_edges(turned_wide)
     half_width = LANES // 2
     even = place % 2 == 0
@@ -1272,29 +1288,23 @@
             for row in (first_row, second_row):
                 rows.append(jnp.where(upper == half, row, 0.0))
     head_all[lane] = jnp.concatenate(rows, axis=0)
-    heads.start()
     clear_edges(turned)
-    rows = []
+    wide_rows = []
     for micro in range(2):
         normed = norm3_ref[micro_rows(micro)]
         out = normed * output_scale[...] + output_shift[...] + x_ref[micro].astype(jnp.float32)
         value = grad_ref[micro_rows(micro)] * silu_slope(out)
         features_ref[micro] = value
-        rows.append(jnp.sum(value, axis=0, keepdims=True))
-        rows.append(jnp.sum(value * normed, axis=0, keepdims=True))
-    heads.wait()
-    sums_a[place, 0:8] = tile_rows(rows, 8)
-    sums_a[place, 8:16] = jnp.zeros((8, 512), jnp.float32)
-    sums_a[place, 4:6, 0:LANES] = gate_ref[...]
-    sums_a[place, 8:16, 0:LANES] = jnp.where(place // 2 == lane, heads.total(), 0.0)
+        wide_rows.append(jnp.sum(value, axis=0, keepdims=True))
+        wide_rows.append(jnp.sum(value * normed, axis=0, keepdims=True))
+    gathered_peers(batch_peers() + chan_peers())
+    sums_a[place] = tile_rows(wide_rows, 8)
     first.start()
+    heads.start()
     local.wait(0, 1, 2, 3, 4)
     weigh(0)
     first.wait()
     totals = first.total()
-    head_scale_out[...] = totals[8:12, 0:LANES]
-    head_shift_out[...] = totals[12:16, 0:LANES]
-    gate_out[...] = totals[4:6, 0:LANES]
     output_scale_out[...] = totals[1:2] + totals[3:4]
     output_shift_out[...] = totals[0:1] + totals[2:3]
     for micro in range(2):
@@ -1314,16 +1324,23 @@
     ).reshape(8, 64, 512)
     expands.start()
     weigh(1)
+    weigh(2)
     grad = pieces.finish()
     normed = norm12_ref[1]
     grad = grad * silu_slope(normed * block_scale[1:2] + block_shift[1:2])
-    sums_b[place] = tile_rows(moments(grad, normed), 8)
+    heads.wait()
+    sums_b[place, 0:8] = tile_rows(moments(grad, normed), 8)
+    sums_b[place, 4:6] = gate_ref[...]
+    sums_b[place, 8:16] = jnp.where(place // 2 == lane, heads.total(), 0.0)
     second.start()
-    local.wait(5, 6, 7)
-    weigh(2)
+    local.wait(5, 6, 7, 9)
+    weigh(3)
     expands.middle()
     second.wait()
     totals = second.total()
+    head_scale_out[...] = totals[8:12]
+    head_shift_out[...] = totals[12:16]
+    gate_out[...] = totals[4:6]
     block_scale_out[1:2] = totals[1:2] + totals[3:4]
     block_shift_out[1:2] = totals[0:1] + totals[2:3]
     for micro in range(2):
@@ -1349,48 +1366,72 @@
         value.T, columns[...], preferred_element_type=jnp.float32
     ).reshape(8, 64, 9 * LANES)
     spatials.start()
-    weigh(3)
+    weigh(4)
+    weigh(5)
     grad = pieces_next.finish()
     normed = norm12_ref[0]
     grad = grad * silu_slope(normed * block_scale[0:1] + block_shift[0:1])
-    sums_c[place] = tile_rows(moments(grad, normed), 8)
+    rows = moments(grad, normed)
+    sums_c[place] = tile_rows(rows, 8)
     third.start()
-    weigh(4)
+    for micro in range(2):
+        act_all[lane, micro_rows(micro)] = (
+            grad[micro_rows(micro)] - rows[2 * micro] / PIXELS
+        ).astype(jnp.bfloat16)
+    acts.start()
+    weigh(6)
     spatials.middle()
     expand_out[...] = expands.finish()
     third.wait()
     totals = third.total()
     block_scale_out[0:1] = totals[1:2] + totals[3:4]
     block_shift_out[0:1] = totals[0:1] + totals[2:3]
+    lines = []
     for micro in range(2):
-        act_all[lane, micro_rows(micro)] = back_part(
-            grad[micro_rows(micro)],
-            normed[micro_rows(micro)],
-            inverse12_ref[micro : micro + 1],
-            block_scale[0:1],
-            totals[2 * micro : 2 * micro + 1],
-            totals[2 * micro + 1 : 2 * micro + 2],
-            count,
-        )
-    acts.start()
-    weigh(5)
+        shift_sum = totals[2 * micro : 2 * micro + 1]
+        scale_sum = totals[2 * micro + 1 : 2 * micro + 2]
+        inverse = inverse12_ref[micro : micro + 1]
+        factor = block_scale[0:1] * inverse
+        lines.append(factor)
+        lines.append(-factor * scale_sum * inverse / count)
+        lines.append(
+            factor
+            * (
+                rows[2 * micro] / PIXELS
+                - (shift_sum + inverse12_ref[4 + micro : 5 + micro] * scale_sum) / count
+            )
+        )
+    fits_all[lane] = tile_rows(lines, 8)
+    fits.start()
+    weigh(7)
+    local.start(8)
     acts.wait()
-    value = jnp.concatenate([act_all[slot] for slot in range(4)], axis=1)
+    fits.wait()
+
+    def whole(slot):
+        parts = []
+        for micro in range(2):
+            line = [fits_all[slot, 3 * micro + row : 3 * micro + row + 1] for row in range(3)]
+            parts.append(
+                act_all[slot, micro_rows(micro)].astype(jnp.float32) * line[0]
+                + raw_ref[slot, micro_rows(micro)].astype(jnp.float32) * line[1]
+                + line[2]
+            )
+        return jnp.concatenate(parts, axis=0).astype(jnp.bfloat16)
+
+    value = jnp.concatenate([whole(slot) for slot in range(4)], axis=1)
     x = x_ref[...].reshape(2 * PIXELS, 512)
     reduces.part[...] = jnp.dot(value.T, x, preferred_element_type=jnp.float32).reshape(8, 64, 512)
     reduces.start()
     more = jnp.dot(value, reduce_all[...].reshape(512, 512), preferred_element_type=jnp.float32)
     for micro in range(2):
         features_ref[micro] = features_ref[micro] + more[micro_rows(micro)]
-    weigh(6)
-    weigh(7)
-    local.start(8)
     reduces.middle()
     result = spatials.finish()
     for number in range(9):
         spatial_out[number] = result[:, number * LANES : (number + 1) * LANES]
     reduce_out[...] = reduces.finish()
-    for item in (first, second, third, heads, acts):
+    for item in (first, second, third, heads, acts, fits):
         item.close()
     local.wait(8)
 
@@ -1414,7 +1455,7 @@
             jax.ShapeDtypeStruct((1, 512), f32),
             jax.ShapeDtypeStruct((9, 256, 512), f32),
         ),
-        in_specs=vmem(13) + anywhere(8),
+        in_specs=vmem(13) + anywhere(9),
         out_specs=tuple(vmem(11) + anywhere(1)),
         scratch_shapes=[
             pltpu.VMEM((9, 256, 512), f32),
@@ -1426,6 +1467,8 @@
             pltpu.VMEM((8, 64, 512), bf16),
             pltpu.VMEM((8, 9, 64, LANES), bf16),
             pltpu.VMEM((8, 64, 512), bf16),
+            pltpu.VMEM((4, 2 * PIXELS, LANES), bf16),
+            pltpu.VMEM((4, 8, LANES), f32),
             pltpu.VMEM((3, 2 * PAD + PIXELS, 512), bf16),
             pltpu.VMEM((2 * PIXELS, 9 * 512), bf16),
             pltpu.VMEM((3, 2 * PAD + PIXELS, LANES), bf16),
@@ -1434,8 +1477,8 @@
             pltpu.VMEM((4, 2 * PIXELS, LANES), bf16),
             pltpu.VMEM((4, 2 * PIXELS, LANES), bf16),
             pltpu.VMEM((4, 2 * PIXELS, LANES), bf16),
-            pltpu.VMEM((8, 16, 512), f32),
-            pltpu.VMEM((8, 8, LANES), f32),
+            pltpu.VMEM((8, 8, 512), f32),
+            pltpu.VMEM((8, 16, LANES), f32),
             pltpu.VMEM((8, 8, LANES), f32),
             pltpu.VMEM((4, 8, LANES), f32),
             pltpu.VMEM((4, 2 * PIXELS, LANES), bf16),
@@ -1449,7 +1492,8 @@
         + exchange_sems(4) * 2
         + scatter_sems() * 3
         + [pltpu.SemaphoreType.DMA((4,))] * 2
-        + [pltpu.SemaphoreType.DMA((9,))],
+        + [pltpu.SemaphoreType.DMA((10,))]
+        + exchange_sems(4),
         compiler_params=kernel_params(5),
     )(*arrays)
 
@@ -1995,11 +2039,11 @@
         )
         item, late = staggered(step)
 
+        reduce.step(step)
+
         @pl.when(late == 1)
         def _():
             weigh(item)
-
-        reduce.step(step)
 
         @pl.when(step == 2)
         def _():
@@ -2039,7 +2083,7 @@
         def _():
             local.wait(5)
 
-        @pl.when((kind == 2) & (step == 4))
+        @pl.when((kind == 2) & (step == 6))
         def _():
             gate(1)
             gather_back.start(1)
@@ -2216,6 +2260,7 @@
         expand_all,
         mask_all,
         cot_all,
+        raw,
     ) = run_front(
         count,
         x,
@@ -2274,6 +2319,7 @@
         reduce_all,
         spatial_all,
         expand_all,
+        raw,
     )
     outs = run_finish(
         depth_out,

time: 354 us -> 344 us (0.972)
  Pallas kernels: 351 us -> 343 us
    pallas_call x1, Pallas kernels: 69.6 us -> 62.2 us  [run_rear(): pl.pallas_call(functools.partial(rear_kernel, count), name='rear', out_sh...]
where the time goes in v8:
time: 344 us
  Pallas kernels  343 us (100%)
    pallas_call x1, Pallas kernels, run_middle(): pl.pallas_call(functools.partial(middle_kernel, count), name='middle', ou...  214 us
    pallas_call x1, Pallas kernels, run_rear(): pl.pallas_call(functools.partial(rear_kernel, count), name='rear', out_sh...  62.2 us
    pallas_call x1, Pallas kernels, run_front(): pl.pallas_call(functools.partial(front_kernel, count), name='front', out_...  59.5 us
    pallas_call x1, Pallas kernels, run_finish(): pl.pallas_call(functools.partial(finish_kernel, len(arrays)), name='finis...  7.63 us

profile of v8, /device:TPU:0, one launch (start us, length us, event | category | flops | bytes accessed | tf_op | source)
XLA Modules:
  0.0 344.1 jit_solution(13919737500281362431)
XLA Ops:
  0.6 59.5 %front.1 = (bf16[2,256,512]{2,1,0:T(8,128)(2,1)}, f32[512,512]{1,0:T(8,128)}, f32[8,512]{1,0:T(8,128)}, f32[2,512,128]{2,1,0:T(8,128)}, f32[8,128]{1,0:T(8,128)}...) custom-call(bf16[2,256,512]{2,1,0:T(8,128)(2,1)} %bitcast.19, ...), custom_call_target="tpu_custom_call" | custom-call | tf_op jit(solution)/shard_map/front/pallas_call | solution.py:1023
  60.2 214.0 %middle.1 = (bf16[2,256,128]{2,1,0:T(8,128)(2,1)}, bf16[2,256,128]{2,1,0:T(8,128)(2,1)}, f32[2,9,4,64,128]{4,3,2,1,0:T(8,128)}, f32[2,128]{1,0:T(2,128)}, f32[2,...) custom-call(bf16[2,256,512]{2,1,0:T(8,128)(2,1)} %get-tuple-element.65, ...), custom_call_target="tpu_custom_call" | custom-call | tf_op jit(solution)/shard_map/middle/pallas_call | solution.py:2130
  274.1 62.2 %rear.1 = (f32[2,256,512]{2,1,0:T(8,128)}, f32[64,512]{1,0:T(8,128)}, f32[9,64,128]{2,1,0:T(8,128)}, f32[64,512]{1,0:T(8,128)}, f32[2,128]{1,0:T(2,128)}, /*inde...) custom-call(f32[512,512]{1,0:T(8,128)} %get-tuple-element.71.grad_re, ...), custom_call_target="tpu_custom_call" | custom-call | tf_op jit(solution)/shard_map/rear/pallas_call | solution.py:1441
  336.3 7.6 %finish.1 = (bf16[2,256,128]{2,1,0:T(8,128)(2,1)}, bf16[2,256,128]{2,1,0:T(8,128)(2,1)}, f32[2,256,512]{2,1,0:T(8,128)}, f32[64,512]{1,0:T(8,128)}, f32[9,64,128...) custom-call(bf16[2,256,128]{2,1,0:T(8,128)(2,1)} %get-tuple-element., ...), custom_call_target="tpu_custom_call" | custom-call | tf_op jit(solution)/shard_map/finish/pallas_call | solution.py:2211

commit v9 on v8

--- a/solution.py
+++ b/solution.py
@@ -1692,12 +1692,13 @@
     cot_hbm,
     depth_out,
     segment_out,
-    distil_grad,
     gate_sums,
     head_sums,
     back_out,
     block_hbm,
     back_hbm,
+    distil_out,
+    distil_grad,
     block_all,
     head_back,
     head_ref,
@@ -1748,6 +1749,7 @@
             (cot_hbm, cot_all),
             (block_all, block_hbm),
             (head_back, back_hbm),
+            (distil_grad, distil_out),
         ),
         sems[18],
     )
@@ -2056,6 +2058,7 @@
         @pl.when(step == 6)
         def _():
             behind.finish(1)
+            local.start(7)
 
         return 0
 
@@ -2105,6 +2108,7 @@
         return 0
 
     lax.fori_loop(0, 66, schedule, 0)
+    local.start(8)
     for micro in range(2):
         reduce.close(micro)
         back_out[micro_rows(micro)] = keep[micro]
@@ -2112,7 +2116,6 @@
     behind.close()
     gather.close()
     gather_back.close()
-    local.start(7)
 
     @pl.when(source)
     def _():
@@ -2120,7 +2123,7 @@
             for step in range(1, 8):
                 own_copy((place + step) % 8, micro, 0, place).wait_send()
 
-    local.wait(6, 7)
+    local.wait(6, 7, 8)
 
 
 def run_middle(count, *arrays):
@@ -2133,16 +2136,17 @@
         out_shape=(
             jax.ShapeDtypeStruct((2, PIXELS, LANES), bf16),
             jax.ShapeDtypeStruct((2, PIXELS, LANES), bf16),
-            jax.ShapeDtypeStruct((2, 9, 4, 64, LANES), f32),
             jax.ShapeDtypeStruct((2, LANES), f32),
             jax.ShapeDtypeStruct((2, LANES), f32),
             jax.ShapeDtypeStruct((2 * PIXELS, 512), f32),
             jax.ShapeDtypeStruct((8, 2) + block, bf16),
             jax.ShapeDtypeStruct((2, 2, 8, PIXELS, LANES), bf16),
+            jax.ShapeDtypeStruct((2, 9, 4, 64, LANES), f32),
         ),
         in_specs=vmem(3) + anywhere(6),
-        out_specs=tuple(vmem(6) + anywhere(2)),
+        out_specs=tuple(vmem(5) + anywhere(3)),
         scratch_shapes=[
+            pltpu.VMEM((2, 9, 4, 64, LANES), f32),
             pltpu.VMEM((8, 2) + block, bf16),
             pltpu.VMEM((2, 2, 8, PIXELS, LANES), bf16),
             pltpu.VMEM((9, 256, 512), bf16),
@@ -2176,7 +2180,7 @@
         + [dma((2, 4)), dma((2, 4)), dma((2, 3)), dma((2, 5))]
         + [dma((4, 8)), dma((4, 8))]
         + [dma((3, 4)), dma((2, 2, 4))] * 2
-        + [dma((8, 2)), dma((2, 2)), dma((8,))],
+        + [dma((8, 2)), dma((2, 2)), dma((9,))],
         compiler_params=kernel_params(2),
     )(*arrays)
 
@@ -2274,7 +2278,7 @@
         head_shift,
         *cots,
     )
-    depth_out, segment_out, distil_grad, gate_sums, head_sums, block_grad, block_all, back_all = run_middle(
+    depth_out, segment_out, gate_sums, head_sums, block_grad, block_all, back_all, distil_grad = run_middle(
         count,
         block_out,
         gate_bias,

time: 344 us -> 343 us (level)
  no operation moved by 1% of the time
where the time goes in v9:
time: 343 us
  Pallas kernels  342 us (100%)
    pallas_call x1, Pallas kernels, run_middle(): pl.pallas_call(functools.partial(middle_kernel, count), name='middle', ou...  212 us
    pallas_call x1, Pallas kernels, run_rear(): pl.pallas_call(functools.partial(rear_kernel, count), name='rear', out_sh...  62.8 us
    pallas_call x1, Pallas kernels, run_front(): pl.pallas_call(functools.partial(front_kernel, count), name='front', out_...  59.5 us
    pallas_call x1, Pallas kernels, run_finish(): pl.pallas_call(functools.partial(finish_kernel, len(arrays)), name='finis...  7.63 us

profile of v9, /device:TPU:0, one launch (start us, length us, event | category | flops | bytes accessed | tf_op | source)
XLA Modules:
  0.0 342.7 jit_solution(17057786260944403327)
XLA Ops:
  0.6 59.5 %front.1 = (bf16[2,256,512]{2,1,0:T(8,128)(2,1)}, f32[512,512]{1,0:T(8,128)}, f32[8,512]{1,0:T(8,128)}, f32[2,512,128]{2,1,0:T(8,128)}, f32[8,128]{1,0:T(8,128)}...) custom-call(bf16[2,256,512]{2,1,0:T(8,128)(2,1)} %bitcast.19, ...), custom_call_target="tpu_custom_call" | custom-call | tf_op jit(solution)/shard_map/front/pallas_call | solution.py:1023
  60.2 211.8 %middle.1 = (bf16[2,256,128]{2,1,0:T(8,128)(2,1)}, bf16[2,256,128]{2,1,0:T(8,128)(2,1)}, f32[2,128]{1,0:T(2,128)}, f32[2,128]{1,0:T(2,128)}, f32[512,512]{1,0:T(...) custom-call(bf16[2,256,512]{2,1,0:T(8,128)(2,1)} %get-tuple-element.65, ...), custom_call_target="tpu_custom_call" | custom-call | tf_op jit(solution)/shard_map/middle/pallas_call | solution.py:2133
  272.0 62.8 %rear.1 = (f32[2,256,512]{2,1,0:T(8,128)}, f32[64,512]{1,0:T(8,128)}, f32[9,64,128]{2,1,0:T(8,128)}, f32[64,512]{1,0:T(8,128)}, f32[2,128]{1,0:T(2,128)}, /*inde...) custom-call(f32[512,512]{1,0:T(8,128)} %get-tuple-element.71.grad_re, ...), custom_call_target="tpu_custom_call" | custom-call | tf_op jit(solution)/shard_map/rear/pallas_call | solution.py:1441
  334.8 7.6 %finish.1 = (bf16[2,256,128]{2,1,0:T(8,128)(2,1)}, bf16[2,256,128]{2,1,0:T(8,128)(2,1)}, f32[2,256,512]{2,1,0:T(8,128)}, f32[64,512]{1,0:T(8,128)}, f32[9,64,128...) custom-call(bf16[2,256,128]{2,1,0:T(8,128)(2,1)} %get-tuple-element., ...), custom_call_target="tpu_custom_call" | custom-call | tf_op jit(solution)/shard_map/finish/pallas_call | solution.py:2215

commit v10 on v9

--- a/solution.py
+++ b/solution.py
@@ -1195,6 +1195,7 @@
     expand_all,
     raw_ref,
     fits_all,
+    spatial_rows,
     turned_wide,
     columns_wide,
     turned,
@@ -1334,6 +1335,10 @@
     sums_b[place, 8:16] = jnp.where(place // 2 == lane, heads.total(), 0.0)
     second.start()
     local.wait(5, 6, 7, 9)
+    for number in range(9):
+        spatial_rows[number * LANES : (number + 1) * LANES] = (
+            spatial_all[:, number].reshape(512, LANES).T
+        )
     weigh(3)
     expands.middle()
     second.wait()
@@ -1354,12 +1359,7 @@
             count,
         )
         fill_columns(value, mask_ref[micro], turned, columns, micro * PIXELS, True)
-    part = jnp.zeros((2 * PIXELS, 512), jnp.float32)
-    for number in range(9):
-        part = part + dot_last(
-            columns[:, number * LANES : (number + 1) * LANES],
-            spatial_all[:, number].reshape(512, LANES),
-        )
+    part = jnp.dot(columns[...], spatial_rows[...], preferred_element_type=jnp.float32)
     pieces_next.start(part)
     value = jnp.concatenate([act1_ref[slot] for slot in range(4)], axis=1)
     spatials.part[...] = jnp.dot(
@@ -1469,6 +1469,7 @@
             pltpu.VMEM((8, 64, 512), bf16),
             pltpu.VMEM((4, 2 * PIXELS, LANES), bf16),
             pltpu.VMEM((4, 8, LANES), f32),
+            pltpu.VMEM((9 * LANES, 512), bf16),
             pltpu.VMEM((3, 2 * PAD + PIXELS, 512), bf16),
             pltpu.VMEM((2 * PIXELS, 9 * 512), bf16),
             pltpu.VMEM((3, 2 * PAD + PIXELS, LANES), bf16),

time: 343 us -> 343 us (level)
  no operation moved by 1% of the time
where the time goes in v10:
time: 343 us
  Pallas kernels  342 us (100%)
    pallas_call x1, Pallas kernels, run_middle(): pl.pallas_call(functools.partial(middle_kernel, count), name='middle', ou...  212 us
    pallas_call x1, Pallas kernels, run_rear(): pl.pallas_call(functools.partial(rear_kernel, count), name='rear', out_sh...  62.8 us
    pallas_call x1, Pallas kernels, run_front(): pl.pallas_call(functools.partial(front_kernel, count), name='front', out_...  59.5 us
    pallas_call x1, Pallas kernels, run_finish(): pl.pallas_call(functools.partial(finish_kernel, len(arrays)), name='finis...  7.63 us

profile of v10, /device:TPU:0, one launch (start us, length us, event | category | flops | bytes accessed | tf_op | source)
XLA Modules:
  0.0 342.7 jit_solution(9113231915867469381)
XLA Ops:
  0.6 59.5 %front.1 = (bf16[2,256,512]{2,1,0:T(8,128)(2,1)}, f32[512,512]{1,0:T(8,128)}, f32[8,512]{1,0:T(8,128)}, f32[2,512,128]{2,1,0:T(8,128)}, f32[8,128]{1,0:T(8,128)}...) custom-call(bf16[2,256,512]{2,1,0:T(8,128)(2,1)} %bitcast.19, ...), custom_call_target="tpu_custom_call" | custom-call | tf_op jit(solution)/shard_map/front/pallas_call | solution.py:1023
  60.2 211.8 %middle.1 = (bf16[2,256,128]{2,1,0:T(8,128)(2,1)}, bf16[2,256,128]{2,1,0:T(8,128)(2,1)}, f32[2,128]{1,0:T(2,128)}, f32[2,128]{1,0:T(2,128)}, f32[512,512]{1,0:T(...) custom-call(bf16[2,256,512]{2,1,0:T(8,128)(2,1)} %get-tuple-element.65, ...), custom_call_target="tpu_custom_call" | custom-call | tf_op jit(solution)/shard_map/middle/pallas_call | solution.py:2134
  272.0 62.8 %rear.1 = (f32[2,256,512]{2,1,0:T(8,128)}, f32[64,512]{1,0:T(8,128)}, f32[9,64,128]{2,1,0:T(8,128)}, f32[64,512]{1,0:T(8,128)}, f32[2,128]{1,0:T(2,128)}, /*inde...) custom-call(f32[512,512]{1,0:T(8,128)} %get-tuple-element.71.grad_re, ...), custom_call_target="tpu_custom_call" | custom-call | tf_op jit(solution)/shard_map/rear/pallas_call | solution.py:1441
  334.8 7.6 %finish.1 = (bf16[2,256,128]{2,1,0:T(8,128)(2,1)}, bf16[2,256,128]{2,1,0:T(8,128)(2,1)}, f32[2,256,512]{2,1,0:T(8,128)}, f32[64,512]{1,0:T(8,128)}, f32[9,64,128...) custom-call(bf16[2,256,128]{2,1,0:T(8,128)(2,1)} %get-tuple-element., ...), custom_call_target="tpu_custom_call" | custom-call | tf_op jit(solution)/shard_map/finish/pallas_call | solution.py:2216
